TPU v7x, 512 devices: a whole 4x8x8 slice. The times are simulated.
512 devices in a mesh: gx: 32 (over z_hi, x, core), gy: 16 (over y, z_lo).
Axes of the slice: x: 4, y: 8, z: 8 (z_hi: 4, z_lo: 2; z = z_hi * 2 + z_lo), core: 2. Of those that a mesh axis runs over, the one named last changes fastest.
Arguments:
- tokens: bfloat16 [2304, 4608], P('gx', 'gy'), may hold values from -6 to 6
- pre_gain: bfloat16 [4608], P('gy'), may hold values from -0.5 to 0.5
- w_q: bfloat16 [4608, 4096], P('gx', 'gy'), may hold values from -0.09375 to 0.09375
- w_k: bfloat16 [4608, 2048], P('gx', 'gy'), may hold values from -0.09375 to 0.09375
- w_v: bfloat16 [4608, 2048], P('gx', 'gy'), may hold values from -0.09375 to 0.09375
- w_o: bfloat16 [4096, 4608], P('gy', 'gx')
- post_gain: bfloat16 [4608], P('gy'), may hold values from -0.5 to 0.5
- k_cache: bfloat16 [32768, 2048], P('gx', 'gy'), may hold values from -6 to 6
- v_cache: bfloat16 [32768, 2048], P('gx', 'gy')
- cached_len: int32 [12], replicated, may hold values from 1 to 10240, as said below
- new_len: int32 [12], replicated, may hold values from 48 to 192, as said below
- slot_offset: int32 [12], replicated, may hold values from 0 to 32575, as said below
Outputs:
- layer_out: bfloat16 [2304, 4608], P('gx', 'gy')
- k_pool: bfloat16 [32768, 2048], P('gx', 'gy')
- v_pool: bfloat16 [32768, 2048], P('gx', 'gy')
Inputs may be any that keep to these rules, and one draw needn't show every extreme that they name: `cached_len`: two requests are long: one has exactly 10240 cached tokens, the other between 10049 and 10240; the others have at most 512, and one of them has exactly 1. `new_len`: some request has all 192 slots real. Request r owns pool slots slot_offset[r] to slot_offset[r] + cached_len[r] + 191; these regions are disjoint and lie inside the pool; one starts at slot 0 and one ends at the pool's last slot.
All inputs are finite; a program needn't handle non-finite values.
Results may differ from a plain program's by a relative error of at most 0.02.
Values may be sent and summed in bfloat16 or wider, within the bound.
No kernel may reach another device: no remote copies, remote signals or barrier semaphores. Data moves between devices by JAX's collectives and lax.ppermute only.
A program may use at most 64 MiB of HBM per device.

v0:
```python
import jax
import jax.numpy as jnp
from jax import lax
from jax.sharding import PartitionSpec as P

D = 4608
HD = 128
REQS = 12
NEWTOK = 192


epsilon = 1e-06
soft_cap = 50.0
query_scale = 144.0 ** (-0.5)


def rotate(values, position, head_size):
    rows = values.shape[0]
    parts = values.reshape(rows, -1, head_size)
    half = head_size // 2
    inverse = jnp.power(10000.0, -2.0 * jnp.arange(half, dtype=jnp.float32) / head_size)
    angle = position.astype(jnp.float32)[:, None] * inverse[None, :]
    cosine = jnp.cos(angle)[:, None, :]
    sine = jnp.sin(angle)[:, None, :]
    first = parts[:, :, :half]
    second = parts[:, :, half:]
    turned = jnp.concatenate(
        [first * cosine - second * sine, second * cosine + first * sine], axis=2
    )
    return turned.reshape(rows, -1)


def on_device(
    tokens,
    pre_gain,
    w_q,
    w_k,
    w_v,
    w_o,
    post_gain,
    k_cache,
    v_cache,
    cached_len,
    new_len,
    slot_offset,
):
    tok_rows = tokens.shape[0]
    whole_in, whole_gain = (
        lax.all_gather(tokens, "gy", axis=1, tiled=True),
        lax.all_gather(pre_gain, "gy", axis=0, tiled=True),
    )
    float_in = whole_in.astype(jnp.float32)
    scale_rows = lax.rsqrt(jnp.mean(float_in * float_in, axis=1, keepdims=True) + epsilon)
    normed = (float_in * scale_rows * (1.0 + whole_gain.astype(jnp.float32))).astype(jnp.bfloat16)
    q_lin = jnp.dot(
        normed, lax.all_gather(w_q, "gx", axis=0, tiled=True), preferred_element_type=jnp.float32
    )
    k_lin = jnp.dot(
        normed, lax.all_gather(w_k, "gx", axis=0, tiled=True), preferred_element_type=jnp.float32
    )
    v_lin = jnp.dot(
        normed, lax.all_gather(w_v, "gx", axis=0, tiled=True), preferred_element_type=jnp.float32
    )
    row_ids = lax.axis_index("gx") * tok_rows + jnp.arange(tok_rows, dtype=jnp.int32)
    request = row_ids // NEWTOK
    within = row_ids % NEWTOK
    owner_mask = request[:, None] == jnp.arange(REQS, dtype=jnp.int32)[None, :]
    row_cached = jnp.sum(jnp.where(owner_mask, cached_len[None, :], 0), axis=1)
    row_fresh = jnp.sum(jnp.where(owner_mask, new_len[None, :], 0), axis=1)
    position = row_cached + within
    q_new = (rotate(q_lin, position, HD) * query_scale).astype(jnp.bfloat16)
    k_new = rotate(k_lin, position, HD).astype(jnp.bfloat16)
    v_new = v_lin.astype(jnp.bfloat16)
    q_all, k_all, v_all = (
        lax.all_gather(q_new, "gx", axis=0, tiled=True),
        lax.all_gather(k_new, "gx", axis=0, tiled=True),
        lax.all_gather(v_new, "gx", axis=0, tiled=True),
    )
    slab_size = k_cache.shape[0]
    first_slot = lax.axis_index("gx") * slab_size
    slot_ids = first_slot + jnp.arange(slab_size, dtype=jnp.int32)
    offset_in = slot_ids[:, None] - slot_offset[None, :] - cached_len[None, :]
    landing = (offset_in >= 0) & (offset_in < new_len[None, :])
    source = jnp.sum(
        jnp.where(landing, jnp.arange(REQS, dtype=jnp.int32)[None, :] * NEWTOK + offset_in, 0),
        axis=1,
    )
    written = jnp.any(landing, axis=1)
    k_pool = jnp.where(written[:, None], jnp.take(k_all, source, axis=0), k_cache)
    v_pool = jnp.where(written[:, None], jnp.take(v_all, source, axis=0), v_cache)
    heads_dev = q_all.shape[1] // HD
    kv_dev = k_all.shape[1] // HD
    group_size = heads_dev // kv_dev
    kblock = min(512, slab_size)
    nblocks = slab_size // kblock
    key_blocks = k_pool.reshape(nblocks, kblock, kv_dev, HD)
    value_blocks = v_pool.reshape(nblocks, kblock, kv_dev, HD)
    total_rows = q_all.shape[0]

    def request_step(request_id, carry):
        numer_all, denom_all = carry
        first_row = request_id * NEWTOK
        rows = lax.dynamic_slice_in_dim(q_all, first_row, NEWTOK, 0).reshape(
            NEWTOK, kv_dev, group_size, HD
        )
        offset = slot_offset[request_id]
        cached = cached_len[request_id]
        fresh_count = new_len[request_id]
        last_seen = cached + jnp.minimum(jnp.arange(NEWTOK, dtype=jnp.int32), fresh_count - 1)
        region_end = offset + cached + fresh_count

        def block_terms(block, running):
            numerator, denominator = running
            key_rows = lax.dynamic_index_in_dim(key_blocks, block, 0, keepdims=False)
            value_rows = lax.dynamic_index_in_dim(value_blocks, block, 0, keepdims=False)
            key_pos = first_slot + block * kblock + jnp.arange(kblock, dtype=jnp.int32) - offset
            visible = (key_pos[None, :] >= 0) & (key_pos[None, :] <= last_seen[:, None])
            logits = jnp.einsum(
                "cgjd,sgd->cgjs", rows, key_rows, preferred_element_type=jnp.float32
            )
            weight = jnp.where(
                visible[:, None, None, :], jnp.exp(soft_cap * jnp.tanh(logits / soft_cap)), 0.0
            )
            denominator = denominator + jnp.sum(weight, axis=3)
            numerator = numerator + jnp.einsum(
                "cgjs,sgd->cgjd",
                weight.astype(jnp.bfloat16),
                value_rows,
                preferred_element_type=jnp.float32,
            )
            return (numerator, denominator)

        def compute(running):
            return lax.fori_loop(0, nblocks, block_terms, running)

        def skipped(running):
            return running

        initial = (
            jnp.zeros((NEWTOK, kv_dev, group_size, HD), jnp.float32),
            jnp.zeros((NEWTOK, kv_dev, group_size), jnp.float32),
        )
        present = (offset < first_slot + slab_size) & (region_end > first_slot)
        numerator, denominator = lax.cond(present, compute, skipped, initial)
        numer_all = lax.dynamic_update_slice_in_dim(
            numer_all, numerator.reshape(NEWTOK, heads_dev * HD), first_row, 0
        )
        denom_all = lax.dynamic_update_slice_in_dim(
            denom_all, denominator.reshape(NEWTOK, heads_dev), first_row, 0
        )
        return (numer_all, denom_all)

    start_sums = (
        jnp.zeros((total_rows, heads_dev * HD), jnp.float32),
        jnp.zeros((total_rows, heads_dev), jnp.float32),
    )
    numer_all, denom_all = lax.fori_loop(0, REQS, request_step, start_sums)
    head_num, head_den = (
        lax.psum_scatter(
            numer_all.astype(jnp.bfloat16), "gx", scatter_dimension=0, tiled=True
        ).astype(jnp.float32),
        lax.psum_scatter(
            denom_all.astype(jnp.bfloat16), "gx", scatter_dimension=0, tiled=True
        ).astype(jnp.float32),
    )
    attended = head_num.reshape(tok_rows, heads_dev, HD) / head_den[:, :, None]
    attended = jnp.where((within < row_fresh)[:, None, None], attended, 0.0)
    attended = attended.reshape(tok_rows, heads_dev * HD).astype(jnp.bfloat16)
    partial_out = jnp.dot(
        attended, lax.all_gather(w_o, "gx", axis=1, tiled=True), preferred_element_type=jnp.float32
    )
    branch = lax.psum_scatter(
        partial_out.astype(jnp.bfloat16), "gy", scatter_dimension=1, tiled=True
    ).astype(jnp.float32)
    mean_square = lax.psum(jnp.sum(branch * branch, axis=1), "gy") / D
    layer_out = (
        tokens.astype(jnp.float32)
        + branch * lax.rsqrt(mean_square + epsilon)[:, None] * (1.0 + post_gain.astype(jnp.float32))
    ).astype(jnp.bfloat16)
    return (layer_out, k_pool, v_pool)


def solution(mesh):
    placed = (
        P("gx", "gy"),
        P("gy"),
        P("gx", "gy"),
        P("gx", "gy"),
        P("gx", "gy"),
        P("gy", "gx"),
        P("gy"),
        P("gx", "gy"),
        P("gx", "gy"),
        P(),
        P(),
        P(),
    )
    return jax.shard_map(
        on_device,
        mesh=mesh,
        in_specs=placed,
        out_specs=(P("gx", "gy"), P("gx", "gy"), P("gx", "gy")),
        check_vma=False,
    )
```

profile of v0, /device:TPU:6, one launch (start us, length us, event | category | flops | bytes accessed | tf_op | source)
XLA Modules:
  0.0 559.7 jit_solution(3836005203226429468)
XLA Ops:
  10.2 46.4 %all-gather.1 = bf16[16,288,72]{1,2,0:T(8,128)(2,1)S(1)} all-gather(bf16[1,288,72]{1,2,0:T(8,128)(2,1)} %bitcast.110), channel_id=1, replica_groups=mesh['gx'=32,'gy'=16] {'gy'}, dimensions={0}, use_global_device_ids=true | all-gather | bytes 705024 | tf_op jit(solution)/shard_map/all_gather | solution.py:49
  57.7 1.3 dynamic-slice
  59.9 59.9 %all-reduce = bf16[4608]{0:T(1024)(128)(2,1)S(1)} all-reduce(bf16[4608]{0:T(1024)(128)(2,1)S(1)} %dynamic-update-slice), channel_id=1, replica_groups=mesh['gx'=32,'gy'=16] {'gy'}, use_global_device_ids=true, to_apply=%add | all-reduce | flops 4608 | bytes 18432
  120.3 2.2 fusion.42
  124.5 10.9 %all-gather.14.cloned.1.call-done = bf16[4608,128]{1,0:T(8,128)(2,1)} async-done(((bf16[144,128]{1,0:T(8,128)(2,1)}), bf16[4608,128]{1,0:T(8,128)(2,1)}) %all-gather.14.cloned.1.call-update) | async-done | bytes 1179664 | tf_op jit(solution)/shard_map/all_gather | solution.py:59
  135.4 1.6 convolution_bitcast_fusion.1
  137.3 37.5 %all-gather = bf16[2304,1,128]{2,0,1:T(8,128)(2,1)S(1)} all-gather(bf16[72,1,128]{2,0,1:T(8,128)(2,1)S(1)} %pad_maximum_fusion), channel_id=2, replica_groups=mesh['gx'=32,'gy'=16] {'gx'}, dimensions={0}, use_global_device_ids=true | all-gather | bytes 608256 | tf_op jit(solution)/shard_map/all_gather | solution.py:76
  174.8 3.2 gather_fusion.1
  178.0 16.2 %all-gather.12.cloned.1.call-done = bf16[4608,128]{1,0:T(8,128)(2,1)} async-done(((bf16[144,128]{1,0:T(8,128)(2,1)}), bf16[4608,128]{1,0:T(8,128)(2,1)}) %all-gather.12.cloned.1.call-update) | async-done | bytes 1179664 | tf_op jit(solution)/shard_map/all_gather | solution.py:62
  194.2 1.6 convolution_convert_fusion.1
  195.8 37.4 %all_gather.32 = bf16[2304,128]{1,0:T(8,128)(2,1)S(1)} all-gather(bf16[72,128]{1,0:T(8,128)(2,1)S(1)} %convolution_convert_fusion.1), channel_id=1, replica_groups=mesh['gx'=32,'gy'=16] {'gx'}, dimensions={0}, use_global_device_ids=true | all-gather | bytes 608256 | tf_op jit(solution)/shard_map/all_gather | solution.py:77
  233.2 3.2 gather_fusion
  236.8 16.7 %all-gather.10.cloned.1.call-done = bf16[2304,256]{1,0:T(8,128)(2,1)} async-done(((bf16[72,256]{1,0:T(8,128)(2,1)}), bf16[2304,256]{1,0:T(8,128)(2,1)}) %all-gather.10.cloned.1.call-update) | async-done | bytes 1179664 | tf_op jit(solution)/shard_map/all_gather | solution.py:75
  253.6 78.5 %while.39 = (s32[]{:T(128)}, bf16[2304,256]{1,0:T(8,128)(2,1)S(1)}, bf16[2304,2]{0,1:T(2,128)(2,1)S(1)}, s32[12]{0:T(128)S(1)}, s32[]{:T(128)}, /*index=5*/s32[1...) while((s32[]{:T(128)}, bf16[2304,256]{1,0:T(8,128)(2,1)S(1)}, ...), condition=%wide.region_11.13_spmd, body=%wide.region_5.12_spmd.sunk | while | flops 101944584 | bytes 3032737 | solution.py:157
  287.3 8.6 %conditional.2 = (bf16[192,256]{1,0:T(8,128)(2,1)S(1)}, f32[192,2]{0,1:T(2,128)}) conditional(s32[]{:T(128)} %convert_element_type.128, () %tuple.102, (s32[]{:T(128)}, s32[]{:T(128)}, s32[192]{0:T(256)S(1)}, bf16[2304,256]{1,0:T(8,128)(2,1)}, s32[]{:T(128)}, /*index=5*/bf16[2,512,1,128]{3,1,2,0:T(8,128)(2,1)S(1)}, s32[]{:T(128)}, s32[]{:T(128)}, ...), branch_computations={%region_6.7_spmd, %region_7.11_spmd} | conditional | flops 101944576 | bytes 2831936 | solution.py:144
  289.6 6.1 %while.38 = (s32[]{:T(128)}, f32[192,1,2,128]{3,0,2,1:T(8,128)S(1)}, f32[192,1,2]{0,2,1:T(2,128)}, bf16[2,512,1,128]{3,1,2,0:T(8,128)(2,1)S(1)}, s32[]{:T(128)},...) while((s32[]{:T(128)}, ...), condition=%wide.region_10.10_spmd.clone, body=%wide.region_8.9_spmd.clone.sunk | while | flops 101944192 | bytes 1748912 | solution.py:134
  294.4 1.3 bitcast_add_fusion.2
  333.2 1.3 dynamic-slice.1
  335.1 75.0 %all-reduce.1 = bf16[2304,2]{0,1:T(2,128)(2,1)S(1)} all-reduce(bf16[2304,2]{0,1:T(2,128)(2,1)S(1)} %get-tuple-element.491), channel_id=4, replica_groups=mesh['gx'=32,'gy'=16] {'gx'}, use_global_device_ids=true, to_apply=%region_13.15.clone | all-reduce | flops 4608 | bytes 18432
  410.4 32.7 %reduce-scatter.6.cloned.1.call-done = bf16[72,256]{1,0:T(8,128)(2,1)} async-done(((bf16[2304,256]{1,0:T(8,128)(2,1)}), bf16[72,256]{1,0:T(8,128)(2,1)}) %reduce-scatter.6.cloned.1.call-update) | async-done | bytes 36880 | tf_op jit(solution)/shard_map/reduce_scatter | solution.py:159
  443.2 2.5 convolution_convert_fusion
  445.8 1.4 copy.39
  447.3 72.7 %reduce-scatter.8.cloned.1.call-done = bf16[288,72]{1,0:T(8,128)(2,1)} async-done(((bf16[4608,72]{1,0:T(8,128)(2,1)}), bf16[288,72]{1,0:T(8,128)(2,1)}) %reduce-scatter.8.cloned.1.call-update) | async-done | bytes 41488
  521.1 31.0 %psum.7 = f32[72]{0:T(128)S(1)} all-reduce(f32[72]{0:T(128)S(1)} %fusion.15), channel_id=1, replica_groups=mesh['gx'=32,'gy'=16] {'gy'}, use_global_device_ids=true, to_apply=%region_16.18 | all-reduce | flops 72 | bytes 576 | tf_op jit(solution)/shard_map/psum | solution.py:175
  (199 shorter events, 63.7 us)
Async XLA Ops:
  7.2 113.1 %all-gather.8.cloned.1.call-start = ((), (), s32[]{:S(2)}) async-start(), calls=%async_computation.2 | async-start | bytes 2433024 | tf_op jit(solution)/shard_map/all_gather | solution.py:56
  7.9 127.5 %all-gather.14.cloned.1.call-start = ((), (), s32[]{:S(2)}) async-start(), calls=%async_computation.5 | async-start | bytes 1216512 | tf_op jit(solution)/shard_map/all_gather | solution.py:59
  8.6 185.5 %all-gather.12.cloned.1.call-start = ((), (), s32[]{:S(2)}) async-start(), calls=%async_computation.4 | async-start | bytes 1216512 | tf_op jit(solution)/shard_map/all_gather | solution.py:62
  9.4 244.1 %all-gather.10.cloned.1.call-start = ((), (), s32[]{:S(2)}) async-start(), calls=%async_computation.3 | async-start | bytes 1216512 | tf_op jit(solution)/shard_map/all_gather | solution.py:75
  57.5 2.2 copy-start.10
  120.2 4.0 copy-start.6
  120.2 4.0 copy-start.7
  120.2 4.0 copy-start.8
  123.5 286.8 %all-gather.16.cloned.1.call-start = ((), (), s32[]{:S(2)}) async-start(), calls=%async_computation.7 | async-start | bytes 2433024 | tf_op jit(solution)/shard_map/all_gather | solution.py:170
  124.1 319.0 %reduce-scatter.6.cloned.1.call-start = ((), (), s32[]{:S(2)}) async-start(), calls=%async_computation.6 | async-start | bytes 1216512 | tf_op jit(solution)/shard_map/reduce_scatter | solution.py:159
  233.2 3.2 copy-start.2
  233.2 3.2 copy-start.3
  332.1 1.0 copy-start.1
  332.1 113.7 %copy-start = (bf16[2,512,1,128]{3,1,2,0:T(8,128)(2,1)}, bf16[2,512,1,128]{3,1,2,0:T(8,128)(2,1)S(1)}, u32[]{:S(2)}) copy-start(bf16[2,512,1,128]{3,1,2,0:T(8,128)(2,1)S(1)} %get-tuple-element.871) | copy-start | bytes 786436
  332.1 113.7 %copy-start.4 = (bf16[2,512,1,128]{3,1,2,0:T(8,128)(2,1)}, bf16[2,512,1,128]{3,1,2,0:T(8,128)(2,1)S(1)}, u32[]{:S(2)}) copy-start(bf16[2,512,1,128]{3,1,2,0:T(8,128)(2,1)S(1)} %get-tuple-element.882) | copy-start | bytes 786436
  333.1 186.8 %reduce-scatter.8.cloned.1.call-start = ((), (), s32[]{:S(2)}) async-start(), calls=%async_computation.8 | async-start | bytes 1253376
  445.8 1.4 copy-start.9
  445.8 106.3 %copy-start.5 = (bf16[72,288]{1,0:T(8,128)(2,1)S(1)}, bf16[72,288]{1,0:T(8,128)(2,1)}, u32[]{:S(2)}) copy-start(bf16[72,288]{1,0:T(8,128)(2,1)} %param.20) | copy-start | bytes 124420
Sparse Core Ops, SparseCore 0:
  11.1 65.5 all-gather.7
  80.0 55.3 all-gather.13
  138.6 55.5 all-gather.11
  197.8 55.6 all-gather.9
  256.4 58.8 all-gather.15
  333.3 109.8 reduce-scatter.5
  447.4 72.5 reduce-scatter.7
where the time goes:
time: 561 us; the launch traced here: 560 us
  blocking collectives  287 us (51%)
  waiting for transfers between devices  152 us (27%)
  local copies, waits for them, and re-layouts  55.4 us (10%)
  loops' own time  30.8 us (5%)
  between operations  15.8 us (3%)
  matrix products  9.64 us (2%)
  other arithmetic  8.62 us (2%)
    unnamed x2, blocking collectives  135 us
    unnamed x8, waiting for transfers between devices  75.3 us
    all_gather x1, blocking collectives, on_device(): lax.all_gather(tokens, 'gy', axis=1, tiled=True)  46.4 us
    all_gather x1, blocking collectives, on_device(): lax.all_gather(k_new, 'gx', axis=0, tiled=True)  37.5 us
    all_gather x1, blocking collectives, on_device(): lax.all_gather(v_new, 'gx', axis=0, tiled=True)  37.4 us
    reduce_scatter x1, waiting for transfers between devices, on_device(): lax.psum_scatter(numer_all.astype(jnp.bfloat16), 'gx', scatter_dimension=...  32.7 us
    psum x1, blocking collectives, on_device(): mean_square = lax.psum(jnp.sum(branch * branch, axis=1), 'gy') / D  31 us
    another operation x1, loops' own time, on_device(): numer_all, denom_all = lax.fori_loop(0, REQS, request_step, start_sums)  29.9 us
  transfers between devices with their start and end apart: 7, of which 5 were waited for; matrix products, arithmetic and copies ran while one was open for 12% of the time, Pallas kernels for 0%

commit v1 on v0

v1 whole, which is shorter than its diff:
```python
import jax
import jax.numpy as jnp
from jax import lax
from jax.experimental import pallas as pl
from jax.experimental.pallas import tpu as pltpu
from jax.sharding import Mesh, PartitionSpec as P

D = 4608
HD = 128
REQS = 12
NEWTOK = 192
TILE = 256
PIECE = 48
epsilon = 1e-06
soft_cap = 50.0
query_scale = 144.0 ** (-0.5)
F32 = jnp.float32
BF16 = jnp.bfloat16

CHIPS = ("zh", "x")
GX = ("zh", "x", "c")
GY = ("y", "zl")


def everywhere(value, axes, count):
    return lax.all_to_all(jnp.broadcast_to(value[None], (count,) + value.shape), axes, 0, 0)


def attend_kernel(meta, qkv, k_old, v_old, k_pool, v_pool, sums, num, den, totals):
    slots = k_old.shape[0]
    tiles = slots // TILE
    first = meta[3 * REQS]
    chunk = sums.shape[1] // (REQS * NEWTOK // (3 * PIECE))
    heads = sums.shape[0]

    k_pool[...] = k_old[...]
    v_pool[...] = v_old[...]
    totals[...] = jnp.zeros_like(totals)

    def write_request(r, carry):
        cached, fresh, offset = meta[r], meta[REQS + r], meta[2 * REQS + r]
        begin = offset + cached - first
        for t in range(tiles):

            @pl.when((begin < (t + 1) * TILE) & (begin + fresh > t * TILE))
            def _():
                rows = qkv[1, pl.ds(pl.multiple_of(r * NEWTOK, 64), NEWTOK), :]
                slot = lax.broadcasted_iota(jnp.int32, (TILE, NEWTOK), 0) + (t * TILE - begin)
                index = lax.broadcasted_iota(jnp.int32, (TILE, NEWTOK), 1)
                pick = jnp.where((slot == index) & (index < fresh), 1.0, 0.0).astype(BF16)
                new = jnp.dot(pick, rows, preferred_element_type=F32)
                place = lax.broadcasted_iota(jnp.int32, (TILE, HD), 0) + (t * TILE - begin)
                written = (place >= 0) & (place < fresh)
                here = pl.ds(t * TILE, TILE)
                k_pool[here, :] = jnp.where(written, new[:, :HD], k_pool[here, :].astype(F32)).astype(BF16)
                v_pool[here, :] = jnp.where(written, new[:, HD:], v_pool[here, :].astype(F32)).astype(BF16)

        return carry

    lax.fori_loop(0, REQS, write_request, 0)

    def read_request(r, carry):
        cached, fresh, offset = meta[r], meta[REQS + r], meta[2 * REQS + r]
        begin = offset - first
        end = begin + cached + fresh
        num[...] = jnp.zeros_like(num)
        den[...] = jnp.zeros_like(den)

        @pl.when((begin < slots) & (end > 0))
        def _():
            rows = qkv[0, pl.ds(pl.multiple_of(r * NEWTOK, 64), NEWTOK), :]
            rows = jnp.concatenate([rows[:, h * HD : (h + 1) * HD] for h in range(heads)], axis=0)
            row = lax.broadcasted_iota(jnp.int32, (heads * NEWTOK, 1), 0)
            row = jnp.where(row >= NEWTOK, row - NEWTOK, row)
            last = cached + jnp.minimum(row, fresh - 1) + begin
            for t in range(tiles):

                @pl.when((begin < (t + 1) * TILE) & (end > t * TILE))
                def _():
                    here = pl.ds(t * TILE, TILE)
                    logits = lax.dot_general(
                        rows, k_pool[here, :], (((1,), (1,)), ((), ())), preferred_element_type=F32
                    )
                    slot = lax.broadcasted_iota(jnp.int32, logits.shape, 1) + t * TILE
                    visible = (slot >= begin) & (slot <= last)
                    weight = jnp.exp(soft_cap * jnp.tanh(logits * (1.0 / soft_cap)))
                    weight = jnp.where(visible, weight, 0.0).astype(BF16)
                    num[...] += jnp.dot(weight, v_pool[here, :], preferred_element_type=F32)
                    den[...] += lax.dot_general(
                        jnp.ones((8, TILE), BF16), weight, (((1,), (1,)), ((), ())), preferred_element_type=F32
                    )

        for piece in range(NEWTOK // PIECE):
            at = r * (NEWTOK // PIECE) + piece
            block, part = at // 3, at % 3
            to = pl.multiple_of(block * chunk + part * PIECE, 16)
            for h in range(heads):
                low = h * NEWTOK + piece * PIECE
                sums[h, pl.ds(to, PIECE), :] = num[low : low + PIECE, :].astype(BF16)
                totals[h, pl.ds(block * 8 + part, 1), 0:PIECE] = den[0:1, low : low + PIECE]
        return carry

    lax.fori_loop(0, REQS, read_request, 0)
    for h in range(heads):
        for block in range(REQS * NEWTOK // (3 * PIECE)):
            rows = totals[h, block * 8 : block * 8 + 8, :]
            rows = jnp.concatenate([rows, jnp.zeros_like(rows)], axis=0)
            sums[h, block * chunk + 3 * PIECE : (block + 1) * chunk, :] = rows.astype(BF16)


def attend(meta, qkv, k_cache, v_cache):
    heads = 2
    blocks = REQS * NEWTOK // (3 * PIECE)
    chunk = 3 * PIECE + 16
    vmem = pl.BlockSpec(memory_space=pltpu.VMEM)
    return pl.pallas_call(
        attend_kernel,
        out_shape=(
            jax.ShapeDtypeStruct(k_cache.shape, BF16),
            jax.ShapeDtypeStruct(v_cache.shape, BF16),
            jax.ShapeDtypeStruct((heads, blocks * chunk, HD), BF16),
        ),
        in_specs=[pl.BlockSpec(memory_space=pltpu.SMEM), vmem, vmem, vmem],
        out_specs=(vmem, vmem, vmem),
        scratch_shapes=[
            pltpu.VMEM((heads * NEWTOK, HD), F32),
            pltpu.VMEM((8, heads * NEWTOK), F32),
            pltpu.VMEM((heads, blocks * 8, HD), F32),
        ],
        compiler_params=pltpu.CompilerParams(vmem_limit_bytes=32 << 20),
        name="attend",
    )(meta, qkv, k_cache, v_cache)


def divide_kernel(meta, parts, out):
    fresh_at = REQS
    begin = meta[3 * REQS + 1]
    total = jnp.sum(parts[...].astype(F32), axis=0)
    for part in range(3):
        row = begin + part * PIECE
        request = row // NEWTOK
        fresh = meta[fresh_at + request]
        within = lax.broadcasted_iota(jnp.int32, (PIECE, HD), 0) + (row - request * NEWTOK)
        den = total[3 * PIECE + part : 3 * PIECE + part + 1, 0:PIECE]
        diagonal = lax.broadcasted_iota(jnp.int32, (PIECE, PIECE), 0) == lax.broadcasted_iota(
            jnp.int32, (PIECE, PIECE), 1
        )
        den = jnp.sum(jnp.where(diagonal, den, 0.0), axis=1, keepdims=True)
        value = total[part * PIECE : (part + 1) * PIECE, :] / den
        out[part * PIECE : (part + 1) * PIECE, :] = jnp.where(within < fresh, value, 0.0).astype(BF16)


def divide(meta, parts):
    vmem = pl.BlockSpec(memory_space=pltpu.VMEM)
    return pl.pallas_call(
        divide_kernel,
        out_shape=jax.ShapeDtypeStruct((3 * PIECE, HD), BF16),
        in_specs=[pl.BlockSpec(memory_space=pltpu.SMEM), vmem],
        out_specs=vmem,
        compiler_params=pltpu.CompilerParams(vmem_limit_bytes=16 << 20),
        name="divide",
    )(meta, parts)


def on_device(
    tokens, pre_gain, w_q, w_k, w_v, w_o, post_gain, k_cache, v_cache, cached_len, new_len, slot_offset
):
    tok_rows = tokens.shape[0]
    n_gy = lax.axis_size(GY)
    n_chips = lax.axis_size(CHIPS)
    me = lax.axis_index(GX)
    weights = lax.all_gather(jnp.concatenate([w_q, w_k, w_v], axis=1), GX, axis=0, tiled=True)
    w_out = lax.all_gather(w_o.T, GX, axis=0, tiled=True)

    float_in = tokens.astype(F32)
    squares = jnp.sum(float_in * float_in, axis=1, keepdims=True)
    high = lax.reduce_precision(squares, 8, 7)
    gained = float_in * (1.0 + pre_gain.astype(F32))
    gained = jnp.concatenate([gained, high, squares - high], axis=1).astype(BF16)
    gained = everywhere(gained, GY, n_gy)
    features = tokens.shape[1]
    mean = jnp.sum(gained[:, :, features:].astype(F32), axis=(0, 2)) / D
    scale_rows = lax.rsqrt(mean + epsilon)[:, None]
    whole = jnp.swapaxes(gained[:, :, :features], 0, 1).reshape(tok_rows, D)
    lin = jnp.dot(whole, weights, preferred_element_type=F32) * scale_rows

    row_ids = me * tok_rows + jnp.arange(tok_rows, dtype=jnp.int32)
    request = row_ids // NEWTOK
    owner_mask = request[:, None] == jnp.arange(REQS, dtype=jnp.int32)[None, :]
    position = jnp.sum(jnp.where(owner_mask, cached_len[None, :], 0), axis=1) + row_ids % NEWTOK
    half = HD // 2
    inverse = jnp.power(10000.0, -2.0 * jnp.arange(half, dtype=F32) / HD)
    angle = position.astype(F32)[:, None] * inverse[None, :]
    cosine, sine = jnp.cos(angle), jnp.sin(angle)

    def rotate(values):
        first, second = values[:, :half], values[:, half:]
        return jnp.concatenate([first * cosine - second * sine, second * cosine + first * sine], axis=1)

    q_cols = w_q.shape[1]
    pieces = [rotate(lin[:, h * HD : (h + 1) * HD]) * query_scale for h in range(q_cols // HD)]
    pieces += [rotate(lin[:, q_cols : q_cols + HD]), lin[:, q_cols + HD :]]
    fresh_rows = jnp.concatenate(pieces, axis=1).astype(BF16)

    mine = lax.all_to_all(fresh_rows, "c", 1, 0, tiled=True)
    mine = everywhere(mine, CHIPS, n_chips).reshape(-1, q_cols)
    qkv = everywhere(mine, "c", 2)

    meta = jnp.concatenate(
        [
            cached_len,
            new_len,
            slot_offset,
            jnp.stack([me * k_cache.shape[0], me // 2 * (2 * tok_rows)]).astype(jnp.int32),
        ]
    )
    k_pool, v_pool, sums = attend(meta, qkv, k_cache, v_cache)

    both = lax.all_to_all(sums, "c", 0, 0)
    head = (both[0].astype(F32) + both[1].astype(F32)).astype(BF16)
    parts = lax.all_to_all(head.reshape(n_chips, -1, HD), CHIPS, 0, 0)
    attended = divide(meta, parts)
    attended = lax.all_to_all(attended.reshape(2, tok_rows, HD), "c", 0, 0)
    attended = jnp.swapaxes(attended, 0, 1).reshape(tok_rows, 2 * HD)

    partial_out = lax.dot_general(attended, w_out, (((1,), (1,)), ((), ())), preferred_element_type=F32)
    partial_out = jnp.swapaxes(partial_out.astype(BF16).reshape(tok_rows, n_gy, features), 0, 1)
    branch = jnp.sum(lax.all_to_all(partial_out, GY, 0, 0).astype(F32), axis=0)
    squares = jnp.sum(branch * branch, axis=1)
    mean = jnp.sum(everywhere(squares[None, :], GY, n_gy), axis=(0, 1)) / D
    layer_out = float_in + branch * lax.rsqrt(mean + epsilon)[:, None] * (1.0 + post_gain.astype(F32))
    return (layer_out.astype(BF16), k_pool, v_pool)


def solution(mesh):
    parts = Mesh(mesh.devices.reshape(4, 4, 2, 8, 2), GX + GY)
    both = P(GX, GY)
    placed = (both, P(GY), both, both, both, P(GY, GX), P(GY), both, both, P(), P(), P())
    return jax.shard_map(
        on_device, mesh=parts, in_specs=placed, out_specs=(both, both, both), check_vma=False
    )
```

time: 561 us -> 246 us (0.44)
  the two profiles are of different devices: /device:TPU:6 before, /device:TPU:1 now
where the time goes in v1:
time: 246 us; the launch traced here: 245 us
  waiting for transfers between devices  112 us (46%)
  blocking collectives  71.5 us (29%)
  starting transfers between devices  23.9 us (10%)
  between operations  14.3 us (6%)
  Pallas kernels  5.98 us (2%)
  local copies, waits for them, and re-layouts  5.82 us (2%)
  matrix products  5.76 us (2%)
  other arithmetic  5.18 us (2%)
    all_to_all x3, waiting for transfers between devices, everywhere(): lax.all_to_all(jnp.broadcast_to(value[None], (count,) + value.shape), axe...  62.2 us
    all_gather x1, waiting for transfers between devices, on_device(): lax.all_gather(jnp.concatenate([w_q, w_k, w_v], axis=1), GX, axis=0, tile...  48.4 us
    all_to_all x1, blocking collectives, on_device(): branch = jnp.sum(lax.all_to_all(partial_out, GY, 0, 0).astype(F32), axis=0)  30.6 us
    all_to_all x1, blocking collectives, on_device(): parts = lax.all_to_all(head.reshape(n_chips, -1, HD), CHIPS, 0, 0)  24.4 us
    all_to_all x3, starting transfers between devices, everywhere(): lax.all_to_all(jnp.broadcast_to(value[None], (count,) + value.shape), axe...  19.8 us
    all_to_all x1, blocking collectives, everywhere(): lax.all_to_all(jnp.broadcast_to(value[None], (count,) + value.shape), axe...  8.22 us
  transfers between devices with their start and end apart: 6, of which 5 were waited for; matrix products, arithmetic and copies ran while one was open for 4% of the time, Pallas kernels for 2%

profile of v1, /device:TPU:1, one launch (start us, length us, event | category | flops | bytes accessed | tf_op | source)
XLA Modules:
  0.0 244.9 jit_solution(11641157962120681953)
XLA Ops:
  7.2 1.6 pad_maximum_fusion
  9.5 0.9 fusion
  10.8 1.0 broadcast_in_dim.24
  11.8 9.6 %all-to-all-start = ((bf16[16,72,290]{2,1,0:T(8,128)(2,1)}), bf16[16,72,290]{2,1,0:T(8,128)(2,1)S(1)}, u32[]{:S(2)}, u32[]{:S(2)}) async-start(bf16[16,72,290]{2,1,0:T(8,128)(2,1)} %broadcast_in_dim.24), calls=%async_computation | async-start | bytes 1769472 | tf_op jit(solution)/shard_map/all_to_all | solution.py:26
  22.3 21.7 %all-to-all-done = bf16[16,72,290]{2,1,0:T(8,128)(2,1)S(1)} async-done(((bf16[16,72,290]{2,1,0:T(8,128)(2,1)}), bf16[16,72,290]{2,1,0:T(8,128)(2,1)S(1)}, u32[]{:S(2)}, u32[]{:S(2)}) %all-to-all-start) | async-done | bytes 668192 | tf_op jit(solution)/shard_map/all_to_all | solution.py:26
  44.2 0.9 reshape.114
  45.3 48.4 %all-gather.3.cloned.1.call-done = bf16[4608,512]{1,0:T(8,128)(2,1)} async-done(((bf16[144,512]{1,0:T(8,128)(2,1)}), bf16[4608,512]{1,0:T(8,128)(2,1)}) %all-gather.3.cloned.1.call-update) | async-done | bytes 4718608 | tf_op jit(solution)/shard_map/all_gather | solution.py:172
  93.7 3.3 %convolution_multiply_fusion = f32[72,512]{1,0:T(8,128)S(1)} fusion(bf16[72,4608]{1,0:T(8,128)(2,1)S(1)} %reshape.114, bf16[4608,512]{1,0:T(8,128)(2,1)} %all-gather.3.cloned.1.call-done, f32[72]{0:T(128)S(1)} %add_rsqrt_fusion.1), kind=kOutput, calls=%fused_computation.3 | convolution fusion | flops 339775488 | bytes 5529888 | tf_op jit(solution)/shard_map/dot_general | solution.py:185
  97.5 3.7 %all_to_all.53 = bf16[72,2,256]{2,0,1:T(8,128)(2,1)S(1)} all-to-all(bf16[72,2,256]{2,0,1:T(8,128)(2,1)S(1)} %bitcast.37), channel_id=1, replica_groups=mesh['zh'=4,'x'=4,'c'=2,'y'=8,'zl'=2] {'c'}, dimensions={1} | all-to-all | bytes 147456 | tf_op jit(solution)/shard_map/all_to_all | solution.py:205
  101.1 1.1 broadcast_in_dim.28
  102.2 6.3 %all-to-all-start.2 = ((bf16[16,144,256]{2,1,0:T(8,128)(2,1)}), bf16[16,144,256]{2,1,0:T(8,128)(2,1)S(1)}, u32[]{:S(2)}, u32[]{:S(2)}) async-start(bf16[16,144,256]{2,1,0:T(8,128)(2,1)} %broadcast_in_dim.28), calls=%async_computation.2 | async-start | bytes 2359296 | tf_op jit(solution)/shard_map/all_to_all | solution.py:26
  108.7 33.2 %all-to-all-done.2 = bf16[16,144,256]{2,1,0:T(8,128)(2,1)S(1)} async-done(((bf16[16,144,256]{2,1,0:T(8,128)(2,1)}), bf16[16,144,256]{2,1,0:T(8,128)(2,1)S(1)}, u32[]{:S(2)}, u32[]{:S(2)}) %all-to-all-start.2) | async-done | bytes 1179680 | tf_op jit(solution)/shard_map/all_to_all | solution.py:26
  142.1 8.2 %all_to_all.54.qkv = bf16[2,2304,256]{2,1,0:T(8,128)(2,1)S(1)} all-to-all(bf16[2,2304,256]{2,1,0:T(8,128)(2,1)S(1)} %broadcast_in_dim.30), channel_id=1, replica_groups=mesh['zh'=4,'x'=4,'c'=2,'y'=8,'zl'=2] {'c'}, dimensions={0} | all-to-all | bytes 4718592 | tf_op jit(solution)/shard_map/all_to_all | solution.py:26
  150.4 4.7 %attend.1 = (bf16[1024,128]{1,0:T(8,128)(2,1)}, bf16[1024,128]{1,0:T(8,128)(2,1)}, bf16[2,2560,128]{2,1,0:T(8,128)(2,1)S(1)}) custom-call(s32[38]{0:T(128)S(1)} %concatenate.24.meta, bf16[2,2304,256]{2,1,0:T(8,128)(2,1)S(1)} %all_to_all.54.qkv, bf16[1024,128]{1,0:T(8,128)(2,1)S(1)} %copy-done, bf16[1024,128]{1,0:T(8,128)(2,1)S(1)} %copy-done.1), custom_call_target="tpu_custom_call" | custom-call | tf_op jit(solution)/shard_map/attend/pallas_call | solution.py:116
  155.1 4.7 %all_to_all.55 = bf16[2,2560,128]{2,1,0:T(8,128)(2,1)S(1)} all-to-all(bf16[2,2560,128]{2,1,0:T(8,128)(2,1)S(1)} %get-tuple-element.6), channel_id=1, replica_groups=mesh['zh'=4,'x'=4,'c'=2,'y'=8,'zl'=2] {'c'}, dimensions={0} | all-to-all | bytes 2621440 | tf_op jit(solution)/shard_map/all_to_all | solution.py:219
  159.9 24.4 %all_to_all.56.parts = bf16[16,160,128]{2,1,0:T(8,128)(2,1)S(1)} all-to-all(bf16[16,160,128]{2,1,0:T(8,128)(2,1)S(1)} %bitcast.35), channel_id=1, replica_groups=mesh['zh'=4,'x'=4,'c'=2,'y'=8,'zl'=2] {'zh','x'}, dimensions={0} | all-to-all | bytes 1310720 | tf_op jit(solution)/shard_map/all_to_all | solution.py:221
  184.3 1.3 divide.1
  185.6 4.0 %all-to-all-start.6 = ((bf16[2,72,128]{2,1,0:T(8,128)(2,1)}), bf16[2,72,128]{2,1,0:T(8,128)(2,1)S(1)}, u32[]{:S(2)}, u32[]{:S(2)}) async-start(bf16[2,72,128]{2,1,0:T(8,128)(2,1)} %bitcast.8), calls=%async_computation.6 | async-start | bytes 73728 | tf_op jit(solution)/shard_map/all_to_all | solution.py:223
  189.6 1.1 all-to-all-done.6
  190.7 2.5 %convolution_convert_fusion = bf16[72,4608]{1,0:T(8,128)(2,1)S(1)} fusion(bf16[4608,256]{1,0:T(8,128)(2,1)} %all-gather.5.cloned.1.call-done, bf16[2,72,128]{2,1,0:T(8,128)(2,1)S(1)} %all-to-all-done.6), kind=kOutput, calls=%fused_computation | convolution fusion | flops 170201088 | bytes 3059712 | tf_op jit(solution)/shard_map/dot_general | solution.py:226
  193.2 1.2 reshape.117
  194.6 30.6 %all_to_all.57 = bf16[16,72,288]{2,1,0:T(8,128)(2,1)S(1)} all-to-all(bf16[16,72,288]{2,1,0:T(8,128)(2,1)S(1)} %bitcast.34), channel_id=1, replica_groups=mesh['zh'=4,'x'=4,'c'=2,'y'=8,'zl'=2] {'y','zl'}, dimensions={0} | all-to-all | bytes 1327104 | tf_op jit(solution)/shard_map/all_to_all | solution.py:228
  226.1 3.9 %all-to-all-start.8 = ((f32[16,1,72]{2,1,0:T(1,128)}), f32[16,1,72]{2,1,0:T(1,128)S(1)}, u32[]{:S(2)}, u32[]{:S(2)}) async-start(f32[16,1,72]{2,1,0:T(1,128)} %broadcast_in_dim.31), calls=%async_computation.8 | async-start | bytes 16384 | tf_op jit(solution)/shard_map/all_to_all | solution.py:26
  230.0 7.3 %all-to-all-done.8 = f32[16,1,72]{2,1,0:T(1,128)S(1)} async-done(((f32[16,1,72]{2,1,0:T(1,128)}), f32[16,1,72]{2,1,0:T(1,128)S(1)}, u32[]{:S(2)}, u32[]{:S(2)}) %all-to-all-start.8) | async-done | bytes 4640 | tf_op jit(solution)/shard_map/all_to_all | solution.py:26
  (48 shorter events, 5.1 us)
Async XLA Ops:
  7.2 15.0 %copy-start.4 = (s32[12]{0:T(128)S(1)}, s32[12]{0:T(128)}, u32[]{:S(2)}) copy-start(s32[12]{0:T(128)} %param.21) | copy-start | bytes 148
  7.2 86.5 %all-gather.3.cloned.1.call-start = ((), (), s32[]{:S(2)}) async-start(), calls=%async_computation.9 | async-start | bytes 4866048 | tf_op jit(solution)/shard_map/all_gather | solution.py:172
  11.8 32.2 %all-to-all-start = ((bf16[16,72,290]{2,1,0:T(8,128)(2,1)}), bf16[16,72,290]{2,1,0:T(8,128)(2,1)S(1)}, u32[]{:S(2)}, u32[]{:S(2)}) async-start(bf16[16,72,290]{2,1,0:T(8,128)(2,1)} %broadcast_in_dim.24), calls=%async_computation | async-start | bytes 1769472 | tf_op jit(solution)/shard_map/all_to_all | solution.py:26
  21.4 168.3 %all-gather.5.cloned.1.call-start = ((), (), s32[]{:S(2)}) async-start(), calls=%async_computation.10 | async-start | bytes 2433024 | tf_op jit(solution)/shard_map/all_gather | solution.py:173
  97.0 11.6 %copy-start.5 = (s32[12]{0:T(128)S(1)}, s32[12]{0:T(128)}, u32[]{:S(2)}) copy-start(s32[12]{0:T(128)} %param.22) | copy-start | bytes 148
  97.0 11.6 %copy-start.6 = (s32[12]{0:T(128)S(1)}, s32[12]{0:T(128)}, u32[]{:S(2)}) copy-start(s32[12]{0:T(128)} %param.23) | copy-start | bytes 148
  102.2 39.7 %all-to-all-start.2 = ((bf16[16,144,256]{2,1,0:T(8,128)(2,1)}), bf16[16,144,256]{2,1,0:T(8,128)(2,1)S(1)}, u32[]{:S(2)}, u32[]{:S(2)}) async-start(bf16[16,144,256]{2,1,0:T(8,128)(2,1)} %broadcast_in_dim.28), calls=%async_computation.2 | async-start | bytes 2359296 | tf_op jit(solution)/shard_map/all_to_all | solution.py:26
  142.1 8.3 %copy-start = (bf16[1024,128]{1,0:T(8,128)(2,1)S(1)}, bf16[1024,128]{1,0:T(8,128)(2,1)}, u32[]{:S(2)}) copy-start(bf16[1024,128]{1,0:T(8,128)(2,1)} %k_old.1) | copy-start | bytes 786436
  142.1 8.2 %copy-start.1 = (bf16[1024,128]{1,0:T(8,128)(2,1)S(1)}, bf16[1024,128]{1,0:T(8,128)(2,1)}, u32[]{:S(2)}) copy-start(bf16[1024,128]{1,0:T(8,128)(2,1)} %v_old.1) | copy-start | bytes 786436
  185.6 5.1 %all-to-all-start.6 = ((bf16[2,72,128]{2,1,0:T(8,128)(2,1)}), bf16[2,72,128]{2,1,0:T(8,128)(2,1)S(1)}, u32[]{:S(2)}, u32[]{:S(2)}) async-start(bf16[2,72,128]{2,1,0:T(8,128)(2,1)} %bitcast.8), calls=%async_computation.6 | async-start | bytes 73728 | tf_op jit(solution)/shard_map/all_to_all | solution.py:223
  194.4 35.6 %copy-start.3 = (bf16[288]{0:T(512)(128)(2,1)S(1)}, bf16[288]{0:T(512)(128)(2,1)}, u32[]{:S(2)}) copy-start(bf16[288]{0:T(512)(128)(2,1)} %param.18) | copy-start | bytes 1732
  194.4 42.9 %copy-start.2 = (bf16[72,288]{1,0:T(8,128)(2,1)S(1)}, bf16[72,288]{1,0:T(8,128)(2,1)}, u32[]{:S(2)}) copy-start(bf16[72,288]{1,0:T(8,128)(2,1)} %param.12) | copy-start | bytes 124420
  226.1 11.2 %all-to-all-start.8 = ((f32[16,1,72]{2,1,0:T(1,128)}), f32[16,1,72]{2,1,0:T(1,128)S(1)}, u32[]{:S(2)}, u32[]{:S(2)}) async-start(f32[16,1,72]{2,1,0:T(1,128)} %broadcast_in_dim.31), calls=%async_computation.8 | async-start | bytes 16384 | tf_op jit(solution)/shard_map/all_to_all | solution.py:26
Sparse Core Ops, SparseCore 0:
  11.7 81.9 all-gather.2
  96.8 71.3 all-gather.4

commit v2 on v1

--- a/solution.py
+++ b/solution.py
@@ -26,12 +26,55 @@
     return lax.all_to_all(jnp.broadcast_to(value[None], (count,) + value.shape), axes, 0, 0)
 
 
-def attend_kernel(meta, qkv, k_old, v_old, k_pool, v_pool, sums, num, den, totals):
+def project_kernel(meta, tokens, turns, *rest):
+    columns, out = rest[:-1], rest[-1]
+    here = meta[3 * REQS + 3]
+    features = tokens.shape[3] - 2
+    count = len(columns)
+    total = jnp.zeros(out.shape, F32)
+    squares = jnp.zeros((out.shape[0], 2), F32)
+    for step in range(count):
+        along = lax.rem(here + step, count)
+        for block in range(tokens.shape[1] // count):
+            at = block * count + along
+            rows = jnp.concatenate([tokens[0, at], tokens[1, at]], axis=0)
+            squares += rows[:, features:].astype(F32)
+            total += jnp.dot(
+                rows[:, :features],
+                columns[step][block * features : (block + 1) * features, :],
+                preferred_element_type=F32,
+            )
+    mean = jnp.sum(squares, axis=1, keepdims=True) * (1.0 / D)
+    total = total * lax.rsqrt(mean + epsilon)
+    for head in range(2):
+        value = total[:, head * HD : (head + 1) * HD]
+        value = value * turns[2 * head] + pltpu.roll(value, HD // 2, 1) * turns[2 * head + 1]
+        out[:, head * HD : (head + 1) * HD] = value.astype(BF16)
+
+
+def project(meta, tokens, turns, columns):
+    vmem = pl.BlockSpec(memory_space=pltpu.VMEM)
+    return pl.pallas_call(
+        project_kernel,
+        out_shape=jax.ShapeDtypeStruct((2 * tokens.shape[2], columns[0].shape[1]), BF16),
+        in_specs=[pl.BlockSpec(memory_space=pltpu.SMEM)] + [vmem] * (2 + len(columns)),
+        out_specs=vmem,
+        compiler_params=pltpu.CompilerParams(vmem_limit_bytes=32 << 20),
+        name="project",
+    )(meta, tokens, turns, *columns)
+
+
+def attend_kernel(meta, mine, others, k_old, v_old, k_pool, v_pool, sums, num, den, totals):
     slots = k_old.shape[0]
     tiles = slots // TILE
     first = meta[3 * REQS]
+    queries_here = meta[3 * REQS + 2] == 0
     chunk = sums.shape[1] // (REQS * NEWTOK // (3 * PIECE))
     heads = sums.shape[0]
+
+    def rows_of(r, on_core_0, on_core_1):
+        here = pl.ds(pl.multiple_of(r * NEWTOK, 64), NEWTOK)
+        return jnp.where(queries_here, on_core_0[here, :], on_core_1[here, :])
 
     k_pool[...] = k_old[...]
     v_pool[...] = v_old[...]
@@ -44,7 +87,7 @@
 
             @pl.when((begin < (t + 1) * TILE) & (begin + fresh > t * TILE))
             def _():
-                rows = qkv[1, pl.ds(pl.multiple_of(r * NEWTOK, 64), NEWTOK), :]
+                rows = rows_of(r, others, mine)
                 slot = lax.broadcasted_iota(jnp.int32, (TILE, NEWTOK), 0) + (t * TILE - begin)
                 index = lax.broadcasted_iota(jnp.int32, (TILE, NEWTOK), 1)
                 pick = jnp.where((slot == index) & (index < fresh), 1.0, 0.0).astype(BF16)
@@ -68,7 +111,7 @@
 
         @pl.when((begin < slots) & (end > 0))
         def _():
-            rows = qkv[0, pl.ds(pl.multiple_of(r * NEWTOK, 64), NEWTOK), :]
+            rows = rows_of(r, mine, others)
             rows = jnp.concatenate([rows[:, h * HD : (h + 1) * HD] for h in range(heads)], axis=0)
             row = lax.broadcasted_iota(jnp.int32, (heads * NEWTOK, 1), 0)
             row = jnp.where(row >= NEWTOK, row - NEWTOK, row)
@@ -108,7 +151,7 @@
             sums[h, block * chunk + 3 * PIECE : (block + 1) * chunk, :] = rows.astype(BF16)
 
 
-def attend(meta, qkv, k_cache, v_cache):
+def attend(meta, mine, others, k_cache, v_cache):
     heads = 2
     blocks = REQS * NEWTOK // (3 * PIECE)
     chunk = 3 * PIECE + 16
@@ -120,7 +163,7 @@
             jax.ShapeDtypeStruct(v_cache.shape, BF16),
             jax.ShapeDtypeStruct((heads, blocks * chunk, HD), BF16),
         ),
-        in_specs=[pl.BlockSpec(memory_space=pltpu.SMEM), vmem, vmem, vmem],
+        in_specs=[pl.BlockSpec(memory_space=pltpu.SMEM), vmem, vmem, vmem, vmem],
         out_specs=(vmem, vmem, vmem),
         scratch_shapes=[
             pltpu.VMEM((heads * NEWTOK, HD), F32),
@@ -129,7 +172,7 @@
         ],
         compiler_params=pltpu.CompilerParams(vmem_limit_bytes=32 << 20),
         name="attend",
-    )(meta, qkv, k_cache, v_cache)
+    )(meta, mine, others, k_cache, v_cache)
 
 
 def divide_kernel(meta, parts, out):
@@ -166,10 +209,16 @@
     tokens, pre_gain, w_q, w_k, w_v, w_o, post_gain, k_cache, v_cache, cached_len, new_len, slot_offset
 ):
     tok_rows = tokens.shape[0]
+    features = tokens.shape[1]
     n_gy = lax.axis_size(GY)
     n_chips = lax.axis_size(CHIPS)
     me = lax.axis_index(GX)
-    weights = lax.all_gather(jnp.concatenate([w_q, w_k, w_v], axis=1), GX, axis=0, tiled=True)
+    core = lax.axis_index("c")
+    cols = w_q.shape[1]
+
+    weights = jnp.concatenate([w_q, w_k, w_v], axis=1)
+    weights = lax.all_to_all(weights, "c", 1, 0, tiled=True)
+    weights = lax.all_gather(weights, "zh", axis=0, tiled=True)
     w_out = lax.all_gather(w_o.T, GX, axis=0, tiled=True)
 
     float_in = tokens.astype(F32)
@@ -177,50 +226,47 @@
     high = lax.reduce_precision(squares, 8, 7)
     gained = float_in * (1.0 + pre_gain.astype(F32))
     gained = jnp.concatenate([gained, high, squares - high], axis=1).astype(BF16)
+    gained, weights = lax.optimization_barrier((gained, weights))
+    columns = [weights]
+    for step in (1, 2, 3):
+        columns.append(lax.ppermute(weights, "x", [((i + step) % 4, i) for i in range(4)]))
     gained = everywhere(gained, GY, n_gy)
-    features = tokens.shape[1]
-    mean = jnp.sum(gained[:, :, features:].astype(F32), axis=(0, 2)) / D
-    scale_rows = lax.rsqrt(mean + epsilon)[:, None]
-    whole = jnp.swapaxes(gained[:, :, :features], 0, 1).reshape(tok_rows, D)
-    lin = jnp.dot(whole, weights, preferred_element_type=F32) * scale_rows
-
-    row_ids = me * tok_rows + jnp.arange(tok_rows, dtype=jnp.int32)
+    gained = everywhere(gained, "c", 2)
+
+    chip_rows = me // 2 * (2 * tok_rows)
+    row_ids = chip_rows + jnp.arange(2 * tok_rows, dtype=jnp.int32)
     request = row_ids // NEWTOK
     owner_mask = request[:, None] == jnp.arange(REQS, dtype=jnp.int32)[None, :]
     position = jnp.sum(jnp.where(owner_mask, cached_len[None, :], 0), axis=1) + row_ids % NEWTOK
     half = HD // 2
     inverse = jnp.power(10000.0, -2.0 * jnp.arange(half, dtype=F32) / HD)
     angle = position.astype(F32)[:, None] * inverse[None, :]
-    cosine, sine = jnp.cos(angle), jnp.sin(angle)
-
-    def rotate(values):
-        first, second = values[:, :half], values[:, half:]
-        return jnp.concatenate([first * cosine - second * sine, second * cosine + first * sine], axis=1)
-
-    q_cols = w_q.shape[1]
-    pieces = [rotate(lin[:, h * HD : (h + 1) * HD]) * query_scale for h in range(q_cols // HD)]
-    pieces += [rotate(lin[:, q_cols : q_cols + HD]), lin[:, q_cols + HD :]]
-    fresh_rows = jnp.concatenate(pieces, axis=1).astype(BF16)
-
-    mine = lax.all_to_all(fresh_rows, "c", 1, 0, tiled=True)
-    mine = everywhere(mine, CHIPS, n_chips).reshape(-1, q_cols)
-    qkv = everywhere(mine, "c", 2)
-
+    scale = jnp.where(core == 0, query_scale, 1.0).astype(F32)
+    cosine, sine = jnp.cos(angle) * scale, jnp.sin(angle) * scale
+    cosine = jnp.concatenate([cosine, cosine], axis=1)
+    sine = jnp.concatenate([-sine, sine], axis=1)
+    turns = jnp.stack([cosine, sine, jnp.where(core == 0, cosine, 1.0), jnp.where(core == 0, sine, 0.0)])
     meta = jnp.concatenate(
         [
             cached_len,
             new_len,
             slot_offset,
-            jnp.stack([me * k_cache.shape[0], me // 2 * (2 * tok_rows)]).astype(jnp.int32),
+            jnp.stack([me * k_cache.shape[0], chip_rows, core, lax.axis_index("x")]).astype(jnp.int32),
         ]
     )
-    k_pool, v_pool, sums = attend(meta, qkv, k_cache, v_cache)
+    mine = project(meta, gained, turns, columns)
+    mine, w_out = lax.optimization_barrier((mine, w_out))
+    mine = everywhere(mine, CHIPS, n_chips).reshape(-1, cols)
+    others = lax.ppermute(mine, "c", [(0, 1), (1, 0)])
+
+    k_pool, v_pool, sums = attend(meta, mine, others, k_cache, v_cache)
 
     both = lax.all_to_all(sums, "c", 0, 0)
     head = (both[0].astype(F32) + both[1].astype(F32)).astype(BF16)
     parts = lax.all_to_all(head.reshape(n_chips, -1, HD), CHIPS, 0, 0)
     attended = divide(meta, parts)
-    attended = lax.all_to_all(attended.reshape(2, tok_rows, HD), "c", 0, 0)
+    attended = lax.all_gather(attended, "c", axis=0)
+    attended = lax.dynamic_slice_in_dim(attended, core * tok_rows, tok_rows, 1)
     attended = jnp.swapaxes(attended, 0, 1).reshape(tok_rows, 2 * HD)
 
     partial_out = lax.dot_general(attended, w_out, (((1,), (1,)), ((), ())), preferred_element_type=F32)

time: 246 us -> 229 us (0.931)
  waiting for transfers between devices: 112 us -> 47.3 us
  starting transfers between devices: 23.9 us -> 53.6 us
  blocking collectives: 71.5 us -> 91.8 us
  matrix products: 5.76 us -> 2.5 us
    all_gather x1 -> x0, waiting for transfers between devices: 48.4 us -> none  [on_device(): lax.all_gather(jnp.concatenate([w_q, w_k, w_v], axis=1), GX, axis=0, tile...]
    all_to_all x3, waiting for transfers between devices: 62.2 us -> 19.5 us  [everywhere(): lax.all_to_all(jnp.broadcast_to(value[None], (count,) + value.shape), axe...]
    all_to_all x2 -> x0, blocking collectives: 28.1 us -> none  [the longest x1 24.4 us: on_device(): parts = lax.all_to_all(head.reshape(n_chips, -1, HD), CHIPS, 0, 0)]
    all_to_all x1, blocking collectives: 8.22 us -> 29.5 us  [everywhere(): lax.all_to_all(jnp.broadcast_to(value[None], (count,) + value.shape), axe...]
    all_gather x0 -> x2, blocking collectives: none -> 20.4 us  [the longest x1 16 us: on_device(): weights = lax.all_gather(weights, 'zh', axis=0, tiled=True)]
    ppermute x0 -> x4, starting transfers between devices: none -> 14.7 us  [the longest x3 9.29 us: on_device(): lax.ppermute(weights, 'x', [((i + step) % 4, i) for i in range(4)])]
    all_to_all x1 -> x2, waiting for transfers between devices: 1.05 us -> 15.6 us  [the longest x1 15.6 us: on_device(): parts = lax.all_to_all(head.reshape(n_chips, -1, HD), CHIPS, 0, 0)]
    all_to_all x1 -> x2, starting transfers between devices: 4.04 us -> 16.9 us  [the longest x1 10.3 us: on_device(): weights = lax.all_to_all(weights, 'c', 1, 0, tiled=True)]
  transfers between devices with their start and end apart: 6 -> 10, of which waited for: 5 -> 5; matrix products, arithmetic and copies ran while one was open for 4% -> 3% of each run, Pallas kernels for 2% -> 1%
where the time goes in v2:
time: 229 us; the launch traced here: 228 us
  blocking collectives  91.8 us (40%)
  starting transfers between devices  53.6 us (23%)
  waiting for transfers between devices  47.3 us (21%)
  between operations  14.3 us (6%)
  Pallas kernels  7.29 us (3%)
  local copies, waits for them, and re-layouts  5.52 us (2%)
  other arithmetic  5.37 us (2%)
  matrix products  2.5 us (1%)
    all_to_all x1, blocking collectives, on_device(): branch = jnp.sum(lax.all_to_all(partial_out, GY, 0, 0).astype(F32), axis=0)  36.3 us
    all_to_all x1, blocking collectives, everywhere(): lax.all_to_all(jnp.broadcast_to(value[None], (count,) + value.shape), axe...  29.5 us
    all_to_all x3, starting transfers between devices, everywhere(): lax.all_to_all(jnp.broadcast_to(value[None], (count,) + value.shape), axe...  22 us
    all_to_all x3, waiting for transfers between devices, everywhere(): lax.all_to_all(jnp.broadcast_to(value[None], (count,) + value.shape), axe...  19.5 us
    all_gather x1, blocking collectives, on_device(): weights = lax.all_gather(weights, 'zh', axis=0, tiled=True)  16 us
    all_to_all x1, waiting for transfers between devices, on_device(): parts = lax.all_to_all(head.reshape(n_chips, -1, HD), CHIPS, 0, 0)  15.6 us
    all_to_all x1, starting transfers between devices, on_device(): weights = lax.all_to_all(weights, 'c', 1, 0, tiled=True)  10.3 us
    ppermute x3, starting transfers between devices, on_device(): lax.ppermute(weights, 'x', [((i + step) % 4, i) for i in range(4)])  9.29 us
  transfers between devices with their start and end apart: 10, of which 5 were waited for; matrix products, arithmetic and copies ran while one was open for 3% of the time, Pallas kernels for 1%

profile of v2, /device:TPU:1, one launch (start us, length us, event | category | flops | bytes accessed | tf_op | source)
XLA Modules:
  0.0 227.8 jit_solution(7630908162029470643)
XLA Ops:
  9.5 10.3 %all-to-all-start = ((bf16[144,2,256]{2,0,1:T(8,128)(2,1)}), bf16[144,2,256]{2,0,1:T(8,128)(2,1)S(1)}, u32[]{:S(2)}, u32[]{:S(2)}) async-start(bf16[144,2,256]{2,0,1:T(8,128)(2,1)} %bitcast.37), calls=%async_computation | async-start | bytes 294912 | tf_op jit(solution)/shard_map/all_to_all | solution.py:220
  21.8 16.0 %all_gather.12.rest_0_ = bf16[1152,256]{1,0:T(8,128)(2,1)S(1)} all-gather(bf16[288,256]{1,0:T(8,128)(2,1)S(1)} %bitcast.42), channel_id=1, replica_groups=mesh['zh'=4,'x'=4,'c'=2,'y'=8,'zl'=2] {'zh'}, dimensions={0}, use_global_device_ids=true | all-gather | bytes 737280 | tf_op jit(solution)/shard_map/all_gather | solution.py:221
  38.8 10.6 %all-to-all-start.1 = ((bf16[16,72,290]{2,1,0:T(8,128)(2,1)}), bf16[16,72,290]{2,1,0:T(8,128)(2,1)S(1)}, u32[]{:S(2)}, u32[]{:S(2)}) async-start(bf16[16,72,290]{2,1,0:T(8,128)(2,1)} %broadcast_in_dim.27), calls=%async_computation.1 | async-start | bytes 1769472 | tf_op jit(solution)/shard_map/all_to_all | solution.py:26
  49.4 4.3 %collective-permute-start = (bf16[1152,256]{1,0:T(8,128)(2,1)S(1)}, bf16[1152,256]{1,0:T(8,128)(2,1)S(1)}, u32[]{:S(2)}, u32[]{:S(2)}) collective-permute-start(bf16[1152,256]{1,0:T(8,128)(2,1)S(1)} %all_gather.12.rest_0_), channel_id=1, source_target_pairs={{32,0},{64,32},{96,64},{0,96},{33,1},{65,33},{97,65},{1,97},{34,2}... | collective-permute-start | bytes 1769480 | tf_op jit(solution)/shard_map/ppermute | solution.py:232
  53.8 2.5 %collective-permute-start.1 = (bf16[1152,256]{1,0:T(8,128)(2,1)S(1)}, bf16[1152,256]{1,0:T(8,128)(2,1)}, u32[]{:S(2)}, u32[]{:S(2)}) collective-permute-start(bf16[1152,256]{1,0:T(8,128)(2,1)S(1)} %all_gather.12.rest_0_), channel_id=1, source_target_pairs={{64,0},{96,32},{0,64},{32,96},{65,1},{97,33},{1,65},{33,97},{66,2}... | collective-permute-start | bytes 1769480 | tf_op jit(solution)/shard_map/ppermute | solution.py:232
  56.2 2.5 %collective-permute-start.2 = (bf16[1152,256]{1,0:T(8,128)(2,1)S(1)}, bf16[1152,256]{1,0:T(8,128)(2,1)}, u32[]{:S(2)}, u32[]{:S(2)}) collective-permute-start(bf16[1152,256]{1,0:T(8,128)(2,1)S(1)} %all_gather.12.rest_0_), channel_id=1, source_target_pairs={{96,0},{0,32},{32,64},{64,96},{97,1},{1,33},{33,65},{65,97},{98,2}... | collective-permute-start | bytes 1769480 | tf_op jit(solution)/shard_map/ppermute | solution.py:232
  59.6 12.3 %all-to-all-done.1 = bf16[16,72,290]{2,1,0:T(8,128)(2,1)S(1)} async-done(((bf16[16,72,290]{2,1,0:T(8,128)(2,1)}), bf16[16,72,290]{2,1,0:T(8,128)(2,1)S(1)}, u32[]{:S(2)}, u32[]{:S(2)}) %all-to-all-start.1) | async-done | bytes 668192 | tf_op jit(solution)/shard_map/all_to_all | solution.py:26
  71.9 1.4 broadcast_in_dim.28
  73.3 7.5 %all-to-all-start.2 = ((bf16[2,16,72,290]{3,2,1,0:T(8,128)(2,1)}), bf16[2,16,72,290]{3,2,1,0:T(8,128)(2,1)S(1)}, u32[]{:S(2)}, u32[]{:S(2)}) async-start(bf16[2,16,72,290]{3,2,1,0:T(8,128)(2,1)} %broadcast_in_dim.28), calls=%async_computation.2 | async-start | bytes 3538944 | tf_op jit(solution)/shard_map/all_to_all | solution.py:26
  80.8 9.1 %collective-permute-done.2.rest_3_ = bf16[1152,256]{1,0:T(8,128)(2,1)} collective-permute-done((bf16[1152,256]{1,0:T(8,128)(2,1)S(1)}, bf16[1152,256]{1,0:T(8,128)(2,1)}, u32[]{:S(2)}, u32[]{:S(2)}) %collective-permute-start.2) | collective-permute-done | bytes 589856 | tf_op jit(solution)/shard_map/ppermute | solution.py:232
  89.8 2.1 project.1
  92.1 29.5 %all_to_all.54 = bf16[16,144,256]{2,1,0:T(8,128)(2,1)S(1)} all-to-all(bf16[16,144,256]{2,1,0:T(8,128)(2,1)S(1)} %broadcast_in_dim.33), channel_id=1, replica_groups=mesh['zh'=4,'x'=4,'c'=2,'y'=8,'zl'=2] {'zh','x'}, dimensions={0} | all-to-all | bytes 2359296 | tf_op jit(solution)/shard_map/all_to_all | solution.py:26
  121.5 5.4 %collective-permute-start.3 = (bf16[2304,256]{1,0:T(8,128)(2,1)S(1)}, bf16[2304,256]{1,0:T(8,128)(2,1)S(1)}, u32[]{:S(2)}, u32[]{:S(2)}) collective-permute-start(bf16[2304,256]{1,0:T(8,128)(2,1)S(1)} %bitcast.38), channel_id=1, source_target_pairs={{0,16},{16,0},{1,17},{17,1},{2,18},{18,2},{3,19},{19,3},{4,20},{20... | collective-permute-start | bytes 3538952 | tf_op jit(solution)/shard_map/ppermute | solution.py:260
  126.9 2.5 %collective-permute-done.3.others = bf16[2304,256]{1,0:T(8,128)(2,1)S(1)} collective-permute-done((bf16[2304,256]{1,0:T(8,128)(2,1)S(1)}, bf16[2304,256]{1,0:T(8,128)(2,1)S(1)}, u32[]{:S(2)}, u32[]{:S(2)}) %collective-permute-start.3) | collective-permute-done | bytes 1179680 | tf_op jit(solution)/shard_map/ppermute | solution.py:260
  129.4 4.5 %attend.1 = (bf16[1024,128]{1,0:T(8,128)(2,1)}, bf16[1024,128]{1,0:T(8,128)(2,1)}, bf16[2,2560,128]{2,1,0:T(8,128)(2,1)S(1)}) custom-call(s32[40]{0:T(128)S(1)} %concatenate.40.meta, bf16[2304,256]{1,0:T(8,128)(2,1)S(1)} %bitcast.39, bf16[2304,256]{1,0:T(8,128)(2,1)S(1)} %collective-permute-done.3.others, bf16[1024,128]{1,0:T(8,128)(2,1)S(1)} %copy-done, ...), custom_call_target="tpu_custom_call" | custom-call | tf_op jit(solution)/shard_map/attend/pallas_call | solution.py:159
  133.9 5.6 %all_to_all.55 = bf16[2,2560,128]{2,1,0:T(8,128)(2,1)S(1)} all-to-all(bf16[2,2560,128]{2,1,0:T(8,128)(2,1)S(1)} %get-tuple-element.13), channel_id=1, replica_groups=mesh['zh'=4,'x'=4,'c'=2,'y'=8,'zl'=2] {'c'}, dimensions={0} | all-to-all | bytes 2621440 | tf_op jit(solution)/shard_map/all_to_all | solution.py:264
  140.5 6.6 %all-to-all-start.5 = ((bf16[16,160,128]{2,1,0:T(8,128)(2,1)}), bf16[16,160,128]{2,1,0:T(8,128)(2,1)S(1)}, u32[]{:S(2)}, u32[]{:S(2)}) async-start(bf16[16,160,128]{2,1,0:T(8,128)(2,1)} %bitcast.14), calls=%async_computation.5 | async-start | bytes 1310720 | tf_op jit(solution)/shard_map/all_to_all | solution.py:266
  147.1 15.6 %all-to-all-done.5.parts = bf16[16,160,128]{2,1,0:T(8,128)(2,1)S(1)} async-done(((bf16[16,160,128]{2,1,0:T(8,128)(2,1)}), bf16[16,160,128]{2,1,0:T(8,128)(2,1)S(1)}, u32[]{:S(2)}, u32[]{:S(2)}) %all-to-all-start.5) | async-done | bytes 655392 | tf_op jit(solution)/shard_map/all_to_all | solution.py:266
  163.4 4.4 %all-gather = bf16[288,128]{1,0:T(8,128)(2,1)S(1)} all-gather(bf16[144,128]{1,0:T(8,128)(2,1)S(1)} %divide.1), channel_id=2, replica_groups=mesh['zh'=4,'x'=4,'c'=2,'y'=8,'zl'=2] {'c'}, dimensions={0}, use_global_device_ids=true | all-gather | bytes 110592 | tf_op jit(solution)/shard_map/all_gather | solution.py:268
  167.8 2.5 %convolution_convert_fusion = bf16[72,4608]{1,0:T(8,128)(2,1)S(1)} fusion(bf16[4608,256]{1,0:T(8,128)(2,1)} %all-gather.3.cloned.1.call-done, bf16[9,8,2,128]{3,2,1,0:T(2,128)(2,1)S(1)} %bitcast.44), kind=kOutput, calls=%fused_computation | convolution fusion | flops 170201088 | bytes 3059712 | tf_op jit(solution)/shard_map/dot_general | solution.py:272
  170.3 1.2 reshape.253
  171.8 36.3 %all_to_all.56 = bf16[16,72,288]{2,1,0:T(8,128)(2,1)S(1)} all-to-all(bf16[16,72,288]{2,1,0:T(8,128)(2,1)S(1)} %bitcast.40), channel_id=1, replica_groups=mesh['zh'=4,'x'=4,'c'=2,'y'=8,'zl'=2] {'y','zl'}, dimensions={0} | all-to-all | bytes 1327104 | tf_op jit(solution)/shard_map/all_to_all | solution.py:274
  208.9 3.9 %all-to-all-start.7 = ((f32[16,1,72]{2,1,0:T(1,128)}), f32[16,1,72]{2,1,0:T(1,128)S(1)}, u32[]{:S(2)}, u32[]{:S(2)}) async-start(f32[16,1,72]{2,1,0:T(1,128)} %broadcast_in_dim.58), calls=%async_computation.7 | async-start | bytes 16384 | tf_op jit(solution)/shard_map/all_to_all | solution.py:26
  212.9 7.3 %all-to-all-done.7 = f32[16,1,72]{2,1,0:T(1,128)S(1)} async-done(((f32[16,1,72]{2,1,0:T(1,128)}), f32[16,1,72]{2,1,0:T(1,128)S(1)}, u32[]{:S(2)}, u32[]{:S(2)}) %all-to-all-start.7) | async-done | bytes 4640 | tf_op jit(solution)/shard_map/all_to_all | solution.py:26
  (52 shorter events, 9.7 us)
Async XLA Ops:
  7.2 84.8 %all-gather.3.cloned.1.call-start = ((), (), s32[]{:S(2)}) async-start(), calls=%async_computation.8 | async-start | bytes 2433024 | tf_op jit(solution)/shard_map/all_gather | solution.py:222
  9.5 12.3 %all-to-all-start = ((bf16[144,2,256]{2,0,1:T(8,128)(2,1)}), bf16[144,2,256]{2,0,1:T(8,128)(2,1)S(1)}, u32[]{:S(2)}, u32[]{:S(2)}) async-start(bf16[144,2,256]{2,0,1:T(8,128)(2,1)} %bitcast.37), calls=%async_computation | async-start | bytes 294912 | tf_op jit(solution)/shard_map/all_to_all | solution.py:220
  37.8 20.9 %copy-start.3 = (s32[12]{0:T(128)S(1)}, s32[12]{0:T(128)}, u32[]{:S(2)}) copy-start(s32[12]{0:T(128)} %param.21) | copy-start | bytes 148
  37.8 21.1 %copy-start.5 = (s32[12]{0:T(128)S(1)}, s32[12]{0:T(128)}, u32[]{:S(2)}) copy-start(s32[12]{0:T(128)} %param.22) | copy-start | bytes 148
  37.8 21.1 %copy-start.6 = (s32[12]{0:T(128)S(1)}, s32[12]{0:T(128)}, u32[]{:S(2)}) copy-start(s32[12]{0:T(128)} %param.23) | copy-start | bytes 148
  38.8 33.0 %all-to-all-start.1 = ((bf16[16,72,290]{2,1,0:T(8,128)(2,1)}), bf16[16,72,290]{2,1,0:T(8,128)(2,1)S(1)}, u32[]{:S(2)}, u32[]{:S(2)}) async-start(bf16[16,72,290]{2,1,0:T(8,128)(2,1)} %broadcast_in_dim.27), calls=%async_computation.1 | async-start | bytes 1769472 | tf_op jit(solution)/shard_map/all_to_all | solution.py:26
  49.4 31.3 %collective-permute-start = (bf16[1152,256]{1,0:T(8,128)(2,1)S(1)}, bf16[1152,256]{1,0:T(8,128)(2,1)S(1)}, u32[]{:S(2)}, u32[]{:S(2)}) collective-permute-start(bf16[1152,256]{1,0:T(8,128)(2,1)S(1)} %all_gather.12.rest_0_), channel_id=1, source_target_pairs={{32,0},{64,32},{96,64},{0,96},{33,1},{65,33},{97,65},{1,97},{34,2}... | collective-permute-start | bytes 1769480 | tf_op jit(solution)/shard_map/ppermute | solution.py:232
  53.8 27.0 %collective-permute-start.1 = (bf16[1152,256]{1,0:T(8,128)(2,1)S(1)}, bf16[1152,256]{1,0:T(8,128)(2,1)}, u32[]{:S(2)}, u32[]{:S(2)}) collective-permute-start(bf16[1152,256]{1,0:T(8,128)(2,1)S(1)} %all_gather.12.rest_0_), channel_id=1, source_target_pairs={{64,0},{96,32},{0,64},{32,96},{65,1},{97,33},{1,65},{33,97},{66,2}... | collective-permute-start | bytes 1769480 | tf_op jit(solution)/shard_map/ppermute | solution.py:232
  56.2 33.6 %collective-permute-start.2 = (bf16[1152,256]{1,0:T(8,128)(2,1)S(1)}, bf16[1152,256]{1,0:T(8,128)(2,1)}, u32[]{:S(2)}, u32[]{:S(2)}) collective-permute-start(bf16[1152,256]{1,0:T(8,128)(2,1)S(1)} %all_gather.12.rest_0_), channel_id=1, source_target_pairs={{96,0},{0,32},{32,64},{64,96},{97,1},{1,33},{33,65},{65,97},{98,2}... | collective-permute-start | bytes 1769480 | tf_op jit(solution)/shard_map/ppermute | solution.py:232
  73.3 16.6 %all-to-all-start.2 = ((bf16[2,16,72,290]{3,2,1,0:T(8,128)(2,1)}), bf16[2,16,72,290]{3,2,1,0:T(8,128)(2,1)S(1)}, u32[]{:S(2)}, u32[]{:S(2)}) async-start(bf16[2,16,72,290]{3,2,1,0:T(8,128)(2,1)} %broadcast_in_dim.28), calls=%async_computation.2 | async-start | bytes 3538944 | tf_op jit(solution)/shard_map/all_to_all | solution.py:26
  92.1 37.3 %copy-start = (bf16[1024,128]{1,0:T(8,128)(2,1)S(1)}, bf16[1024,128]{1,0:T(8,128)(2,1)}, u32[]{:S(2)}) copy-start(bf16[1024,128]{1,0:T(8,128)(2,1)} %k_old.1) | copy-start | bytes 786436
  92.1 37.3 %copy-start.1 = (bf16[1024,128]{1,0:T(8,128)(2,1)S(1)}, bf16[1024,128]{1,0:T(8,128)(2,1)}, u32[]{:S(2)}) copy-start(bf16[1024,128]{1,0:T(8,128)(2,1)} %v_old.1) | copy-start | bytes 786436
  121.5 7.8 %collective-permute-start.3 = (bf16[2304,256]{1,0:T(8,128)(2,1)S(1)}, bf16[2304,256]{1,0:T(8,128)(2,1)S(1)}, u32[]{:S(2)}, u32[]{:S(2)}) collective-permute-start(bf16[2304,256]{1,0:T(8,128)(2,1)S(1)} %bitcast.38), channel_id=1, source_target_pairs={{0,16},{16,0},{1,17},{17,1},{2,18},{18,2},{3,19},{19,3},{4,20},{20... | collective-permute-start | bytes 3538952 | tf_op jit(solution)/shard_map/ppermute | solution.py:260
  140.5 22.2 %all-to-all-start.5 = ((bf16[16,160,128]{2,1,0:T(8,128)(2,1)}), bf16[16,160,128]{2,1,0:T(8,128)(2,1)S(1)}, u32[]{:S(2)}, u32[]{:S(2)}) async-start(bf16[16,160,128]{2,1,0:T(8,128)(2,1)} %bitcast.14), calls=%async_computation.5 | async-start | bytes 1310720 | tf_op jit(solution)/shard_map/all_to_all | solution.py:266
  171.8 41.1 %copy-start.4 = (bf16[288]{0:T(512)(128)(2,1)S(1)}, bf16[288]{0:T(512)(128)(2,1)}, u32[]{:S(2)}) copy-start(bf16[288]{0:T(512)(128)(2,1)} %param.18) | copy-start | bytes 1732
  171.8 48.4 %copy-start.2 = (bf16[72,288]{1,0:T(8,128)(2,1)S(1)}, bf16[72,288]{1,0:T(8,128)(2,1)}, u32[]{:S(2)}) copy-start(bf16[72,288]{1,0:T(8,128)(2,1)} %param.12) | copy-start | bytes 124420
  208.9 11.2 %all-to-all-start.7 = ((f32[16,1,72]{2,1,0:T(1,128)}), f32[16,1,72]{2,1,0:T(1,128)S(1)}, u32[]{:S(2)}, u32[]{:S(2)}) async-start(f32[16,1,72]{2,1,0:T(1,128)} %broadcast_in_dim.58), calls=%async_computation.7 | async-start | bytes 16384 | tf_op jit(solution)/shard_map/all_to_all | solution.py:26
Sparse Core Ops, SparseCore 0:
  11.1 75.9 all-gather.2

commit v3 on v2

--- a/solution.py
+++ b/solution.py
@@ -26,24 +26,27 @@
     return lax.all_to_all(jnp.broadcast_to(value[None], (count,) + value.shape), axes, 0, 0)
 
 
-def project_kernel(meta, tokens, turns, *rest):
-    columns, out = rest[:-1], rest[-1]
+def project_kernel(meta, mine, others, turns, own, right, ahead, behind, left, out):
+    on_core_0 = meta[3 * REQS + 2] == 0
     here = meta[3 * REQS + 3]
-    features = tokens.shape[3] - 2
-    count = len(columns)
+    features = mine.shape[2] - 2
+    count = 4
     total = jnp.zeros(out.shape, F32)
     squares = jnp.zeros((out.shape[0], 2), F32)
     for step in range(count):
         along = lax.rem(here + step, count)
-        for block in range(tokens.shape[1] // count):
+        for block in range(count):
             at = block * count + along
-            rows = jnp.concatenate([tokens[0, at], tokens[1, at]], axis=0)
+            a, b = mine[at], others[at]
+            rows = jnp.concatenate([jnp.where(on_core_0, a, b), jnp.where(on_core_0, b, a)], axis=0)
             squares += rows[:, features:].astype(F32)
-            total += jnp.dot(
-                rows[:, :features],
-                columns[step][block * features : (block + 1) * features, :],
-                preferred_element_type=F32,
-            )
+            if step == 2:
+                columns = ahead if block < 2 else behind
+                low = block % 2 * features
+            else:
+                columns = (own, right, None, left)[step]
+                low = block * features
+            total += jnp.dot(rows[:, :features], columns[low : low + features, :], preferred_element_type=F32)
     mean = jnp.sum(squares, axis=1, keepdims=True) * (1.0 / D)
     total = total * lax.rsqrt(mean + epsilon)
     for head in range(2):
@@ -52,16 +55,16 @@
         out[:, head * HD : (head + 1) * HD] = value.astype(BF16)
 
 
-def project(meta, tokens, turns, columns):
+def project(meta, mine, others, turns, columns):
     vmem = pl.BlockSpec(memory_space=pltpu.VMEM)
     return pl.pallas_call(
         project_kernel,
-        out_shape=jax.ShapeDtypeStruct((2 * tokens.shape[2], columns[0].shape[1]), BF16),
-        in_specs=[pl.BlockSpec(memory_space=pltpu.SMEM)] + [vmem] * (2 + len(columns)),
+        out_shape=jax.ShapeDtypeStruct((2 * mine.shape[1], columns[0].shape[1]), BF16),
+        in_specs=[pl.BlockSpec(memory_space=pltpu.SMEM)] + [vmem] * (3 + len(columns)),
         out_specs=vmem,
         compiler_params=pltpu.CompilerParams(vmem_limit_bytes=32 << 20),
         name="project",
-    )(meta, tokens, turns, *columns)
+    )(meta, mine, others, turns, *columns)
 
 
 def attend_kernel(meta, mine, others, k_old, v_old, k_pool, v_pool, sums, num, den, totals):
@@ -216,22 +219,33 @@
     core = lax.axis_index("c")
     cols = w_q.shape[1]
 
-    weights = jnp.concatenate([w_q, w_k, w_v], axis=1)
-    weights = lax.all_to_all(weights, "c", 1, 0, tiled=True)
-    weights = lax.all_gather(weights, "zh", axis=0, tiled=True)
-    w_out = lax.all_gather(w_o.T, GX, axis=0, tiled=True)
-
     float_in = tokens.astype(F32)
     squares = jnp.sum(float_in * float_in, axis=1, keepdims=True)
     high = lax.reduce_precision(squares, 8, 7)
     gained = float_in * (1.0 + pre_gain.astype(F32))
     gained = jnp.concatenate([gained, high, squares - high], axis=1).astype(BF16)
+    weights = jnp.concatenate([w_q, w_k, w_v], axis=1)
     gained, weights = lax.optimization_barrier((gained, weights))
-    columns = [weights]
-    for step in (1, 2, 3):
-        columns.append(lax.ppermute(weights, "x", [((i + step) % 4, i) for i in range(4)]))
     gained = everywhere(gained, GY, n_gy)
-    gained = everywhere(gained, "c", 2)
+    w_out = lax.all_gather(w_o.T, GX, axis=0, tiled=True)
+
+    weights = lax.all_gather(weights, "c", axis=0, tiled=True)
+    weights = lax.dynamic_slice_in_dim(weights, core * cols, cols, 1)
+    weights = lax.all_gather(weights, "zh", axis=0, tiled=True)
+    from_right = [((i + 1) % 4, i) for i in range(4)]
+    from_left = [((i - 1) % 4, i) for i in range(4)]
+    right = lax.ppermute(weights, "x", from_right)
+    left = lax.ppermute(weights, "x", from_left)
+    middle = weights.shape[0] // 2
+    columns = [
+        weights,
+        right,
+        lax.ppermute(right[:middle], "x", from_right),
+        lax.ppermute(left[middle:], "x", from_left),
+        left,
+    ]
+    swap = [(0, 1), (1, 0)]
+    other = lax.ppermute(gained, "c", swap)
 
     chip_rows = me // 2 * (2 * tok_rows)
     row_ids = chip_rows + jnp.arange(2 * tok_rows, dtype=jnp.int32)
@@ -254,10 +268,10 @@
             jnp.stack([me * k_cache.shape[0], chip_rows, core, lax.axis_index("x")]).astype(jnp.int32),
         ]
     )
-    mine = project(meta, gained, turns, columns)
+    mine = project(meta, gained, other, turns, columns)
     mine, w_out = lax.optimization_barrier((mine, w_out))
     mine = everywhere(mine, CHIPS, n_chips).reshape(-1, cols)
-    others = lax.ppermute(mine, "c", [(0, 1), (1, 0)])
+    others = lax.ppermute(mine, "c", swap)
 
     k_pool, v_pool, sums = attend(meta, mine, others, k_cache, v_cache)
 

time: 229 us -> 227 us (level)
  blocking collectives: 91.8 us -> 106 us
  starting transfers between devices: 53.6 us -> 40.5 us
    all_gather x1, blocking collectives: 16 us -> 31 us  [on_device(): weights = lax.all_gather(weights, 'zh', axis=0, tiled=True)]
    all_to_all x3 -> x2, waiting for transfers between devices: 19.5 us -> 7.26 us  [everywhere(): lax.all_to_all(jnp.broadcast_to(value[None], (count,) + value.shape), axe...]
    all_to_all x1 -> x0, starting transfers between devices: 10.3 us -> none  [on_device(): weights = lax.all_to_all(weights, 'c', 1, 0, tiled=True)]
    ppermute x4 -> x6, starting transfers between devices: 14.7 us -> 23.3 us  [the longest x1 5.32 us: on_device(): lax.ppermute(right[:middle], 'x', from_right)]
    all_to_all x3 -> x2, starting transfers between devices: 22 us -> 13.6 us  [everywhere(): lax.all_to_all(jnp.broadcast_to(value[None], (count,) + value.shape), axe...]
    all_to_all x1, blocking collectives: 29.5 us -> 36 us  [everywhere(): lax.all_to_all(jnp.broadcast_to(value[None], (count,) + value.shape), axe...]
    all_to_all x1, blocking collectives: 36.3 us -> 29.8 us  [on_device(): branch = jnp.sum(lax.all_to_all(partial_out, GY, 0, 0).astype(F32), axis=0)]
    all_to_all x1, waiting for transfers between devices: 15.6 us -> 20.6 us  [on_device(): parts = lax.all_to_all(head.reshape(n_chips, -1, HD), CHIPS, 0, 0)]
  transfers between devices with their start and end apart: 10 -> 10, of which waited for: 5 -> 8; matrix products, arithmetic and copies ran while one was open for 3% -> 2% of each run, Pallas kernels for 1% -> 1%
where the time goes in v3:
time: 227 us; the launch traced here: 226 us
  blocking collectives  106 us (47%)
  waiting for transfers between devices  45.7 us (20%)
  starting transfers between devices  40.5 us (18%)
  between operations  14.3 us (6%)
  Pallas kernels  8.47 us (4%)
  other arithmetic  5.38 us (2%)
  local copies, waits for them, and re-layouts  3.53 us (2%)
  matrix products  2.5 us (1%)
    all_to_all x1, blocking collectives, everywhere(): lax.all_to_all(jnp.broadcast_to(value[None], (count,) + value.shape), axe...  36 us
    all_gather x1, blocking collectives, on_device(): weights = lax.all_gather(weights, 'zh', axis=0, tiled=True)  31 us
    all_to_all x1, blocking collectives, on_device(): branch = jnp.sum(lax.all_to_all(partial_out, GY, 0, 0).astype(F32), axis=0)  29.8 us
    all_to_all x1, waiting for transfers between devices, on_device(): parts = lax.all_to_all(head.reshape(n_chips, -1, HD), CHIPS, 0, 0)  20.6 us
    all_to_all x2, starting transfers between devices, everywhere(): lax.all_to_all(jnp.broadcast_to(value[None], (count,) + value.shape), axe...  13.6 us
    all_to_all x2, waiting for transfers between devices, everywhere(): lax.all_to_all(jnp.broadcast_to(value[None], (count,) + value.shape), axe...  7.26 us
    pallas_call x1, Pallas kernels, attend(): pl.pallas_call(attend_kernel, out_shape=(jax.ShapeDtypeStruct(k_cache.sha...  6.38 us
    ppermute x1, waiting for transfers between devices, on_device(): lax.ppermute(left[middle:], 'x', from_left)  5.64 us
  transfers between devices with their start and end apart: 10, of which 8 were waited for; matrix products, arithmetic and copies ran while one was open for 2% of the time, Pallas kernels for 1%

profile of v3, /device:TPU:1, one launch (start us, length us, event | category | flops | bytes accessed | tf_op | source)
XLA Modules:
  0.0 226.4 jit_solution(2801894923865934471)
XLA Ops:
  11.8 9.7 %all-to-all-start = ((bf16[16,72,290]{2,1,0:T(8,128)(2,1)}), bf16[16,72,290]{2,1,0:T(8,128)(2,1)S(1)}, u32[]{:S(2)}, u32[]{:S(2)}) async-start(bf16[16,72,290]{2,1,0:T(8,128)(2,1)} %broadcast_in_dim.25), calls=%async_computation | async-start | bytes 1769472 | tf_op jit(solution)/shard_map/all_to_all | solution.py:26
  21.5 2.6 %all_gather.15 = bf16[288,512]{1,0:T(8,128)(2,1)S(1)} all-gather(bf16[144,512]{1,0:T(8,128)(2,1)S(1)} %pad_maximum_fusion.1), channel_id=1, replica_groups=mesh['zh'=4,'x'=4,'c'=2,'y'=8,'zl'=2] {'c'}, dimensions={0}, use_global_device_ids=true | all-gather | bytes 442368 | tf_op jit(solution)/shard_map/all_gather | solution.py:232
  24.2 31.0 %all_gather.16.own = bf16[1152,256]{1,0:T(8,128)(2,1)S(1)} all-gather(bf16[288,256]{1,0:T(8,128)(2,1)S(1)} %constant_dynamic-slice_fusion), channel_id=1, replica_groups=mesh['zh'=4,'x'=4,'c'=2,'y'=8,'zl'=2] {'zh'}, dimensions={0}, use_global_device_ids=true | all-gather | bytes 737280 | tf_op jit(solution)/shard_map/all_gather | solution.py:234
  55.2 5.2 %collective-permute-start.1 = (bf16[1152,256]{1,0:T(8,128)(2,1)S(1)}, bf16[1152,256]{1,0:T(8,128)(2,1)S(1)}, u32[]{:S(2)}, u32[]{:S(2)}) collective-permute-start(bf16[1152,256]{1,0:T(8,128)(2,1)S(1)} %all_gather.16.own), channel_id=1, source_target_pairs={{32,0},{64,32},{96,64},{0,96},{33,1},{65,33},{97,65},{1,97},{34,2}... | collective-permute-start | bytes 1769480 | tf_op jit(solution)/shard_map/ppermute | solution.py:237
  60.5 1.9 collective-permute-start.3
  62.7 4.6 %collective-permute-start = (bf16[16,72,290]{2,1,0:T(8,128)(2,1)S(1)}, bf16[16,72,290]{2,1,0:T(8,128)(2,1)S(1)}, u32[]{:S(2)}, u32[]{:S(2)}) collective-permute-start(bf16[16,72,290]{2,1,0:T(8,128)(2,1)S(1)} %all-to-all-done.mine), channel_id=1, source_target_pairs={{0,16},{16,0},{1,17},{17,1},{2,18},{18,2},{3,19},{19,3},{4,20},{20... | collective-permute-start | bytes 2004488 | tf_op jit(solution)/shard_map/ppermute | solution.py:248
  67.6 3.1 %collective-permute-done.1.right = bf16[1152,256]{1,0:T(8,128)(2,1)S(1)} collective-permute-done((bf16[1152,256]{1,0:T(8,128)(2,1)S(1)}, bf16[1152,256]{1,0:T(8,128)(2,1)S(1)}, u32[]{:S(2)}, u32[]{:S(2)}) %collective-permute-start.1) | collective-permute-done | bytes 589856 | tf_op jit(solution)/shard_map/ppermute | solution.py:237
  70.7 5.3 %collective-permute-start.2 = (bf16[576,256]{1,0:T(8,128)(2,1)S(1)}, bf16[576,256]{1,0:T(8,128)(2,1)S(1)}, u32[]{:S(2)}, u32[]{:S(2)}) collective-permute-start(bf16[576,256]{1,0:T(8,128)(2,1)S(1)} %slice.16), channel_id=1, source_target_pairs={{32,0},{64,32},{96,64},{0,96},{33,1},{65,33},{97,65},{1,97},{34,2}... | collective-permute-start | bytes 884744 | tf_op jit(solution)/shard_map/ppermute | solution.py:243
  77.4 1.9 collective-permute-start.4
  79.6 1.6 collective-permute-done.2.ahead
  81.2 5.6 %collective-permute-done.4.behind = bf16[576,256]{1,0:T(8,128)(2,1)S(1)} collective-permute-done((bf16[576,256]{1,0:T(8,128)(2,1)S(1)}, bf16[576,256]{1,0:T(8,128)(2,1)S(1)}, u32[]{:S(2)}, u32[]{:S(2)}) %collective-permute-start.4) | collective-permute-done | bytes 294944 | tf_op jit(solution)/shard_map/ppermute | solution.py:244
  88.3 3.0 %all-gather.3.cloned.1.call-done = bf16[4608,256]{1,0:T(8,128)(2,1)} async-done(((bf16[144,256]{1,0:T(8,128)(2,1)}), bf16[4608,256]{1,0:T(8,128)(2,1)}) %all-gather.3.cloned.1.call-update) | async-done | bytes 2359312 | tf_op jit(solution)/shard_map/all_gather | solution.py:230
  91.4 36.0 %all_to_all.30 = bf16[16,144,256]{2,1,0:T(8,128)(2,1)S(1)} all-to-all(bf16[16,144,256]{2,1,0:T(8,128)(2,1)S(1)} %broadcast_in_dim.50), channel_id=1, replica_groups=mesh['zh'=4,'x'=4,'c'=2,'y'=8,'zl'=2] {'zh','x'}, dimensions={0} | all-to-all | bytes 2359296 | tf_op jit(solution)/shard_map/all_to_all | solution.py:26
  127.5 4.3 %collective-permute-start.5 = (bf16[2304,256]{1,0:T(8,128)(2,1)S(1)}, bf16[2304,256]{1,0:T(8,128)(2,1)S(1)}, u32[]{:S(2)}, u32[]{:S(2)}) collective-permute-start(bf16[2304,256]{1,0:T(8,128)(2,1)S(1)} %bitcast.31), channel_id=1, source_target_pairs={{0,16},{16,0},{1,17},{17,1},{2,18},{18,2},{3,19},{19,3},{4,20},{20... | collective-permute-start | bytes 3538952 | tf_op jit(solution)/shard_map/ppermute | solution.py:274
  131.8 2.5 %collective-permute-done.5.others = bf16[2304,256]{1,0:T(8,128)(2,1)S(1)} collective-permute-done((bf16[2304,256]{1,0:T(8,128)(2,1)S(1)}, bf16[2304,256]{1,0:T(8,128)(2,1)S(1)}, u32[]{:S(2)}, u32[]{:S(2)}) %collective-permute-start.5) | collective-permute-done | bytes 1179680 | tf_op jit(solution)/shard_map/ppermute | solution.py:274
  134.2 6.4 %attend.1 = (bf16[1024,128]{1,0:T(8,128)(2,1)}, bf16[1024,128]{1,0:T(8,128)(2,1)}, bf16[2,2560,128]{2,1,0:T(8,128)(2,1)S(1)}) custom-call(s32[40]{0:T(128)S(1)} %concatenate.40.meta, bf16[2304,256]{1,0:T(8,128)(2,1)S(1)} %bitcast.32, bf16[2304,256]{1,0:T(8,128)(2,1)S(1)} %collective-permute-done.5.others, bf16[1024,128]{1,0:T(8,128)(2,1)S(1)} %copy-done, ...), custom_call_target="tpu_custom_call" | custom-call | tf_op jit(solution)/shard_map/attend/pallas_call | solution.py:162
  140.6 4.4 %all_to_all.31 = bf16[2,2560,128]{2,1,0:T(8,128)(2,1)S(1)} all-to-all(bf16[2,2560,128]{2,1,0:T(8,128)(2,1)S(1)} %get-tuple-element.13), channel_id=1, replica_groups=mesh['zh'=4,'x'=4,'c'=2,'y'=8,'zl'=2] {'c'}, dimensions={0} | all-to-all | bytes 2621440 | tf_op jit(solution)/shard_map/all_to_all | solution.py:278
  146.0 3.6 %all-to-all-start.3 = ((bf16[16,160,128]{2,1,0:T(8,128)(2,1)}), bf16[16,160,128]{2,1,0:T(8,128)(2,1)S(1)}, u32[]{:S(2)}, u32[]{:S(2)}) async-start(bf16[16,160,128]{2,1,0:T(8,128)(2,1)} %bitcast.12), calls=%async_computation.3 | async-start | bytes 1310720 | tf_op jit(solution)/shard_map/all_to_all | solution.py:280
  149.6 20.6 %all-to-all-done.3.parts = bf16[16,160,128]{2,1,0:T(8,128)(2,1)S(1)} async-done(((bf16[16,160,128]{2,1,0:T(8,128)(2,1)}), bf16[16,160,128]{2,1,0:T(8,128)(2,1)S(1)}, u32[]{:S(2)}, u32[]{:S(2)}) %all-to-all-start.3) | async-done | bytes 655392 | tf_op jit(solution)/shard_map/all_to_all | solution.py:280
  170.9 2.0 all-gather
  173.0 2.5 %convolution_convert_fusion = bf16[72,4608]{1,0:T(8,128)(2,1)S(1)} fusion(bf16[4608,256]{1,0:T(8,128)(2,1)} %all-gather.3.cloned.1.call-done, bf16[9,8,2,128]{3,2,1,0:T(2,128)(2,1)S(1)} %bitcast.35), kind=kOutput, calls=%fused_computation | convolution fusion | flops 170201088 | bytes 3059712 | tf_op jit(solution)/shard_map/dot_general | solution.py:286
  176.9 29.8 %all_to_all.32 = bf16[16,72,288]{2,1,0:T(8,128)(2,1)S(1)} all-to-all(bf16[16,72,288]{2,1,0:T(8,128)(2,1)S(1)} %bitcast.33), channel_id=1, replica_groups=mesh['zh'=4,'x'=4,'c'=2,'y'=8,'zl'=2] {'y','zl'}, dimensions={0} | all-to-all | bytes 1327104 | tf_op jit(solution)/shard_map/all_to_all | solution.py:288
  207.6 3.9 %all-to-all-start.5 = ((f32[16,1,72]{2,1,0:T(1,128)}), f32[16,1,72]{2,1,0:T(1,128)S(1)}, u32[]{:S(2)}, u32[]{:S(2)}) async-start(f32[16,1,72]{2,1,0:T(1,128)} %broadcast_in_dim.51), calls=%async_computation.5 | async-start | bytes 16384 | tf_op jit(solution)/shard_map/all_to_all | solution.py:26
  211.6 7.3 %all-to-all-done.5 = f32[16,1,72]{2,1,0:T(1,128)S(1)} async-done(((f32[16,1,72]{2,1,0:T(1,128)}), f32[16,1,72]{2,1,0:T(1,128)S(1)}, u32[]{:S(2)}, u32[]{:S(2)}) %all-to-all-start.5) | async-done | bytes 4640 | tf_op jit(solution)/shard_map/all_to_all | solution.py:26
  (54 shorter events, 13.1 us)
Async XLA Ops:
  7.2 84.1 %all-gather.3.cloned.1.call-start = ((), (), s32[]{:S(2)}) async-start(), calls=%async_computation.6 | async-start | bytes 2433024 | tf_op jit(solution)/shard_map/all_gather | solution.py:230
  11.8 50.6 %copy-start.3 = (s32[12]{0:T(128)S(1)}, s32[12]{0:T(128)}, u32[]{:S(2)}) copy-start(s32[12]{0:T(128)} %param.21) | copy-start | bytes 148
  11.8 50.7 %copy-start.5 = (s32[12]{0:T(128)S(1)}, s32[12]{0:T(128)}, u32[]{:S(2)}) copy-start(s32[12]{0:T(128)} %param.22) | copy-start | bytes 148
  11.8 50.7 %copy-start.6 = (s32[12]{0:T(128)S(1)}, s32[12]{0:T(128)}, u32[]{:S(2)}) copy-start(s32[12]{0:T(128)} %param.23) | copy-start | bytes 148
  11.8 50.8 %all-to-all-start = ((bf16[16,72,290]{2,1,0:T(8,128)(2,1)}), bf16[16,72,290]{2,1,0:T(8,128)(2,1)S(1)}, u32[]{:S(2)}, u32[]{:S(2)}) async-start(bf16[16,72,290]{2,1,0:T(8,128)(2,1)} %broadcast_in_dim.25), calls=%async_computation | async-start | bytes 1769472 | tf_op jit(solution)/shard_map/all_to_all | solution.py:26
  55.2 15.5 %collective-permute-start.1 = (bf16[1152,256]{1,0:T(8,128)(2,1)S(1)}, bf16[1152,256]{1,0:T(8,128)(2,1)S(1)}, u32[]{:S(2)}, u32[]{:S(2)}) collective-permute-start(bf16[1152,256]{1,0:T(8,128)(2,1)S(1)} %all_gather.16.own), channel_id=1, source_target_pairs={{32,0},{64,32},{96,64},{0,96},{33,1},{65,33},{97,65},{1,97},{34,2}... | collective-permute-start | bytes 1769480 | tf_op jit(solution)/shard_map/ppermute | solution.py:237
  60.5 17.0 %collective-permute-start.3 = (bf16[1152,256]{1,0:T(8,128)(2,1)S(1)}, bf16[1152,256]{1,0:T(8,128)(2,1)S(1)}, u32[]{:S(2)}, u32[]{:S(2)}) collective-permute-start(bf16[1152,256]{1,0:T(8,128)(2,1)S(1)} %all_gather.16.own), channel_id=1, source_target_pairs={{96,0},{0,32},{32,64},{64,96},{97,1},{1,33},{33,65},{65,97},{98,2}... | collective-permute-start | bytes 1769480 | tf_op jit(solution)/shard_map/ppermute | solution.py:238
  62.7 24.2 %collective-permute-start = (bf16[16,72,290]{2,1,0:T(8,128)(2,1)S(1)}, bf16[16,72,290]{2,1,0:T(8,128)(2,1)S(1)}, u32[]{:S(2)}, u32[]{:S(2)}) collective-permute-start(bf16[16,72,290]{2,1,0:T(8,128)(2,1)S(1)} %all-to-all-done.mine), channel_id=1, source_target_pairs={{0,16},{16,0},{1,17},{17,1},{2,18},{18,2},{3,19},{19,3},{4,20},{20... | collective-permute-start | bytes 2004488 | tf_op jit(solution)/shard_map/ppermute | solution.py:248
  70.7 10.6 %collective-permute-start.2 = (bf16[576,256]{1,0:T(8,128)(2,1)S(1)}, bf16[576,256]{1,0:T(8,128)(2,1)S(1)}, u32[]{:S(2)}, u32[]{:S(2)}) collective-permute-start(bf16[576,256]{1,0:T(8,128)(2,1)S(1)} %slice.16), channel_id=1, source_target_pairs={{32,0},{64,32},{96,64},{0,96},{33,1},{65,33},{97,65},{1,97},{34,2}... | collective-permute-start | bytes 884744 | tf_op jit(solution)/shard_map/ppermute | solution.py:243
  77.4 9.5 %collective-permute-start.4 = (bf16[576,256]{1,0:T(8,128)(2,1)S(1)}, bf16[576,256]{1,0:T(8,128)(2,1)S(1)}, u32[]{:S(2)}, u32[]{:S(2)}) collective-permute-start(bf16[576,256]{1,0:T(8,128)(2,1)S(1)} %slice.17), channel_id=1, source_target_pairs={{96,0},{0,32},{32,64},{64,96},{97,1},{1,33},{33,65},{65,97},{98,2}... | collective-permute-start | bytes 884744 | tf_op jit(solution)/shard_map/ppermute | solution.py:244
  91.4 42.8 %copy-start = (bf16[1024,128]{1,0:T(8,128)(2,1)S(1)}, bf16[1024,128]{1,0:T(8,128)(2,1)}, u32[]{:S(2)}) copy-start(bf16[1024,128]{1,0:T(8,128)(2,1)} %k_old.1) | copy-start | bytes 786436
  91.4 42.8 %copy-start.1 = (bf16[1024,128]{1,0:T(8,128)(2,1)S(1)}, bf16[1024,128]{1,0:T(8,128)(2,1)}, u32[]{:S(2)}) copy-start(bf16[1024,128]{1,0:T(8,128)(2,1)} %v_old.1) | copy-start | bytes 786436
  127.5 6.7 %collective-permute-start.5 = (bf16[2304,256]{1,0:T(8,128)(2,1)S(1)}, bf16[2304,256]{1,0:T(8,128)(2,1)S(1)}, u32[]{:S(2)}, u32[]{:S(2)}) collective-permute-start(bf16[2304,256]{1,0:T(8,128)(2,1)S(1)} %bitcast.31), channel_id=1, source_target_pairs={{0,16},{16,0},{1,17},{17,1},{2,18},{18,2},{3,19},{19,3},{4,20},{20... | collective-permute-start | bytes 3538952 | tf_op jit(solution)/shard_map/ppermute | solution.py:274
  146.0 24.2 %all-to-all-start.3 = ((bf16[16,160,128]{2,1,0:T(8,128)(2,1)}), bf16[16,160,128]{2,1,0:T(8,128)(2,1)S(1)}, u32[]{:S(2)}, u32[]{:S(2)}) async-start(bf16[16,160,128]{2,1,0:T(8,128)(2,1)} %bitcast.12), calls=%async_computation.3 | async-start | bytes 1310720 | tf_op jit(solution)/shard_map/all_to_all | solution.py:280
  176.9 34.7 %copy-start.4 = (bf16[288]{0:T(512)(128)(2,1)S(1)}, bf16[288]{0:T(512)(128)(2,1)}, u32[]{:S(2)}) copy-start(bf16[288]{0:T(512)(128)(2,1)} %param.18) | copy-start | bytes 1732
  176.9 42.0 %copy-start.2 = (bf16[72,288]{1,0:T(8,128)(2,1)S(1)}, bf16[72,288]{1,0:T(8,128)(2,1)}, u32[]{:S(2)}) copy-start(bf16[72,288]{1,0:T(8,128)(2,1)} %param.12) | copy-start | bytes 124420
  207.6 11.2 %all-to-all-start.5 = ((f32[16,1,72]{2,1,0:T(1,128)}), f32[16,1,72]{2,1,0:T(1,128)S(1)}, u32[]{:S(2)}, u32[]{:S(2)}) async-start(f32[16,1,72]{2,1,0:T(1,128)} %broadcast_in_dim.51), calls=%async_computation.5 | async-start | bytes 16384 | tf_op jit(solution)/shard_map/all_to_all | solution.py:26
Sparse Core Ops, SparseCore 0:
  11.1 80.1 all-gather.2

commit v4 on v3

--- a/solution.py
+++ b/solution.py
@@ -226,12 +226,15 @@
     gained = jnp.concatenate([gained, high, squares - high], axis=1).astype(BF16)
     weights = jnp.concatenate([w_q, w_k, w_v], axis=1)
     gained, weights = lax.optimization_barrier((gained, weights))
-    gained = everywhere(gained, GY, n_gy)
-    w_out = lax.all_gather(w_o.T, GX, axis=0, tiled=True)
+    gained = lax.all_gather(gained, "zl", axis=0, tiled=True)
+    gained = everywhere(gained, "y", n_gy // 2).reshape(n_gy, tok_rows, -1)
 
     weights = lax.all_gather(weights, "c", axis=0, tiled=True)
     weights = lax.dynamic_slice_in_dim(weights, core * cols, cols, 1)
-    weights = lax.all_gather(weights, "zh", axis=0, tiled=True)
+    weights = jnp.concatenate([weights, w_o.T], axis=0)
+    weights = lax.all_gather(weights, "zh", axis=0)
+    w_out = weights[:, 2 * w_q.shape[0] :, :]
+    weights = weights[:, : 2 * w_q.shape[0], :].reshape(-1, cols)
     from_right = [((i + 1) % 4, i) for i in range(4)]
     from_left = [((i - 1) % 4, i) for i in range(4)]
     right = lax.ppermute(weights, "x", from_right)
@@ -270,6 +273,8 @@
     )
     mine = project(meta, gained, other, turns, columns)
     mine, w_out = lax.optimization_barrier((mine, w_out))
+    w_out = lax.all_gather(w_out, ("x", "c"), axis=0).reshape((4, 2) + w_out.shape)
+    w_out = w_out.transpose(2, 0, 1, 3, 4).reshape(D, cols)
     mine = everywhere(mine, CHIPS, n_chips).reshape(-1, cols)
     others = lax.ppermute(mine, "c", swap)
 

time: 227 us -> 222 us (0.978)
  blocking collectives: 106 us -> 80.2 us
  starting transfers between devices: 40.5 us -> 56.1 us
  local copies, waits for them, and re-layouts: 3.53 us -> 8.67 us
    all_to_all x1 -> x0, blocking collectives: 36 us -> none  [everywhere(): lax.all_to_all(jnp.broadcast_to(value[None], (count,) + value.shape), axe...]
    all_to_all x2 -> x3, waiting for transfers between devices: 7.26 us -> 24.6 us  [everywhere(): lax.all_to_all(jnp.broadcast_to(value[None], (count,) + value.shape), axe...]
    all_to_all x1, waiting for transfers between devices: 20.6 us -> 12.2 us  [on_device(): parts = lax.all_to_all(head.reshape(n_chips, -1, HD), CHIPS, 0, 0)]
    all_to_all x1, starting transfers between devices: 3.59 us -> 11.6 us  [on_device(): parts = lax.all_to_all(head.reshape(n_chips, -1, HD), CHIPS, 0, 0)]
    all_to_all x1, blocking collectives: 29.8 us -> 37.6 us  [on_device(): branch = jnp.sum(lax.all_to_all(partial_out, GY, 0, 0).astype(F32), axis=0)]
    ppermute x1, starting transfers between devices: 4.29 us -> 10.7 us  [on_device(): others = lax.ppermute(mine, 'c', swap)]
    all_gather x1 -> x2, blocking collectives: 31 us -> 27.5 us  [the longest x1 22.3 us: on_device(): weights = lax.all_gather(weights, 'zh', axis=0)]
    transpose x0 -> x1, local copies, waits for them, and re-layouts: none -> 3.33 us  [on_device(): w_out = w_out.transpose(2, 0, 1, 3, 4).reshape(D, cols)]
  transfers between devices with their start and end apart: 10 -> 11, of which waited for: 8 -> 7; matrix products, arithmetic and copies ran while one was open for 2% -> 3% of each run, Pallas kernels for 1% -> 2%
where the time goes in v4:
time: 222 us; the launch traced here: 221 us
  blocking collectives  80.2 us (36%)
  starting transfers between devices  56.1 us (25%)
  waiting for transfers between devices  46.8 us (21%)
  between operations  14.4 us (6%)
  local copies, waits for them, and re-layouts  8.67 us (4%)
  Pallas kernels  6.61 us (3%)
  other arithmetic  5.41 us (2%)
  matrix products  2.49 us (1%)
    all_to_all x1, blocking collectives, on_device(): branch = jnp.sum(lax.all_to_all(partial_out, GY, 0, 0).astype(F32), axis=0)  37.6 us
    all_to_all x3, waiting for transfers between devices, everywhere(): lax.all_to_all(jnp.broadcast_to(value[None], (count,) + value.shape), axe...  24.6 us
    all_gather x1, blocking collectives, on_device(): weights = lax.all_gather(weights, 'zh', axis=0)  22.3 us
    all_to_all x3, starting transfers between devices, everywhere(): lax.all_to_all(jnp.broadcast_to(value[None], (count,) + value.shape), axe...  14.7 us
    all_to_all x1, waiting for transfers between devices, on_device(): parts = lax.all_to_all(head.reshape(n_chips, -1, HD), CHIPS, 0, 0)  12.2 us
    all_to_all x1, starting transfers between devices, on_device(): parts = lax.all_to_all(head.reshape(n_chips, -1, HD), CHIPS, 0, 0)  11.6 us
    ppermute x1, starting transfers between devices, on_device(): others = lax.ppermute(mine, 'c', swap)  10.7 us
    all_to_all x1, blocking collectives, on_device(): both = lax.all_to_all(sums, 'c', 0, 0)  5.79 us
  transfers between devices with their start and end apart: 11, of which 7 were waited for; matrix products, arithmetic and copies ran while one was open for 3% of the time, Pallas kernels for 2%

profile of v4, /device:TPU:1, one launch (start us, length us, event | category | flops | bytes accessed | tf_op | source)
XLA Modules:
  0.0 220.7 jit_solution(10700033803094183006)
XLA Ops:
  10.1 5.1 %all_gather.24 = bf16[144,290]{1,0:T(8,128)(2,1)S(1)} all-gather(bf16[72,290]{1,0:T(8,128)(2,1)S(1)} %pad_maximum_fusion.3), channel_id=1, replica_groups=mesh['zh'=4,'x'=4,'c'=2,'y'=8,'zl'=2] {'zl'}, dimensions={0}, use_global_device_ids=true | all-gather | bytes 125280 | tf_op jit(solution)/shard_map/all_gather | solution.py:229
  16.2 7.0 %all-to-all-start = ((bf16[8,144,290]{2,1,0:T(8,128)(2,1)}), bf16[8,144,290]{2,1,0:T(8,128)(2,1)S(1)}, u32[]{:S(2)}, u32[]{:S(2)}) async-start(bf16[8,144,290]{2,1,0:T(8,128)(2,1)} %broadcast_in_dim.25), calls=%async_computation | async-start | bytes 1769472 | tf_op jit(solution)/shard_map/all_to_all | solution.py:26
  23.1 5.0 %all_gather.25 = bf16[288,512]{1,0:T(8,128)(2,1)S(1)} all-gather(bf16[144,512]{1,0:T(8,128)(2,1)S(1)} %pad_maximum_fusion.2), channel_id=1, replica_groups=mesh['zh'=4,'x'=4,'c'=2,'y'=8,'zl'=2] {'c'}, dimensions={0}, use_global_device_ids=true | all-gather | bytes 442368 | tf_op jit(solution)/shard_map/all_gather | solution.py:232
  28.2 22.3 %all-gather = bf16[1728,256]{1,0:T(8,128)(2,1)S(1)} all-gather(bf16[432,256]{1,0:T(8,128)(2,1)S(1)} %pad_maximum_fusion.1), channel_id=2, replica_groups=mesh['zh'=4,'x'=4,'c'=2,'y'=8,'zl'=2] {'zh'}, dimensions={0}, use_global_device_ids=true | all-gather | bytes 1105920 | tf_op jit(solution)/shard_map/all_gather | solution.py:235
  50.6 4.4 %collective-permute-start.1 = (bf16[1152,256]{1,0:T(8,128)(2,1)S(1)}, bf16[1152,256]{1,0:T(8,128)(2,1)S(1)}, u32[]{:S(2)}, u32[]{:S(2)}) collective-permute-start(bf16[1152,256]{1,0:T(8,128)(2,1)S(1)} %bitcast.42), channel_id=1, source_target_pairs={{32,0},{64,32},{96,64},{0,96},{33,1},{65,33},{97,65},{1,97},{34,2}... | collective-permute-start | bytes 1769480 | tf_op jit(solution)/shard_map/ppermute | solution.py:240
  55.0 1.9 collective-permute-start.3
  57.9 5.6 %collective-permute-start = (bf16[16,72,290]{2,1,0:T(8,128)(2,1)S(1)}, bf16[16,72,290]{2,1,0:T(8,128)(2,1)S(1)}, u32[]{:S(2)}, u32[]{:S(2)}) collective-permute-start(bf16[16,72,290]{2,1,0:T(8,128)(2,1)S(1)} %bitcast.40), channel_id=1, source_target_pairs={{0,16},{16,0},{1,17},{17,1},{2,18},{18,2},{3,19},{19,3},{4,20},{20... | collective-permute-start | bytes 2004488 | tf_op jit(solution)/shard_map/ppermute | solution.py:251
  64.2 5.3 %collective-permute-start.2 = (bf16[576,256]{1,0:T(8,128)(2,1)S(1)}, bf16[576,256]{1,0:T(8,128)(2,1)S(1)}, u32[]{:S(2)}, u32[]{:S(2)}) collective-permute-start(bf16[576,256]{1,0:T(8,128)(2,1)S(1)} %slice.25), channel_id=1, source_target_pairs={{32,0},{64,32},{96,64},{0,96},{33,1},{65,33},{97,65},{1,97},{34,2}... | collective-permute-start | bytes 884744 | tf_op jit(solution)/shard_map/ppermute | solution.py:246
  69.6 1.9 collective-permute-start.4
  73.2 5.1 %collective-permute-done.4.behind = bf16[576,256]{1,0:T(8,128)(2,1)S(1)} collective-permute-done((bf16[576,256]{1,0:T(8,128)(2,1)S(1)}, bf16[576,256]{1,0:T(8,128)(2,1)S(1)}, u32[]{:S(2)}, u32[]{:S(2)}) %collective-permute-start.4) | collective-permute-done | bytes 294944 | tf_op jit(solution)/shard_map/ppermute | solution.py:247
  80.8 3.8 %all-to-all-start.1 = ((bf16[16,144,256]{2,1,0:T(8,128)(2,1)}), bf16[16,144,256]{2,1,0:T(8,128)(2,1)S(1)}, u32[]{:S(2)}, u32[]{:S(2)}) async-start(bf16[16,144,256]{2,1,0:T(8,128)(2,1)} %broadcast_in_dim.50), calls=%async_computation.1 | async-start | bytes 2359296 | tf_op jit(solution)/shard_map/all_to_all | solution.py:26
  85.4 17.4 %all-to-all-done.1 = bf16[16,144,256]{2,1,0:T(8,128)(2,1)S(1)} async-done(((bf16[16,144,256]{2,1,0:T(8,128)(2,1)}), bf16[16,144,256]{2,1,0:T(8,128)(2,1)S(1)}, u32[]{:S(2)}, u32[]{:S(2)}) %all-to-all-start.1) | async-done | bytes 1179680 | tf_op jit(solution)/shard_map/all_to_all | solution.py:26
  102.8 10.7 %collective-permute-start.5 = (bf16[2304,256]{1,0:T(8,128)(2,1)S(1)}, bf16[2304,256]{1,0:T(8,128)(2,1)S(1)}, u32[]{:S(2)}, u32[]{:S(2)}) collective-permute-start(bf16[2304,256]{1,0:T(8,128)(2,1)S(1)} %bitcast.38), channel_id=1, source_target_pairs={{0,16},{16,0},{1,17},{17,1},{2,18},{18,2},{3,19},{19,3},{4,20},{20... | collective-permute-start | bytes 3538952 | tf_op jit(solution)/shard_map/ppermute | solution.py:279
  113.4 2.5 %collective-permute-done.5.others = bf16[2304,256]{1,0:T(8,128)(2,1)S(1)} collective-permute-done((bf16[2304,256]{1,0:T(8,128)(2,1)S(1)}, bf16[2304,256]{1,0:T(8,128)(2,1)S(1)}, u32[]{:S(2)}, u32[]{:S(2)}) %collective-permute-start.5) | collective-permute-done | bytes 1179680 | tf_op jit(solution)/shard_map/ppermute | solution.py:279
  115.9 4.5 %attend.1 = (bf16[1024,128]{1,0:T(8,128)(2,1)}, bf16[1024,128]{1,0:T(8,128)(2,1)}, bf16[2,2560,128]{2,1,0:T(8,128)(2,1)S(1)}) custom-call(s32[40]{0:T(128)S(1)} %concatenate.43.meta, bf16[2304,256]{1,0:T(8,128)(2,1)S(1)} %bitcast.39, bf16[2304,256]{1,0:T(8,128)(2,1)S(1)} %collective-permute-done.5.others, bf16[1024,128]{1,0:T(8,128)(2,1)S(1)} %copy-done, ...), custom_call_target="tpu_custom_call" | custom-call | tf_op jit(solution)/shard_map/attend/pallas_call | solution.py:162
  120.4 5.8 %all_to_all.30 = bf16[2,2560,128]{2,1,0:T(8,128)(2,1)S(1)} all-to-all(bf16[2,2560,128]{2,1,0:T(8,128)(2,1)S(1)} %get-tuple-element.13), channel_id=1, replica_groups=mesh['zh'=4,'x'=4,'c'=2,'y'=8,'zl'=2] {'c'}, dimensions={0} | all-to-all | bytes 2621440 | tf_op jit(solution)/shard_map/all_to_all | solution.py:283
  127.3 11.6 %all-to-all-start.3 = ((bf16[16,160,128]{2,1,0:T(8,128)(2,1)}), bf16[16,160,128]{2,1,0:T(8,128)(2,1)S(1)}, u32[]{:S(2)}, u32[]{:S(2)}) async-start(bf16[16,160,128]{2,1,0:T(8,128)(2,1)} %bitcast.15), calls=%async_computation.3 | async-start | bytes 1310720 | tf_op jit(solution)/shard_map/all_to_all | solution.py:285
  138.8 3.3 %copy.37 = bf16[4,4,2,144,256]{4,3,2,1,0:T(8,128)(2,1)} copy(bf16[4,4,2,144,256]{4,3,0,2,1:T(8,128)(2,1)} %bitcast.49) | data formatting | bytes 4718592 | tf_op jit(solution)/shard_map/transpose | solution.py:277
  142.2 12.2 %all-to-all-done.3.parts = bf16[16,160,128]{2,1,0:T(8,128)(2,1)S(1)} async-done(((bf16[16,160,128]{2,1,0:T(8,128)(2,1)}), bf16[16,160,128]{2,1,0:T(8,128)(2,1)S(1)}, u32[]{:S(2)}, u32[]{:S(2)}) %all-to-all-start.3) | async-done | bytes 655392 | tf_op jit(solution)/shard_map/all_to_all | solution.py:285
  155.1 4.4 %all-gather.1 = bf16[288,128]{1,0:T(8,128)(2,1)S(1)} all-gather(bf16[144,128]{1,0:T(8,128)(2,1)S(1)} %divide.1), channel_id=3, replica_groups=mesh['zh'=4,'x'=4,'c'=2,'y'=8,'zl'=2] {'c'}, dimensions={0}, use_global_device_ids=true | all-gather | bytes 110592 | tf_op jit(solution)/shard_map/all_gather | solution.py:287
  159.5 2.5 %convolution_convert_fusion = bf16[72,4608]{1,0:T(8,128)(2,1)S(1)} fusion(bf16[4608,256]{1,0:T(8,128)(2,1)} %bitcast.45, bf16[9,8,2,128]{3,2,1,0:T(2,128)(2,1)S(1)} %bitcast.51), kind=kOutput, calls=%fused_computation | convolution fusion | flops 170201088 | bytes 3059712 | tf_op jit(solution)/shard_map/dot_general | solution.py:291
  163.5 37.6 %all_to_all.31 = bf16[16,72,288]{2,1,0:T(8,128)(2,1)S(1)} all-to-all(bf16[16,72,288]{2,1,0:T(8,128)(2,1)S(1)} %bitcast.46), channel_id=1, replica_groups=mesh['zh'=4,'x'=4,'c'=2,'y'=8,'zl'=2] {'y','zl'}, dimensions={0} | all-to-all | bytes 1327104 | tf_op jit(solution)/shard_map/all_to_all | solution.py:293
  201.9 3.9 %all-to-all-start.5 = ((f32[16,1,72]{2,1,0:T(1,128)}), f32[16,1,72]{2,1,0:T(1,128)S(1)}, u32[]{:S(2)}, u32[]{:S(2)}) async-start(f32[16,1,72]{2,1,0:T(1,128)} %broadcast_in_dim.51), calls=%async_computation.5 | async-start | bytes 16384 | tf_op jit(solution)/shard_map/all_to_all | solution.py:26
  205.9 7.3 %all-to-all-done.5 = f32[16,1,72]{2,1,0:T(1,128)S(1)} async-done(((f32[16,1,72]{2,1,0:T(1,128)}), f32[16,1,72]{2,1,0:T(1,128)S(1)}, u32[]{:S(2)}, u32[]{:S(2)}) %all-to-all-start.5) | async-done | bytes 4640 | tf_op jit(solution)/shard_map/all_to_all | solution.py:26
  (62 shorter events, 15.3 us)
Async XLA Ops:
  16.2 12.0 %copy-start.3 = (bf16[256,144]{0,1:T(8,128)(2,1)S(1)}, bf16[256,144]{0,1:T(8,128)(2,1)}, u32[]{:S(2)}) copy-start(bf16[256,144]{0,1:T(8,128)(2,1)} %param.17) | copy-start | bytes 221188
  16.2 41.7 %all-to-all-start = ((bf16[8,144,290]{2,1,0:T(8,128)(2,1)}), bf16[8,144,290]{2,1,0:T(8,128)(2,1)S(1)}, u32[]{:S(2)}, u32[]{:S(2)}) async-start(bf16[8,144,290]{2,1,0:T(8,128)(2,1)} %broadcast_in_dim.25), calls=%async_computation | async-start | bytes 1769472 | tf_op jit(solution)/shard_map/all_to_all | solution.py:26
  28.2 28.8 %copy-start.4 = (s32[12]{0:T(128)S(1)}, s32[12]{0:T(128)}, u32[]{:S(2)}) copy-start(s32[12]{0:T(128)} %param.21) | copy-start | bytes 148
  28.2 29.6 %copy-start.6 = (s32[12]{0:T(128)S(1)}, s32[12]{0:T(128)}, u32[]{:S(2)}) copy-start(s32[12]{0:T(128)} %param.22) | copy-start | bytes 148
  28.2 29.6 %copy-start.7 = (s32[12]{0:T(128)S(1)}, s32[12]{0:T(128)}, u32[]{:S(2)}) copy-start(s32[12]{0:T(128)} %param.23) | copy-start | bytes 148
  50.6 13.6 %collective-permute-start.1 = (bf16[1152,256]{1,0:T(8,128)(2,1)S(1)}, bf16[1152,256]{1,0:T(8,128)(2,1)S(1)}, u32[]{:S(2)}, u32[]{:S(2)}) collective-permute-start(bf16[1152,256]{1,0:T(8,128)(2,1)S(1)} %bitcast.42), channel_id=1, source_target_pairs={{32,0},{64,32},{96,64},{0,96},{33,1},{65,33},{97,65},{1,97},{34,2}... | collective-permute-start | bytes 1769480 | tf_op jit(solution)/shard_map/ppermute | solution.py:240
  55.0 14.5 %collective-permute-start.3 = (bf16[1152,256]{1,0:T(8,128)(2,1)S(1)}, bf16[1152,256]{1,0:T(8,128)(2,1)S(1)}, u32[]{:S(2)}, u32[]{:S(2)}) collective-permute-start(bf16[1152,256]{1,0:T(8,128)(2,1)S(1)} %bitcast.43), channel_id=1, source_target_pairs={{96,0},{0,32},{32,64},{64,96},{97,1},{1,33},{33,65},{65,97},{98,2}... | collective-permute-start | bytes 1769480 | tf_op jit(solution)/shard_map/ppermute | solution.py:241
  57.9 20.3 %collective-permute-start = (bf16[16,72,290]{2,1,0:T(8,128)(2,1)S(1)}, bf16[16,72,290]{2,1,0:T(8,128)(2,1)S(1)}, u32[]{:S(2)}, u32[]{:S(2)}) collective-permute-start(bf16[16,72,290]{2,1,0:T(8,128)(2,1)S(1)} %bitcast.40), channel_id=1, source_target_pairs={{0,16},{16,0},{1,17},{17,1},{2,18},{18,2},{3,19},{19,3},{4,20},{20... | collective-permute-start | bytes 2004488 | tf_op jit(solution)/shard_map/ppermute | solution.py:251
  64.2 9.0 %collective-permute-start.2 = (bf16[576,256]{1,0:T(8,128)(2,1)S(1)}, bf16[576,256]{1,0:T(8,128)(2,1)S(1)}, u32[]{:S(2)}, u32[]{:S(2)}) collective-permute-start(bf16[576,256]{1,0:T(8,128)(2,1)S(1)} %slice.25), channel_id=1, source_target_pairs={{32,0},{64,32},{96,64},{0,96},{33,1},{65,33},{97,65},{1,97},{34,2}... | collective-permute-start | bytes 884744 | tf_op jit(solution)/shard_map/ppermute | solution.py:246
  69.6 8.7 %collective-permute-start.4 = (bf16[576,256]{1,0:T(8,128)(2,1)S(1)}, bf16[576,256]{1,0:T(8,128)(2,1)S(1)}, u32[]{:S(2)}, u32[]{:S(2)}) collective-permute-start(bf16[576,256]{1,0:T(8,128)(2,1)S(1)} %slice.26), channel_id=1, source_target_pairs={{96,0},{0,32},{32,64},{64,96},{97,1},{1,33},{33,65},{65,97},{98,2}... | collective-permute-start | bytes 884744 | tf_op jit(solution)/shard_map/ppermute | solution.py:247
  80.8 35.1 %copy-start = (bf16[1024,128]{1,0:T(8,128)(2,1)S(1)}, bf16[1024,128]{1,0:T(8,128)(2,1)}, u32[]{:S(2)}) copy-start(bf16[1024,128]{1,0:T(8,128)(2,1)} %k_old.1) | copy-start | bytes 786436
  80.8 35.1 %copy-start.1 = (bf16[1024,128]{1,0:T(8,128)(2,1)S(1)}, bf16[1024,128]{1,0:T(8,128)(2,1)}, u32[]{:S(2)}) copy-start(bf16[1024,128]{1,0:T(8,128)(2,1)} %v_old.1) | copy-start | bytes 786436
  80.8 22.0 %all-to-all-start.1 = ((bf16[16,144,256]{2,1,0:T(8,128)(2,1)}), bf16[16,144,256]{2,1,0:T(8,128)(2,1)S(1)}, u32[]{:S(2)}, u32[]{:S(2)}) async-start(bf16[16,144,256]{2,1,0:T(8,128)(2,1)} %broadcast_in_dim.50), calls=%async_computation.1 | async-start | bytes 2359296 | tf_op jit(solution)/shard_map/all_to_all | solution.py:26
  84.6 54.2 %all-gather.5.cloned.1.call-start = ((), (), s32[]{:S(2)}) async-start(), calls=%async_computation.6 | async-start | bytes 2654208 | tf_op jit(solution)/shard_map/all_gather | solution.py:276
  102.8 13.1 %collective-permute-start.5 = (bf16[2304,256]{1,0:T(8,128)(2,1)S(1)}, bf16[2304,256]{1,0:T(8,128)(2,1)S(1)}, u32[]{:S(2)}, u32[]{:S(2)}) collective-permute-start(bf16[2304,256]{1,0:T(8,128)(2,1)S(1)} %bitcast.38), channel_id=1, source_target_pairs={{0,16},{16,0},{1,17},{17,1},{2,18},{18,2},{3,19},{19,3},{4,20},{20... | collective-permute-start | bytes 3538952 | tf_op jit(solution)/shard_map/ppermute | solution.py:279
  127.3 27.2 %all-to-all-start.3 = ((bf16[16,160,128]{2,1,0:T(8,128)(2,1)}), bf16[16,160,128]{2,1,0:T(8,128)(2,1)S(1)}, u32[]{:S(2)}, u32[]{:S(2)}) async-start(bf16[16,160,128]{2,1,0:T(8,128)(2,1)} %bitcast.15), calls=%async_computation.3 | async-start | bytes 1310720 | tf_op jit(solution)/shard_map/all_to_all | solution.py:285
  163.4 42.4 %copy-start.5 = (bf16[288]{0:T(512)(128)(2,1)S(1)}, bf16[288]{0:T(512)(128)(2,1)}, u32[]{:S(2)}) copy-start(bf16[288]{0:T(512)(128)(2,1)} %param.18) | copy-start | bytes 1732
  163.4 49.7 %copy-start.2 = (bf16[72,288]{1,0:T(8,128)(2,1)S(1)}, bf16[72,288]{1,0:T(8,128)(2,1)}, u32[]{:S(2)}) copy-start(bf16[72,288]{1,0:T(8,128)(2,1)} %param.12) | copy-start | bytes 124420
  201.9 11.2 %all-to-all-start.5 = ((f32[16,1,72]{2,1,0:T(1,128)}), f32[16,1,72]{2,1,0:T(1,128)S(1)}, u32[]{:S(2)}, u32[]{:S(2)}) async-start(f32[16,1,72]{2,1,0:T(1,128)} %broadcast_in_dim.51), calls=%async_computation.5 | async-start | bytes 16384 | tf_op jit(solution)/shard_map/all_to_all | solution.py:26
Sparse Core Ops, SparseCore 0:
  87.6 41.2 all-gather.4

commit v5 on v3

--- a/solution.py
+++ b/solution.py
@@ -41,12 +41,10 @@
             rows = jnp.concatenate([jnp.where(on_core_0, a, b), jnp.where(on_core_0, b, a)], axis=0)
             squares += rows[:, features:].astype(F32)
             if step == 2:
-                columns = ahead if block < 2 else behind
-                low = block % 2 * features
+                columns = (ahead if block < 2 else behind)[block % 2]
             else:
-                columns = (own, right, None, left)[step]
-                low = block * features
-            total += jnp.dot(rows[:, :features], columns[low : low + features, :], preferred_element_type=F32)
+                columns = (own, right, None, left)[step][block]
+            total += jnp.dot(rows[:, :features], columns[:features, :], preferred_element_type=F32)
     mean = jnp.sum(squares, axis=1, keepdims=True) * (1.0 / D)
     total = total * lax.rsqrt(mean + epsilon)
     for head in range(2):
@@ -59,7 +57,7 @@
     vmem = pl.BlockSpec(memory_space=pltpu.VMEM)
     return pl.pallas_call(
         project_kernel,
-        out_shape=jax.ShapeDtypeStruct((2 * mine.shape[1], columns[0].shape[1]), BF16),
+        out_shape=jax.ShapeDtypeStruct((2 * mine.shape[1], columns[0].shape[2]), BF16),
         in_specs=[pl.BlockSpec(memory_space=pltpu.SMEM)] + [vmem] * (3 + len(columns)),
         out_specs=vmem,
         compiler_params=pltpu.CompilerParams(vmem_limit_bytes=32 << 20),
@@ -208,6 +206,41 @@
     )(meta, parts)
 
 
+def spread_kernel(meta, attended, mine, others, out):
+    on_core_0 = meta[3 * REQS + 2] == 0
+    here = meta[3 * REQS + 3]
+    count = 4
+    rows = attended.shape[1] // 2
+    heads = [jnp.where(on_core_0, attended[h, :rows], attended[h, rows:]) for h in range(attended.shape[0])]
+    heads = jnp.concatenate(heads, axis=1)
+    padded = jnp.concatenate([heads, jnp.zeros((HD - rows, heads.shape[1]), BF16)], axis=0)
+    last = (((1,), (1,)), ((), ()))
+    for step in range(count):
+        along = lax.rem(here + step, count)
+        for block in range(count):
+            at = block * count + along
+            a, b = mine[step * count + block], others[step * count + block]
+            weights = jnp.concatenate([jnp.where(on_core_0, a, b), jnp.where(on_core_0, b, a)], axis=0)
+            wide = lax.dot_general(heads, weights[: 2 * HD], last, preferred_element_type=F32)
+            rest = lax.dot_general(weights[2 * HD :], padded, last, preferred_element_type=F32)
+            out[at, :rows, :] = wide[:, :HD].astype(BF16)
+            out[at, rows : 2 * rows, :] = wide[:, HD:].astype(BF16)
+            out[at, 2 * rows :, :] = rest.astype(BF16)
+
+
+def spread(meta, attended, mine, others, chunks):
+    vmem = pl.BlockSpec(memory_space=pltpu.VMEM)
+    rows = attended.shape[1] + 2 * mine.shape[1] - 2 * HD
+    return pl.pallas_call(
+        spread_kernel,
+        out_shape=jax.ShapeDtypeStruct((chunks, rows, HD), BF16),
+        in_specs=[pl.BlockSpec(memory_space=pltpu.SMEM)] + [vmem] * 3,
+        out_specs=vmem,
+        compiler_params=pltpu.CompilerParams(vmem_limit_bytes=32 << 20),
+        name="spread",
+    )(meta, attended, mine, others)
+
+
 def on_device(
     tokens, pre_gain, w_q, w_k, w_v, w_o, post_gain, k_cache, v_cache, cached_len, new_len, slot_offset
 ):
@@ -225,26 +258,25 @@
     gained = float_in * (1.0 + pre_gain.astype(F32))
     gained = jnp.concatenate([gained, high, squares - high], axis=1).astype(BF16)
     weights = jnp.concatenate([w_q, w_k, w_v], axis=1)
-    gained, weights = lax.optimization_barrier((gained, weights))
-    gained = everywhere(gained, GY, n_gy)
-    w_out = lax.all_gather(w_o.T, GX, axis=0, tiled=True)
-
     weights = lax.all_gather(weights, "c", axis=0, tiled=True)
     weights = lax.dynamic_slice_in_dim(weights, core * cols, cols, 1)
-    weights = lax.all_gather(weights, "zh", axis=0, tiled=True)
+    inner = weights.shape[0]
+    weights = jnp.concatenate([weights, w_o.T], axis=0)
+    weights = lax.all_gather(weights, "zh", axis=0)
     from_right = [((i + 1) % 4, i) for i in range(4)]
     from_left = [((i - 1) % 4, i) for i in range(4)]
     right = lax.ppermute(weights, "x", from_right)
     left = lax.ppermute(weights, "x", from_left)
-    middle = weights.shape[0] // 2
-    columns = [
-        weights,
-        right,
-        lax.ppermute(right[:middle], "x", from_right),
-        lax.ppermute(left[middle:], "x", from_left),
-        left,
-    ]
+    ahead = lax.ppermute(right[:2], "x", from_right)
+    behind = lax.ppermute(left[2:], "x", from_left)
+    columns = [weights, right, ahead, behind, left]
+    w_out = jnp.concatenate([part[:, inner:, :] for part in columns], axis=0)
     swap = [(0, 1), (1, 0)]
+    w_out_other = lax.ppermute(w_out, "c", swap)
+
+    gained, weights = lax.optimization_barrier((gained, weights))
+    gained = lax.all_gather(gained, "zl", axis=0, tiled=True)
+    gained = everywhere(gained, "y", n_gy // 2).reshape(n_gy, tok_rows, -1)
     other = lax.ppermute(gained, "c", swap)
 
     chip_rows = me // 2 * (2 * tok_rows)
@@ -269,7 +301,6 @@
         ]
     )
     mine = project(meta, gained, other, turns, columns)
-    mine, w_out = lax.optimization_barrier((mine, w_out))
     mine = everywhere(mine, CHIPS, n_chips).reshape(-1, cols)
     others = lax.ppermute(mine, "c", swap)
 
@@ -280,12 +311,11 @@
     parts = lax.all_to_all(head.reshape(n_chips, -1, HD), CHIPS, 0, 0)
     attended = divide(meta, parts)
     attended = lax.all_gather(attended, "c", axis=0)
-    attended = lax.dynamic_slice_in_dim(attended, core * tok_rows, tok_rows, 1)
-    attended = jnp.swapaxes(attended, 0, 1).reshape(tok_rows, 2 * HD)
-
-    partial_out = lax.dot_general(attended, w_out, (((1,), (1,)), ((), ())), preferred_element_type=F32)
-    partial_out = jnp.swapaxes(partial_out.astype(BF16).reshape(tok_rows, n_gy, features), 0, 1)
-    branch = jnp.sum(lax.all_to_all(partial_out, GY, 0, 0).astype(F32), axis=0)
+    partial_out = spread(meta, attended, w_out, w_out_other, n_gy)
+    total = jnp.sum(lax.all_to_all(partial_out, GY, 0, 0).astype(F32), axis=0)
+    branch = jnp.concatenate(
+        [total[:tok_rows], total[tok_rows : 2 * tok_rows], total[2 * tok_rows :, :tok_rows].T], axis=1
+    )
     squares = jnp.sum(branch * branch, axis=1)
     mean = jnp.sum(everywhere(squares[None, :], GY, n_gy), axis=(0, 1)) / D
     layer_out = float_in + branch * lax.rsqrt(mean + epsilon)[:, None] * (1.0 + post_gain.astype(F32))

time: 227 us -> 218 us (0.960)
  between operations: 14.3 us -> 0.95 us
  local copies, waits for them, and re-layouts: 3.53 us -> 9.13 us
  blocking collectives: 106 us -> 102 us
  other arithmetic: 5.38 us -> 8.15 us
  Pallas kernels: 8.47 us -> 11.1 us
  matrix products: 2.5 us -> 0 us
    all_to_all x2, waiting for transfers between devices: 7.26 us -> 26.1 us  [everywhere(): lax.all_to_all(jnp.broadcast_to(value[None], (count,) + value.shape), axe...]
    all_to_all x1, waiting for transfers between devices: 20.6 us -> 12.3 us  [on_device(): parts = lax.all_to_all(head.reshape(n_chips, -1, HD), CHIPS, 0, 0)]
    all_gather x1 -> x2, blocking collectives: 31 us -> 25 us  [the longest x1 19.9 us: on_device(): weights = lax.all_gather(weights, 'zh', axis=0)]
    all_gather x1, blocking collectives: 2.61 us -> 8.53 us  [on_device(): weights = lax.all_gather(weights, 'c', axis=0, tiled=True)]
    all_to_all x1, blocking collectives: 36 us -> 31.3 us  [everywhere(): lax.all_to_all(jnp.broadcast_to(value[None], (count,) + value.shape), axe...]
    unnamed x15 -> x20, local copies, waits for them, and re-layouts: 0.07 us -> 4.65 us
    all_to_all x2, starting transfers between devices: 13.6 us -> 10.4 us  [everywhere(): lax.all_to_all(jnp.broadcast_to(value[None], (count,) + value.shape), axe...]
    ppermute x1, waiting for transfers between devices: 3.06 us -> 0.01 us  [on_device(): right = lax.ppermute(weights, 'x', from_right)]
  transfers between devices with their start and end apart: 10 -> 10, of which waited for: 8 -> 5; matrix products, arithmetic and copies ran while one was open for 2% -> 5% of each run, Pallas kernels for 1% -> 0%
where the time goes in v5:
time: 218 us; the launch traced here: 217 us
  blocking collectives  102 us (47%)
  waiting for transfers between devices  45.3 us (21%)
  starting transfers between devices  40.5 us (19%)
  Pallas kernels  11.1 us (5%)
  local copies, waits for them, and re-layouts  9.13 us (4%)
  other arithmetic  8.15 us (4%)
    all_to_all x1, blocking collectives, everywhere(): lax.all_to_all(jnp.broadcast_to(value[None], (count,) + value.shape), axe...  31.3 us
    all_to_all x1, blocking collectives, on_device(): total = jnp.sum(lax.all_to_all(partial_out, GY, 0, 0).astype(F32), axis=0)  28.2 us
    all_to_all x2, waiting for transfers between devices, everywhere(): lax.all_to_all(jnp.broadcast_to(value[None], (count,) + value.shape), axe...  26.1 us
    all_gather x1, blocking collectives, on_device(): weights = lax.all_gather(weights, 'zh', axis=0)  19.9 us
    all_to_all x1, waiting for transfers between devices, on_device(): parts = lax.all_to_all(head.reshape(n_chips, -1, HD), CHIPS, 0, 0)  12.3 us
    all_to_all x2, starting transfers between devices, everywhere(): lax.all_to_all(jnp.broadcast_to(value[None], (count,) + value.shape), axe...  10.4 us
    all_gather x1, blocking collectives, on_device(): weights = lax.all_gather(weights, 'c', axis=0, tiled=True)  8.53 us
    all_to_all x1, starting transfers between devices, on_device(): parts = lax.all_to_all(head.reshape(n_chips, -1, HD), CHIPS, 0, 0)  6.09 us
  transfers between devices with their start and end apart: 10, of which 5 were waited for; matrix products, arithmetic and copies ran while one was open for 5% of the time, Pallas kernels for 0%

profile of v5, /device:TPU:1, one launch (start us, length us, event | category | flops | bytes accessed | tf_op | source)
XLA Modules:
  0.0 216.8 jit_solution(5720585727844674533)
XLA Ops:
  3.5 8.5 %all_gather.18 = bf16[288,512]{1,0:T(8,128)(2,1)S(1)} all-gather(bf16[144,512]{1,0:T(8,128)(2,1)S(1)} %pad_maximum_fusion.2), channel_id=1, replica_groups=mesh['zh'=4,'x'=4,'c'=2,'y'=8,'zl'=2] {'c'}, dimensions={0}, use_global_device_ids=true | all-gather | bytes 442368 | tf_op jit(solution)/shard_map/all_gather | solution.py:261
  12.1 19.9 %all-gather = bf16[1728,256]{1,0:T(8,128)(2,1)S(1)} all-gather(bf16[432,256]{1,0:T(8,128)(2,1)S(1)} %pad_maximum_fusion.1), channel_id=2, replica_groups=mesh['zh'=4,'x'=4,'c'=2,'y'=8,'zl'=2] {'zh'}, dimensions={0}, use_global_device_ids=true | all-gather | bytes 1105920 | tf_op jit(solution)/shard_map/all_gather | solution.py:265
  32.0 5.1 %all_gather.21 = bf16[144,290]{1,0:T(8,128)(2,1)S(1)} all-gather(bf16[72,290]{1,0:T(8,128)(2,1)S(1)} %pad_maximum_fusion.4), channel_id=1, replica_groups=mesh['zh'=4,'x'=4,'c'=2,'y'=8,'zl'=2] {'zl'}, dimensions={0}, use_global_device_ids=true | all-gather | bytes 125280 | tf_op jit(solution)/shard_map/all_gather | solution.py:278
  38.1 6.8 %all-to-all-start = ((bf16[8,144,290]{2,1,0:T(8,128)(2,1)}), bf16[8,144,290]{2,1,0:T(8,128)(2,1)S(1)}, u32[]{:S(2)}, u32[]{:S(2)}) async-start(bf16[8,144,290]{2,1,0:T(8,128)(2,1)} %broadcast_in_dim.25), calls=%async_computation | async-start | bytes 1769472 | tf_op jit(solution)/shard_map/all_to_all | solution.py:26
  45.0 3.3 %collective-permute-start.3 = (bf16[4,432,256]{2,1,0:T(8,128)(2,1)S(1)}, bf16[4,432,256]{2,1,0:T(8,128)(2,1)S(1)}, u32[]{:S(2)}, u32[]{:S(2)}) collective-permute-start(bf16[4,432,256]{2,1,0:T(8,128)(2,1)S(1)} %bitcast.26), channel_id=1, source_target_pairs={{96,0},{0,32},{32,64},{64,96},{97,1},{1,33},{33,65},{65,97},{98,2}... | collective-permute-start | bytes 2654216 | tf_op jit(solution)/shard_map/ppermute | solution.py:269
  48.2 3.4 %collective-permute-start.1 = (bf16[4,432,256]{2,1,0:T(8,128)(2,1)S(1)}, bf16[4,432,256]{2,1,0:T(8,128)(2,1)S(1)}, u32[]{:S(2)}, u32[]{:S(2)}) collective-permute-start(bf16[4,432,256]{2,1,0:T(8,128)(2,1)S(1)} %bitcast.27), channel_id=1, source_target_pairs={{32,0},{64,32},{96,64},{0,96},{33,1},{65,33},{97,65},{1,97},{34,2}... | collective-permute-start | bytes 2654216 | tf_op jit(solution)/shard_map/ppermute | solution.py:268
  51.8 18.9 %all-to-all-done = bf16[8,144,290]{2,1,0:T(8,128)(2,1)S(1)} async-done(((bf16[8,144,290]{2,1,0:T(8,128)(2,1)}), bf16[8,144,290]{2,1,0:T(8,128)(2,1)S(1)}, u32[]{:S(2)}, u32[]{:S(2)}) %all-to-all-start) | async-done | bytes 668192 | tf_op jit(solution)/shard_map/all_to_all | solution.py:26
  70.6 2.4 %collective-permute-start = (bf16[16,72,290]{2,1,0:T(8,128)(2,1)S(1)}, bf16[16,72,290]{2,1,0:T(8,128)(2,1)}, u32[]{:S(2)}, u32[]{:S(2)}) collective-permute-start(bf16[16,72,290]{2,1,0:T(8,128)(2,1)S(1)} %bitcast.32), channel_id=1, source_target_pairs={{0,16},{16,0},{1,17},{17,1},{2,18},{18,2},{3,19},{19,3},{4,20},{20... | collective-permute-start | bytes 2004488 | tf_op jit(solution)/shard_map/ppermute | solution.py:280
  73.9 3.1 %collective-permute-start.4 = (bf16[2,432,256]{2,1,0:T(8,128)(2,1)}, bf16[2,432,256]{2,1,0:T(8,128)(2,1)}, u32[]{:S(2)}, u32[]{:S(2)}) collective-permute-start(bf16[2,432,256]{2,1,0:T(8,128)(2,1)} %slice.49), channel_id=1, source_target_pairs={{96,0},{0,32},{32,64},{64,96},{97,1},{1,33},{33,65},{65,97},{98,2}... | collective-permute-start | bytes 1327112 | tf_op jit(solution)/shard_map/ppermute | solution.py:271
  77.8 3.4 %collective-permute-start.2 = (bf16[2,432,256]{2,1,0:T(8,128)(2,1)}, bf16[2,432,256]{2,1,0:T(8,128)(2,1)}, u32[]{:S(2)}, u32[]{:S(2)}) collective-permute-start(bf16[2,432,256]{2,1,0:T(8,128)(2,1)} %slice.48), channel_id=1, source_target_pairs={{32,0},{64,32},{96,64},{0,96},{33,1},{65,33},{97,65},{1,97},{34,2}... | collective-permute-start | bytes 1327112 | tf_op jit(solution)/shard_map/ppermute | solution.py:270
  84.6 4.4 %collective-permute-done.4.behind = bf16[2,432,256]{2,1,0:T(8,128)(2,1)} collective-permute-done((bf16[2,432,256]{2,1,0:T(8,128)(2,1)}, bf16[2,432,256]{2,1,0:T(8,128)(2,1)}, u32[]{:S(2)}, u32[]{:S(2)}) %collective-permute-start.4) | collective-permute-done | bytes 442400 | tf_op jit(solution)/shard_map/ppermute | solution.py:271
  89.1 2.4 %collective-permute-done.2.ahead = bf16[2,432,256]{2,1,0:T(8,128)(2,1)} collective-permute-done((bf16[2,432,256]{2,1,0:T(8,128)(2,1)}, bf16[2,432,256]{2,1,0:T(8,128)(2,1)}, u32[]{:S(2)}, u32[]{:S(2)}) %collective-permute-start.2) | collective-permute-done | bytes 442400 | tf_op jit(solution)/shard_map/ppermute | solution.py:270
  91.5 2.3 %project.1 = bf16[144,256]{1,0:T(8,128)(2,1)S(1)} custom-call(s32[40]{0:T(128)S(1)} %concatenate.49.meta, bf16[16,72,290]{2,1,0:T(8,128)(2,1)S(1)} %bitcast.33, bf16[16,72,290]{2,1,0:T(8,128)(2,1)} %collective-permute-done.others, f32[4,144,128]{2,1,0:T(8,128)S(1)} %pad_maximum_fusion.turns, bf16[4,432,256]{2,1,0:T(8,128)(2,1)S(1)} %bitcast.28, ...), custom_call_target="tpu_custom_call" | custom-call | tf_op jit(solution)/shard_map/project/pallas_call | solution.py:58
  93.9 31.3 %all_to_all.30 = bf16[16,144,256]{2,1,0:T(8,128)(2,1)S(1)} all-to-all(bf16[16,144,256]{2,1,0:T(8,128)(2,1)S(1)} %broadcast_in_dim.50), channel_id=1, replica_groups=mesh['zh'=4,'x'=4,'c'=2,'y'=8,'zl'=2] {'zh','x'}, dimensions={0} | all-to-all | bytes 2359296 | tf_op jit(solution)/shard_map/all_to_all | solution.py:26
  125.2 5.9 %collective-permute-start.5 = (bf16[2304,256]{1,0:T(8,128)(2,1)S(1)}, bf16[2304,256]{1,0:T(8,128)(2,1)S(1)}, u32[]{:S(2)}, u32[]{:S(2)}) collective-permute-start(bf16[2304,256]{1,0:T(8,128)(2,1)S(1)} %bitcast.30), channel_id=1, source_target_pairs={{0,16},{16,0},{1,17},{17,1},{2,18},{18,2},{3,19},{19,3},{4,20},{20... | collective-permute-start | bytes 3538952 | tf_op jit(solution)/shard_map/ppermute | solution.py:305
  135.7 5.9 %attend.1 = (bf16[1024,128]{1,0:T(8,128)(2,1)}, bf16[1024,128]{1,0:T(8,128)(2,1)}, bf16[2,2560,128]{2,1,0:T(8,128)(2,1)S(1)}) custom-call(s32[40]{0:T(128)S(1)} %concatenate.49.meta, bf16[2304,256]{1,0:T(8,128)(2,1)S(1)} %bitcast.31, bf16[2304,256]{1,0:T(8,128)(2,1)S(1)} %collective-permute-done.5.others, bf16[1024,128]{1,0:T(8,128)(2,1)S(1)} %copy-done, ...), custom_call_target="tpu_custom_call" | custom-call | tf_op jit(solution)/shard_map/attend/pallas_call | solution.py:160
  141.7 4.4 %all_to_all.31 = bf16[2,2560,128]{2,1,0:T(8,128)(2,1)S(1)} all-to-all(bf16[2,2560,128]{2,1,0:T(8,128)(2,1)S(1)} %get-tuple-element.8), channel_id=1, replica_groups=mesh['zh'=4,'x'=4,'c'=2,'y'=8,'zl'=2] {'c'}, dimensions={0} | all-to-all | bytes 2621440 | tf_op jit(solution)/shard_map/all_to_all | solution.py:309
  147.1 6.1 %all-to-all-start.3 = ((bf16[16,160,128]{2,1,0:T(8,128)(2,1)}), bf16[16,160,128]{2,1,0:T(8,128)(2,1)S(1)}, u32[]{:S(2)}, u32[]{:S(2)}) async-start(bf16[16,160,128]{2,1,0:T(8,128)(2,1)} %bitcast.14), calls=%async_computation.3 | async-start | bytes 1310720 | tf_op jit(solution)/shard_map/all_to_all | solution.py:311
  153.9 2.5 %collective-permute-start.6 = (bf16[16,144,256]{2,1,0:T(8,128)(2,1)}, bf16[16,144,256]{2,1,0:T(8,128)(2,1)S(1)}, u32[]{:S(2)}, u32[]{:S(2)}) collective-permute-start(bf16[16,144,256]{2,1,0:T(8,128)(2,1)} %slice_dynamic-update-slice_fusion.mine), channel_id=1, source_target_pairs={{0,16},{16,0},{1,17},{17,1},{2,18},{18,2},{3,19},{19,3},{4,20},{20... | collective-permute-start | bytes 3538952 | tf_op jit(solution)/shard_map/ppermute | solution.py:275
  156.5 12.3 %all-to-all-done.3.parts = bf16[16,160,128]{2,1,0:T(8,128)(2,1)S(1)} async-done(((bf16[16,160,128]{2,1,0:T(8,128)(2,1)}), bf16[16,160,128]{2,1,0:T(8,128)(2,1)S(1)}, u32[]{:S(2)}, u32[]{:S(2)}) %all-to-all-start.3) | async-done | bytes 655392 | tf_op jit(solution)/shard_map/all_to_all | solution.py:311
  169.5 4.4 %all-gather.1 = bf16[288,128]{1,0:T(8,128)(2,1)S(1)} all-gather(bf16[144,128]{1,0:T(8,128)(2,1)S(1)} %divide.1), channel_id=3, replica_groups=mesh['zh'=4,'x'=4,'c'=2,'y'=8,'zl'=2] {'c'}, dimensions={0}, use_global_device_ids=true | all-gather | bytes 110592 | tf_op jit(solution)/shard_map/all_gather | solution.py:313
  176.0 28.2 %all_to_all.32 = bf16[16,176,128]{2,1,0:T(8,128)(2,1)S(1)} all-to-all(bf16[16,176,128]{2,1,0:T(8,128)(2,1)S(1)} %spread.1), channel_id=1, replica_groups=mesh['zh'=4,'x'=4,'c'=2,'y'=8,'zl'=2] {'y','zl'}, dimensions={0} | all-to-all | bytes 1441792 | tf_op jit(solution)/shard_map/all_to_all | solution.py:315
  205.2 3.6 %all-to-all-start.5 = ((f32[16,1,72]{2,1,0:T(1,128)}), f32[16,1,72]{2,1,0:T(1,128)S(1)}, u32[]{:S(2)}, u32[]{:S(2)}) async-start(f32[16,1,72]{2,1,0:T(1,128)} %broadcast_in_dim.51), calls=%async_computation.5 | async-start | bytes 16384 | tf_op jit(solution)/shard_map/all_to_all | solution.py:26
  208.8 7.3 %all-to-all-done.5 = f32[16,1,72]{2,1,0:T(1,128)S(1)} async-done(((f32[16,1,72]{2,1,0:T(1,128)}), f32[16,1,72]{2,1,0:T(1,128)S(1)}, u32[]{:S(2)}, u32[]{:S(2)}) %all-to-all-start.5) | async-done | bytes 4640 | tf_op jit(solution)/shard_map/all_to_all | solution.py:26
  (61 shorter events, 20.1 us)
Async XLA Ops:
  0.6 11.4 %copy-start.3 = (bf16[256,144]{0,1:T(8,128)(2,1)S(1)}, bf16[256,144]{0,1:T(8,128)(2,1)}, u32[]{:S(2)}) copy-start(bf16[256,144]{0,1:T(8,128)(2,1)} %param.17) | copy-start | bytes 221188
  37.1 14.5 %copy-start.4 = (s32[12]{0:T(128)S(1)}, s32[12]{0:T(128)}, u32[]{:S(2)}) copy-start(s32[12]{0:T(128)} %param.21) | copy-start | bytes 148
  38.1 32.5 %all-to-all-start = ((bf16[8,144,290]{2,1,0:T(8,128)(2,1)}), bf16[8,144,290]{2,1,0:T(8,128)(2,1)S(1)}, u32[]{:S(2)}, u32[]{:S(2)}) async-start(bf16[8,144,290]{2,1,0:T(8,128)(2,1)} %broadcast_in_dim.25), calls=%async_computation | async-start | bytes 1769472 | tf_op jit(solution)/shard_map/all_to_all | solution.py:26
  45.0 37.4 %copy-start.6 = (s32[12]{0:T(128)S(1)}, s32[12]{0:T(128)}, u32[]{:S(2)}) copy-start(s32[12]{0:T(128)} %param.22) | copy-start | bytes 148
  45.0 37.4 %copy-start.7 = (s32[12]{0:T(128)S(1)}, s32[12]{0:T(128)}, u32[]{:S(2)}) copy-start(s32[12]{0:T(128)} %param.23) | copy-start | bytes 148
  45.0 28.1 %collective-permute-start.3 = (bf16[4,432,256]{2,1,0:T(8,128)(2,1)S(1)}, bf16[4,432,256]{2,1,0:T(8,128)(2,1)S(1)}, u32[]{:S(2)}, u32[]{:S(2)}) collective-permute-start(bf16[4,432,256]{2,1,0:T(8,128)(2,1)S(1)} %bitcast.26), channel_id=1, source_target_pairs={{96,0},{0,32},{32,64},{64,96},{97,1},{1,33},{33,65},{65,97},{98,2}... | collective-permute-start | bytes 2654216 | tf_op jit(solution)/shard_map/ppermute | solution.py:269
  48.2 28.8 %collective-permute-start.1 = (bf16[4,432,256]{2,1,0:T(8,128)(2,1)S(1)}, bf16[4,432,256]{2,1,0:T(8,128)(2,1)S(1)}, u32[]{:S(2)}, u32[]{:S(2)}) collective-permute-start(bf16[4,432,256]{2,1,0:T(8,128)(2,1)S(1)} %bitcast.27), channel_id=1, source_target_pairs={{32,0},{64,32},{96,64},{0,96},{33,1},{65,33},{97,65},{1,97},{34,2}... | collective-permute-start | bytes 2654216 | tf_op jit(solution)/shard_map/ppermute | solution.py:268
  70.6 20.9 %collective-permute-start = (bf16[16,72,290]{2,1,0:T(8,128)(2,1)S(1)}, bf16[16,72,290]{2,1,0:T(8,128)(2,1)}, u32[]{:S(2)}, u32[]{:S(2)}) collective-permute-start(bf16[16,72,290]{2,1,0:T(8,128)(2,1)S(1)} %bitcast.32), channel_id=1, source_target_pairs={{0,16},{16,0},{1,17},{17,1},{2,18},{18,2},{3,19},{19,3},{4,20},{20... | collective-permute-start | bytes 2004488 | tf_op jit(solution)/shard_map/ppermute | solution.py:280
  73.9 15.2 %collective-permute-start.4 = (bf16[2,432,256]{2,1,0:T(8,128)(2,1)}, bf16[2,432,256]{2,1,0:T(8,128)(2,1)}, u32[]{:S(2)}, u32[]{:S(2)}) collective-permute-start(bf16[2,432,256]{2,1,0:T(8,128)(2,1)} %slice.49), channel_id=1, source_target_pairs={{96,0},{0,32},{32,64},{64,96},{97,1},{1,33},{33,65},{65,97},{98,2}... | collective-permute-start | bytes 1327112 | tf_op jit(solution)/shard_map/ppermute | solution.py:271
  77.8 13.7 %collective-permute-start.2 = (bf16[2,432,256]{2,1,0:T(8,128)(2,1)}, bf16[2,432,256]{2,1,0:T(8,128)(2,1)}, u32[]{:S(2)}, u32[]{:S(2)}) collective-permute-start(bf16[2,432,256]{2,1,0:T(8,128)(2,1)} %slice.48), channel_id=1, source_target_pairs={{32,0},{64,32},{96,64},{0,96},{33,1},{65,33},{97,65},{1,97},{34,2}... | collective-permute-start | bytes 1327112 | tf_op jit(solution)/shard_map/ppermute | solution.py:270
  125.2 10.5 %copy-start = (bf16[1024,128]{1,0:T(8,128)(2,1)S(1)}, bf16[1024,128]{1,0:T(8,128)(2,1)}, u32[]{:S(2)}) copy-start(bf16[1024,128]{1,0:T(8,128)(2,1)} %k_old.1) | copy-start | bytes 786436
  125.2 10.5 %copy-start.1 = (bf16[1024,128]{1,0:T(8,128)(2,1)S(1)}, bf16[1024,128]{1,0:T(8,128)(2,1)}, u32[]{:S(2)}) copy-start(bf16[1024,128]{1,0:T(8,128)(2,1)} %v_old.1) | copy-start | bytes 786436
  125.2 10.5 %collective-permute-start.5 = (bf16[2304,256]{1,0:T(8,128)(2,1)S(1)}, bf16[2304,256]{1,0:T(8,128)(2,1)S(1)}, u32[]{:S(2)}, u32[]{:S(2)}) collective-permute-start(bf16[2304,256]{1,0:T(8,128)(2,1)S(1)} %bitcast.30), channel_id=1, source_target_pairs={{0,16},{16,0},{1,17},{17,1},{2,18},{18,2},{3,19},{19,3},{4,20},{20... | collective-permute-start | bytes 3538952 | tf_op jit(solution)/shard_map/ppermute | solution.py:305
  147.1 21.7 %all-to-all-start.3 = ((bf16[16,160,128]{2,1,0:T(8,128)(2,1)}), bf16[16,160,128]{2,1,0:T(8,128)(2,1)S(1)}, u32[]{:S(2)}, u32[]{:S(2)}) async-start(bf16[16,160,128]{2,1,0:T(8,128)(2,1)} %bitcast.14), calls=%async_computation.3 | async-start | bytes 1310720 | tf_op jit(solution)/shard_map/all_to_all | solution.py:311
  153.9 19.9 %collective-permute-start.6 = (bf16[16,144,256]{2,1,0:T(8,128)(2,1)}, bf16[16,144,256]{2,1,0:T(8,128)(2,1)S(1)}, u32[]{:S(2)}, u32[]{:S(2)}) collective-permute-start(bf16[16,144,256]{2,1,0:T(8,128)(2,1)} %slice_dynamic-update-slice_fusion.mine), channel_id=1, source_target_pairs={{0,16},{16,0},{1,17},{17,1},{2,18},{18,2},{3,19},{19,3},{4,20},{20... | collective-permute-start | bytes 3538952 | tf_op jit(solution)/shard_map/ppermute | solution.py:275
  176.0 32.8 %copy-start.5 = (bf16[288]{0:T(512)(128)(2,1)S(1)}, bf16[288]{0:T(512)(128)(2,1)}, u32[]{:S(2)}) copy-start(bf16[288]{0:T(512)(128)(2,1)} %param.18) | copy-start | bytes 1732
  176.0 40.1 %copy-start.2 = (bf16[72,288]{1,0:T(8,128)(2,1)S(1)}, bf16[72,288]{1,0:T(8,128)(2,1)}, u32[]{:S(2)}) copy-start(bf16[72,288]{1,0:T(8,128)(2,1)} %param.12) | copy-start | bytes 124420
  205.2 10.9 %all-to-all-start.5 = ((f32[16,1,72]{2,1,0:T(1,128)}), f32[16,1,72]{2,1,0:T(1,128)S(1)}, u32[]{:S(2)}, u32[]{:S(2)}) async-start(f32[16,1,72]{2,1,0:T(1,128)} %broadcast_in_dim.51), calls=%async_computation.5 | async-start | bytes 16384 | tf_op jit(solution)/shard_map/all_to_all | solution.py:26

commit v6 on v5

--- a/solution.py
+++ b/solution.py
@@ -206,39 +206,38 @@
     )(meta, parts)
 
 
-def spread_kernel(meta, attended, mine, others, out):
-    on_core_0 = meta[3 * REQS + 2] == 0
+def spread_kernel(meta, attended, own, right, ahead, behind, left, out):
     here = meta[3 * REQS + 3]
     count = 4
-    rows = attended.shape[1] // 2
-    heads = [jnp.where(on_core_0, attended[h, :rows], attended[h, rows:]) for h in range(attended.shape[0])]
-    heads = jnp.concatenate(heads, axis=1)
-    padded = jnp.concatenate([heads, jnp.zeros((HD - rows, heads.shape[1]), BF16)], axis=0)
+    rows = attended.shape[1]
+    heads = jnp.concatenate([attended[h] for h in range(attended.shape[0])], axis=1)
+    padded = jnp.concatenate([heads, jnp.zeros((2 * HD - rows, heads.shape[1]), BF16)], axis=0)
     last = (((1,), (1,)), ((), ()))
     for step in range(count):
         along = lax.rem(here + step, count)
         for block in range(count):
             at = block * count + along
-            a, b = mine[step * count + block], others[step * count + block]
-            weights = jnp.concatenate([jnp.where(on_core_0, a, b), jnp.where(on_core_0, b, a)], axis=0)
-            wide = lax.dot_general(heads, weights[: 2 * HD], last, preferred_element_type=F32)
-            rest = lax.dot_general(weights[2 * HD :], padded, last, preferred_element_type=F32)
-            out[at, :rows, :] = wide[:, :HD].astype(BF16)
-            out[at, rows : 2 * rows, :] = wide[:, HD:].astype(BF16)
-            out[at, 2 * rows :, :] = rest.astype(BF16)
-
-
-def spread(meta, attended, mine, others, chunks):
+            if step == 2:
+                weights = (ahead if block < 2 else behind)[block % 2]
+            else:
+                weights = (own, right, None, left)[step][block]
+            wide = lax.dot_general(heads, weights[:HD], last, preferred_element_type=F32)
+            rest = lax.dot_general(weights[HD:], padded, last, preferred_element_type=F32)
+            out[at, :rows, :] = wide.astype(BF16)
+            out[at, rows : rows + 16, :] = rest[:, :HD].astype(BF16)
+            out[at, rows + 16 :, :] = rest[:, HD:].astype(BF16)
+
+
+def spread(meta, attended, columns, chunks):
     vmem = pl.BlockSpec(memory_space=pltpu.VMEM)
-    rows = attended.shape[1] + 2 * mine.shape[1] - 2 * HD
     return pl.pallas_call(
         spread_kernel,
-        out_shape=jax.ShapeDtypeStruct((chunks, rows, HD), BF16),
-        in_specs=[pl.BlockSpec(memory_space=pltpu.SMEM)] + [vmem] * 3,
+        out_shape=jax.ShapeDtypeStruct((chunks, attended.shape[1] + 32, HD), BF16),
+        in_specs=[pl.BlockSpec(memory_space=pltpu.SMEM)] + [vmem] * (1 + len(columns)),
         out_specs=vmem,
         compiler_params=pltpu.CompilerParams(vmem_limit_bytes=32 << 20),
         name="spread",
-    )(meta, attended, mine, others)
+    )(meta, attended, *columns)
 
 
 def on_device(
@@ -258,11 +257,17 @@
     gained = float_in * (1.0 + pre_gain.astype(F32))
     gained = jnp.concatenate([gained, high, squares - high], axis=1).astype(BF16)
     weights = jnp.concatenate([w_q, w_k, w_v], axis=1)
+    gained, weights = lax.optimization_barrier((gained, weights))
+    gained = lax.all_gather(gained, "zl", axis=0, tiled=True)
+    gained = everywhere(gained, "y", n_gy // 2).reshape(n_gy, tok_rows, -1)
+
     weights = lax.all_gather(weights, "c", axis=0, tiled=True)
     weights = lax.dynamic_slice_in_dim(weights, core * cols, cols, 1)
     inner = weights.shape[0]
     weights = jnp.concatenate([weights, w_o.T], axis=0)
     weights = lax.all_gather(weights, "zh", axis=0)
+    w_out = weights[:, inner:, :]
+    weights = weights[:, :inner, :]
     from_right = [((i + 1) % 4, i) for i in range(4)]
     from_left = [((i - 1) % 4, i) for i in range(4)]
     right = lax.ppermute(weights, "x", from_right)
@@ -270,13 +275,7 @@
     ahead = lax.ppermute(right[:2], "x", from_right)
     behind = lax.ppermute(left[2:], "x", from_left)
     columns = [weights, right, ahead, behind, left]
-    w_out = jnp.concatenate([part[:, inner:, :] for part in columns], axis=0)
     swap = [(0, 1), (1, 0)]
-    w_out_other = lax.ppermute(w_out, "c", swap)
-
-    gained, weights = lax.optimization_barrier((gained, weights))
-    gained = lax.all_gather(gained, "zl", axis=0, tiled=True)
-    gained = everywhere(gained, "y", n_gy // 2).reshape(n_gy, tok_rows, -1)
     other = lax.ppermute(gained, "c", swap)
 
     chip_rows = me // 2 * (2 * tok_rows)
@@ -301,8 +300,19 @@
         ]
     )
     mine = project(meta, gained, other, turns, columns)
+    mine, w_out = lax.optimization_barrier((mine, w_out))
+    out_right = lax.ppermute(w_out, "x", from_right)
+    out_left = lax.ppermute(w_out, "x", from_left)
     mine = everywhere(mine, CHIPS, n_chips).reshape(-1, cols)
+    mine, out_right, out_left = lax.optimization_barrier((mine, out_right, out_left))
     others = lax.ppermute(mine, "c", swap)
+    out_columns = [
+        w_out,
+        out_right,
+        lax.ppermute(out_right[:2], "x", from_right),
+        lax.ppermute(out_left[2:], "x", from_left),
+        out_left,
+    ]
 
     k_pool, v_pool, sums = attend(meta, mine, others, k_cache, v_cache)
 
@@ -311,13 +321,19 @@
     parts = lax.all_to_all(head.reshape(n_chips, -1, HD), CHIPS, 0, 0)
     attended = divide(meta, parts)
     attended = lax.all_gather(attended, "c", axis=0)
-    partial_out = spread(meta, attended, w_out, w_out_other, n_gy)
+    partial_out = spread(meta, attended, out_columns, n_gy)
     total = jnp.sum(lax.all_to_all(partial_out, GY, 0, 0).astype(F32), axis=0)
-    branch = jnp.concatenate(
-        [total[:tok_rows], total[tok_rows : 2 * tok_rows], total[2 * tok_rows :, :tok_rows].T], axis=1
-    )
-    squares = jnp.sum(branch * branch, axis=1)
-    mean = jnp.sum(everywhere(squares[None, :], GY, n_gy), axis=(0, 1)) / D
+    rows = 2 * tok_rows
+    rest = jnp.concatenate([total[rows : rows + 16], total[rows + 16 :, : rows - HD]], axis=1)
+    branch = jnp.concatenate([total[:rows], rest.T], axis=1)
+    squares = jnp.sum(branch * branch, axis=1).reshape(2, 1, 1, tok_rows)
+    squares = jnp.broadcast_to(squares, (2, n_gy, 1, tok_rows)).reshape(2 * n_gy, 1, tok_rows)
+    squares = lax.all_to_all(squares, ("c",) + GY, 0, 0)
+    mean = jnp.sum(squares, axis=(0, 1)) / D
+    kept = lax.dynamic_slice_in_dim(branch, core * tok_rows, tok_rows, 0)
+    sent = lax.dynamic_slice_in_dim(branch, (1 - core) * tok_rows, tok_rows, 0)
+    came = lax.ppermute(sent, "c", swap)
+    branch = jnp.concatenate([jnp.where(core == 0, kept, came), jnp.where(core == 0, came, kept)], axis=1)
     layer_out = float_in + branch * lax.rsqrt(mean + epsilon)[:, None] * (1.0 + post_gain.astype(F32))
     return (layer_out.astype(BF16), k_pool, v_pool)
 

time: 218 us -> 207 us (0.950)
  blocking collectives: 102 us -> 42 us
  starting transfers between devices: 40.5 us -> 90.1 us
  waiting for transfers between devices: 45.3 us -> 52.5 us
  local copies, waits for them, and re-layouts: 9.13 us -> 5.31 us
  other arithmetic: 8.15 us -> 5.48 us
    all_to_all x2 -> x0, blocking collectives: 59.4 us -> none  [the longest x1 31.3 us: everywhere(): lax.all_to_all(jnp.broadcast_to(value[None], (count,) + value.shape), axe...]
    all_to_all x2, waiting for transfers between devices: 26.1 us -> 0.01 us  [everywhere(): lax.all_to_all(jnp.broadcast_to(value[None], (count,) + value.shape), axe...]
    all_to_all x0 -> x2, waiting for transfers between devices: none -> 25.1 us  [the longest x1 19.6 us: on_device(): total = jnp.sum(lax.all_to_all(partial_out, GY, 0, 0).astype(F32), axis=0)]
    all_to_all x0 -> x2, starting transfers between devices: none -> 17.9 us  [the longest x1 11.1 us: on_device(): total = jnp.sum(lax.all_to_all(partial_out, GY, 0, 0).astype(F32), axis=0)]
    ppermute x1 -> x5, starting transfers between devices: 2.55 us -> 15.1 us  [the longest x1 3.27 us: on_device(): lax.ppermute(out_left[2:], 'x', from_left)]
    ppermute x1 -> x5, waiting for transfers between devices: 0.01 us -> 11.2 us  [the longest x1 9.15 us: on_device(): out_left = lax.ppermute(w_out, 'x', from_left)]
    all_to_all x1, starting transfers between devices: 6.09 us -> 14.3 us  [on_device(): parts = lax.all_to_all(head.reshape(n_chips, -1, HD), CHIPS, 0, 0)]
    ppermute x1, starting transfers between devices: 5.92 us -> 10.4 us  [on_device(): others = lax.ppermute(mine, 'c', swap)]
  transfers between devices with their start and end apart: 10 -> 16, of which waited for: 5 -> 9; matrix products, arithmetic and copies ran while one was open for 5% -> 1% of each run, Pallas kernels for 0% -> 0%
where the time goes in v6:
time: 207 us; the launch traced here: 206 us
  starting transfers between devices  90.1 us (44%)
  waiting for transfers between devices  52.5 us (25%)
  blocking collectives  42 us (20%)
  Pallas kernels  9.82 us (5%)
  other arithmetic  5.48 us (3%)
  local copies, waits for them, and re-layouts  5.31 us (3%)
    all_gather x1, blocking collectives, on_device(): weights = lax.all_gather(weights, 'zh', axis=0)  22.3 us
    all_to_all x1, waiting for transfers between devices, on_device(): total = jnp.sum(lax.all_to_all(partial_out, GY, 0, 0).astype(F32), axis=0)  19.6 us
    all_to_all x1, starting transfers between devices, on_device(): parts = lax.all_to_all(head.reshape(n_chips, -1, HD), CHIPS, 0, 0)  14.3 us
    all_to_all x2, starting transfers between devices, everywhere(): lax.all_to_all(jnp.broadcast_to(value[None], (count,) + value.shape), axe...  13.5 us
    all_to_all x1, starting transfers between devices, on_device(): total = jnp.sum(lax.all_to_all(partial_out, GY, 0, 0).astype(F32), axis=0)  11.1 us
    ppermute x1, starting transfers between devices, on_device(): others = lax.ppermute(mine, 'c', swap)  10.4 us
    all_to_all x1, waiting for transfers between devices, on_device(): parts = lax.all_to_all(head.reshape(n_chips, -1, HD), CHIPS, 0, 0)  9.98 us
    ppermute x1, waiting for transfers between devices, on_device(): out_left = lax.ppermute(w_out, 'x', from_left)  9.15 us
  transfers between devices with their start and end apart: 16, of which 9 were waited for; matrix products, arithmetic and copies ran while one was open for 1% of the time, Pallas kernels for 0%

profile of v6, /device:TPU:1, one launch (start us, length us, event | category | flops | bytes accessed | tf_op | source)
XLA Modules:
  0.0 206.2 jit_solution(13488149025979468051)
XLA Ops:
  3.5 5.1 %all_gather.18 = bf16[144,290]{1,0:T(8,128)(2,1)S(1)} all-gather(bf16[72,290]{1,0:T(8,128)(2,1)S(1)} %pad_maximum_fusion.4), channel_id=1, replica_groups=mesh['zh'=4,'x'=4,'c'=2,'y'=8,'zl'=2] {'zl'}, dimensions={0}, use_global_device_ids=true | all-gather | bytes 125280 | tf_op jit(solution)/shard_map/all_gather | solution.py:261
  9.7 7.0 %all-to-all-start = ((bf16[8,144,290]{2,1,0:T(8,128)(2,1)}), bf16[8,144,290]{2,1,0:T(8,128)(2,1)S(1)}, u32[]{:S(2)}, u32[]{:S(2)}) async-start(bf16[8,144,290]{2,1,0:T(8,128)(2,1)} %broadcast_in_dim.29), calls=%async_computation | async-start | bytes 1769472 | tf_op jit(solution)/shard_map/all_to_all | solution.py:26
  16.6 5.0 %all_gather.19 = bf16[288,512]{1,0:T(8,128)(2,1)S(1)} all-gather(bf16[144,512]{1,0:T(8,128)(2,1)S(1)} %pad_maximum_fusion.3), channel_id=1, replica_groups=mesh['zh'=4,'x'=4,'c'=2,'y'=8,'zl'=2] {'c'}, dimensions={0}, use_global_device_ids=true | all-gather | bytes 442368 | tf_op jit(solution)/shard_map/all_gather | solution.py:264
  21.7 22.3 %all-gather = bf16[1728,256]{1,0:T(8,128)(2,1)S(1)} all-gather(bf16[432,256]{1,0:T(8,128)(2,1)S(1)} %pad_maximum_fusion.1), channel_id=2, replica_groups=mesh['zh'=4,'x'=4,'c'=2,'y'=8,'zl'=2] {'zh'}, dimensions={0}, use_global_device_ids=true | all-gather | bytes 1105920 | tf_op jit(solution)/shard_map/all_gather | solution.py:268
  45.0 3.1 %collective-permute-start.3 = (bf16[4,288,256]{2,1,0:T(8,128)(2,1)S(1)}, bf16[4,288,256]{2,1,0:T(8,128)(2,1)S(1)}, u32[]{:S(2)}, u32[]{:S(2)}) collective-permute-start(bf16[4,288,256]{2,1,0:T(8,128)(2,1)S(1)} %slice.44.own), channel_id=1, source_target_pairs={{96,0},{0,32},{32,64},{64,96},{97,1},{1,33},{33,65},{65,97},{98,2}... | collective-permute-start | bytes 1769480 | tf_op jit(solution)/shard_map/ppermute | solution.py:274
  48.1 3.4 %collective-permute-start.1 = (bf16[4,288,256]{2,1,0:T(8,128)(2,1)S(1)}, bf16[4,288,256]{2,1,0:T(8,128)(2,1)S(1)}, u32[]{:S(2)}, u32[]{:S(2)}) collective-permute-start(bf16[4,288,256]{2,1,0:T(8,128)(2,1)S(1)} %slice.44.own), channel_id=1, source_target_pairs={{32,0},{64,32},{96,64},{0,96},{33,1},{65,33},{97,65},{1,97},{34,2}... | collective-permute-start | bytes 1769480 | tf_op jit(solution)/shard_map/ppermute | solution.py:273
  52.8 5.9 %collective-permute-start = (bf16[16,72,290]{2,1,0:T(8,128)(2,1)S(1)}, bf16[16,72,290]{2,1,0:T(8,128)(2,1)S(1)}, u32[]{:S(2)}, u32[]{:S(2)}) collective-permute-start(bf16[16,72,290]{2,1,0:T(8,128)(2,1)S(1)} %bitcast.27), channel_id=1, source_target_pairs={{0,16},{16,0},{1,17},{17,1},{2,18},{18,2},{3,19},{19,3},{4,20},{20... | collective-permute-start | bytes 2004488 | tf_op jit(solution)/shard_map/ppermute | solution.py:279
  61.5 4.6 %collective-permute-start.2 = (bf16[2,288,256]{2,1,0:T(8,128)(2,1)S(1)}, bf16[2,288,256]{2,1,0:T(8,128)(2,1)S(1)}, u32[]{:S(2)}, u32[]{:S(2)}) collective-permute-start(bf16[2,288,256]{2,1,0:T(8,128)(2,1)S(1)} %slice.45), channel_id=1, source_target_pairs={{32,0},{64,32},{96,64},{0,96},{33,1},{65,33},{97,65},{1,97},{34,2}... | collective-permute-start | bytes 884744 | tf_op jit(solution)/shard_map/ppermute | solution.py:275
  72.3 6.6 %all-to-all-start.1 = ((bf16[16,144,256]{2,1,0:T(8,128)(2,1)}), bf16[16,144,256]{2,1,0:T(8,128)(2,1)S(1)}, u32[]{:S(2)}, u32[]{:S(2)}) async-start(bf16[16,144,256]{2,1,0:T(8,128)(2,1)} %broadcast_in_dim.54), calls=%async_computation.1 | async-start | bytes 2359296 | tf_op jit(solution)/shard_map/all_to_all | solution.py:26
  78.9 3.3 %collective-permute-start.6 = (bf16[4,144,256]{2,1,0:T(8,128)(2,1)S(1)}, bf16[4,144,256]{2,1,0:T(8,128)(2,1)S(1)}, u32[]{:S(2)}, u32[]{:S(2)}) collective-permute-start(bf16[4,144,256]{2,1,0:T(8,128)(2,1)S(1)} %slice.47.own), channel_id=1, source_target_pairs={{96,0},{0,32},{32,64},{64,96},{97,1},{1,33},{33,65},{65,97},{98,2}... | collective-permute-start | bytes 884744 | tf_op jit(solution)/shard_map/ppermute | solution.py:305
  82.1 3.2 %collective-permute-start.5 = (bf16[4,144,256]{2,1,0:T(8,128)(2,1)S(1)}, bf16[4,144,256]{2,1,0:T(8,128)(2,1)S(1)}, u32[]{:S(2)}, u32[]{:S(2)}) collective-permute-start(bf16[4,144,256]{2,1,0:T(8,128)(2,1)S(1)} %slice.47.own), channel_id=1, source_target_pairs={{32,0},{64,32},{96,64},{0,96},{33,1},{65,33},{97,65},{1,97},{34,2}... | collective-permute-start | bytes 884744 | tf_op jit(solution)/shard_map/ppermute | solution.py:304
  85.4 9.2 %collective-permute-done.6.left = bf16[4,144,256]{2,1,0:T(8,128)(2,1)S(1)} collective-permute-done((bf16[4,144,256]{2,1,0:T(8,128)(2,1)S(1)}, bf16[4,144,256]{2,1,0:T(8,128)(2,1)S(1)}, u32[]{:S(2)}, u32[]{:S(2)}) %collective-permute-start.6) | collective-permute-done | bytes 294944 | tf_op jit(solution)/shard_map/ppermute | solution.py:305
  96.5 10.4 %collective-permute-start.7 = (bf16[2304,256]{1,0:T(8,128)(2,1)S(1)}, bf16[2304,256]{1,0:T(8,128)(2,1)S(1)}, u32[]{:S(2)}, u32[]{:S(2)}) collective-permute-start(bf16[2304,256]{1,0:T(8,128)(2,1)S(1)} %bitcast.25), channel_id=1, source_target_pairs={{0,16},{16,0},{1,17},{17,1},{2,18},{18,2},{3,19},{19,3},{4,20},{20... | collective-permute-start | bytes 3538952 | tf_op jit(solution)/shard_map/ppermute | solution.py:308
  109.4 5.6 %attend.1 = (bf16[1024,128]{1,0:T(8,128)(2,1)}, bf16[1024,128]{1,0:T(8,128)(2,1)}, bf16[2,2560,128]{2,1,0:T(8,128)(2,1)S(1)}) custom-call(s32[40]{0:T(128)S(1)} %concatenate.52.meta, bf16[2304,256]{1,0:T(8,128)(2,1)S(1)} %bitcast.26, bf16[2304,256]{1,0:T(8,128)(2,1)S(1)} %collective-permute-done.7.others, bf16[1024,128]{1,0:T(8,128)(2,1)S(1)} %copy-done, ...), custom_call_target="tpu_custom_call" | custom-call | tf_op jit(solution)/shard_map/attend/pallas_call | solution.py:160
  115.0 5.2 %all_to_all.30 = bf16[2,2560,128]{2,1,0:T(8,128)(2,1)S(1)} all-to-all(bf16[2,2560,128]{2,1,0:T(8,128)(2,1)S(1)} %get-tuple-element.18), channel_id=1, replica_groups=mesh['zh'=4,'x'=4,'c'=2,'y'=8,'zl'=2] {'c'}, dimensions={0} | all-to-all | bytes 2621440 | tf_op jit(solution)/shard_map/all_to_all | solution.py:319
  121.2 14.3 %all-to-all-start.3 = ((bf16[16,160,128]{2,1,0:T(8,128)(2,1)}), bf16[16,160,128]{2,1,0:T(8,128)(2,1)S(1)}, u32[]{:S(2)}, u32[]{:S(2)}) async-start(bf16[16,160,128]{2,1,0:T(8,128)(2,1)} %bitcast.14), calls=%async_computation.3 | async-start | bytes 1310720 | tf_op jit(solution)/shard_map/all_to_all | solution.py:321
  135.5 3.3 %collective-permute-start.9 = (bf16[2,144,256]{2,1,0:T(8,128)(2,1)S(1)}, bf16[2,144,256]{2,1,0:T(8,128)(2,1)S(1)}, u32[]{:S(2)}, u32[]{:S(2)}) collective-permute-start(bf16[2,144,256]{2,1,0:T(8,128)(2,1)S(1)} %slice.40), channel_id=1, source_target_pairs={{96,0},{0,32},{32,64},{64,96},{97,1},{1,33},{33,65},{65,97},{98,2}... | collective-permute-start | bytes 442376 | tf_op jit(solution)/shard_map/ppermute | solution.py:313
  138.7 3.2 %collective-permute-start.8 = (bf16[2,144,256]{2,1,0:T(8,128)(2,1)S(1)}, bf16[2,144,256]{2,1,0:T(8,128)(2,1)S(1)}, u32[]{:S(2)}, u32[]{:S(2)}) collective-permute-start(bf16[2,144,256]{2,1,0:T(8,128)(2,1)S(1)} %slice.39), channel_id=1, source_target_pairs={{32,0},{64,32},{96,64},{0,96},{33,1},{65,33},{97,65},{1,97},{34,2}... | collective-permute-start | bytes 442376 | tf_op jit(solution)/shard_map/ppermute | solution.py:312
  142.0 10.0 %all-to-all-done.3.parts = bf16[16,160,128]{2,1,0:T(8,128)(2,1)S(1)} async-done(((bf16[16,160,128]{2,1,0:T(8,128)(2,1)}), bf16[16,160,128]{2,1,0:T(8,128)(2,1)S(1)}, u32[]{:S(2)}, u32[]{:S(2)}) %all-to-all-start.3) | async-done | bytes 655392 | tf_op jit(solution)/shard_map/all_to_all | solution.py:321
  152.6 4.4 %all-gather.1 = bf16[288,128]{1,0:T(8,128)(2,1)S(1)} all-gather(bf16[144,128]{1,0:T(8,128)(2,1)S(1)} %divide.1), channel_id=3, replica_groups=mesh['zh'=4,'x'=4,'c'=2,'y'=8,'zl'=2] {'c'}, dimensions={0}, use_global_device_ids=true | all-gather | bytes 110592 | tf_op jit(solution)/shard_map/all_gather | solution.py:323
  159.2 11.1 %all-to-all-start.4 = ((bf16[16,176,128]{2,1,0:T(8,128)(2,1)}), bf16[16,176,128]{2,1,0:T(8,128)(2,1)S(1)}, u32[]{:S(2)}, u32[]{:S(2)}) async-start(bf16[16,176,128]{2,1,0:T(8,128)(2,1)} %spread.1), calls=%async_computation.4 | async-start | bytes 1441792 | tf_op jit(solution)/shard_map/all_to_all | solution.py:325
  170.3 19.6 %all-to-all-done.4 = bf16[16,176,128]{2,1,0:T(8,128)(2,1)S(1)} async-done(((bf16[16,176,128]{2,1,0:T(8,128)(2,1)}), bf16[16,176,128]{2,1,0:T(8,128)(2,1)S(1)}, u32[]{:S(2)}, u32[]{:S(2)}) %all-to-all-start.4) | async-done | bytes 720928 | tf_op jit(solution)/shard_map/all_to_all | solution.py:325
  190.9 6.8 %all-to-all-start.5 = ((f32[32,1,72]{2,1,0:T(1,128)}), f32[32,1,72]{2,1,0:T(1,128)S(1)}, u32[]{:S(2)}, u32[]{:S(2)}) async-start(f32[32,1,72]{2,1,0:T(1,128)} %bitcast.17), calls=%async_computation.5 | async-start | bytes 32768 | tf_op jit(solution)/shard_map/all_to_all | solution.py:331
  199.9 5.5 %all-to-all-done.5 = f32[32,1,72]{2,1,0:T(1,128)S(1)} async-done(((f32[32,1,72]{2,1,0:T(1,128)}), f32[32,1,72]{2,1,0:T(1,128)S(1)}, u32[]{:S(2)}, u32[]{:S(2)}) %all-to-all-start.5) | async-done | bytes 9248 | tf_op jit(solution)/shard_map/all_to_all | solution.py:331
  (77 shorter events, 27.4 us)
Async XLA Ops:
  9.7 12.0 %copy-start.4 = (bf16[256,144]{0,1:T(8,128)(2,1)S(1)}, bf16[256,144]{0,1:T(8,128)(2,1)}, u32[]{:S(2)}) copy-start(bf16[256,144]{0,1:T(8,128)(2,1)} %param.17) | copy-start | bytes 221188
  9.7 43.1 %all-to-all-start = ((bf16[8,144,290]{2,1,0:T(8,128)(2,1)}), bf16[8,144,290]{2,1,0:T(8,128)(2,1)S(1)}, u32[]{:S(2)}, u32[]{:S(2)}) async-start(bf16[8,144,290]{2,1,0:T(8,128)(2,1)} %broadcast_in_dim.29), calls=%async_computation | async-start | bytes 1769472 | tf_op jit(solution)/shard_map/all_to_all | solution.py:26
  21.6 29.9 %copy-start.5 = (s32[12]{0:T(128)S(1)}, s32[12]{0:T(128)}, u32[]{:S(2)}) copy-start(s32[12]{0:T(128)} %param.21) | copy-start | bytes 148
  21.7 31.0 %copy-start.7 = (s32[12]{0:T(128)S(1)}, s32[12]{0:T(128)}, u32[]{:S(2)}) copy-start(s32[12]{0:T(128)} %param.22) | copy-start | bytes 148
  21.7 31.0 %copy-start.8 = (s32[12]{0:T(128)S(1)}, s32[12]{0:T(128)}, u32[]{:S(2)}) copy-start(s32[12]{0:T(128)} %param.23) | copy-start | bytes 148
  45.0 14.5 %collective-permute-start.3 = (bf16[4,288,256]{2,1,0:T(8,128)(2,1)S(1)}, bf16[4,288,256]{2,1,0:T(8,128)(2,1)S(1)}, u32[]{:S(2)}, u32[]{:S(2)}) collective-permute-start(bf16[4,288,256]{2,1,0:T(8,128)(2,1)S(1)} %slice.44.own), channel_id=1, source_target_pairs={{96,0},{0,32},{32,64},{64,96},{97,1},{1,33},{33,65},{65,97},{98,2}... | collective-permute-start | bytes 1769480 | tf_op jit(solution)/shard_map/ppermute | solution.py:274
  48.1 13.3 %collective-permute-start.1 = (bf16[4,288,256]{2,1,0:T(8,128)(2,1)S(1)}, bf16[4,288,256]{2,1,0:T(8,128)(2,1)S(1)}, u32[]{:S(2)}, u32[]{:S(2)}) collective-permute-start(bf16[4,288,256]{2,1,0:T(8,128)(2,1)S(1)} %slice.44.own), channel_id=1, source_target_pairs={{32,0},{64,32},{96,64},{0,96},{33,1},{65,33},{97,65},{1,97},{34,2}... | collective-permute-start | bytes 1769480 | tf_op jit(solution)/shard_map/ppermute | solution.py:273
  52.8 16.9 %collective-permute-start = (bf16[16,72,290]{2,1,0:T(8,128)(2,1)S(1)}, bf16[16,72,290]{2,1,0:T(8,128)(2,1)S(1)}, u32[]{:S(2)}, u32[]{:S(2)}) collective-permute-start(bf16[16,72,290]{2,1,0:T(8,128)(2,1)S(1)} %bitcast.27), channel_id=1, source_target_pairs={{0,16},{16,0},{1,17},{17,1},{2,18},{18,2},{3,19},{19,3},{4,20},{20... | collective-permute-start | bytes 2004488 | tf_op jit(solution)/shard_map/ppermute | solution.py:279
  59.5 8.7 %collective-permute-start.4 = (bf16[2,288,256]{2,1,0:T(8,128)(2,1)S(1)}, bf16[2,288,256]{2,1,0:T(8,128)(2,1)S(1)}, u32[]{:S(2)}, u32[]{:S(2)}) collective-permute-start(bf16[2,288,256]{2,1,0:T(8,128)(2,1)S(1)} %slice.46), channel_id=1, source_target_pairs={{96,0},{0,32},{32,64},{64,96},{97,1},{1,33},{33,65},{65,97},{98,2}... | collective-permute-start | bytes 884744 | tf_op jit(solution)/shard_map/ppermute | solution.py:276
  61.5 8.2 %collective-permute-start.2 = (bf16[2,288,256]{2,1,0:T(8,128)(2,1)S(1)}, bf16[2,288,256]{2,1,0:T(8,128)(2,1)S(1)}, u32[]{:S(2)}, u32[]{:S(2)}) collective-permute-start(bf16[2,288,256]{2,1,0:T(8,128)(2,1)S(1)} %slice.45), channel_id=1, source_target_pairs={{32,0},{64,32},{96,64},{0,96},{33,1},{65,33},{97,65},{1,97},{34,2}... | collective-permute-start | bytes 884744 | tf_op jit(solution)/shard_map/ppermute | solution.py:275
  72.3 37.1 %copy-start = (bf16[1024,128]{1,0:T(8,128)(2,1)S(1)}, bf16[1024,128]{1,0:T(8,128)(2,1)}, u32[]{:S(2)}) copy-start(bf16[1024,128]{1,0:T(8,128)(2,1)} %k_old.1) | copy-start | bytes 786436
  72.3 37.1 %copy-start.1 = (bf16[1024,128]{1,0:T(8,128)(2,1)S(1)}, bf16[1024,128]{1,0:T(8,128)(2,1)}, u32[]{:S(2)}) copy-start(bf16[1024,128]{1,0:T(8,128)(2,1)} %v_old.1) | copy-start | bytes 786436
  72.3 24.3 %all-to-all-start.1 = ((bf16[16,144,256]{2,1,0:T(8,128)(2,1)}), bf16[16,144,256]{2,1,0:T(8,128)(2,1)S(1)}, u32[]{:S(2)}, u32[]{:S(2)}) async-start(bf16[16,144,256]{2,1,0:T(8,128)(2,1)} %broadcast_in_dim.54), calls=%async_computation.1 | async-start | bytes 2359296 | tf_op jit(solution)/shard_map/all_to_all | solution.py:26
  78.9 15.7 %collective-permute-start.6 = (bf16[4,144,256]{2,1,0:T(8,128)(2,1)S(1)}, bf16[4,144,256]{2,1,0:T(8,128)(2,1)S(1)}, u32[]{:S(2)}, u32[]{:S(2)}) collective-permute-start(bf16[4,144,256]{2,1,0:T(8,128)(2,1)S(1)} %slice.47.own), channel_id=1, source_target_pairs={{96,0},{0,32},{32,64},{64,96},{97,1},{1,33},{33,65},{65,97},{98,2}... | collective-permute-start | bytes 884744 | tf_op jit(solution)/shard_map/ppermute | solution.py:305
  82.1 14.4 %collective-permute-start.5 = (bf16[4,144,256]{2,1,0:T(8,128)(2,1)S(1)}, bf16[4,144,256]{2,1,0:T(8,128)(2,1)S(1)}, u32[]{:S(2)}, u32[]{:S(2)}) collective-permute-start(bf16[4,144,256]{2,1,0:T(8,128)(2,1)S(1)} %slice.47.own), channel_id=1, source_target_pairs={{32,0},{64,32},{96,64},{0,96},{33,1},{65,33},{97,65},{1,97},{34,2}... | collective-permute-start | bytes 884744 | tf_op jit(solution)/shard_map/ppermute | solution.py:304
  96.5 12.9 %collective-permute-start.7 = (bf16[2304,256]{1,0:T(8,128)(2,1)S(1)}, bf16[2304,256]{1,0:T(8,128)(2,1)S(1)}, u32[]{:S(2)}, u32[]{:S(2)}) collective-permute-start(bf16[2304,256]{1,0:T(8,128)(2,1)S(1)} %bitcast.25), channel_id=1, source_target_pairs={{0,16},{16,0},{1,17},{17,1},{2,18},{18,2},{3,19},{19,3},{4,20},{20... | collective-permute-start | bytes 3538952 | tf_op jit(solution)/shard_map/ppermute | solution.py:308
  121.2 30.8 %all-to-all-start.3 = ((bf16[16,160,128]{2,1,0:T(8,128)(2,1)}), bf16[16,160,128]{2,1,0:T(8,128)(2,1)S(1)}, u32[]{:S(2)}, u32[]{:S(2)}) async-start(bf16[16,160,128]{2,1,0:T(8,128)(2,1)} %bitcast.14), calls=%async_computation.3 | async-start | bytes 1310720 | tf_op jit(solution)/shard_map/all_to_all | solution.py:321
  135.5 21.5 %collective-permute-start.9 = (bf16[2,144,256]{2,1,0:T(8,128)(2,1)S(1)}, bf16[2,144,256]{2,1,0:T(8,128)(2,1)S(1)}, u32[]{:S(2)}, u32[]{:S(2)}) collective-permute-start(bf16[2,144,256]{2,1,0:T(8,128)(2,1)S(1)} %slice.40), channel_id=1, source_target_pairs={{96,0},{0,32},{32,64},{64,96},{97,1},{1,33},{33,65},{65,97},{98,2}... | collective-permute-start | bytes 442376 | tf_op jit(solution)/shard_map/ppermute | solution.py:313
  138.7 18.2 %collective-permute-start.8 = (bf16[2,144,256]{2,1,0:T(8,128)(2,1)S(1)}, bf16[2,144,256]{2,1,0:T(8,128)(2,1)S(1)}, u32[]{:S(2)}, u32[]{:S(2)}) collective-permute-start(bf16[2,144,256]{2,1,0:T(8,128)(2,1)S(1)} %slice.39), channel_id=1, source_target_pairs={{32,0},{64,32},{96,64},{0,96},{33,1},{65,33},{97,65},{1,97},{34,2}... | collective-permute-start | bytes 442376 | tf_op jit(solution)/shard_map/ppermute | solution.py:312
  157.0 13.3 %copy-start.6 = (bf16[288]{0:T(512)(128)(2,1)S(1)}, bf16[288]{0:T(512)(128)(2,1)}, u32[]{:S(2)}) copy-start(bf16[288]{0:T(512)(128)(2,1)} %param.18) | copy-start | bytes 1732
  159.2 30.7 %all-to-all-start.4 = ((bf16[16,176,128]{2,1,0:T(8,128)(2,1)}), bf16[16,176,128]{2,1,0:T(8,128)(2,1)S(1)}, u32[]{:S(2)}, u32[]{:S(2)}) async-start(bf16[16,176,128]{2,1,0:T(8,128)(2,1)} %spread.1), calls=%async_computation.4 | async-start | bytes 1441792 | tf_op jit(solution)/shard_map/all_to_all | solution.py:325
  170.3 35.2 %copy-start.3 = (bf16[72,288]{1,0:T(8,128)(2,1)S(1)}, bf16[72,288]{1,0:T(8,128)(2,1)}, u32[]{:S(2)}) copy-start(bf16[72,288]{1,0:T(8,128)(2,1)} %param.12) | copy-start | bytes 124420
  190.9 14.5 %all-to-all-start.5 = ((f32[32,1,72]{2,1,0:T(1,128)}), f32[32,1,72]{2,1,0:T(1,128)S(1)}, u32[]{:S(2)}, u32[]{:S(2)}) async-start(f32[32,1,72]{2,1,0:T(1,128)} %bitcast.17), calls=%async_computation.5 | async-start | bytes 32768 | tf_op jit(solution)/shard_map/all_to_all | solution.py:331
  197.7 7.7 %collective-permute-start.10 = (f32[72,144]{1,0:T(8,128)S(1)}, f32[72,144]{1,0:T(8,128)S(1)}, u32[]{:S(2)}, u32[]{:S(2)}) collective-permute-start(f32[72,144]{1,0:T(8,128)S(1)} %fusion.9), channel_id=1, source_target_pairs={{0,16},{16,0},{1,17},{17,1},{2,18},{18,2},{3,19},{19,3},{4,20},{20... | collective-permute-start | bytes 124424 | tf_op jit(solution)/shard_map/ppermute | solution.py:335
  (1 other events, 1.0 us)

commit v7 on v6

--- a/solution.py
+++ b/solution.py
@@ -9,7 +9,8 @@
 HD = 128
 REQS = 12
 NEWTOK = 192
-TILE = 256
+READ_TILE = 512
+WRITE_TILE = 256
 PIECE = 48
 epsilon = 1e-06
 soft_cap = 50.0
@@ -65,43 +66,50 @@
     )(meta, mine, others, turns, *columns)
 
 
-def attend_kernel(meta, mine, others, k_old, v_old, k_pool, v_pool, sums, num, den, totals):
-    slots = k_old.shape[0]
-    tiles = slots // TILE
+def attend_kernel(meta, mine, others, k_old, v_old, k_other, v_other, k_pool, v_pool, sums, keys, values, num, den, totals):
+    own = k_old.shape[0]
+    slots = keys.shape[0]
     first = meta[3 * REQS]
-    queries_here = meta[3 * REQS + 2] == 0
-    chunk = sums.shape[1] // (REQS * NEWTOK // (3 * PIECE))
-    heads = sums.shape[0]
-
-    def rows_of(r, on_core_0, on_core_1):
-        here = pl.ds(pl.multiple_of(r * NEWTOK, 64), NEWTOK)
-        return jnp.where(queries_here, on_core_0[here, :], on_core_1[here, :])
-
-    k_pool[...] = k_old[...]
-    v_pool[...] = v_old[...]
+    core = meta[3 * REQS + 2]
+    on_core_0 = core == 0
+    blocks = REQS * NEWTOK // (3 * PIECE)
+    chunk = sums.shape[0] // blocks
+
+    my_slots = pl.ds(pl.multiple_of(core * own, own), own)
+    other_slots = pl.ds(pl.multiple_of((1 - core) * own, own), own)
+    keys[my_slots, :] = k_old[...]
+    keys[other_slots, :] = k_other[...]
+    values[my_slots, :] = v_old[...]
+    values[other_slots, :] = v_other[...]
     totals[...] = jnp.zeros_like(totals)
 
     def write_request(r, carry):
         cached, fresh, offset = meta[r], meta[REQS + r], meta[2 * REQS + r]
         begin = offset + cached - first
-        for t in range(tiles):
-
-            @pl.when((begin < (t + 1) * TILE) & (begin + fresh > t * TILE))
-            def _():
-                rows = rows_of(r, others, mine)
-                slot = lax.broadcasted_iota(jnp.int32, (TILE, NEWTOK), 0) + (t * TILE - begin)
-                index = lax.broadcasted_iota(jnp.int32, (TILE, NEWTOK), 1)
-                pick = jnp.where((slot == index) & (index < fresh), 1.0, 0.0).astype(BF16)
-                new = jnp.dot(pick, rows, preferred_element_type=F32)
-                place = lax.broadcasted_iota(jnp.int32, (TILE, HD), 0) + (t * TILE - begin)
-                written = (place >= 0) & (place < fresh)
-                here = pl.ds(t * TILE, TILE)
-                k_pool[here, :] = jnp.where(written, new[:, :HD], k_pool[here, :].astype(F32)).astype(BF16)
-                v_pool[here, :] = jnp.where(written, new[:, HD:], v_pool[here, :].astype(F32)).astype(BF16)
-
+
+        def write_tile(t, carry):
+            rows = pl.ds(pl.multiple_of(r * NEWTOK, 64), NEWTOK)
+            a, b = mine[rows, HD:], others[rows, :]
+            rows = jnp.concatenate([jnp.where(on_core_0, a, b), jnp.where(on_core_0, b, a)], axis=1)
+            slot = lax.broadcasted_iota(jnp.int32, (WRITE_TILE, NEWTOK), 0) + (t * WRITE_TILE - begin)
+            index = lax.broadcasted_iota(jnp.int32, (WRITE_TILE, NEWTOK), 1)
+            pick = jnp.where((slot == index) & (index < fresh), 1.0, 0.0).astype(BF16)
+            new = jnp.dot(pick, rows, preferred_element_type=F32)
+            place = lax.broadcasted_iota(jnp.int32, (WRITE_TILE, HD), 0) + (t * WRITE_TILE - begin)
+            written = (place >= 0) & (place < fresh)
+            here = pl.ds(pl.multiple_of(t * WRITE_TILE, WRITE_TILE), WRITE_TILE)
+            keys[here, :] = jnp.where(written, new[:, :HD], keys[here, :].astype(F32)).astype(BF16)
+            values[here, :] = jnp.where(written, new[:, HD:], values[here, :].astype(F32)).astype(BF16)
+            return carry
+
+        low, high = jnp.maximum(begin, 0), jnp.minimum(begin + fresh, slots)
+        tiles = jnp.where(high > low, pl.cdiv(high, WRITE_TILE), 0)
+        lax.fori_loop(lax.div(low, WRITE_TILE), tiles, write_tile, 0)
         return carry
 
     lax.fori_loop(0, REQS, write_request, 0)
+    k_pool[...] = keys[my_slots, :]
+    v_pool[...] = values[my_slots, :]
 
     def read_request(r, carry):
         cached, fresh, offset = meta[r], meta[REQS + r], meta[2 * REQS + r]
@@ -110,70 +118,66 @@
         num[...] = jnp.zeros_like(num)
         den[...] = jnp.zeros_like(den)
 
-        @pl.when((begin < slots) & (end > 0))
-        def _():
-            rows = rows_of(r, mine, others)
-            rows = jnp.concatenate([rows[:, h * HD : (h + 1) * HD] for h in range(heads)], axis=0)
-            row = lax.broadcasted_iota(jnp.int32, (heads * NEWTOK, 1), 0)
-            row = jnp.where(row >= NEWTOK, row - NEWTOK, row)
+        def read_tile(t, carry):
+            rows = mine[pl.ds(pl.multiple_of(r * NEWTOK, 64), NEWTOK), :HD]
+            row = lax.broadcasted_iota(jnp.int32, (NEWTOK, 1), 0)
             last = cached + jnp.minimum(row, fresh - 1) + begin
-            for t in range(tiles):
-
-                @pl.when((begin < (t + 1) * TILE) & (end > t * TILE))
-                def _():
-                    here = pl.ds(t * TILE, TILE)
-                    logits = lax.dot_general(
-                        rows, k_pool[here, :], (((1,), (1,)), ((), ())), preferred_element_type=F32
-                    )
-                    slot = lax.broadcasted_iota(jnp.int32, logits.shape, 1) + t * TILE
-                    visible = (slot >= begin) & (slot <= last)
-                    weight = jnp.exp(soft_cap * jnp.tanh(logits * (1.0 / soft_cap)))
-                    weight = jnp.where(visible, weight, 0.0).astype(BF16)
-                    num[...] += jnp.dot(weight, v_pool[here, :], preferred_element_type=F32)
-                    den[...] += lax.dot_general(
-                        jnp.ones((8, TILE), BF16), weight, (((1,), (1,)), ((), ())), preferred_element_type=F32
-                    )
+            here = pl.ds(pl.multiple_of(t * READ_TILE, READ_TILE), READ_TILE)
+            logits = lax.dot_general(rows, keys[here, :], (((1,), (1,)), ((), ())), preferred_element_type=F32)
+            slot = lax.broadcasted_iota(jnp.int32, logits.shape, 1) + t * READ_TILE
+            visible = (slot >= begin) & (slot <= last)
+            weight = jnp.exp(soft_cap * jnp.tanh(logits * (1.0 / soft_cap)))
+            weight = jnp.where(visible, weight, 0.0).astype(BF16)
+            num[...] += jnp.dot(weight, values[here, :], preferred_element_type=F32)
+            den[...] += lax.dot_general(
+                jnp.ones((8, READ_TILE), BF16), weight, (((1,), (1,)), ((), ())), preferred_element_type=F32
+            )
+            return carry
+
+        low, high = jnp.maximum(begin, 0), jnp.minimum(end, slots)
+        tiles = jnp.where(high > low, pl.cdiv(high, READ_TILE), 0)
+        lax.fori_loop(lax.div(low, READ_TILE), tiles, read_tile, 0)
 
         for piece in range(NEWTOK // PIECE):
             at = r * (NEWTOK // PIECE) + piece
-            block, part = at // 3, at % 3
+            block, part = lax.div(at, 3), lax.rem(at, 3)
             to = pl.multiple_of(block * chunk + part * PIECE, 16)
-            for h in range(heads):
-                low = h * NEWTOK + piece * PIECE
-                sums[h, pl.ds(to, PIECE), :] = num[low : low + PIECE, :].astype(BF16)
-                totals[h, pl.ds(block * 8 + part, 1), 0:PIECE] = den[0:1, low : low + PIECE]
+            at_row = piece * PIECE
+            sums[pl.ds(to, PIECE), :] = num[at_row : at_row + PIECE, :].astype(BF16)
+            totals[pl.ds(block * 8 + part, 1), 0:PIECE] = den[0:1, at_row : at_row + PIECE]
         return carry
 
     lax.fori_loop(0, REQS, read_request, 0)
-    for h in range(heads):
-        for block in range(REQS * NEWTOK // (3 * PIECE)):
-            rows = totals[h, block * 8 : block * 8 + 8, :]
-            rows = jnp.concatenate([rows, jnp.zeros_like(rows)], axis=0)
-            sums[h, block * chunk + 3 * PIECE : (block + 1) * chunk, :] = rows.astype(BF16)
-
-
-def attend(meta, mine, others, k_cache, v_cache):
-    heads = 2
+    for block in range(blocks):
+        rows = totals[block * 8 : block * 8 + 8, :]
+        rows = jnp.concatenate([rows, jnp.zeros_like(rows)], axis=0)
+        sums[block * chunk + 3 * PIECE : (block + 1) * chunk, :] = rows.astype(BF16)
+
+
+def attend(meta, mine, others, k_cache, v_cache, k_other, v_other):
     blocks = REQS * NEWTOK // (3 * PIECE)
     chunk = 3 * PIECE + 16
     vmem = pl.BlockSpec(memory_space=pltpu.VMEM)
+    slots = 2 * k_cache.shape[0]
     return pl.pallas_call(
         attend_kernel,
         out_shape=(
             jax.ShapeDtypeStruct(k_cache.shape, BF16),
             jax.ShapeDtypeStruct(v_cache.shape, BF16),
-            jax.ShapeDtypeStruct((heads, blocks * chunk, HD), BF16),
+            jax.ShapeDtypeStruct((blocks * chunk, HD), BF16),
         ),
-        in_specs=[pl.BlockSpec(memory_space=pltpu.SMEM), vmem, vmem, vmem, vmem],
+        in_specs=[pl.BlockSpec(memory_space=pltpu.SMEM)] + [vmem] * 6,
         out_specs=(vmem, vmem, vmem),
         scratch_shapes=[
-            pltpu.VMEM((heads * NEWTOK, HD), F32),
-            pltpu.VMEM((8, heads * NEWTOK), F32),
-            pltpu.VMEM((heads, blocks * 8, HD), F32),
+            pltpu.VMEM((slots, HD), BF16),
+            pltpu.VMEM((slots, HD), BF16),
+            pltpu.VMEM((NEWTOK, HD), F32),
+            pltpu.VMEM((8, NEWTOK), F32),
+            pltpu.VMEM((blocks * 8, HD), F32),
         ],
         compiler_params=pltpu.CompilerParams(vmem_limit_bytes=32 << 20),
         name="attend",
-    )(meta, mine, others, k_cache, v_cache)
+    )(meta, mine, others, k_cache, v_cache, k_other, v_other)
 
 
 def divide_kernel(meta, parts, out):
@@ -256,7 +260,7 @@
     high = lax.reduce_precision(squares, 8, 7)
     gained = float_in * (1.0 + pre_gain.astype(F32))
     gained = jnp.concatenate([gained, high, squares - high], axis=1).astype(BF16)
-    weights = jnp.concatenate([w_q, w_k, w_v], axis=1)
+    weights = jnp.concatenate([w_q[:, :HD], w_k, w_q[:, HD:], w_v], axis=1)
     gained, weights = lax.optimization_barrier((gained, weights))
     gained = lax.all_gather(gained, "zl", axis=0, tiled=True)
     gained = everywhere(gained, "y", n_gy // 2).reshape(n_gy, tok_rows, -1)
@@ -286,17 +290,23 @@
     half = HD // 2
     inverse = jnp.power(10000.0, -2.0 * jnp.arange(half, dtype=F32) / HD)
     angle = position.astype(F32)[:, None] * inverse[None, :]
-    scale = jnp.where(core == 0, query_scale, 1.0).astype(F32)
-    cosine, sine = jnp.cos(angle) * scale, jnp.sin(angle) * scale
+    cosine, sine = jnp.cos(angle), jnp.sin(angle)
     cosine = jnp.concatenate([cosine, cosine], axis=1)
     sine = jnp.concatenate([-sine, sine], axis=1)
-    turns = jnp.stack([cosine, sine, jnp.where(core == 0, cosine, 1.0), jnp.where(core == 0, sine, 0.0)])
+    turns = jnp.stack(
+        [
+            cosine * query_scale,
+            sine * query_scale,
+            jnp.where(core == 0, cosine, 1.0),
+            jnp.where(core == 0, sine, 0.0),
+        ]
+    )
     meta = jnp.concatenate(
         [
             cached_len,
             new_len,
             slot_offset,
-            jnp.stack([me * k_cache.shape[0], chip_rows, core, lax.axis_index("x")]).astype(jnp.int32),
+            jnp.stack([me // 2 * (2 * k_cache.shape[0]), chip_rows, core, lax.axis_index("x")]).astype(jnp.int32),
         ]
     )
     mine = project(meta, gained, other, turns, columns)
@@ -304,8 +314,12 @@
     out_right = lax.ppermute(w_out, "x", from_right)
     out_left = lax.ppermute(w_out, "x", from_left)
     mine = everywhere(mine, CHIPS, n_chips).reshape(-1, cols)
-    mine, out_right, out_left = lax.optimization_barrier((mine, out_right, out_left))
-    others = lax.ppermute(mine, "c", swap)
+    k_other = lax.ppermute(k_cache, "c", swap)
+    v_other = lax.ppermute(v_cache, "c", swap)
+    mine, out_right, out_left, k_other, v_other = lax.optimization_barrier(
+        (mine, out_right, out_left, k_other, v_other)
+    )
+    others = lax.ppermute(mine[:, HD:], "c", swap)
     out_columns = [
         w_out,
         out_right,
@@ -314,11 +328,8 @@
         out_left,
     ]
 
-    k_pool, v_pool, sums = attend(meta, mine, others, k_cache, v_cache)
-
-    both = lax.all_to_all(sums, "c", 0, 0)
-    head = (both[0].astype(F32) + both[1].astype(F32)).astype(BF16)
-    parts = lax.all_to_all(head.reshape(n_chips, -1, HD), CHIPS, 0, 0)
+    k_pool, v_pool, sums = attend(meta, mine, others, k_cache, v_cache, k_other, v_other)
+    parts = lax.all_to_all(sums.reshape(n_chips, -1, HD), CHIPS, 0, 0)
     attended = divide(meta, parts)
     attended = lax.all_gather(attended, "c", axis=0)
     partial_out = spread(meta, attended, out_columns, n_gy)

time: 207 us -> 203 us (0.981)
  waiting for transfers between devices: 52.5 us -> 39.8 us
  starting transfers between devices: 90.1 us -> 99.7 us
  blocking collectives: 42 us -> 36.9 us
  local copies, waits for them, and re-layouts: 5.31 us -> 8.3 us
    ppermute x1, waiting for transfers between devices: 9.15 us -> 0.01 us  [on_device(): out_left = lax.ppermute(w_out, 'x', from_left)]
    ppermute x1 -> x3, starting transfers between devices: 10.4 us -> 19.4 us  [the longest x1 8.94 us: on_device(): k_other = lax.ppermute(k_cache, 'c', swap)]
    all_to_all x1 -> x0, blocking collectives: 5.16 us -> none  [on_device(): both = lax.all_to_all(sums, 'c', 0, 0)]
    all_to_all x1, starting transfers between devices: 11.1 us -> 13.6 us  [on_device(): total = jnp.sum(lax.all_to_all(partial_out, GY, 0, 0).astype(F32), axis=0)]
  transfers between devices with their start and end apart: 16 -> 18, of which waited for: 9 -> 7; matrix products, arithmetic and copies ran while one was open for 1% -> 2% of each run, Pallas kernels for 0% -> 0%
where the time goes in v7:
time: 203 us; the launch traced here: 202 us
  starting transfers between devices  99.7 us (49%)
  waiting for transfers between devices  39.8 us (20%)
  blocking collectives  36.9 us (18%)
  Pallas kernels  10.6 us (5%)
  local copies, waits for them, and re-layouts  8.3 us (4%)
  other arithmetic  5.86 us (3%)
    all_gather x1, blocking collectives, on_device(): weights = lax.all_gather(weights, 'zh', axis=0)  22.3 us
    all_to_all x1, waiting for transfers between devices, on_device(): total = jnp.sum(lax.all_to_all(partial_out, GY, 0, 0).astype(F32), axis=0)  19.5 us
    all_to_all x1, starting transfers between devices, on_device(): total = jnp.sum(lax.all_to_all(partial_out, GY, 0, 0).astype(F32), axis=0)  13.6 us
    all_to_all x2, starting transfers between devices, everywhere(): lax.all_to_all(jnp.broadcast_to(value[None], (count,) + value.shape), axe...  13 us
    all_to_all x1, starting transfers between devices, on_device(): parts = lax.all_to_all(sums.reshape(n_chips, -1, HD), CHIPS, 0, 0)  12.7 us
    all_to_all x1, waiting for transfers between devices, on_device(): parts = lax.all_to_all(sums.reshape(n_chips, -1, HD), CHIPS, 0, 0)  9.03 us
    ppermute x1, starting transfers between devices, on_device(): k_other = lax.ppermute(k_cache, 'c', swap)  8.94 us
    ppermute x1, starting transfers between devices, on_device(): others = lax.ppermute(mine[:, HD:], 'c', swap)  8.54 us
  transfers between devices with their start and end apart: 18, of which 7 were waited for; matrix products, arithmetic and copies ran while one was open for 2% of the time, Pallas kernels for 0%

profile of v7, /device:TPU:1, one launch (start us, length us, event | category | flops | bytes accessed | tf_op | source)
XLA Modules:
  0.0 202.2 jit_solution(5977489308961244608)
XLA Ops:
  4.2 5.1 %all_gather.18 = bf16[144,290]{1,0:T(8,128)(2,1)S(1)} all-gather(bf16[72,290]{1,0:T(8,128)(2,1)S(1)} %pad_maximum_fusion.6), channel_id=1, replica_groups=mesh['zh'=4,'x'=4,'c'=2,'y'=8,'zl'=2] {'zl'}, dimensions={0}, use_global_device_ids=true | all-gather | bytes 125280 | tf_op jit(solution)/shard_map/all_gather | solution.py:265
  10.3 7.0 %all-to-all-start = ((bf16[8,144,290]{2,1,0:T(8,128)(2,1)}), bf16[8,144,290]{2,1,0:T(8,128)(2,1)S(1)}, u32[]{:S(2)}, u32[]{:S(2)}) async-start(bf16[8,144,290]{2,1,0:T(8,128)(2,1)} %broadcast_in_dim.29), calls=%async_computation | async-start | bytes 1769472 | tf_op jit(solution)/shard_map/all_to_all | solution.py:27
  17.3 5.0 %all_gather.19 = bf16[288,512]{1,0:T(8,128)(2,1)S(1)} all-gather(bf16[144,512]{1,0:T(8,128)(2,1)S(1)} %pad_maximum_fusion.3), channel_id=1, replica_groups=mesh['zh'=4,'x'=4,'c'=2,'y'=8,'zl'=2] {'c'}, dimensions={0}, use_global_device_ids=true | all-gather | bytes 442368 | tf_op jit(solution)/shard_map/all_gather | solution.py:268
  22.3 22.3 %all-gather = bf16[1728,256]{1,0:T(8,128)(2,1)S(1)} all-gather(bf16[432,256]{1,0:T(8,128)(2,1)S(1)} %pad_maximum_fusion.1), channel_id=2, replica_groups=mesh['zh'=4,'x'=4,'c'=2,'y'=8,'zl'=2] {'zh'}, dimensions={0}, use_global_device_ids=true | all-gather | bytes 1105920 | tf_op jit(solution)/shard_map/all_gather | solution.py:272
  45.6 3.2 %collective-permute-start.3 = (bf16[4,288,256]{2,1,0:T(8,128)(2,1)S(1)}, bf16[4,288,256]{2,1,0:T(8,128)(2,1)S(1)}, u32[]{:S(2)}, u32[]{:S(2)}) collective-permute-start(bf16[4,288,256]{2,1,0:T(8,128)(2,1)S(1)} %slice.48.own), channel_id=1, source_target_pairs={{96,0},{0,32},{32,64},{64,96},{97,1},{1,33},{33,65},{65,97},{98,2}... | collective-permute-start | bytes 1769480 | tf_op jit(solution)/shard_map/ppermute | solution.py:278
  48.9 3.4 %collective-permute-start.1 = (bf16[4,288,256]{2,1,0:T(8,128)(2,1)S(1)}, bf16[4,288,256]{2,1,0:T(8,128)(2,1)S(1)}, u32[]{:S(2)}, u32[]{:S(2)}) collective-permute-start(bf16[4,288,256]{2,1,0:T(8,128)(2,1)S(1)} %slice.48.own), channel_id=1, source_target_pairs={{32,0},{64,32},{96,64},{0,96},{33,1},{65,33},{97,65},{1,97},{34,2}... | collective-permute-start | bytes 1769480 | tf_op jit(solution)/shard_map/ppermute | solution.py:277
  52.4 5.9 %collective-permute-start = (bf16[16,72,290]{2,1,0:T(8,128)(2,1)S(1)}, bf16[16,72,290]{2,1,0:T(8,128)(2,1)}, u32[]{:S(2)}, u32[]{:S(2)}) collective-permute-start(bf16[16,72,290]{2,1,0:T(8,128)(2,1)S(1)} %bitcast.23), channel_id=1, source_target_pairs={{0,16},{16,0},{1,17},{17,1},{2,18},{18,2},{3,19},{19,3},{4,20},{20... | collective-permute-start | bytes 2004488 | tf_op jit(solution)/shard_map/ppermute | solution.py:283
  63.7 4.6 %collective-permute-start.2 = (bf16[2,288,256]{2,1,0:T(8,128)(2,1)}, bf16[2,288,256]{2,1,0:T(8,128)(2,1)S(1)}, u32[]{:S(2)}, u32[]{:S(2)}) collective-permute-start(bf16[2,288,256]{2,1,0:T(8,128)(2,1)} %slice.49), channel_id=1, source_target_pairs={{32,0},{64,32},{96,64},{0,96},{33,1},{65,33},{97,65},{1,97},{34,2}... | collective-permute-start | bytes 884744 | tf_op jit(solution)/shard_map/ppermute | solution.py:279
  75.4 6.1 %all-to-all-start.1 = ((bf16[16,144,256]{2,1,0:T(8,128)(2,1)}), bf16[16,144,256]{2,1,0:T(8,128)(2,1)S(1)}, u32[]{:S(2)}, u32[]{:S(2)}) async-start(bf16[16,144,256]{2,1,0:T(8,128)(2,1)} %broadcast_in_dim.54), calls=%async_computation.1 | async-start | bytes 2359296 | tf_op jit(solution)/shard_map/all_to_all | solution.py:27
  81.5 3.3 %collective-permute-start.6 = (bf16[4,144,256]{2,1,0:T(8,128)(2,1)S(1)}, bf16[4,144,256]{2,1,0:T(8,128)(2,1)S(1)}, u32[]{:S(2)}, u32[]{:S(2)}) collective-permute-start(bf16[4,144,256]{2,1,0:T(8,128)(2,1)S(1)} %slice.51.own), channel_id=1, source_target_pairs={{96,0},{0,32},{32,64},{64,96},{97,1},{1,33},{33,65},{65,97},{98,2}... | collective-permute-start | bytes 884744 | tf_op jit(solution)/shard_map/ppermute | solution.py:315
  84.8 3.2 %collective-permute-start.5 = (bf16[4,144,256]{2,1,0:T(8,128)(2,1)S(1)}, bf16[4,144,256]{2,1,0:T(8,128)(2,1)S(1)}, u32[]{:S(2)}, u32[]{:S(2)}) collective-permute-start(bf16[4,144,256]{2,1,0:T(8,128)(2,1)S(1)} %slice.51.own), channel_id=1, source_target_pairs={{32,0},{64,32},{96,64},{0,96},{33,1},{65,33},{97,65},{1,97},{34,2}... | collective-permute-start | bytes 884744 | tf_op jit(solution)/shard_map/ppermute | solution.py:314
  88.0 8.9 %collective-permute-start.7 = (bf16[1024,128]{1,0:T(8,128)(2,1)S(1)}, bf16[1024,128]{1,0:T(8,128)(2,1)S(1)}, u32[]{:S(2)}, u32[]{:S(2)}) collective-permute-start(bf16[1024,128]{1,0:T(8,128)(2,1)S(1)} %copy-done), channel_id=1, source_target_pairs={{0,16},{16,0},{1,17},{17,1},{2,18},{18,2},{3,19},{19,3},{4,20},{20... | collective-permute-start | bytes 786440 | tf_op jit(solution)/shard_map/ppermute | solution.py:317
  101.2 8.5 %collective-permute-start.9 = (bf16[2304,128]{1,0:T(8,128)(2,1)S(1)}, bf16[2304,128]{1,0:T(8,128)(2,1)S(1)}, u32[]{:S(2)}, u32[]{:S(2)}) collective-permute-start(bf16[2304,128]{1,0:T(8,128)(2,1)S(1)} %slice.42), channel_id=1, source_target_pairs={{0,16},{16,0},{1,17},{17,1},{2,18},{18,2},{3,19},{19,3},{4,20},{20... | collective-permute-start | bytes 1769480 | tf_op jit(solution)/shard_map/ppermute | solution.py:322
  111.3 5.7 %attend.1 = (bf16[1024,128]{1,0:T(8,128)(2,1)}, bf16[1024,128]{1,0:T(8,128)(2,1)}, bf16[2560,128]{1,0:T(8,128)(2,1)}) custom-call(s32[40]{0:T(128)S(1)} %concatenate.62.meta, bf16[2304,256]{1,0:T(8,128)(2,1)S(1)} %bitcast.22, bf16[2304,128]{1,0:T(8,128)(2,1)S(1)} %collective-permute-done.9.others, bf16[1024,128]{1,0:T(8,128)(2,1)S(1)} %copy-done, ...), custom_call_target="tpu_custom_call" | custom-call | tf_op jit(solution)/shard_map/attend/pallas_call | solution.py:162
  117.0 12.7 %all-to-all-start.2 = ((bf16[16,160,128]{2,1,0:T(8,128)(2,1)}), bf16[16,160,128]{2,1,0:T(8,128)(2,1)S(1)}, u32[]{:S(2)}, u32[]{:S(2)}) async-start(bf16[16,160,128]{2,1,0:T(8,128)(2,1)} %bitcast.12), calls=%async_computation.2 | async-start | bytes 1310720 | tf_op jit(solution)/shard_map/all_to_all | solution.py:332
  129.8 3.3 %collective-permute-start.11 = (bf16[2,144,256]{2,1,0:T(8,128)(2,1)S(1)}, bf16[2,144,256]{2,1,0:T(8,128)(2,1)S(1)}, u32[]{:S(2)}, u32[]{:S(2)}) collective-permute-start(bf16[2,144,256]{2,1,0:T(8,128)(2,1)S(1)} %slice.44), channel_id=1, source_target_pairs={{96,0},{0,32},{32,64},{64,96},{97,1},{1,33},{33,65},{65,97},{98,2}... | collective-permute-start | bytes 442376 | tf_op jit(solution)/shard_map/ppermute | solution.py:327
  133.1 3.2 %collective-permute-start.10 = (bf16[2,144,256]{2,1,0:T(8,128)(2,1)S(1)}, bf16[2,144,256]{2,1,0:T(8,128)(2,1)S(1)}, u32[]{:S(2)}, u32[]{:S(2)}) collective-permute-start(bf16[2,144,256]{2,1,0:T(8,128)(2,1)S(1)} %slice.43), channel_id=1, source_target_pairs={{32,0},{64,32},{96,64},{0,96},{33,1},{65,33},{97,65},{1,97},{34,2}... | collective-permute-start | bytes 442376 | tf_op jit(solution)/shard_map/ppermute | solution.py:326
  136.3 9.0 %all-to-all-done.2.parts = bf16[16,160,128]{2,1,0:T(8,128)(2,1)S(1)} async-done(((bf16[16,160,128]{2,1,0:T(8,128)(2,1)}), bf16[16,160,128]{2,1,0:T(8,128)(2,1)S(1)}, u32[]{:S(2)}, u32[]{:S(2)}) %all-to-all-start.2) | async-done | bytes 655392 | tf_op jit(solution)/shard_map/all_to_all | solution.py:332
  146.0 4.4 %all-gather.1 = bf16[288,128]{1,0:T(8,128)(2,1)S(1)} all-gather(bf16[144,128]{1,0:T(8,128)(2,1)S(1)} %divide.1), channel_id=3, replica_groups=mesh['zh'=4,'x'=4,'c'=2,'y'=8,'zl'=2] {'c'}, dimensions={0}, use_global_device_ids=true | all-gather | bytes 110592 | tf_op jit(solution)/shard_map/all_gather | solution.py:334
  150.4 2.2 %spread.1 = bf16[16,176,128]{2,1,0:T(8,128)(2,1)} custom-call(s32[40]{0:T(128)S(1)} %concatenate.62.meta, bf16[2,144,128]{2,1,0:T(8,128)(2,1)S(1)} %bitcast.25, bf16[4,144,256]{2,1,0:T(8,128)(2,1)S(1)} %slice.51.own, bf16[4,144,256]{2,1,0:T(8,128)(2,1)S(1)} %collective-permute-done.5.right, bf16[2,144,256]{2,1,0:T(8,128)(2,1)S(1)} %collective-permute-done.10.ahead, ...), custom_call_target="tpu_custom_call" | custom-call | tf_op jit(solution)/shard_map/spread/pallas_call | solution.py:237
  152.6 13.6 %all-to-all-start.3 = ((bf16[16,176,128]{2,1,0:T(8,128)(2,1)}), bf16[16,176,128]{2,1,0:T(8,128)(2,1)S(1)}, u32[]{:S(2)}, u32[]{:S(2)}) async-start(bf16[16,176,128]{2,1,0:T(8,128)(2,1)} %spread.1), calls=%async_computation.3 | async-start | bytes 1441792 | tf_op jit(solution)/shard_map/all_to_all | solution.py:336
  166.3 19.5 %all-to-all-done.3 = bf16[16,176,128]{2,1,0:T(8,128)(2,1)S(1)} async-done(((bf16[16,176,128]{2,1,0:T(8,128)(2,1)}), bf16[16,176,128]{2,1,0:T(8,128)(2,1)S(1)}, u32[]{:S(2)}, u32[]{:S(2)}) %all-to-all-start.3) | async-done | bytes 720928 | tf_op jit(solution)/shard_map/all_to_all | solution.py:336
  186.9 6.8 %all-to-all-start.4 = ((f32[32,1,72]{2,1,0:T(1,128)}), f32[32,1,72]{2,1,0:T(1,128)S(1)}, u32[]{:S(2)}, u32[]{:S(2)}) async-start(f32[32,1,72]{2,1,0:T(1,128)} %bitcast.15), calls=%async_computation.4 | async-start | bytes 32768 | tf_op jit(solution)/shard_map/all_to_all | solution.py:342
  195.9 5.5 %all-to-all-done.4 = f32[32,1,72]{2,1,0:T(1,128)S(1)} async-done(((f32[32,1,72]{2,1,0:T(1,128)}), f32[32,1,72]{2,1,0:T(1,128)S(1)}, u32[]{:S(2)}, u32[]{:S(2)}) %all-to-all-start.4) | async-done | bytes 9248 | tf_op jit(solution)/shard_map/all_to_all | solution.py:342
  (84 shorter events, 28.6 us)
Async XLA Ops:
  10.3 42.1 %all-to-all-start = ((bf16[8,144,290]{2,1,0:T(8,128)(2,1)}), bf16[8,144,290]{2,1,0:T(8,128)(2,1)S(1)}, u32[]{:S(2)}, u32[]{:S(2)}) async-start(bf16[8,144,290]{2,1,0:T(8,128)(2,1)} %broadcast_in_dim.29), calls=%async_computation | async-start | bytes 1769472 | tf_op jit(solution)/shard_map/all_to_all | solution.py:27
  22.3 30.0 %copy-start.7 = (s32[12]{0:T(128)S(1)}, s32[12]{0:T(128)}, u32[]{:S(2)}) copy-start(s32[12]{0:T(128)} %param.21) | copy-start | bytes 148
  45.6 24.6 %copy-start.9 = (s32[12]{0:T(128)S(1)}, s32[12]{0:T(128)}, u32[]{:S(2)}) copy-start(s32[12]{0:T(128)} %param.22) | copy-start | bytes 148
  45.6 24.6 %copy-start.10 = (s32[12]{0:T(128)S(1)}, s32[12]{0:T(128)}, u32[]{:S(2)}) copy-start(s32[12]{0:T(128)} %param.23) | copy-start | bytes 148
  45.6 14.6 %collective-permute-start.3 = (bf16[4,288,256]{2,1,0:T(8,128)(2,1)S(1)}, bf16[4,288,256]{2,1,0:T(8,128)(2,1)S(1)}, u32[]{:S(2)}, u32[]{:S(2)}) collective-permute-start(bf16[4,288,256]{2,1,0:T(8,128)(2,1)S(1)} %slice.48.own), channel_id=1, source_target_pairs={{96,0},{0,32},{32,64},{64,96},{97,1},{1,33},{33,65},{65,97},{98,2}... | collective-permute-start | bytes 1769480 | tf_op jit(solution)/shard_map/ppermute | solution.py:278
  48.9 14.0 %collective-permute-start.1 = (bf16[4,288,256]{2,1,0:T(8,128)(2,1)S(1)}, bf16[4,288,256]{2,1,0:T(8,128)(2,1)S(1)}, u32[]{:S(2)}, u32[]{:S(2)}) collective-permute-start(bf16[4,288,256]{2,1,0:T(8,128)(2,1)S(1)} %slice.48.own), channel_id=1, source_target_pairs={{32,0},{64,32},{96,64},{0,96},{33,1},{65,33},{97,65},{1,97},{34,2}... | collective-permute-start | bytes 1769480 | tf_op jit(solution)/shard_map/ppermute | solution.py:277
  52.4 19.8 %collective-permute-start = (bf16[16,72,290]{2,1,0:T(8,128)(2,1)S(1)}, bf16[16,72,290]{2,1,0:T(8,128)(2,1)}, u32[]{:S(2)}, u32[]{:S(2)}) collective-permute-start(bf16[16,72,290]{2,1,0:T(8,128)(2,1)S(1)} %bitcast.23), channel_id=1, source_target_pairs={{0,16},{16,0},{1,17},{17,1},{2,18},{18,2},{3,19},{19,3},{4,20},{20... | collective-permute-start | bytes 2004488 | tf_op jit(solution)/shard_map/ppermute | solution.py:283
  61.0 10.5 %collective-permute-start.4 = (bf16[2,288,256]{2,1,0:T(8,128)(2,1)}, bf16[2,288,256]{2,1,0:T(8,128)(2,1)S(1)}, u32[]{:S(2)}, u32[]{:S(2)}) collective-permute-start(bf16[2,288,256]{2,1,0:T(8,128)(2,1)} %slice.50), channel_id=1, source_target_pairs={{96,0},{0,32},{32,64},{64,96},{97,1},{1,33},{33,65},{65,97},{98,2}... | collective-permute-start | bytes 884744 | tf_op jit(solution)/shard_map/ppermute | solution.py:280
  63.7 8.5 %collective-permute-start.2 = (bf16[2,288,256]{2,1,0:T(8,128)(2,1)}, bf16[2,288,256]{2,1,0:T(8,128)(2,1)S(1)}, u32[]{:S(2)}, u32[]{:S(2)}) collective-permute-start(bf16[2,288,256]{2,1,0:T(8,128)(2,1)} %slice.49), channel_id=1, source_target_pairs={{32,0},{64,32},{96,64},{0,96},{33,1},{65,33},{97,65},{1,97},{34,2}... | collective-permute-start | bytes 884744 | tf_op jit(solution)/shard_map/ppermute | solution.py:279
  75.4 21.6 %copy-start.1 = (bf16[1024,128]{1,0:T(8,128)(2,1)S(1)}, bf16[1024,128]{1,0:T(8,128)(2,1)}, u32[]{:S(2)}) copy-start(bf16[1024,128]{1,0:T(8,128)(2,1)} %v_old.1) | copy-start | bytes 786436
  75.4 25.7 %all-to-all-start.1 = ((bf16[16,144,256]{2,1,0:T(8,128)(2,1)}), bf16[16,144,256]{2,1,0:T(8,128)(2,1)S(1)}, u32[]{:S(2)}, u32[]{:S(2)}) async-start(bf16[16,144,256]{2,1,0:T(8,128)(2,1)} %broadcast_in_dim.54), calls=%async_computation.1 | async-start | bytes 2359296 | tf_op jit(solution)/shard_map/all_to_all | solution.py:27
  81.5 19.6 %collective-permute-start.6 = (bf16[4,144,256]{2,1,0:T(8,128)(2,1)S(1)}, bf16[4,144,256]{2,1,0:T(8,128)(2,1)S(1)}, u32[]{:S(2)}, u32[]{:S(2)}) collective-permute-start(bf16[4,144,256]{2,1,0:T(8,128)(2,1)S(1)} %slice.51.own), channel_id=1, source_target_pairs={{96,0},{0,32},{32,64},{64,96},{97,1},{1,33},{33,65},{65,97},{98,2}... | collective-permute-start | bytes 884744 | tf_op jit(solution)/shard_map/ppermute | solution.py:315
  84.8 16.3 %collective-permute-start.5 = (bf16[4,144,256]{2,1,0:T(8,128)(2,1)S(1)}, bf16[4,144,256]{2,1,0:T(8,128)(2,1)S(1)}, u32[]{:S(2)}, u32[]{:S(2)}) collective-permute-start(bf16[4,144,256]{2,1,0:T(8,128)(2,1)S(1)} %slice.51.own), channel_id=1, source_target_pairs={{32,0},{64,32},{96,64},{0,96},{33,1},{65,33},{97,65},{1,97},{34,2}... | collective-permute-start | bytes 884744 | tf_op jit(solution)/shard_map/ppermute | solution.py:314
  88.0 10.9 %collective-permute-start.7 = (bf16[1024,128]{1,0:T(8,128)(2,1)S(1)}, bf16[1024,128]{1,0:T(8,128)(2,1)S(1)}, u32[]{:S(2)}, u32[]{:S(2)}) collective-permute-start(bf16[1024,128]{1,0:T(8,128)(2,1)S(1)} %copy-done), channel_id=1, source_target_pairs={{0,16},{16,0},{1,17},{17,1},{2,18},{18,2},{3,19},{19,3},{4,20},{20... | collective-permute-start | bytes 786440 | tf_op jit(solution)/shard_map/ppermute | solution.py:317
  97.0 3.4 %collective-permute-start.8 = (bf16[1024,128]{1,0:T(8,128)(2,1)S(1)}, bf16[1024,128]{1,0:T(8,128)(2,1)S(1)}, u32[]{:S(2)}, u32[]{:S(2)}) collective-permute-start(bf16[1024,128]{1,0:T(8,128)(2,1)S(1)} %copy-done.1), channel_id=1, source_target_pairs={{0,16},{16,0},{1,17},{17,1},{2,18},{18,2},{3,19},{19,3},{4,20},{20... | collective-permute-start | bytes 786440 | tf_op jit(solution)/shard_map/ppermute | solution.py:318
  101.2 10.2 %collective-permute-start.9 = (bf16[2304,128]{1,0:T(8,128)(2,1)S(1)}, bf16[2304,128]{1,0:T(8,128)(2,1)S(1)}, u32[]{:S(2)}, u32[]{:S(2)}) collective-permute-start(bf16[2304,128]{1,0:T(8,128)(2,1)S(1)} %slice.42), channel_id=1, source_target_pairs={{0,16},{16,0},{1,17},{17,1},{2,18},{18,2},{3,19},{19,3},{4,20},{20... | collective-permute-start | bytes 1769480 | tf_op jit(solution)/shard_map/ppermute | solution.py:322
  117.0 28.3 %all-to-all-start.2 = ((bf16[16,160,128]{2,1,0:T(8,128)(2,1)}), bf16[16,160,128]{2,1,0:T(8,128)(2,1)S(1)}, u32[]{:S(2)}, u32[]{:S(2)}) async-start(bf16[16,160,128]{2,1,0:T(8,128)(2,1)} %bitcast.12), calls=%async_computation.2 | async-start | bytes 1310720 | tf_op jit(solution)/shard_map/all_to_all | solution.py:332
  129.8 20.6 %collective-permute-start.11 = (bf16[2,144,256]{2,1,0:T(8,128)(2,1)S(1)}, bf16[2,144,256]{2,1,0:T(8,128)(2,1)S(1)}, u32[]{:S(2)}, u32[]{:S(2)}) collective-permute-start(bf16[2,144,256]{2,1,0:T(8,128)(2,1)S(1)} %slice.44), channel_id=1, source_target_pairs={{96,0},{0,32},{32,64},{64,96},{97,1},{1,33},{33,65},{65,97},{98,2}... | collective-permute-start | bytes 442376 | tf_op jit(solution)/shard_map/ppermute | solution.py:327
  133.1 17.3 %collective-permute-start.10 = (bf16[2,144,256]{2,1,0:T(8,128)(2,1)S(1)}, bf16[2,144,256]{2,1,0:T(8,128)(2,1)S(1)}, u32[]{:S(2)}, u32[]{:S(2)}) collective-permute-start(bf16[2,144,256]{2,1,0:T(8,128)(2,1)S(1)} %slice.43), channel_id=1, source_target_pairs={{32,0},{64,32},{96,64},{0,96},{33,1},{65,33},{97,65},{1,97},{34,2}... | collective-permute-start | bytes 442376 | tf_op jit(solution)/shard_map/ppermute | solution.py:326
  152.6 13.6 %copy-start.8 = (bf16[288]{0:T(512)(128)(2,1)S(1)}, bf16[288]{0:T(512)(128)(2,1)}, u32[]{:S(2)}) copy-start(bf16[288]{0:T(512)(128)(2,1)} %param.18) | copy-start | bytes 1732
  152.6 33.2 %all-to-all-start.3 = ((bf16[16,176,128]{2,1,0:T(8,128)(2,1)}), bf16[16,176,128]{2,1,0:T(8,128)(2,1)S(1)}, u32[]{:S(2)}, u32[]{:S(2)}) async-start(bf16[16,176,128]{2,1,0:T(8,128)(2,1)} %spread.1), calls=%async_computation.3 | async-start | bytes 1441792 | tf_op jit(solution)/shard_map/all_to_all | solution.py:336
  166.2 35.2 %copy-start.5 = (bf16[72,288]{1,0:T(8,128)(2,1)S(1)}, bf16[72,288]{1,0:T(8,128)(2,1)}, u32[]{:S(2)}) copy-start(bf16[72,288]{1,0:T(8,128)(2,1)} %param.12) | copy-start | bytes 124420
  186.9 14.5 %all-to-all-start.4 = ((f32[32,1,72]{2,1,0:T(1,128)}), f32[32,1,72]{2,1,0:T(1,128)S(1)}, u32[]{:S(2)}, u32[]{:S(2)}) async-start(f32[32,1,72]{2,1,0:T(1,128)} %bitcast.15), calls=%async_computation.4 | async-start | bytes 32768 | tf_op jit(solution)/shard_map/all_to_all | solution.py:342
  193.7 7.7 %collective-permute-start.12 = (f32[72,144]{1,0:T(8,128)S(1)}, f32[72,144]{1,0:T(8,128)S(1)}, u32[]{:S(2)}, u32[]{:S(2)}) collective-permute-start(f32[72,144]{1,0:T(8,128)S(1)} %fusion.11), channel_id=1, source_target_pairs={{0,16},{16,0},{1,17},{17,1},{2,18},{18,2},{3,19},{19,3},{4,20},{20... | collective-permute-start | bytes 124424 | tf_op jit(solution)/shard_map/ppermute | solution.py:346
  (5 other events, 36.5 us)

commit v8 on v7

--- a/solution.py
+++ b/solution.py
@@ -27,13 +27,13 @@
     return lax.all_to_all(jnp.broadcast_to(value[None], (count,) + value.shape), axes, 0, 0)
 
 
-def project_kernel(meta, mine, others, turns, own, right, ahead, behind, left, out):
+def project_kernel(meta, mine, others, turns, own, right, ahead, behind, left, *outs):
     on_core_0 = meta[3 * REQS + 2] == 0
     here = meta[3 * REQS + 3]
     features = mine.shape[2] - 2
     count = 4
-    total = jnp.zeros(out.shape, F32)
-    squares = jnp.zeros((out.shape[0], 2), F32)
+    total = jnp.zeros((outs[0].shape[0], 2 * HD), F32)
+    squares = jnp.zeros((outs[0].shape[0], 2), F32)
     for step in range(count):
         along = lax.rem(here + step, count)
         for block in range(count):
@@ -51,37 +51,131 @@
     for head in range(2):
         value = total[:, head * HD : (head + 1) * HD]
         value = value * turns[2 * head] + pltpu.roll(value, HD // 2, 1) * turns[2 * head + 1]
-        out[:, head * HD : (head + 1) * HD] = value.astype(BF16)
+        outs[head][...] = value.astype(BF16)
 
 
 def project(meta, mine, others, turns, columns):
     vmem = pl.BlockSpec(memory_space=pltpu.VMEM)
     return pl.pallas_call(
         project_kernel,
-        out_shape=jax.ShapeDtypeStruct((2 * mine.shape[1], columns[0].shape[2]), BF16),
+        out_shape=[jax.ShapeDtypeStruct((2 * mine.shape[1], HD), BF16)] * 2,
         in_specs=[pl.BlockSpec(memory_space=pltpu.SMEM)] + [vmem] * (3 + len(columns)),
-        out_specs=vmem,
+        out_specs=[vmem, vmem],
         compiler_params=pltpu.CompilerParams(vmem_limit_bytes=32 << 20),
         name="project",
     )(meta, mine, others, turns, *columns)
 
 
-def attend_kernel(meta, mine, others, k_old, v_old, k_other, v_other, k_pool, v_pool, sums, keys, values, num, den, totals):
-    own = k_old.shape[0]
-    slots = keys.shape[0]
+def attend_kernel(meta, queries, k_own, v_own, k_other, v_other, sums, num, den, totals):
+    own = k_own.shape[0]
     first = meta[3 * REQS]
     core = meta[3 * REQS + 2]
-    on_core_0 = core == 0
     blocks = REQS * NEWTOK // (3 * PIECE)
     chunk = sums.shape[0] // blocks
-
-    my_slots = pl.ds(pl.multiple_of(core * own, own), own)
-    other_slots = pl.ds(pl.multiple_of((1 - core) * own, own), own)
-    keys[my_slots, :] = k_old[...]
-    keys[other_slots, :] = k_other[...]
-    values[my_slots, :] = v_old[...]
-    values[other_slots, :] = v_other[...]
     totals[...] = jnp.zeros_like(totals)
+
+    def read_request(r, carry):
+        cached, offset = meta[r], meta[2 * REQS + r]
+        num[...] = jnp.zeros_like(num)
+        den[...] = jnp.zeros_like(den)
+        for keys, values, at in ((k_own, v_own, core), (k_other, v_other, 1 - core)):
+            begin = offset - first - at * own
+            low, high = jnp.maximum(begin, 0), jnp.minimum(begin + cached, own)
+
+            def read_tile(t, carry):
+                rows = queries[pl.ds(pl.multiple_of(r * NEWTOK, 64), NEWTOK), :]
+                here = pl.ds(pl.multiple_of(t * READ_TILE, READ_TILE), READ_TILE)
+                logits = lax.dot_general(
+                    rows, keys[here, :], (((1,), (1,)), ((), ())), preferred_element_type=F32
+                )
+                slot = lax.broadcasted_iota(jnp.int32, logits.shape, 1) + t * READ_TILE
+                weight = jnp.exp(soft_cap * jnp.tanh(logits * (1.0 / soft_cap)))
+                weight = jnp.where((slot >= low) & (slot < high), weight, 0.0).astype(BF16)
+                num[...] += jnp.dot(weight, values[here, :], preferred_element_type=F32)
+                den[...] += lax.dot_general(
+                    jnp.ones((8, READ_TILE), BF16), weight, (((1,), (1,)), ((), ())), preferred_element_type=F32
+                )
+                return carry
+
+            tiles = jnp.where(high > low, pl.cdiv(high, READ_TILE), 0)
+            lax.fori_loop(lax.div(low, READ_TILE), tiles, read_tile, 0)
+
+        for piece in range(NEWTOK // PIECE):
+            at = r * (NEWTOK // PIECE) + piece
+            block, part = lax.div(at, 3), lax.rem(at, 3)
+            to = pl.multiple_of(block * chunk + part * PIECE, 16)
+            at_row = piece * PIECE
+            sums[pl.ds(to, PIECE), :] = num[at_row : at_row + PIECE, :].astype(BF16)
+            totals[pl.ds(block * 8 + part, 1), 0:PIECE] = den[0:1, at_row : at_row + PIECE]
+        return carry
+
+    lax.fori_loop(0, REQS, read_request, 0)
+    for block in range(blocks):
+        rows = totals[block * 8 : block * 8 + 8, :]
+        rows = jnp.concatenate([rows, jnp.zeros_like(rows)], axis=0)
+        sums[block * chunk + 3 * PIECE : (block + 1) * chunk, :] = rows.astype(BF16)
+
+
+def attend(meta, queries, k_cache, v_cache, k_other, v_other):
+    blocks = REQS * NEWTOK // (3 * PIECE)
+    chunk = 3 * PIECE + 16
+    vmem = pl.BlockSpec(memory_space=pltpu.VMEM)
+    return pl.pallas_call(
+        attend_kernel,
+        out_shape=jax.ShapeDtypeStruct((blocks * chunk, HD), BF16),
+        in_specs=[pl.BlockSpec(memory_space=pltpu.SMEM)] + [vmem] * 5,
+        out_specs=vmem,
+        scratch_shapes=[
+            pltpu.VMEM((NEWTOK, HD), F32),
+            pltpu.VMEM((8, NEWTOK), F32),
+            pltpu.VMEM((blocks * 8, HD), F32),
+        ],
+        compiler_params=pltpu.CompilerParams(vmem_limit_bytes=32 << 20),
+        name="attend",
+    )(meta, queries, k_cache, v_cache, k_other, v_other)
+
+
+def attend_new_kernel(meta, queries, fresh_rows, num, den):
+    here = meta[3 * REQS + 3]
+    rows, count = queries.shape[0], fresh_rows.shape[0] // 2
+    request = lax.div(meta[3 * REQS + 1] - here * rows, NEWTOK)
+    row = lax.broadcasted_iota(jnp.int32, (rows, 1), 0) + here * rows
+    start, limit = jnp.zeros_like(row), jnp.zeros_like(row)
+    for part in range(count * rows // NEWTOK):
+        at = part * NEWTOK
+        inside = (row >= at) & (row < at + NEWTOK)
+        start = jnp.where(inside, at, start)
+        limit = jnp.where(inside, jnp.minimum(row, at + meta[REQS + request + part] - 1), limit)
+    keys = jnp.concatenate([fresh_rows[2 * step] for step in range(count)], axis=0)
+    values = jnp.concatenate([fresh_rows[2 * step + 1] for step in range(count)], axis=0)
+    logits = lax.dot_general(queries[...], keys, (((1,), (1,)), ((), ())), preferred_element_type=F32)
+    column = lax.broadcasted_iota(jnp.int32, logits.shape, 1)
+    weight = jnp.exp(soft_cap * jnp.tanh(logits * (1.0 / soft_cap)))
+    weight = jnp.where((column >= start) & (column <= limit), weight, 0.0)
+    den[...] = jnp.sum(weight, axis=1, keepdims=True)
+    num[...] = jnp.dot(weight.astype(BF16), values, preferred_element_type=F32)
+
+
+def attend_new(meta, queries, fresh_rows):
+    vmem = pl.BlockSpec(memory_space=pltpu.VMEM)
+    rows = queries.shape[0]
+    return pl.pallas_call(
+        attend_new_kernel,
+        out_shape=(jax.ShapeDtypeStruct((rows, HD), F32), jax.ShapeDtypeStruct((rows, 1), F32)),
+        in_specs=[pl.BlockSpec(memory_space=pltpu.SMEM), vmem, vmem],
+        out_specs=(vmem, vmem),
+        compiler_params=pltpu.CompilerParams(vmem_limit_bytes=16 << 20),
+        name="attend_new",
+    )(meta, queries, fresh_rows)
+
+
+def write_kernel(meta, mine, others, k_old, v_old, k_pool, v_pool):
+    slots = k_old.shape[0]
+    core = meta[3 * REQS + 2]
+    on_core_0 = core == 0
+    first = meta[3 * REQS] + core * slots
+    k_pool[...] = k_old[...]
+    v_pool[...] = v_old[...]
 
     def write_request(r, carry):
         cached, fresh, offset = meta[r], meta[REQS + r], meta[2 * REQS + r]
@@ -89,7 +183,7 @@
 
         def write_tile(t, carry):
             rows = pl.ds(pl.multiple_of(r * NEWTOK, 64), NEWTOK)
-            a, b = mine[rows, HD:], others[rows, :]
+            a, b = mine[rows, :], others[rows, :]
             rows = jnp.concatenate([jnp.where(on_core_0, a, b), jnp.where(on_core_0, b, a)], axis=1)
             slot = lax.broadcasted_iota(jnp.int32, (WRITE_TILE, NEWTOK), 0) + (t * WRITE_TILE - begin)
             index = lax.broadcasted_iota(jnp.int32, (WRITE_TILE, NEWTOK), 1)
@@ -98,8 +192,8 @@
             place = lax.broadcasted_iota(jnp.int32, (WRITE_TILE, HD), 0) + (t * WRITE_TILE - begin)
             written = (place >= 0) & (place < fresh)
             here = pl.ds(pl.multiple_of(t * WRITE_TILE, WRITE_TILE), WRITE_TILE)
-            keys[here, :] = jnp.where(written, new[:, :HD], keys[here, :].astype(F32)).astype(BF16)
-            values[here, :] = jnp.where(written, new[:, HD:], values[here, :].astype(F32)).astype(BF16)
+            k_pool[here, :] = jnp.where(written, new[:, :HD], k_pool[here, :].astype(F32)).astype(BF16)
+            v_pool[here, :] = jnp.where(written, new[:, HD:], v_pool[here, :].astype(F32)).astype(BF16)
             return carry
 
         low, high = jnp.maximum(begin, 0), jnp.minimum(begin + fresh, slots)
@@ -108,79 +202,24 @@
         return carry
 
     lax.fori_loop(0, REQS, write_request, 0)
-    k_pool[...] = keys[my_slots, :]
-    v_pool[...] = values[my_slots, :]
-
-    def read_request(r, carry):
-        cached, fresh, offset = meta[r], meta[REQS + r], meta[2 * REQS + r]
-        begin = offset - first
-        end = begin + cached + fresh
-        num[...] = jnp.zeros_like(num)
-        den[...] = jnp.zeros_like(den)
-
-        def read_tile(t, carry):
-            rows = mine[pl.ds(pl.multiple_of(r * NEWTOK, 64), NEWTOK), :HD]
-            row = lax.broadcasted_iota(jnp.int32, (NEWTOK, 1), 0)
-            last = cached + jnp.minimum(row, fresh - 1) + begin
-            here = pl.ds(pl.multiple_of(t * READ_TILE, READ_TILE), READ_TILE)
-            logits = lax.dot_general(rows, keys[here, :], (((1,), (1,)), ((), ())), preferred_element_type=F32)
-            slot = lax.broadcasted_iota(jnp.int32, logits.shape, 1) + t * READ_TILE
-            visible = (slot >= begin) & (slot <= last)
-            weight = jnp.exp(soft_cap * jnp.tanh(logits * (1.0 / soft_cap)))
-            weight = jnp.where(visible, weight, 0.0).astype(BF16)
-            num[...] += jnp.dot(weight, values[here, :], preferred_element_type=F32)
-            den[...] += lax.dot_general(
-                jnp.ones((8, READ_TILE), BF16), weight, (((1,), (1,)), ((), ())), preferred_element_type=F32
-            )
-            return carry
-
-        low, high = jnp.maximum(begin, 0), jnp.minimum(end, slots)
-        tiles = jnp.where(high > low, pl.cdiv(high, READ_TILE), 0)
-        lax.fori_loop(lax.div(low, READ_TILE), tiles, read_tile, 0)
-
-        for piece in range(NEWTOK // PIECE):
-            at = r * (NEWTOK // PIECE) + piece
-            block, part = lax.div(at, 3), lax.rem(at, 3)
-            to = pl.multiple_of(block * chunk + part * PIECE, 16)
-            at_row = piece * PIECE
-            sums[pl.ds(to, PIECE), :] = num[at_row : at_row + PIECE, :].astype(BF16)
-            totals[pl.ds(block * 8 + part, 1), 0:PIECE] = den[0:1, at_row : at_row + PIECE]
-        return carry
-
-    lax.fori_loop(0, REQS, read_request, 0)
-    for block in range(blocks):
-        rows = totals[block * 8 : block * 8 + 8, :]
-        rows = jnp.concatenate([rows, jnp.zeros_like(rows)], axis=0)
-        sums[block * chunk + 3 * PIECE : (block + 1) * chunk, :] = rows.astype(BF16)
-
-
-def attend(meta, mine, others, k_cache, v_cache, k_other, v_other):
-    blocks = REQS * NEWTOK // (3 * PIECE)
-    chunk = 3 * PIECE + 16
-    vmem = pl.BlockSpec(memory_space=pltpu.VMEM)
-    slots = 2 * k_cache.shape[0]
-    return pl.pallas_call(
-        attend_kernel,
+
+
+def write(meta, mine, others, k_cache, v_cache):
+    vmem = pl.BlockSpec(memory_space=pltpu.VMEM)
+    return pl.pallas_call(
+        write_kernel,
         out_shape=(
             jax.ShapeDtypeStruct(k_cache.shape, BF16),
             jax.ShapeDtypeStruct(v_cache.shape, BF16),
-            jax.ShapeDtypeStruct((blocks * chunk, HD), BF16),
         ),
-        in_specs=[pl.BlockSpec(memory_space=pltpu.SMEM)] + [vmem] * 6,
-        out_specs=(vmem, vmem, vmem),
-        scratch_shapes=[
-            pltpu.VMEM((slots, HD), BF16),
-            pltpu.VMEM((slots, HD), BF16),
-            pltpu.VMEM((NEWTOK, HD), F32),
-            pltpu.VMEM((8, NEWTOK), F32),
-            pltpu.VMEM((blocks * 8, HD), F32),
-        ],
+        in_specs=[pl.BlockSpec(memory_space=pltpu.SMEM)] + [vmem] * 4,
+        out_specs=(vmem, vmem),
         compiler_params=pltpu.CompilerParams(vmem_limit_bytes=32 << 20),
-        name="attend",
-    )(meta, mine, others, k_cache, v_cache, k_other, v_other)
-
-
-def divide_kernel(meta, parts, out):
+        name="write",
+    )(meta, mine, others, k_cache, v_cache)
+
+
+def divide_kernel(meta, parts, new_num, new_den, out):
     fresh_at = REQS
     begin = meta[3 * REQS + 1]
     total = jnp.sum(parts[...].astype(F32), axis=0)
@@ -193,21 +232,22 @@
         diagonal = lax.broadcasted_iota(jnp.int32, (PIECE, PIECE), 0) == lax.broadcasted_iota(
             jnp.int32, (PIECE, PIECE), 1
         )
-        den = jnp.sum(jnp.where(diagonal, den, 0.0), axis=1, keepdims=True)
-        value = total[part * PIECE : (part + 1) * PIECE, :] / den
-        out[part * PIECE : (part + 1) * PIECE, :] = jnp.where(within < fresh, value, 0.0).astype(BF16)
-
-
-def divide(meta, parts):
+        here = slice(part * PIECE, (part + 1) * PIECE)
+        den = jnp.sum(jnp.where(diagonal, den, 0.0), axis=1, keepdims=True) + new_den[here, :]
+        value = (total[here, :] + new_num[here, :]) / den
+        out[here, :] = jnp.where(within < fresh, value, 0.0).astype(BF16)
+
+
+def divide(meta, parts, new_num, new_den):
     vmem = pl.BlockSpec(memory_space=pltpu.VMEM)
     return pl.pallas_call(
         divide_kernel,
         out_shape=jax.ShapeDtypeStruct((3 * PIECE, HD), BF16),
-        in_specs=[pl.BlockSpec(memory_space=pltpu.SMEM), vmem],
+        in_specs=[pl.BlockSpec(memory_space=pltpu.SMEM), vmem, vmem, vmem],
         out_specs=vmem,
         compiler_params=pltpu.CompilerParams(vmem_limit_bytes=16 << 20),
         name="divide",
-    )(meta, parts)
+    )(meta, parts, new_num, new_den)
 
 
 def spread_kernel(meta, attended, own, right, ahead, behind, left, out):
@@ -309,17 +349,19 @@
             jnp.stack([me // 2 * (2 * k_cache.shape[0]), chip_rows, core, lax.axis_index("x")]).astype(jnp.int32),
         ]
     )
-    mine = project(meta, gained, other, turns, columns)
-    mine, w_out = lax.optimization_barrier((mine, w_out))
+    k_other = lax.ppermute(k_cache, "c", swap)
+    v_other = lax.ppermute(v_cache, "c", swap)
+    other, k_other, v_other = lax.optimization_barrier((other, k_other, v_other))
+    queries, fresh_rows = project(meta, gained, other, turns, columns)
+
+    queries, fresh_rows, w_out = lax.optimization_barrier((queries, fresh_rows, w_out))
     out_right = lax.ppermute(w_out, "x", from_right)
     out_left = lax.ppermute(w_out, "x", from_left)
-    mine = everywhere(mine, CHIPS, n_chips).reshape(-1, cols)
-    k_other = lax.ppermute(k_cache, "c", swap)
-    v_other = lax.ppermute(v_cache, "c", swap)
-    mine, out_right, out_left, k_other, v_other = lax.optimization_barrier(
-        (mine, out_right, out_left, k_other, v_other)
+    near_rows = lax.all_gather(fresh_rows, ("x", "c"), axis=0)
+    all_queries = everywhere(queries, CHIPS, n_chips).reshape(-1, HD)
+    all_queries, near_rows, out_right, out_left = lax.optimization_barrier(
+        (all_queries, near_rows, out_right, out_left)
     )
-    others = lax.ppermute(mine[:, HD:], "c", swap)
     out_columns = [
         w_out,
         out_right,
@@ -328,11 +370,16 @@
         out_left,
     ]
 
-    k_pool, v_pool, sums = attend(meta, mine, others, k_cache, v_cache, k_other, v_other)
+    sums = attend(meta, all_queries, k_cache, v_cache, k_other, v_other)
+    sums, near_rows = lax.optimization_barrier((sums, near_rows))
     parts = lax.all_to_all(sums.reshape(n_chips, -1, HD), CHIPS, 0, 0)
-    attended = divide(meta, parts)
+    attended = divide(meta, parts, *attend_new(meta, queries, near_rows))
     attended = lax.all_gather(attended, "c", axis=0)
     partial_out = spread(meta, attended, out_columns, n_gy)
+    partial_out, near_rows = lax.optimization_barrier((partial_out, near_rows))
+    kind = lax.dynamic_index_in_dim(near_rows.reshape(4, 2, 2 * tok_rows, HD), core, 1, keepdims=False)
+    kind = lax.all_gather(kind.reshape(-1, HD), "zh", axis=0, tiled=True)
+    k_pool, v_pool = write(meta, kind, lax.ppermute(kind, "c", swap), k_cache, v_cache)
     total = jnp.sum(lax.all_to_all(partial_out, GY, 0, 0).astype(F32), axis=0)
     rows = 2 * tok_rows
     rest = jnp.concatenate([total[rows : rows + 16], total[rows + 16 :, : rows - HD]], axis=1)

time: 203 us -> 207 us (1.020)
  blocking collectives: 36.9 us -> 77.3 us
  waiting for transfers between devices: 39.8 us -> 15.9 us
  starting transfers between devices: 99.7 us -> 84.5 us
  Pallas kernels: 10.6 us -> 13.6 us
    all_gather x0 -> x2, blocking collectives: none -> 40.9 us  [the longest x1 21.9 us: on_device(): kind = lax.all_gather(kind.reshape(-1, HD), 'zh', axis=0, tiled=True)]
    all_to_all x1, waiting for transfers between devices: 19.5 us -> 0.01 us  [on_device(): total = jnp.sum(lax.all_to_all(partial_out, GY, 0, 0).astype(F32), axis=0)]
    all_to_all x1, starting transfers between devices: 12.7 us -> 6.06 us  [on_device(): parts = lax.all_to_all(sums.reshape(n_chips, -1, HD), CHIPS, 0, 0)]
    ppermute x1, starting transfers between devices: 8.54 us -> 2.96 us  [on_device(): lax.ppermute(kind, 'c', swap)]
    ppermute x1, starting transfers between devices: 5.88 us -> 2.41 us  [on_device(): other = lax.ppermute(gained, 'c', swap)]
    ppermute x1, starting transfers between devices: 8.94 us -> 5.88 us  [on_device(): k_other = lax.ppermute(k_cache, 'c', swap)]
    pallas_call x2 -> x4, Pallas kernels: 7.76 us -> 10.7 us  [the longest x1 5.5 us: attend(): pl.pallas_call(attend_kernel, out_shape=jax.ShapeDtypeStruct((blocks * ch...]
    all_to_all x1, starting transfers between devices: 6.79 us -> 9.54 us  [on_device(): squares = lax.all_to_all(squares, ('c',) + GY, 0, 0)]
  transfers between devices with their start and end apart: 18 -> 18, of which waited for: 7 -> 4; matrix products, arithmetic and copies ran while one was open for 2% -> 3% of each run, Pallas kernels for 0% -> 2%
where the time goes in v8:
time: 207 us; the launch traced here: 205 us
  starting transfers between devices  84.5 us (41%)
  blocking collectives  77.3 us (37%)
  waiting for transfers between devices  15.9 us (8%)
  Pallas kernels  13.6 us (7%)
  local copies, waits for them, and re-layouts  7.12 us (3%)
  other arithmetic  5.76 us (3%)
    all_gather x1, blocking collectives, on_device(): weights = lax.all_gather(weights, 'zh', axis=0)  22.5 us
    all_gather x1, blocking collectives, on_device(): kind = lax.all_gather(kind.reshape(-1, HD), 'zh', axis=0, tiled=True)  21.9 us
    all_gather x1, blocking collectives, on_device(): near_rows = lax.all_gather(fresh_rows, ('x', 'c'), axis=0)  19 us
    all_to_all x2, starting transfers between devices, everywhere(): lax.all_to_all(jnp.broadcast_to(value[None], (count,) + value.shape), axe...  15 us
    all_to_all x1, starting transfers between devices, on_device(): total = jnp.sum(lax.all_to_all(partial_out, GY, 0, 0).astype(F32), axis=0)  12.7 us
    all_to_all x1, starting transfers between devices, on_device(): squares = lax.all_to_all(squares, ('c',) + GY, 0, 0)  9.54 us
    all_to_all x1, waiting for transfers between devices, on_device(): parts = lax.all_to_all(sums.reshape(n_chips, -1, HD), CHIPS, 0, 0)  8.14 us
    all_to_all x1, starting transfers between devices, on_device(): parts = lax.all_to_all(sums.reshape(n_chips, -1, HD), CHIPS, 0, 0)  6.06 us
  transfers between devices with their start and end apart: 18, of which 4 were waited for; matrix products, arithmetic and copies ran while one was open for 3% of the time, Pallas kernels for 2%

profile of v8, /device:TPU:1, one launch (start us, length us, event | category | flops | bytes accessed | tf_op | source)
XLA Modules:
  0.0 205.4 jit_solution(1551322782970377713)
XLA Ops:
  4.2 5.1 %all_gather.27 = bf16[144,290]{1,0:T(8,128)(2,1)S(1)} all-gather(bf16[72,290]{1,0:T(8,128)(2,1)S(1)} %pad_maximum_fusion.6), channel_id=1, replica_groups=mesh['zh'=4,'x'=4,'c'=2,'y'=8,'zl'=2] {'zl'}, dimensions={0}, use_global_device_ids=true | all-gather | bytes 125280 | tf_op jit(solution)/shard_map/all_gather | solution.py:305
  10.3 7.0 %all-to-all-start = ((bf16[8,144,290]{2,1,0:T(8,128)(2,1)}), bf16[8,144,290]{2,1,0:T(8,128)(2,1)S(1)}, u32[]{:S(2)}, u32[]{:S(2)}) async-start(bf16[8,144,290]{2,1,0:T(8,128)(2,1)} %broadcast_in_dim.29), calls=%async_computation | async-start | bytes 1769472 | tf_op jit(solution)/shard_map/all_to_all | solution.py:27
  17.3 5.0 %all_gather.28 = bf16[288,512]{1,0:T(8,128)(2,1)S(1)} all-gather(bf16[144,512]{1,0:T(8,128)(2,1)S(1)} %pad_maximum_fusion.3), channel_id=1, replica_groups=mesh['zh'=4,'x'=4,'c'=2,'y'=8,'zl'=2] {'c'}, dimensions={0}, use_global_device_ids=true | all-gather | bytes 442368 | tf_op jit(solution)/shard_map/all_gather | solution.py:308
  22.3 22.5 %all-gather = bf16[1728,256]{1,0:T(8,128)(2,1)S(1)} all-gather(bf16[432,256]{1,0:T(8,128)(2,1)S(1)} %pad_maximum_fusion.1), channel_id=2, replica_groups=mesh['zh'=4,'x'=4,'c'=2,'y'=8,'zl'=2] {'zh'}, dimensions={0}, use_global_device_ids=true | all-gather | bytes 1105920 | tf_op jit(solution)/shard_map/all_gather | solution.py:312
  44.9 3.1 %collective-permute-start.5 = (bf16[4,288,256]{2,1,0:T(8,128)(2,1)S(1)}, bf16[4,288,256]{2,1,0:T(8,128)(2,1)S(1)}, u32[]{:S(2)}, u32[]{:S(2)}) collective-permute-start(bf16[4,288,256]{2,1,0:T(8,128)(2,1)S(1)} %slice.44.own), channel_id=1, source_target_pairs={{96,0},{0,32},{32,64},{64,96},{97,1},{1,33},{33,65},{65,97},{98,2}... | collective-permute-start | bytes 1769480 | tf_op jit(solution)/shard_map/ppermute | solution.py:318
  48.0 3.4 %collective-permute-start.3 = (bf16[4,288,256]{2,1,0:T(8,128)(2,1)S(1)}, bf16[4,288,256]{2,1,0:T(8,128)(2,1)S(1)}, u32[]{:S(2)}, u32[]{:S(2)}) collective-permute-start(bf16[4,288,256]{2,1,0:T(8,128)(2,1)S(1)} %slice.44.own), channel_id=1, source_target_pairs={{32,0},{64,32},{96,64},{0,96},{33,1},{65,33},{97,65},{1,97},{34,2}... | collective-permute-start | bytes 1769480 | tf_op jit(solution)/shard_map/ppermute | solution.py:317
  51.4 5.9 %collective-permute-start.1 = (bf16[1024,128]{1,0:T(8,128)(2,1)S(1)}, bf16[1024,128]{1,0:T(8,128)(2,1)}, u32[]{:S(2)}, u32[]{:S(2)}) collective-permute-start(bf16[1024,128]{1,0:T(8,128)(2,1)S(1)} %copy-done), channel_id=1, source_target_pairs={{0,16},{16,0},{1,17},{17,1},{2,18},{18,2},{3,19},{19,3},{4,20},{20... | collective-permute-start | bytes 786440 | tf_op jit(solution)/shard_map/ppermute | solution.py:352
  59.4 2.4 %collective-permute-start = (bf16[16,72,290]{2,1,0:T(8,128)(2,1)S(1)}, bf16[16,72,290]{2,1,0:T(8,128)(2,1)}, u32[]{:S(2)}, u32[]{:S(2)}) collective-permute-start(bf16[16,72,290]{2,1,0:T(8,128)(2,1)S(1)} %bitcast.26), channel_id=1, source_target_pairs={{0,16},{16,0},{1,17},{17,1},{2,18},{18,2},{3,19},{19,3},{4,20},{20... | collective-permute-start | bytes 2004488 | tf_op jit(solution)/shard_map/ppermute | solution.py:323
  65.3 4.6 %collective-permute-start.4 = (bf16[2,288,256]{2,1,0:T(8,128)(2,1)}, bf16[2,288,256]{2,1,0:T(8,128)(2,1)}, u32[]{:S(2)}, u32[]{:S(2)}) collective-permute-start(bf16[2,288,256]{2,1,0:T(8,128)(2,1)} %slice.45), channel_id=1, source_target_pairs={{32,0},{64,32},{96,64},{0,96},{33,1},{65,33},{97,65},{1,97},{34,2}... | collective-permute-start | bytes 884744 | tf_op jit(solution)/shard_map/ppermute | solution.py:319
  77.4 8.0 %all-to-all-start.1 = ((bf16[16,144,128]{2,1,0:T(8,128)(2,1)}), bf16[16,144,128]{2,1,0:T(8,128)(2,1)S(1)}, u32[]{:S(2)}, u32[]{:S(2)}) async-start(bf16[16,144,128]{2,1,0:T(8,128)(2,1)} %broadcast_in_dim.54), calls=%async_computation.1 | async-start | bytes 1179648 | tf_op jit(solution)/shard_map/all_to_all | solution.py:27
  85.4 3.3 %collective-permute-start.8 = (bf16[4,144,256]{2,1,0:T(8,128)(2,1)S(1)}, bf16[4,144,256]{2,1,0:T(8,128)(2,1)S(1)}, u32[]{:S(2)}, u32[]{:S(2)}) collective-permute-start(bf16[4,144,256]{2,1,0:T(8,128)(2,1)S(1)} %slice.47.own), channel_id=1, source_target_pairs={{96,0},{0,32},{32,64},{64,96},{97,1},{1,33},{33,65},{65,97},{98,2}... | collective-permute-start | bytes 884744 | tf_op jit(solution)/shard_map/ppermute | solution.py:359
  88.7 3.2 %collective-permute-start.7 = (bf16[4,144,256]{2,1,0:T(8,128)(2,1)S(1)}, bf16[4,144,256]{2,1,0:T(8,128)(2,1)S(1)}, u32[]{:S(2)}, u32[]{:S(2)}) collective-permute-start(bf16[4,144,256]{2,1,0:T(8,128)(2,1)S(1)} %slice.47.own), channel_id=1, source_target_pairs={{32,0},{64,32},{96,64},{0,96},{33,1},{65,33},{97,65},{1,97},{34,2}... | collective-permute-start | bytes 884744 | tf_op jit(solution)/shard_map/ppermute | solution.py:358
  91.9 19.0 %all-gather.1 = bf16[1152,128]{1,0:T(8,128)(2,1)S(1)} all-gather(bf16[144,128]{1,0:T(8,128)(2,1)S(1)} %get-tuple-element.31), channel_id=3, replica_groups=mesh['zh'=4,'x'=4,'c'=2,'y'=8,'zl'=2] {'x','c'}, dimensions={0}, use_global_device_ids=true | all-gather | bytes 331776 | tf_op jit(solution)/shard_map/all_gather | solution.py:360
  111.0 5.5 %attend.1 = bf16[2560,128]{1,0:T(8,128)(2,1)} custom-call(s32[40]{0:T(128)S(1)} %concatenate.62.meta, bf16[2304,128]{1,0:T(8,128)(2,1)S(1)} %bitcast.28, bf16[1024,128]{1,0:T(8,128)(2,1)S(1)} %copy-done, bf16[1024,128]{1,0:T(8,128)(2,1)S(1)} %copy-done.1, bf16[1024,128]{1,0:T(8,128)(2,1)} %collective-permute-done.1.k_other, ...), custom_call_target="tpu_custom_call" | custom-call | tf_op jit(solution)/shard_map/attend/pallas_call | solution.py:123
  116.5 6.1 %all-to-all-start.2 = ((bf16[16,160,128]{2,1,0:T(8,128)(2,1)}), bf16[16,160,128]{2,1,0:T(8,128)(2,1)S(1)}, u32[]{:S(2)}, u32[]{:S(2)}) async-start(bf16[16,160,128]{2,1,0:T(8,128)(2,1)} %bitcast.13), calls=%async_computation.2 | async-start | bytes 1310720 | tf_op jit(solution)/shard_map/all_to_all | solution.py:375
  122.6 3.3 %collective-permute-start.10 = (bf16[2,144,256]{2,1,0:T(8,128)(2,1)S(1)}, bf16[2,144,256]{2,1,0:T(8,128)(2,1)S(1)}, u32[]{:S(2)}, u32[]{:S(2)}) collective-permute-start(bf16[2,144,256]{2,1,0:T(8,128)(2,1)S(1)} %slice.40), channel_id=1, source_target_pairs={{96,0},{0,32},{32,64},{64,96},{97,1},{1,33},{33,65},{65,97},{98,2}... | collective-permute-start | bytes 442376 | tf_op jit(solution)/shard_map/ppermute | solution.py:369
  125.8 3.2 %collective-permute-start.9 = (bf16[2,144,256]{2,1,0:T(8,128)(2,1)S(1)}, bf16[2,144,256]{2,1,0:T(8,128)(2,1)S(1)}, u32[]{:S(2)}, u32[]{:S(2)}) collective-permute-start(bf16[2,144,256]{2,1,0:T(8,128)(2,1)S(1)} %slice.39), channel_id=1, source_target_pairs={{32,0},{64,32},{96,64},{0,96},{33,1},{65,33},{97,65},{1,97},{34,2}... | collective-permute-start | bytes 442376 | tf_op jit(solution)/shard_map/ppermute | solution.py:368
  130.1 8.1 %all-to-all-done.2.parts = bf16[16,160,128]{2,1,0:T(8,128)(2,1)S(1)} async-done(((bf16[16,160,128]{2,1,0:T(8,128)(2,1)}), bf16[16,160,128]{2,1,0:T(8,128)(2,1)S(1)}, u32[]{:S(2)}, u32[]{:S(2)}) %all-to-all-start.2) | async-done | bytes 655392 | tf_op jit(solution)/shard_map/all_to_all | solution.py:375
  139.0 3.9 %all-gather.2 = bf16[288,128]{1,0:T(8,128)(2,1)S(1)} all-gather(bf16[144,128]{1,0:T(8,128)(2,1)S(1)} %divide.1), channel_id=4, replica_groups=mesh['zh'=4,'x'=4,'c'=2,'y'=8,'zl'=2] {'c'}, dimensions={0}, use_global_device_ids=true | all-gather | bytes 110592 | tf_op jit(solution)/shard_map/all_gather | solution.py:377
  145.0 12.7 %all-to-all-start.3 = ((bf16[16,176,128]{2,1,0:T(8,128)(2,1)}), bf16[16,176,128]{2,1,0:T(8,128)(2,1)S(1)}, u32[]{:S(2)}, u32[]{:S(2)}) async-start(bf16[16,176,128]{2,1,0:T(8,128)(2,1)} %spread.1), calls=%async_computation.3 | async-start | bytes 1441792 | tf_op jit(solution)/shard_map/all_to_all | solution.py:383
  157.8 21.9 %all_gather.35.mine = bf16[2304,128]{1,0:T(8,128)(2,1)S(1)} all-gather(bf16[576,128]{1,0:T(8,128)(2,1)S(1)} %bitcast.37), channel_id=1, replica_groups=mesh['zh'=4,'x'=4,'c'=2,'y'=8,'zl'=2] {'zh'}, dimensions={0}, use_global_device_ids=true | all-gather | bytes 737280 | tf_op jit(solution)/shard_map/all_gather | solution.py:381
  179.6 3.0 %collective-permute-start.12 = (bf16[2304,128]{1,0:T(8,128)(2,1)S(1)}, bf16[2304,128]{1,0:T(8,128)(2,1)S(1)}, u32[]{:S(2)}, u32[]{:S(2)}) collective-permute-start(bf16[2304,128]{1,0:T(8,128)(2,1)S(1)} %all_gather.35.mine), channel_id=1, source_target_pairs={{0,16},{16,0},{1,17},{17,1},{2,18},{18,2},{3,19},{19,3},{4,20},{20... | collective-permute-start | bytes 1769480 | tf_op jit(solution)/shard_map/ppermute | solution.py:382
  187.3 9.5 %all-to-all-start.4 = ((f32[32,1,72]{2,1,0:T(1,128)}), f32[32,1,72]{2,1,0:T(1,128)S(1)}, u32[]{:S(2)}, u32[]{:S(2)}) async-start(f32[32,1,72]{2,1,0:T(1,128)} %bitcast.16), calls=%async_computation.4 | async-start | bytes 32768 | tf_op jit(solution)/shard_map/all_to_all | solution.py:389
  199.0 5.6 %all-to-all-done.4 = f32[32,1,72]{2,1,0:T(1,128)S(1)} async-done(((f32[32,1,72]{2,1,0:T(1,128)}), f32[32,1,72]{2,1,0:T(1,128)S(1)}, u32[]{:S(2)}, u32[]{:S(2)}) %all-to-all-start.4) | async-done | bytes 9248 | tf_op jit(solution)/shard_map/all_to_all | solution.py:389
  (80 shorter events, 29.2 us)
Async XLA Ops:
  10.3 12.0 %copy-start.4 = (bf16[256,144]{0,1:T(8,128)(2,1)S(1)}, bf16[256,144]{0,1:T(8,128)(2,1)}, u32[]{:S(2)}) copy-start(bf16[256,144]{0,1:T(8,128)(2,1)} %param.17) | copy-start | bytes 221188
  10.3 49.1 %all-to-all-start = ((bf16[8,144,290]{2,1,0:T(8,128)(2,1)}), bf16[8,144,290]{2,1,0:T(8,128)(2,1)S(1)}, u32[]{:S(2)}, u32[]{:S(2)}) async-start(bf16[8,144,290]{2,1,0:T(8,128)(2,1)} %broadcast_in_dim.29), calls=%async_computation | async-start | bytes 1769472 | tf_op jit(solution)/shard_map/all_to_all | solution.py:27
  22.3 29.1 %copy-start = (bf16[1024,128]{1,0:T(8,128)(2,1)S(1)}, bf16[1024,128]{1,0:T(8,128)(2,1)}, u32[]{:S(2)}) copy-start(bf16[1024,128]{1,0:T(8,128)(2,1)} %k_old.1) | copy-start | bytes 786436
  22.3 35.0 %copy-start.1 = (bf16[1024,128]{1,0:T(8,128)(2,1)S(1)}, bf16[1024,128]{1,0:T(8,128)(2,1)}, u32[]{:S(2)}) copy-start(bf16[1024,128]{1,0:T(8,128)(2,1)} %v_old.1) | copy-start | bytes 786436
  44.8 14.5 %copy-start.5 = (s32[12]{0:T(128)S(1)}, s32[12]{0:T(128)}, u32[]{:S(2)}) copy-start(s32[12]{0:T(128)} %param.21) | copy-start | bytes 148
  44.9 17.0 %collective-permute-start.5 = (bf16[4,288,256]{2,1,0:T(8,128)(2,1)S(1)}, bf16[4,288,256]{2,1,0:T(8,128)(2,1)S(1)}, u32[]{:S(2)}, u32[]{:S(2)}) collective-permute-start(bf16[4,288,256]{2,1,0:T(8,128)(2,1)S(1)} %slice.44.own), channel_id=1, source_target_pairs={{96,0},{0,32},{32,64},{64,96},{97,1},{1,33},{33,65},{65,97},{98,2}... | collective-permute-start | bytes 1769480 | tf_op jit(solution)/shard_map/ppermute | solution.py:318
  48.0 16.5 %collective-permute-start.3 = (bf16[4,288,256]{2,1,0:T(8,128)(2,1)S(1)}, bf16[4,288,256]{2,1,0:T(8,128)(2,1)S(1)}, u32[]{:S(2)}, u32[]{:S(2)}) collective-permute-start(bf16[4,288,256]{2,1,0:T(8,128)(2,1)S(1)} %slice.44.own), channel_id=1, source_target_pairs={{32,0},{64,32},{96,64},{0,96},{33,1},{65,33},{97,65},{1,97},{34,2}... | collective-permute-start | bytes 1769480 | tf_op jit(solution)/shard_map/ppermute | solution.py:317
  51.4 22.3 %collective-permute-start.1 = (bf16[1024,128]{1,0:T(8,128)(2,1)S(1)}, bf16[1024,128]{1,0:T(8,128)(2,1)}, u32[]{:S(2)}, u32[]{:S(2)}) collective-permute-start(bf16[1024,128]{1,0:T(8,128)(2,1)S(1)} %copy-done), channel_id=1, source_target_pairs={{0,16},{16,0},{1,17},{17,1},{2,18},{18,2},{3,19},{19,3},{4,20},{20... | collective-permute-start | bytes 786440 | tf_op jit(solution)/shard_map/ppermute | solution.py:352
  57.3 16.4 %collective-permute-start.2 = (bf16[1024,128]{1,0:T(8,128)(2,1)S(1)}, bf16[1024,128]{1,0:T(8,128)(2,1)}, u32[]{:S(2)}, u32[]{:S(2)}) collective-permute-start(bf16[1024,128]{1,0:T(8,128)(2,1)S(1)} %copy-done.1), channel_id=1, source_target_pairs={{0,16},{16,0},{1,17},{17,1},{2,18},{18,2},{3,19},{19,3},{4,20},{20... | collective-permute-start | bytes 786440 | tf_op jit(solution)/shard_map/ppermute | solution.py:353
  59.4 14.3 %collective-permute-start = (bf16[16,72,290]{2,1,0:T(8,128)(2,1)S(1)}, bf16[16,72,290]{2,1,0:T(8,128)(2,1)}, u32[]{:S(2)}, u32[]{:S(2)}) collective-permute-start(bf16[16,72,290]{2,1,0:T(8,128)(2,1)S(1)} %bitcast.26), channel_id=1, source_target_pairs={{0,16},{16,0},{1,17},{17,1},{2,18},{18,2},{3,19},{19,3},{4,20},{20... | collective-permute-start | bytes 2004488 | tf_op jit(solution)/shard_map/ppermute | solution.py:323
  62.6 11.1 %collective-permute-start.6 = (bf16[2,288,256]{2,1,0:T(8,128)(2,1)}, bf16[2,288,256]{2,1,0:T(8,128)(2,1)}, u32[]{:S(2)}, u32[]{:S(2)}) collective-permute-start(bf16[2,288,256]{2,1,0:T(8,128)(2,1)} %slice.46), channel_id=1, source_target_pairs={{96,0},{0,32},{32,64},{64,96},{97,1},{1,33},{33,65},{65,97},{98,2}... | collective-permute-start | bytes 884744 | tf_op jit(solution)/shard_map/ppermute | solution.py:320
  65.3 9.0 %collective-permute-start.4 = (bf16[2,288,256]{2,1,0:T(8,128)(2,1)}, bf16[2,288,256]{2,1,0:T(8,128)(2,1)}, u32[]{:S(2)}, u32[]{:S(2)}) collective-permute-start(bf16[2,288,256]{2,1,0:T(8,128)(2,1)} %slice.45), channel_id=1, source_target_pairs={{32,0},{64,32},{96,64},{0,96},{33,1},{65,33},{97,65},{1,97},{34,2}... | collective-permute-start | bytes 884744 | tf_op jit(solution)/shard_map/ppermute | solution.py:319
  77.4 33.6 %all-to-all-start.1 = ((bf16[16,144,128]{2,1,0:T(8,128)(2,1)}), bf16[16,144,128]{2,1,0:T(8,128)(2,1)S(1)}, u32[]{:S(2)}, u32[]{:S(2)}) async-start(bf16[16,144,128]{2,1,0:T(8,128)(2,1)} %broadcast_in_dim.54), calls=%async_computation.1 | async-start | bytes 1179648 | tf_op jit(solution)/shard_map/all_to_all | solution.py:27
  85.4 25.6 %collective-permute-start.8 = (bf16[4,144,256]{2,1,0:T(8,128)(2,1)S(1)}, bf16[4,144,256]{2,1,0:T(8,128)(2,1)S(1)}, u32[]{:S(2)}, u32[]{:S(2)}) collective-permute-start(bf16[4,144,256]{2,1,0:T(8,128)(2,1)S(1)} %slice.47.own), channel_id=1, source_target_pairs={{96,0},{0,32},{32,64},{64,96},{97,1},{1,33},{33,65},{65,97},{98,2}... | collective-permute-start | bytes 884744 | tf_op jit(solution)/shard_map/ppermute | solution.py:359
  88.7 22.3 %collective-permute-start.7 = (bf16[4,144,256]{2,1,0:T(8,128)(2,1)S(1)}, bf16[4,144,256]{2,1,0:T(8,128)(2,1)S(1)}, u32[]{:S(2)}, u32[]{:S(2)}) collective-permute-start(bf16[4,144,256]{2,1,0:T(8,128)(2,1)S(1)} %slice.47.own), channel_id=1, source_target_pairs={{32,0},{64,32},{96,64},{0,96},{33,1},{65,33},{97,65},{1,97},{34,2}... | collective-permute-start | bytes 884744 | tf_op jit(solution)/shard_map/ppermute | solution.py:358
  116.5 21.8 %all-to-all-start.2 = ((bf16[16,160,128]{2,1,0:T(8,128)(2,1)}), bf16[16,160,128]{2,1,0:T(8,128)(2,1)S(1)}, u32[]{:S(2)}, u32[]{:S(2)}) async-start(bf16[16,160,128]{2,1,0:T(8,128)(2,1)} %bitcast.13), calls=%async_computation.2 | async-start | bytes 1310720 | tf_op jit(solution)/shard_map/all_to_all | solution.py:375
  122.6 20.3 %collective-permute-start.10 = (bf16[2,144,256]{2,1,0:T(8,128)(2,1)S(1)}, bf16[2,144,256]{2,1,0:T(8,128)(2,1)S(1)}, u32[]{:S(2)}, u32[]{:S(2)}) collective-permute-start(bf16[2,144,256]{2,1,0:T(8,128)(2,1)S(1)} %slice.40), channel_id=1, source_target_pairs={{96,0},{0,32},{32,64},{64,96},{97,1},{1,33},{33,65},{65,97},{98,2}... | collective-permute-start | bytes 442376 | tf_op jit(solution)/shard_map/ppermute | solution.py:369
  125.8 17.0 %collective-permute-start.9 = (bf16[2,144,256]{2,1,0:T(8,128)(2,1)S(1)}, bf16[2,144,256]{2,1,0:T(8,128)(2,1)S(1)}, u32[]{:S(2)}, u32[]{:S(2)}) collective-permute-start(bf16[2,144,256]{2,1,0:T(8,128)(2,1)S(1)} %slice.39), channel_id=1, source_target_pairs={{32,0},{64,32},{96,64},{0,96},{33,1},{65,33},{97,65},{1,97},{34,2}... | collective-permute-start | bytes 442376 | tf_op jit(solution)/shard_map/ppermute | solution.py:368
  145.0 41.2 %all-to-all-start.3 = ((bf16[16,176,128]{2,1,0:T(8,128)(2,1)}), bf16[16,176,128]{2,1,0:T(8,128)(2,1)S(1)}, u32[]{:S(2)}, u32[]{:S(2)}) async-start(bf16[16,176,128]{2,1,0:T(8,128)(2,1)} %spread.1), calls=%async_computation.3 | async-start | bytes 1441792 | tf_op jit(solution)/shard_map/all_to_all | solution.py:383
  157.7 24.9 %copy-start.6 = (bf16[288]{0:T(512)(128)(2,1)S(1)}, bf16[288]{0:T(512)(128)(2,1)}, u32[]{:S(2)}) copy-start(bf16[288]{0:T(512)(128)(2,1)} %param.18) | copy-start | bytes 1732
  179.6 4.6 %collective-permute-start.12 = (bf16[2304,128]{1,0:T(8,128)(2,1)S(1)}, bf16[2304,128]{1,0:T(8,128)(2,1)S(1)}, u32[]{:S(2)}, u32[]{:S(2)}) collective-permute-start(bf16[2304,128]{1,0:T(8,128)(2,1)S(1)} %all_gather.35.mine), channel_id=1, source_target_pairs={{0,16},{16,0},{1,17},{17,1},{2,18},{18,2},{3,19},{19,3},{4,20},{20... | collective-permute-start | bytes 1769480 | tf_op jit(solution)/shard_map/ppermute | solution.py:382
  186.2 18.5 %copy-start.3 = (bf16[72,288]{1,0:T(8,128)(2,1)S(1)}, bf16[72,288]{1,0:T(8,128)(2,1)}, u32[]{:S(2)}) copy-start(bf16[72,288]{1,0:T(8,128)(2,1)} %param.12) | copy-start | bytes 124420
  187.3 17.3 %all-to-all-start.4 = ((f32[32,1,72]{2,1,0:T(1,128)}), f32[32,1,72]{2,1,0:T(1,128)S(1)}, u32[]{:S(2)}, u32[]{:S(2)}) async-start(f32[32,1,72]{2,1,0:T(1,128)} %bitcast.16), calls=%async_computation.4 | async-start | bytes 32768 | tf_op jit(solution)/shard_map/all_to_all | solution.py:389
  196.8 7.8 %collective-permute-start.11 = (f32[72,144]{1,0:T(8,128)S(1)}, f32[72,144]{1,0:T(8,128)S(1)}, u32[]{:S(2)}, u32[]{:S(2)}) collective-permute-start(f32[72,144]{1,0:T(8,128)S(1)} %fusion.11), channel_id=1, source_target_pairs={{0,16},{16,0},{1,17},{17,1},{2,18},{18,2},{3,19},{19,3},{4,20},{20... | collective-permute-start | bytes 124424 | tf_op jit(solution)/shard_map/ppermute | solution.py:393
  (1 other events, 6.6 us)

commit v9 on v8

--- a/solution.py
+++ b/solution.py
@@ -357,7 +357,7 @@
     queries, fresh_rows, w_out = lax.optimization_barrier((queries, fresh_rows, w_out))
     out_right = lax.ppermute(w_out, "x", from_right)
     out_left = lax.ppermute(w_out, "x", from_left)
-    near_rows = lax.all_gather(fresh_rows, ("x", "c"), axis=0)
+    near_rows = lax.all_gather(fresh_rows, "c", axis=0)
     all_queries = everywhere(queries, CHIPS, n_chips).reshape(-1, HD)
     all_queries, near_rows, out_right, out_left = lax.optimization_barrier(
         (all_queries, near_rows, out_right, out_left)
@@ -372,6 +372,7 @@
 
     sums = attend(meta, all_queries, k_cache, v_cache, k_other, v_other)
     sums, near_rows = lax.optimization_barrier((sums, near_rows))
+    near_rows = lax.all_gather(near_rows, "x", axis=0, tiled=True)
     parts = lax.all_to_all(sums.reshape(n_chips, -1, HD), CHIPS, 0, 0)
     attended = divide(meta, parts, *attend_new(meta, queries, near_rows))
     attended = lax.all_gather(attended, "c", axis=0)
@@ -379,14 +380,15 @@
     partial_out, near_rows = lax.optimization_barrier((partial_out, near_rows))
     kind = lax.dynamic_index_in_dim(near_rows.reshape(4, 2, 2 * tok_rows, HD), core, 1, keepdims=False)
     kind = lax.all_gather(kind.reshape(-1, HD), "zh", axis=0, tiled=True)
-    k_pool, v_pool = write(meta, kind, lax.ppermute(kind, "c", swap), k_cache, v_cache)
     total = jnp.sum(lax.all_to_all(partial_out, GY, 0, 0).astype(F32), axis=0)
     rows = 2 * tok_rows
     rest = jnp.concatenate([total[rows : rows + 16], total[rows + 16 :, : rows - HD]], axis=1)
     branch = jnp.concatenate([total[:rows], rest.T], axis=1)
     squares = jnp.sum(branch * branch, axis=1).reshape(2, 1, 1, tok_rows)
     squares = jnp.broadcast_to(squares, (2, n_gy, 1, tok_rows)).reshape(2 * n_gy, 1, tok_rows)
+    squares, kind = lax.optimization_barrier((squares, kind))
     squares = lax.all_to_all(squares, ("c",) + GY, 0, 0)
+    k_pool, v_pool = write(meta, kind, lax.ppermute(kind, "c", swap), k_cache, v_cache)
     mean = jnp.sum(squares, axis=(0, 1)) / D
     kept = lax.dynamic_slice_in_dim(branch, core * tok_rows, tok_rows, 0)
     sent = lax.dynamic_slice_in_dim(branch, (1 - core) * tok_rows, tok_rows, 0)

time: 207 us -> 201 us (0.971)
  waiting for transfers between devices: 15.9 us -> 8.88 us
  starting transfers between devices: 84.5 us -> 88.2 us
    all_to_all x1, waiting for transfers between devices: 8.14 us -> 0.01 us  [on_device(): parts = lax.all_to_all(sums.reshape(n_chips, -1, HD), CHIPS, 0, 0)]
    ppermute x1, waiting for transfers between devices: 0.01 us -> 4.88 us  [on_device(): out_left = lax.ppermute(w_out, 'x', from_left)]
    all_gather x1 -> x2, blocking collectives: 19 us -> 16.6 us  [the longest x1 12 us: on_device(): near_rows = lax.all_gather(near_rows, 'x', axis=0, tiled=True)]
    all_to_all x1, waiting for transfers between devices: 5.58 us -> 3.38 us  [on_device(): squares = lax.all_to_all(squares, ('c',) + GY, 0, 0)]
    all_to_all x1, starting transfers between devices: 6.06 us -> 8.13 us  [on_device(): parts = lax.all_to_all(sums.reshape(n_chips, -1, HD), CHIPS, 0, 0)]
  transfers between devices with their start and end apart: 18 -> 18, of which waited for: 4 -> 3; matrix products, arithmetic and copies ran while one was open for 3% -> 3% of each run, Pallas kernels for 2% -> 1%
where the time goes in v9:
time: 201 us; the launch traced here: 199 us
  starting transfers between devices  88.2 us (44%)
  blocking collectives  76.6 us (38%)
  Pallas kernels  11.7 us (6%)
  waiting for transfers between devices  8.88 us (4%)
  local copies, waits for them, and re-layouts  7.12 us (4%)
  other arithmetic  5.76 us (3%)
    all_gather x1, blocking collectives, on_device(): weights = lax.all_gather(weights, 'zh', axis=0)  22.5 us
    all_gather x1, blocking collectives, on_device(): kind = lax.all_gather(kind.reshape(-1, HD), 'zh', axis=0, tiled=True)  21.7 us
    all_to_all x2, starting transfers between devices, everywhere(): lax.all_to_all(jnp.broadcast_to(value[None], (count,) + value.shape), axe...  14.9 us
    all_to_all x1, starting transfers between devices, on_device(): total = jnp.sum(lax.all_to_all(partial_out, GY, 0, 0).astype(F32), axis=0)  14.1 us
    all_gather x1, blocking collectives, on_device(): near_rows = lax.all_gather(near_rows, 'x', axis=0, tiled=True)  12 us
    all_to_all x1, starting transfers between devices, on_device(): squares = lax.all_to_all(squares, ('c',) + GY, 0, 0)  10.5 us
    all_to_all x1, starting transfers between devices, on_device(): parts = lax.all_to_all(sums.reshape(n_chips, -1, HD), CHIPS, 0, 0)  8.13 us
    ppermute x1, starting transfers between devices, on_device(): k_other = lax.ppermute(k_cache, 'c', swap)  5.88 us
  transfers between devices with their start and end apart: 18, of which 3 were waited for; matrix products, arithmetic and copies ran while one was open for 3% of the time, Pallas kernels for 1%

profile of v9, /device:TPU:1, one launch (start us, length us, event | category | flops | bytes accessed | tf_op | source)
XLA Modules:
  0.0 199.3 jit_solution(12574893457849520104)
XLA Ops:
  4.2 5.1 %all_gather.30 = bf16[144,290]{1,0:T(8,128)(2,1)S(1)} all-gather(bf16[72,290]{1,0:T(8,128)(2,1)S(1)} %pad_maximum_fusion.6), channel_id=1, replica_groups=mesh['zh'=4,'x'=4,'c'=2,'y'=8,'zl'=2] {'zl'}, dimensions={0}, use_global_device_ids=true | all-gather | bytes 125280 | tf_op jit(solution)/shard_map/all_gather | solution.py:305
  10.3 7.0 %all-to-all-start = ((bf16[8,144,290]{2,1,0:T(8,128)(2,1)}), bf16[8,144,290]{2,1,0:T(8,128)(2,1)S(1)}, u32[]{:S(2)}, u32[]{:S(2)}) async-start(bf16[8,144,290]{2,1,0:T(8,128)(2,1)} %broadcast_in_dim.29), calls=%async_computation | async-start | bytes 1769472 | tf_op jit(solution)/shard_map/all_to_all | solution.py:27
  17.3 5.0 %all_gather.31 = bf16[288,512]{1,0:T(8,128)(2,1)S(1)} all-gather(bf16[144,512]{1,0:T(8,128)(2,1)S(1)} %pad_maximum_fusion.3), channel_id=1, replica_groups=mesh['zh'=4,'x'=4,'c'=2,'y'=8,'zl'=2] {'c'}, dimensions={0}, use_global_device_ids=true | all-gather | bytes 442368 | tf_op jit(solution)/shard_map/all_gather | solution.py:308
  22.3 22.5 %all-gather = bf16[1728,256]{1,0:T(8,128)(2,1)S(1)} all-gather(bf16[432,256]{1,0:T(8,128)(2,1)S(1)} %pad_maximum_fusion.1), channel_id=2, replica_groups=mesh['zh'=4,'x'=4,'c'=2,'y'=8,'zl'=2] {'zh'}, dimensions={0}, use_global_device_ids=true | all-gather | bytes 1105920 | tf_op jit(solution)/shard_map/all_gather | solution.py:312
  44.9 3.1 %collective-permute-start.5 = (bf16[4,288,256]{2,1,0:T(8,128)(2,1)S(1)}, bf16[4,288,256]{2,1,0:T(8,128)(2,1)S(1)}, u32[]{:S(2)}, u32[]{:S(2)}) collective-permute-start(bf16[4,288,256]{2,1,0:T(8,128)(2,1)S(1)} %slice.44.own), channel_id=1, source_target_pairs={{96,0},{0,32},{32,64},{64,96},{97,1},{1,33},{33,65},{65,97},{98,2}... | collective-permute-start | bytes 1769480 | tf_op jit(solution)/shard_map/ppermute | solution.py:318
  48.0 3.4 %collective-permute-start.3 = (bf16[4,288,256]{2,1,0:T(8,128)(2,1)S(1)}, bf16[4,288,256]{2,1,0:T(8,128)(2,1)S(1)}, u32[]{:S(2)}, u32[]{:S(2)}) collective-permute-start(bf16[4,288,256]{2,1,0:T(8,128)(2,1)S(1)} %slice.44.own), channel_id=1, source_target_pairs={{32,0},{64,32},{96,64},{0,96},{33,1},{65,33},{97,65},{1,97},{34,2}... | collective-permute-start | bytes 1769480 | tf_op jit(solution)/shard_map/ppermute | solution.py:317
  51.4 5.9 %collective-permute-start.1 = (bf16[1024,128]{1,0:T(8,128)(2,1)S(1)}, bf16[1024,128]{1,0:T(8,128)(2,1)}, u32[]{:S(2)}, u32[]{:S(2)}) collective-permute-start(bf16[1024,128]{1,0:T(8,128)(2,1)S(1)} %copy-done), channel_id=1, source_target_pairs={{0,16},{16,0},{1,17},{17,1},{2,18},{18,2},{3,19},{19,3},{4,20},{20... | collective-permute-start | bytes 786440 | tf_op jit(solution)/shard_map/ppermute | solution.py:352
  59.4 2.4 %collective-permute-start = (bf16[16,72,290]{2,1,0:T(8,128)(2,1)S(1)}, bf16[16,72,290]{2,1,0:T(8,128)(2,1)}, u32[]{:S(2)}, u32[]{:S(2)}) collective-permute-start(bf16[16,72,290]{2,1,0:T(8,128)(2,1)S(1)} %bitcast.26), channel_id=1, source_target_pairs={{0,16},{16,0},{1,17},{17,1},{2,18},{18,2},{3,19},{19,3},{4,20},{20... | collective-permute-start | bytes 2004488 | tf_op jit(solution)/shard_map/ppermute | solution.py:323
  65.3 4.6 %collective-permute-start.4 = (bf16[2,288,256]{2,1,0:T(8,128)(2,1)}, bf16[2,288,256]{2,1,0:T(8,128)(2,1)}, u32[]{:S(2)}, u32[]{:S(2)}) collective-permute-start(bf16[2,288,256]{2,1,0:T(8,128)(2,1)} %slice.45), channel_id=1, source_target_pairs={{32,0},{64,32},{96,64},{0,96},{33,1},{65,33},{97,65},{1,97},{34,2}... | collective-permute-start | bytes 884744 | tf_op jit(solution)/shard_map/ppermute | solution.py:319
  77.4 8.0 %all-to-all-start.1 = ((bf16[16,144,128]{2,1,0:T(8,128)(2,1)}), bf16[16,144,128]{2,1,0:T(8,128)(2,1)S(1)}, u32[]{:S(2)}, u32[]{:S(2)}) async-start(bf16[16,144,128]{2,1,0:T(8,128)(2,1)} %broadcast_in_dim.54), calls=%async_computation.1 | async-start | bytes 1179648 | tf_op jit(solution)/shard_map/all_to_all | solution.py:27
  85.4 3.3 %collective-permute-start.8 = (bf16[4,144,256]{2,1,0:T(8,128)(2,1)S(1)}, bf16[4,144,256]{2,1,0:T(8,128)(2,1)S(1)}, u32[]{:S(2)}, u32[]{:S(2)}) collective-permute-start(bf16[4,144,256]{2,1,0:T(8,128)(2,1)S(1)} %slice.47.own), channel_id=1, source_target_pairs={{96,0},{0,32},{32,64},{64,96},{97,1},{1,33},{33,65},{65,97},{98,2}... | collective-permute-start | bytes 884744 | tf_op jit(solution)/shard_map/ppermute | solution.py:359
  88.7 3.2 %collective-permute-start.7 = (bf16[4,144,256]{2,1,0:T(8,128)(2,1)S(1)}, bf16[4,144,256]{2,1,0:T(8,128)(2,1)S(1)}, u32[]{:S(2)}, u32[]{:S(2)}) collective-permute-start(bf16[4,144,256]{2,1,0:T(8,128)(2,1)S(1)} %slice.47.own), channel_id=1, source_target_pairs={{32,0},{64,32},{96,64},{0,96},{33,1},{65,33},{97,65},{1,97},{34,2}... | collective-permute-start | bytes 884744 | tf_op jit(solution)/shard_map/ppermute | solution.py:358
  91.9 4.6 %all-gather.1 = bf16[288,128]{1,0:T(8,128)(2,1)S(1)} all-gather(bf16[144,128]{1,0:T(8,128)(2,1)S(1)} %get-tuple-element.33), channel_id=3, replica_groups=mesh['zh'=4,'x'=4,'c'=2,'y'=8,'zl'=2] {'c'}, dimensions={0}, use_global_device_ids=true | all-gather | bytes 110592 | tf_op jit(solution)/shard_map/all_gather | solution.py:360
  96.6 4.9 %collective-permute-done.8.left = bf16[4,144,256]{2,1,0:T(8,128)(2,1)S(1)} collective-permute-done((bf16[4,144,256]{2,1,0:T(8,128)(2,1)S(1)}, bf16[4,144,256]{2,1,0:T(8,128)(2,1)S(1)}, u32[]{:S(2)}, u32[]{:S(2)}) %collective-permute-start.8) | collective-permute-done | bytes 294944 | tf_op jit(solution)/shard_map/ppermute | solution.py:359
  101.4 3.9 %attend.1 = bf16[2560,128]{1,0:T(8,128)(2,1)} custom-call(s32[40]{0:T(128)S(1)} %concatenate.62.meta, bf16[2304,128]{1,0:T(8,128)(2,1)S(1)} %bitcast.28, bf16[1024,128]{1,0:T(8,128)(2,1)S(1)} %copy-done, bf16[1024,128]{1,0:T(8,128)(2,1)S(1)} %copy-done.1, bf16[1024,128]{1,0:T(8,128)(2,1)} %collective-permute-done.1.k_other, ...), custom_call_target="tpu_custom_call" | custom-call | tf_op jit(solution)/shard_map/attend/pallas_call | solution.py:123
  105.3 8.1 %all-to-all-start.2 = ((bf16[16,160,128]{2,1,0:T(8,128)(2,1)}), bf16[16,160,128]{2,1,0:T(8,128)(2,1)S(1)}, u32[]{:S(2)}, u32[]{:S(2)}) async-start(bf16[16,160,128]{2,1,0:T(8,128)(2,1)} %bitcast.13), calls=%async_computation.2 | async-start | bytes 1310720 | tf_op jit(solution)/shard_map/all_to_all | solution.py:376
  113.5 3.3 %collective-permute-start.10 = (bf16[2,144,256]{2,1,0:T(8,128)(2,1)S(1)}, bf16[2,144,256]{2,1,0:T(8,128)(2,1)S(1)}, u32[]{:S(2)}, u32[]{:S(2)}) collective-permute-start(bf16[2,144,256]{2,1,0:T(8,128)(2,1)S(1)} %slice.40), channel_id=1, source_target_pairs={{96,0},{0,32},{32,64},{64,96},{97,1},{1,33},{33,65},{65,97},{98,2}... | collective-permute-start | bytes 442376 | tf_op jit(solution)/shard_map/ppermute | solution.py:369
  116.8 3.2 %collective-permute-start.9 = (bf16[2,144,256]{2,1,0:T(8,128)(2,1)S(1)}, bf16[2,144,256]{2,1,0:T(8,128)(2,1)S(1)}, u32[]{:S(2)}, u32[]{:S(2)}) collective-permute-start(bf16[2,144,256]{2,1,0:T(8,128)(2,1)S(1)} %slice.39), channel_id=1, source_target_pairs={{32,0},{64,32},{96,64},{0,96},{33,1},{65,33},{97,65},{1,97},{34,2}... | collective-permute-start | bytes 442376 | tf_op jit(solution)/shard_map/ppermute | solution.py:368
  120.0 12.0 %all_gather.36.fresh_rows = bf16[8,144,128]{2,1,0:T(8,128)(2,1)S(1)} all-gather(bf16[2,144,128]{2,1,0:T(8,128)(2,1)S(1)} %bitcast.37), channel_id=1, replica_groups=mesh['zh'=4,'x'=4,'c'=2,'y'=8,'zl'=2] {'x'}, dimensions={0}, use_global_device_ids=true | all-gather | bytes 368640 | tf_op jit(solution)/shard_map/all_gather | solution.py:375
  133.8 5.7 %all-gather.2 = bf16[288,128]{1,0:T(8,128)(2,1)S(1)} all-gather(bf16[144,128]{1,0:T(8,128)(2,1)S(1)} %divide.1), channel_id=4, replica_groups=mesh['zh'=4,'x'=4,'c'=2,'y'=8,'zl'=2] {'c'}, dimensions={0}, use_global_device_ids=true | all-gather | bytes 110592 | tf_op jit(solution)/shard_map/all_gather | solution.py:378
  141.6 14.1 %all-to-all-start.3 = ((bf16[16,176,128]{2,1,0:T(8,128)(2,1)}), bf16[16,176,128]{2,1,0:T(8,128)(2,1)S(1)}, u32[]{:S(2)}, u32[]{:S(2)}) async-start(bf16[16,176,128]{2,1,0:T(8,128)(2,1)} %spread.1), calls=%async_computation.3 | async-start | bytes 1441792 | tf_op jit(solution)/shard_map/all_to_all | solution.py:383
  155.8 21.7 %all_gather.39.mine = bf16[2304,128]{1,0:T(8,128)(2,1)S(1)} all-gather(bf16[576,128]{1,0:T(8,128)(2,1)S(1)} %bitcast.36), channel_id=1, replica_groups=mesh['zh'=4,'x'=4,'c'=2,'y'=8,'zl'=2] {'zh'}, dimensions={0}, use_global_device_ids=true | all-gather | bytes 737280 | tf_op jit(solution)/shard_map/all_gather | solution.py:382
  178.6 10.5 %all-to-all-start.4 = ((f32[32,1,72]{2,1,0:T(1,128)}), f32[32,1,72]{2,1,0:T(1,128)S(1)}, u32[]{:S(2)}, u32[]{:S(2)}) async-start(f32[32,1,72]{2,1,0:T(1,128)} %bitcast.16), calls=%async_computation.4 | async-start | bytes 32768 | tf_op jit(solution)/shard_map/all_to_all | solution.py:390
  193.5 3.4 %all-to-all-done.4 = f32[32,1,72]{2,1,0:T(1,128)S(1)} async-done(((f32[32,1,72]{2,1,0:T(1,128)}), f32[32,1,72]{2,1,0:T(1,128)S(1)}, u32[]{:S(2)}, u32[]{:S(2)}) %all-to-all-start.4) | async-done | bytes 9248 | tf_op jit(solution)/shard_map/all_to_all | solution.py:390
  (81 shorter events, 29.4 us)
Async XLA Ops:
  10.3 12.0 %copy-start.4 = (bf16[256,144]{0,1:T(8,128)(2,1)S(1)}, bf16[256,144]{0,1:T(8,128)(2,1)}, u32[]{:S(2)}) copy-start(bf16[256,144]{0,1:T(8,128)(2,1)} %param.17) | copy-start | bytes 221188
  10.3 49.1 %all-to-all-start = ((bf16[8,144,290]{2,1,0:T(8,128)(2,1)}), bf16[8,144,290]{2,1,0:T(8,128)(2,1)S(1)}, u32[]{:S(2)}, u32[]{:S(2)}) async-start(bf16[8,144,290]{2,1,0:T(8,128)(2,1)} %broadcast_in_dim.29), calls=%async_computation | async-start | bytes 1769472 | tf_op jit(solution)/shard_map/all_to_all | solution.py:27
  22.3 29.1 %copy-start = (bf16[1024,128]{1,0:T(8,128)(2,1)S(1)}, bf16[1024,128]{1,0:T(8,128)(2,1)}, u32[]{:S(2)}) copy-start(bf16[1024,128]{1,0:T(8,128)(2,1)} %k_old.1) | copy-start | bytes 786436
  22.3 35.0 %copy-start.1 = (bf16[1024,128]{1,0:T(8,128)(2,1)S(1)}, bf16[1024,128]{1,0:T(8,128)(2,1)}, u32[]{:S(2)}) copy-start(bf16[1024,128]{1,0:T(8,128)(2,1)} %v_old.1) | copy-start | bytes 786436
  44.8 14.5 %copy-start.5 = (s32[12]{0:T(128)S(1)}, s32[12]{0:T(128)}, u32[]{:S(2)}) copy-start(s32[12]{0:T(128)} %param.21) | copy-start | bytes 148
  44.9 17.0 %collective-permute-start.5 = (bf16[4,288,256]{2,1,0:T(8,128)(2,1)S(1)}, bf16[4,288,256]{2,1,0:T(8,128)(2,1)S(1)}, u32[]{:S(2)}, u32[]{:S(2)}) collective-permute-start(bf16[4,288,256]{2,1,0:T(8,128)(2,1)S(1)} %slice.44.own), channel_id=1, source_target_pairs={{96,0},{0,32},{32,64},{64,96},{97,1},{1,33},{33,65},{65,97},{98,2}... | collective-permute-start | bytes 1769480 | tf_op jit(solution)/shard_map/ppermute | solution.py:318
  48.0 16.5 %collective-permute-start.3 = (bf16[4,288,256]{2,1,0:T(8,128)(2,1)S(1)}, bf16[4,288,256]{2,1,0:T(8,128)(2,1)S(1)}, u32[]{:S(2)}, u32[]{:S(2)}) collective-permute-start(bf16[4,288,256]{2,1,0:T(8,128)(2,1)S(1)} %slice.44.own), channel_id=1, source_target_pairs={{32,0},{64,32},{96,64},{0,96},{33,1},{65,33},{97,65},{1,97},{34,2}... | collective-permute-start | bytes 1769480 | tf_op jit(solution)/shard_map/ppermute | solution.py:317
  51.4 22.3 %collective-permute-start.1 = (bf16[1024,128]{1,0:T(8,128)(2,1)S(1)}, bf16[1024,128]{1,0:T(8,128)(2,1)}, u32[]{:S(2)}, u32[]{:S(2)}) collective-permute-start(bf16[1024,128]{1,0:T(8,128)(2,1)S(1)} %copy-done), channel_id=1, source_target_pairs={{0,16},{16,0},{1,17},{17,1},{2,18},{18,2},{3,19},{19,3},{4,20},{20... | collective-permute-start | bytes 786440 | tf_op jit(solution)/shard_map/ppermute | solution.py:352
  57.3 16.4 %collective-permute-start.2 = (bf16[1024,128]{1,0:T(8,128)(2,1)S(1)}, bf16[1024,128]{1,0:T(8,128)(2,1)}, u32[]{:S(2)}, u32[]{:S(2)}) collective-permute-start(bf16[1024,128]{1,0:T(8,128)(2,1)S(1)} %copy-done.1), channel_id=1, source_target_pairs={{0,16},{16,0},{1,17},{17,1},{2,18},{18,2},{3,19},{19,3},{4,20},{20... | collective-permute-start | bytes 786440 | tf_op jit(solution)/shard_map/ppermute | solution.py:353
  59.4 14.3 %collective-permute-start = (bf16[16,72,290]{2,1,0:T(8,128)(2,1)S(1)}, bf16[16,72,290]{2,1,0:T(8,128)(2,1)}, u32[]{:S(2)}, u32[]{:S(2)}) collective-permute-start(bf16[16,72,290]{2,1,0:T(8,128)(2,1)S(1)} %bitcast.26), channel_id=1, source_target_pairs={{0,16},{16,0},{1,17},{17,1},{2,18},{18,2},{3,19},{19,3},{4,20},{20... | collective-permute-start | bytes 2004488 | tf_op jit(solution)/shard_map/ppermute | solution.py:323
  62.6 11.1 %collective-permute-start.6 = (bf16[2,288,256]{2,1,0:T(8,128)(2,1)}, bf16[2,288,256]{2,1,0:T(8,128)(2,1)}, u32[]{:S(2)}, u32[]{:S(2)}) collective-permute-start(bf16[2,288,256]{2,1,0:T(8,128)(2,1)} %slice.46), channel_id=1, source_target_pairs={{96,0},{0,32},{32,64},{64,96},{97,1},{1,33},{33,65},{65,97},{98,2}... | collective-permute-start | bytes 884744 | tf_op jit(solution)/shard_map/ppermute | solution.py:320
  65.3 9.0 %collective-permute-start.4 = (bf16[2,288,256]{2,1,0:T(8,128)(2,1)}, bf16[2,288,256]{2,1,0:T(8,128)(2,1)}, u32[]{:S(2)}, u32[]{:S(2)}) collective-permute-start(bf16[2,288,256]{2,1,0:T(8,128)(2,1)} %slice.45), channel_id=1, source_target_pairs={{32,0},{64,32},{96,64},{0,96},{33,1},{65,33},{97,65},{1,97},{34,2}... | collective-permute-start | bytes 884744 | tf_op jit(solution)/shard_map/ppermute | solution.py:319
  77.4 24.0 %all-to-all-start.1 = ((bf16[16,144,128]{2,1,0:T(8,128)(2,1)}), bf16[16,144,128]{2,1,0:T(8,128)(2,1)S(1)}, u32[]{:S(2)}, u32[]{:S(2)}) async-start(bf16[16,144,128]{2,1,0:T(8,128)(2,1)} %broadcast_in_dim.54), calls=%async_computation.1 | async-start | bytes 1179648 | tf_op jit(solution)/shard_map/all_to_all | solution.py:27
  85.4 16.0 %collective-permute-start.8 = (bf16[4,144,256]{2,1,0:T(8,128)(2,1)S(1)}, bf16[4,144,256]{2,1,0:T(8,128)(2,1)S(1)}, u32[]{:S(2)}, u32[]{:S(2)}) collective-permute-start(bf16[4,144,256]{2,1,0:T(8,128)(2,1)S(1)} %slice.47.own), channel_id=1, source_target_pairs={{96,0},{0,32},{32,64},{64,96},{97,1},{1,33},{33,65},{65,97},{98,2}... | collective-permute-start | bytes 884744 | tf_op jit(solution)/shard_map/ppermute | solution.py:359
  88.7 12.8 %collective-permute-start.7 = (bf16[4,144,256]{2,1,0:T(8,128)(2,1)S(1)}, bf16[4,144,256]{2,1,0:T(8,128)(2,1)S(1)}, u32[]{:S(2)}, u32[]{:S(2)}) collective-permute-start(bf16[4,144,256]{2,1,0:T(8,128)(2,1)S(1)} %slice.47.own), channel_id=1, source_target_pairs={{32,0},{64,32},{96,64},{0,96},{33,1},{65,33},{97,65},{1,97},{34,2}... | collective-permute-start | bytes 884744 | tf_op jit(solution)/shard_map/ppermute | solution.py:358
  105.3 27.7 %all-to-all-start.2 = ((bf16[16,160,128]{2,1,0:T(8,128)(2,1)}), bf16[16,160,128]{2,1,0:T(8,128)(2,1)S(1)}, u32[]{:S(2)}, u32[]{:S(2)}) async-start(bf16[16,160,128]{2,1,0:T(8,128)(2,1)} %bitcast.13), calls=%async_computation.2 | async-start | bytes 1310720 | tf_op jit(solution)/shard_map/all_to_all | solution.py:376
  113.5 25.9 %collective-permute-start.10 = (bf16[2,144,256]{2,1,0:T(8,128)(2,1)S(1)}, bf16[2,144,256]{2,1,0:T(8,128)(2,1)S(1)}, u32[]{:S(2)}, u32[]{:S(2)}) collective-permute-start(bf16[2,144,256]{2,1,0:T(8,128)(2,1)S(1)} %slice.40), channel_id=1, source_target_pairs={{96,0},{0,32},{32,64},{64,96},{97,1},{1,33},{33,65},{65,97},{98,2}... | collective-permute-start | bytes 442376 | tf_op jit(solution)/shard_map/ppermute | solution.py:369
  116.8 22.6 %collective-permute-start.9 = (bf16[2,144,256]{2,1,0:T(8,128)(2,1)S(1)}, bf16[2,144,256]{2,1,0:T(8,128)(2,1)S(1)}, u32[]{:S(2)}, u32[]{:S(2)}) collective-permute-start(bf16[2,144,256]{2,1,0:T(8,128)(2,1)S(1)} %slice.39), channel_id=1, source_target_pairs={{32,0},{64,32},{96,64},{0,96},{33,1},{65,33},{97,65},{1,97},{34,2}... | collective-permute-start | bytes 442376 | tf_op jit(solution)/shard_map/ppermute | solution.py:368
  141.6 14.1 %copy-start.6 = (bf16[288]{0:T(512)(128)(2,1)S(1)}, bf16[288]{0:T(512)(128)(2,1)}, u32[]{:S(2)}) copy-start(bf16[288]{0:T(512)(128)(2,1)} %param.18) | copy-start | bytes 1732
  141.6 35.9 %all-to-all-start.3 = ((bf16[16,176,128]{2,1,0:T(8,128)(2,1)}), bf16[16,176,128]{2,1,0:T(8,128)(2,1)S(1)}, u32[]{:S(2)}, u32[]{:S(2)}) async-start(bf16[16,176,128]{2,1,0:T(8,128)(2,1)} %spread.1), calls=%async_computation.3 | async-start | bytes 1441792 | tf_op jit(solution)/shard_map/all_to_all | solution.py:383
  177.5 19.4 %copy-start.3 = (bf16[72,288]{1,0:T(8,128)(2,1)S(1)}, bf16[72,288]{1,0:T(8,128)(2,1)}, u32[]{:S(2)}) copy-start(bf16[72,288]{1,0:T(8,128)(2,1)} %param.12) | copy-start | bytes 124420
  178.6 18.3 %all-to-all-start.4 = ((f32[32,1,72]{2,1,0:T(1,128)}), f32[32,1,72]{2,1,0:T(1,128)S(1)}, u32[]{:S(2)}, u32[]{:S(2)}) async-start(f32[32,1,72]{2,1,0:T(1,128)} %bitcast.16), calls=%async_computation.4 | async-start | bytes 32768 | tf_op jit(solution)/shard_map/all_to_all | solution.py:390
  189.1 7.8 %collective-permute-start.11 = (f32[72,144]{1,0:T(8,128)S(1)}, f32[72,144]{1,0:T(8,128)S(1)}, u32[]{:S(2)}, u32[]{:S(2)}) collective-permute-start(f32[72,144]{1,0:T(8,128)S(1)} %fusion.11), channel_id=1, source_target_pairs={{0,16},{16,0},{1,17},{17,1},{2,18},{18,2},{3,19},{19,3},{4,20},{20... | collective-permute-start | bytes 124424 | tf_op jit(solution)/shard_map/ppermute | solution.py:395
  191.3 6.4 %collective-permute-start.12 = (bf16[2304,128]{1,0:T(8,128)(2,1)S(1)}, bf16[2304,128]{1,0:T(8,128)(2,1)S(1)}, u32[]{:S(2)}, u32[]{:S(2)}) collective-permute-start(bf16[2304,128]{1,0:T(8,128)(2,1)S(1)} %all_gather.39.mine), channel_id=1, source_target_pairs={{0,16},{16,0},{1,17},{17,1},{2,18},{18,2},{3,19},{19,3},{4,20},{20... | collective-permute-start | bytes 1769480 | tf_op jit(solution)/shard_map/ppermute | solution.py:391
  (1 other events, 6.6 us)

commit v10 on v9

--- a/solution.py
+++ b/solution.py
@@ -135,9 +135,10 @@
     )(meta, queries, k_cache, v_cache, k_other, v_other)
 
 
-def attend_new_kernel(meta, queries, fresh_rows, num, den):
+def attend_new_kernel(meta, queries, own, right, far, left, num, den, kind):
     here = meta[3 * REQS + 3]
-    rows, count = queries.shape[0], fresh_rows.shape[0] // 2
+    on_core_0 = meta[3 * REQS + 2] == 0
+    rows, count = queries.shape[0], 4
     request = lax.div(meta[3 * REQS + 1] - here * rows, NEWTOK)
     row = lax.broadcasted_iota(jnp.int32, (rows, 1), 0) + here * rows
     start, limit = jnp.zeros_like(row), jnp.zeros_like(row)
@@ -146,14 +147,18 @@
         inside = (row >= at) & (row < at + NEWTOK)
         start = jnp.where(inside, at, start)
         limit = jnp.where(inside, jnp.minimum(row, at + meta[REQS + request + part] - 1), limit)
-    keys = jnp.concatenate([fresh_rows[2 * step] for step in range(count)], axis=0)
-    values = jnp.concatenate([fresh_rows[2 * step + 1] for step in range(count)], axis=0)
-    logits = lax.dot_general(queries[...], keys, (((1,), (1,)), ((), ())), preferred_element_type=F32)
-    column = lax.broadcasted_iota(jnp.int32, logits.shape, 1)
-    weight = jnp.exp(soft_cap * jnp.tanh(logits * (1.0 / soft_cap)))
-    weight = jnp.where((column >= start) & (column <= limit), weight, 0.0)
-    den[...] = jnp.sum(weight, axis=1, keepdims=True)
-    num[...] = jnp.dot(weight.astype(BF16), values, preferred_element_type=F32)
+    total, weights = jnp.zeros((rows, HD), F32), jnp.zeros((rows, 1), F32)
+    for step, block in enumerate((own, right, far, left)):
+        at = lax.rem(here + step, count) * rows
+        logits = lax.dot_general(queries[...], block[0], (((1,), (1,)), ((), ())), preferred_element_type=F32)
+        column = lax.broadcasted_iota(jnp.int32, logits.shape, 1) + at
+        weight = jnp.exp(soft_cap * jnp.tanh(logits * (1.0 / soft_cap)))
+        weight = jnp.where((column >= start) & (column <= limit), weight, 0.0)
+        weights += jnp.sum(weight, axis=1, keepdims=True)
+        total += jnp.dot(weight.astype(BF16), block[1], preferred_element_type=F32)
+        kind[pl.ds(pl.multiple_of(at, 16), rows), :] = jnp.where(on_core_0, block[0], block[1])
+    num[...] = total
+    den[...] = weights
 
 
 def attend_new(meta, queries, fresh_rows):
@@ -161,12 +166,16 @@
     rows = queries.shape[0]
     return pl.pallas_call(
         attend_new_kernel,
-        out_shape=(jax.ShapeDtypeStruct((rows, HD), F32), jax.ShapeDtypeStruct((rows, 1), F32)),
-        in_specs=[pl.BlockSpec(memory_space=pltpu.SMEM), vmem, vmem],
-        out_specs=(vmem, vmem),
+        out_shape=(
+            jax.ShapeDtypeStruct((rows, HD), F32),
+            jax.ShapeDtypeStruct((rows, 1), F32),
+            jax.ShapeDtypeStruct((len(fresh_rows) * rows, HD), BF16),
+        ),
+        in_specs=[pl.BlockSpec(memory_space=pltpu.SMEM)] + [vmem] * (1 + len(fresh_rows)),
+        out_specs=(vmem, vmem, vmem),
         compiler_params=pltpu.CompilerParams(vmem_limit_bytes=16 << 20),
         name="attend_new",
-    )(meta, queries, fresh_rows)
+    )(meta, queries, *fresh_rows)
 
 
 def write_kernel(meta, mine, others, k_old, v_old, k_pool, v_pool):
@@ -359,9 +368,12 @@
     out_left = lax.ppermute(w_out, "x", from_left)
     near_rows = lax.all_gather(fresh_rows, "c", axis=0)
     all_queries = everywhere(queries, CHIPS, n_chips).reshape(-1, HD)
-    all_queries, near_rows, out_right, out_left = lax.optimization_barrier(
-        (all_queries, near_rows, out_right, out_left)
-    )
+    all_queries, near_rows = lax.optimization_barrier((all_queries, near_rows))
+    sums = attend(meta, all_queries, k_cache, v_cache, k_other, v_other)
+    sums, near_rows, out_right, out_left = lax.optimization_barrier((sums, near_rows, out_right, out_left))
+    near_rows = [near_rows] + [
+        lax.ppermute(near_rows, "x", [((i + step) % 4, i) for i in range(4)]) for step in (1, 2, 3)
+    ]
     out_columns = [
         w_out,
         out_right,
@@ -370,16 +382,13 @@
         out_left,
     ]
 
-    sums = attend(meta, all_queries, k_cache, v_cache, k_other, v_other)
-    sums, near_rows = lax.optimization_barrier((sums, near_rows))
-    near_rows = lax.all_gather(near_rows, "x", axis=0, tiled=True)
     parts = lax.all_to_all(sums.reshape(n_chips, -1, HD), CHIPS, 0, 0)
-    attended = divide(meta, parts, *attend_new(meta, queries, near_rows))
+    new_num, new_den, kind = attend_new(meta, queries, near_rows)
+    attended = divide(meta, parts, new_num, new_den)
     attended = lax.all_gather(attended, "c", axis=0)
     partial_out = spread(meta, attended, out_columns, n_gy)
-    partial_out, near_rows = lax.optimization_barrier((partial_out, near_rows))
-    kind = lax.dynamic_index_in_dim(near_rows.reshape(4, 2, 2 * tok_rows, HD), core, 1, keepdims=False)
-    kind = lax.all_gather(kind.reshape(-1, HD), "zh", axis=0, tiled=True)
+    partial_out, kind = lax.optimization_barrier((partial_out, kind))
+    kind = lax.all_gather(kind, "zh", axis=0, tiled=True)
     total = jnp.sum(lax.all_to_all(partial_out, GY, 0, 0).astype(F32), axis=0)
     rows = 2 * tok_rows
     rest = jnp.concatenate([total[rows : rows + 16], total[rows + 16 :, : rows - HD]], axis=1)

time: 201 us -> 198 us (0.985)
  blocking collectives: 76.6 us -> 69.4 us
  starting transfers between devices: 88.2 us -> 92.5 us
    all_gather x2 -> x1, blocking collectives: 33.7 us -> 23 us  [on_device(): kind = lax.all_gather(kind, 'zh', axis=0, tiled=True)]
    ppermute x0 -> x3, starting transfers between devices: none -> 9.45 us  [on_device(): lax.ppermute(near_rows, 'x', [((i + step) % 4, i) for i in range(4)])]
    all_to_all x1, starting transfers between devices: 14.1 us -> 8.46 us  [on_device(): total = jnp.sum(lax.all_to_all(partial_out, GY, 0, 0).astype(F32), axis=0)]
    ppermute x1, waiting for transfers between devices: 4.88 us -> 0.01 us  [on_device(): out_left = lax.ppermute(w_out, 'x', from_left)]
    all_gather x1, blocking collectives: 5.66 us -> 9.11 us  [on_device(): attended = lax.all_gather(attended, 'c', axis=0)]
    ppermute x0 -> x3, waiting for transfers between devices: none -> 2.44 us  [on_device(): lax.ppermute(near_rows, 'x', [((i + step) % 4, i) for i in range(4)])]
  transfers between devices with their start and end apart: 18 -> 21, of which waited for: 3 -> 4; matrix products, arithmetic and copies ran while one was open for 3% -> 3% of each run, Pallas kernels for 1% -> 3%
where the time goes in v10:
time: 198 us; the launch traced here: 197 us
  starting transfers between devices  92.5 us (47%)
  blocking collectives  69.4 us (35%)
  Pallas kernels  12.9 us (7%)
  waiting for transfers between devices  7.69 us (4%)
  local copies, waits for them, and re-layouts  7.13 us (4%)
  other arithmetic  5.76 us (3%)
    all_gather x1, blocking collectives, on_device(): kind = lax.all_gather(kind, 'zh', axis=0, tiled=True)  23 us
    all_gather x1, blocking collectives, on_device(): weights = lax.all_gather(weights, 'zh', axis=0)  22.5 us
    all_to_all x2, starting transfers between devices, everywhere(): lax.all_to_all(jnp.broadcast_to(value[None], (count,) + value.shape), axe...  14.9 us
    all_to_all x1, starting transfers between devices, on_device(): squares = lax.all_to_all(squares, ('c',) + GY, 0, 0)  12.1 us
    ppermute x3, starting transfers between devices, on_device(): lax.ppermute(near_rows, 'x', [((i + step) % 4, i) for i in range(4)])  9.45 us
    all_gather x1, blocking collectives, on_device(): attended = lax.all_gather(attended, 'c', axis=0)  9.11 us
    all_to_all x1, starting transfers between devices, on_device(): total = jnp.sum(lax.all_to_all(partial_out, GY, 0, 0).astype(F32), axis=0)  8.46 us
    all_to_all x1, starting transfers between devices, on_device(): parts = lax.all_to_all(sums.reshape(n_chips, -1, HD), CHIPS, 0, 0)  7.08 us
  transfers between devices with their start and end apart: 21, of which 4 were waited for; matrix products, arithmetic and copies ran while one was open for 3% of the time, Pallas kernels for 3%

profile of v10, /device:TPU:1, one launch (start us, length us, event | category | flops | bytes accessed | tf_op | source)
XLA Modules:
  0.0 196.5 jit_solution(6966752405042953890)
XLA Ops:
  4.2 5.1 %all_gather.27 = bf16[144,290]{1,0:T(8,128)(2,1)S(1)} all-gather(bf16[72,290]{1,0:T(8,128)(2,1)S(1)} %pad_maximum_fusion.6), channel_id=1, replica_groups=mesh['zh'=4,'x'=4,'c'=2,'y'=8,'zl'=2] {'zl'}, dimensions={0}, use_global_device_ids=true | all-gather | bytes 125280 | tf_op jit(solution)/shard_map/all_gather | solution.py:314
  10.3 7.0 %all-to-all-start = ((bf16[8,144,290]{2,1,0:T(8,128)(2,1)}), bf16[8,144,290]{2,1,0:T(8,128)(2,1)S(1)}, u32[]{:S(2)}, u32[]{:S(2)}) async-start(bf16[8,144,290]{2,1,0:T(8,128)(2,1)} %broadcast_in_dim.29), calls=%async_computation | async-start | bytes 1769472 | tf_op jit(solution)/shard_map/all_to_all | solution.py:27
  17.3 5.0 %all_gather.28 = bf16[288,512]{1,0:T(8,128)(2,1)S(1)} all-gather(bf16[144,512]{1,0:T(8,128)(2,1)S(1)} %pad_maximum_fusion.3), channel_id=1, replica_groups=mesh['zh'=4,'x'=4,'c'=2,'y'=8,'zl'=2] {'c'}, dimensions={0}, use_global_device_ids=true | all-gather | bytes 442368 | tf_op jit(solution)/shard_map/all_gather | solution.py:317
  22.3 22.5 %all-gather = bf16[1728,256]{1,0:T(8,128)(2,1)S(1)} all-gather(bf16[432,256]{1,0:T(8,128)(2,1)S(1)} %pad_maximum_fusion.1), channel_id=2, replica_groups=mesh['zh'=4,'x'=4,'c'=2,'y'=8,'zl'=2] {'zh'}, dimensions={0}, use_global_device_ids=true | all-gather | bytes 1105920 | tf_op jit(solution)/shard_map/all_gather | solution.py:321
  44.9 3.1 %collective-permute-start.5 = (bf16[4,288,256]{2,1,0:T(8,128)(2,1)S(1)}, bf16[4,288,256]{2,1,0:T(8,128)(2,1)S(1)}, u32[]{:S(2)}, u32[]{:S(2)}) collective-permute-start(bf16[4,288,256]{2,1,0:T(8,128)(2,1)S(1)} %slice.44.own), channel_id=1, source_target_pairs={{96,0},{0,32},{32,64},{64,96},{97,1},{1,33},{33,65},{65,97},{98,2}... | collective-permute-start | bytes 1769480 | tf_op jit(solution)/shard_map/ppermute | solution.py:327
  48.0 3.4 %collective-permute-start.3 = (bf16[4,288,256]{2,1,0:T(8,128)(2,1)S(1)}, bf16[4,288,256]{2,1,0:T(8,128)(2,1)S(1)}, u32[]{:S(2)}, u32[]{:S(2)}) collective-permute-start(bf16[4,288,256]{2,1,0:T(8,128)(2,1)S(1)} %slice.44.own), channel_id=1, source_target_pairs={{32,0},{64,32},{96,64},{0,96},{33,1},{65,33},{97,65},{1,97},{34,2}... | collective-permute-start | bytes 1769480 | tf_op jit(solution)/shard_map/ppermute | solution.py:326
  51.4 5.9 %collective-permute-start.1 = (bf16[1024,128]{1,0:T(8,128)(2,1)S(1)}, bf16[1024,128]{1,0:T(8,128)(2,1)}, u32[]{:S(2)}, u32[]{:S(2)}) collective-permute-start(bf16[1024,128]{1,0:T(8,128)(2,1)S(1)} %copy-done), channel_id=1, source_target_pairs={{0,16},{16,0},{1,17},{17,1},{2,18},{18,2},{3,19},{19,3},{4,20},{20... | collective-permute-start | bytes 786440 | tf_op jit(solution)/shard_map/ppermute | solution.py:361
  65.3 4.6 %collective-permute-start.4 = (bf16[2,288,256]{2,1,0:T(8,128)(2,1)}, bf16[2,288,256]{2,1,0:T(8,128)(2,1)}, u32[]{:S(2)}, u32[]{:S(2)}) collective-permute-start(bf16[2,288,256]{2,1,0:T(8,128)(2,1)} %slice.45), channel_id=1, source_target_pairs={{32,0},{64,32},{96,64},{0,96},{33,1},{65,33},{97,65},{1,97},{34,2}... | collective-permute-start | bytes 884744 | tf_op jit(solution)/shard_map/ppermute | solution.py:328
  77.4 8.0 %all-to-all-start.1 = ((bf16[16,144,128]{2,1,0:T(8,128)(2,1)}), bf16[16,144,128]{2,1,0:T(8,128)(2,1)S(1)}, u32[]{:S(2)}, u32[]{:S(2)}) async-start(bf16[16,144,128]{2,1,0:T(8,128)(2,1)} %broadcast_in_dim.54), calls=%async_computation.1 | async-start | bytes 1179648 | tf_op jit(solution)/shard_map/all_to_all | solution.py:27
  85.4 3.3 %collective-permute-start.8 = (bf16[4,144,256]{2,1,0:T(8,128)(2,1)S(1)}, bf16[4,144,256]{2,1,0:T(8,128)(2,1)S(1)}, u32[]{:S(2)}, u32[]{:S(2)}) collective-permute-start(bf16[4,144,256]{2,1,0:T(8,128)(2,1)S(1)} %slice.47.own), channel_id=1, source_target_pairs={{96,0},{0,32},{32,64},{64,96},{97,1},{1,33},{33,65},{65,97},{98,2}... | collective-permute-start | bytes 884744 | tf_op jit(solution)/shard_map/ppermute | solution.py:368
  88.7 3.2 %collective-permute-start.7 = (bf16[4,144,256]{2,1,0:T(8,128)(2,1)S(1)}, bf16[4,144,256]{2,1,0:T(8,128)(2,1)S(1)}, u32[]{:S(2)}, u32[]{:S(2)}) collective-permute-start(bf16[4,144,256]{2,1,0:T(8,128)(2,1)S(1)} %slice.47.own), channel_id=1, source_target_pairs={{32,0},{64,32},{96,64},{0,96},{33,1},{65,33},{97,65},{1,97},{34,2}... | collective-permute-start | bytes 884744 | tf_op jit(solution)/shard_map/ppermute | solution.py:367
  91.9 4.6 %all-gather.1 = bf16[288,128]{1,0:T(8,128)(2,1)S(1)} all-gather(bf16[144,128]{1,0:T(8,128)(2,1)S(1)} %get-tuple-element.34), channel_id=3, replica_groups=mesh['zh'=4,'x'=4,'c'=2,'y'=8,'zl'=2] {'c'}, dimensions={0}, use_global_device_ids=true | all-gather | bytes 110592 | tf_op jit(solution)/shard_map/all_gather | solution.py:369
  97.8 5.1 %attend.1 = bf16[2560,128]{1,0:T(8,128)(2,1)} custom-call(s32[40]{0:T(128)S(1)} %concatenate.62.meta, bf16[2304,128]{1,0:T(8,128)(2,1)S(1)} %bitcast.24, bf16[1024,128]{1,0:T(8,128)(2,1)S(1)} %copy-done, bf16[1024,128]{1,0:T(8,128)(2,1)S(1)} %copy-done.1, bf16[1024,128]{1,0:T(8,128)(2,1)} %collective-permute-done.1.k_other, ...), custom_call_target="tpu_custom_call" | custom-call | tf_op jit(solution)/shard_map/attend/pallas_call | solution.py:123
  102.9 7.1 %all-to-all-start.2 = ((bf16[16,160,128]{2,1,0:T(8,128)(2,1)}), bf16[16,160,128]{2,1,0:T(8,128)(2,1)S(1)}, u32[]{:S(2)}, u32[]{:S(2)}) async-start(bf16[16,160,128]{2,1,0:T(8,128)(2,1)} %bitcast.13), calls=%async_computation.2 | async-start | bytes 1310720 | tf_op jit(solution)/shard_map/all_to_all | solution.py:385
  110.0 3.3 %collective-permute-start.13 = (bf16[2,144,256]{2,1,0:T(8,128)(2,1)S(1)}, bf16[2,144,256]{2,1,0:T(8,128)(2,1)S(1)}, u32[]{:S(2)}, u32[]{:S(2)}) collective-permute-start(bf16[2,144,256]{2,1,0:T(8,128)(2,1)S(1)} %slice.40), channel_id=1, source_target_pairs={{96,0},{0,32},{32,64},{64,96},{97,1},{1,33},{33,65},{65,97},{98,2}... | collective-permute-start | bytes 442376 | tf_op jit(solution)/shard_map/ppermute | solution.py:381
  113.3 3.2 %collective-permute-start.12 = (bf16[2,144,256]{2,1,0:T(8,128)(2,1)S(1)}, bf16[2,144,256]{2,1,0:T(8,128)(2,1)S(1)}, u32[]{:S(2)}, u32[]{:S(2)}) collective-permute-start(bf16[2,144,256]{2,1,0:T(8,128)(2,1)S(1)} %slice.39), channel_id=1, source_target_pairs={{32,0},{64,32},{96,64},{0,96},{33,1},{65,33},{97,65},{1,97},{34,2}... | collective-permute-start | bytes 442376 | tf_op jit(solution)/shard_map/ppermute | solution.py:380
  118.6 4.3 %collective-permute-start.10 = (bf16[2,144,128]{2,1,0:T(8,128)(2,1)S(1)}, bf16[2,144,128]{2,1,0:T(8,128)(2,1)S(1)}, u32[]{:S(2)}, u32[]{:S(2)}) collective-permute-start(bf16[2,144,128]{2,1,0:T(8,128)(2,1)S(1)} %bitcast.27), channel_id=1, source_target_pairs={{64,0},{96,32},{0,64},{32,96},{65,1},{97,33},{1,65},{33,97},{66,2}... | collective-permute-start | bytes 221192 | tf_op jit(solution)/shard_map/ppermute | solution.py:375
  122.9 3.1 %collective-permute-start.9 = (bf16[2,144,128]{2,1,0:T(8,128)(2,1)S(1)}, bf16[2,144,128]{2,1,0:T(8,128)(2,1)S(1)}, u32[]{:S(2)}, u32[]{:S(2)}) collective-permute-start(bf16[2,144,128]{2,1,0:T(8,128)(2,1)S(1)} %bitcast.28), channel_id=1, source_target_pairs={{32,0},{64,32},{96,64},{0,96},{33,1},{65,33},{97,65},{1,97},{34,2}... | collective-permute-start | bytes 221192 | tf_op jit(solution)/shard_map/ppermute | solution.py:375
  126.1 2.4 %collective-permute-done.9.right = bf16[2,144,128]{2,1,0:T(8,128)(2,1)S(1)} collective-permute-done((bf16[2,144,128]{2,1,0:T(8,128)(2,1)S(1)}, bf16[2,144,128]{2,1,0:T(8,128)(2,1)S(1)}, u32[]{:S(2)}, u32[]{:S(2)}) %collective-permute-start.9) | collective-permute-done | bytes 73760 | tf_op jit(solution)/shard_map/ppermute | solution.py:375
  130.3 9.1 %all-gather.2 = bf16[288,128]{1,0:T(8,128)(2,1)S(1)} all-gather(bf16[144,128]{1,0:T(8,128)(2,1)S(1)} %divide.1), channel_id=4, replica_groups=mesh['zh'=4,'x'=4,'c'=2,'y'=8,'zl'=2] {'c'}, dimensions={0}, use_global_device_ids=true | all-gather | bytes 110592 | tf_op jit(solution)/shard_map/all_gather | solution.py:388
  141.6 8.5 %all-to-all-start.3 = ((bf16[16,176,128]{2,1,0:T(8,128)(2,1)}), bf16[16,176,128]{2,1,0:T(8,128)(2,1)S(1)}, u32[]{:S(2)}, u32[]{:S(2)}) async-start(bf16[16,176,128]{2,1,0:T(8,128)(2,1)} %spread.1), calls=%async_computation.3 | async-start | bytes 1441792 | tf_op jit(solution)/shard_map/all_to_all | solution.py:392
  150.1 23.0 %all_gather.35.mine = bf16[2304,128]{1,0:T(8,128)(2,1)S(1)} all-gather(bf16[576,128]{1,0:T(8,128)(2,1)S(1)} %get-tuple-element.48), channel_id=1, replica_groups=mesh['zh'=4,'x'=4,'c'=2,'y'=8,'zl'=2] {'zh'}, dimensions={0}, use_global_device_ids=true | all-gather | bytes 737280 | tf_op jit(solution)/shard_map/all_gather | solution.py:391
  174.2 12.1 %all-to-all-start.4 = ((f32[32,1,72]{2,1,0:T(1,128)}), f32[32,1,72]{2,1,0:T(1,128)S(1)}, u32[]{:S(2)}, u32[]{:S(2)}) async-start(f32[32,1,72]{2,1,0:T(1,128)} %bitcast.16), calls=%async_computation.4 | async-start | bytes 32768 | tf_op jit(solution)/shard_map/all_to_all | solution.py:399
  190.7 3.4 %all-to-all-done.4 = f32[32,1,72]{2,1,0:T(1,128)S(1)} async-done(((f32[32,1,72]{2,1,0:T(1,128)}), f32[32,1,72]{2,1,0:T(1,128)S(1)}, u32[]{:S(2)}, u32[]{:S(2)}) %all-to-all-start.4) | async-done | bytes 9248 | tf_op jit(solution)/shard_map/all_to_all | solution.py:399
  (85 shorter events, 35.2 us)
Async XLA Ops:
  10.3 49.1 %all-to-all-start = ((bf16[8,144,290]{2,1,0:T(8,128)(2,1)}), bf16[8,144,290]{2,1,0:T(8,128)(2,1)S(1)}, u32[]{:S(2)}, u32[]{:S(2)}) async-start(bf16[8,144,290]{2,1,0:T(8,128)(2,1)} %broadcast_in_dim.29), calls=%async_computation | async-start | bytes 1769472 | tf_op jit(solution)/shard_map/all_to_all | solution.py:27
  22.3 29.1 %copy-start = (bf16[1024,128]{1,0:T(8,128)(2,1)S(1)}, bf16[1024,128]{1,0:T(8,128)(2,1)}, u32[]{:S(2)}) copy-start(bf16[1024,128]{1,0:T(8,128)(2,1)} %k_old.1) | copy-start | bytes 786436
  22.3 35.0 %copy-start.1 = (bf16[1024,128]{1,0:T(8,128)(2,1)S(1)}, bf16[1024,128]{1,0:T(8,128)(2,1)}, u32[]{:S(2)}) copy-start(bf16[1024,128]{1,0:T(8,128)(2,1)} %v_old.1) | copy-start | bytes 786436
  44.9 17.0 %collective-permute-start.5 = (bf16[4,288,256]{2,1,0:T(8,128)(2,1)S(1)}, bf16[4,288,256]{2,1,0:T(8,128)(2,1)S(1)}, u32[]{:S(2)}, u32[]{:S(2)}) collective-permute-start(bf16[4,288,256]{2,1,0:T(8,128)(2,1)S(1)} %slice.44.own), channel_id=1, source_target_pairs={{96,0},{0,32},{32,64},{64,96},{97,1},{1,33},{33,65},{65,97},{98,2}... | collective-permute-start | bytes 1769480 | tf_op jit(solution)/shard_map/ppermute | solution.py:327
  48.0 16.5 %collective-permute-start.3 = (bf16[4,288,256]{2,1,0:T(8,128)(2,1)S(1)}, bf16[4,288,256]{2,1,0:T(8,128)(2,1)S(1)}, u32[]{:S(2)}, u32[]{:S(2)}) collective-permute-start(bf16[4,288,256]{2,1,0:T(8,128)(2,1)S(1)} %slice.44.own), channel_id=1, source_target_pairs={{32,0},{64,32},{96,64},{0,96},{33,1},{65,33},{97,65},{1,97},{34,2}... | collective-permute-start | bytes 1769480 | tf_op jit(solution)/shard_map/ppermute | solution.py:326
  51.4 22.3 %collective-permute-start.1 = (bf16[1024,128]{1,0:T(8,128)(2,1)S(1)}, bf16[1024,128]{1,0:T(8,128)(2,1)}, u32[]{:S(2)}, u32[]{:S(2)}) collective-permute-start(bf16[1024,128]{1,0:T(8,128)(2,1)S(1)} %copy-done), channel_id=1, source_target_pairs={{0,16},{16,0},{1,17},{17,1},{2,18},{18,2},{3,19},{19,3},{4,20},{20... | collective-permute-start | bytes 786440 | tf_op jit(solution)/shard_map/ppermute | solution.py:361
  57.3 16.4 %collective-permute-start.2 = (bf16[1024,128]{1,0:T(8,128)(2,1)S(1)}, bf16[1024,128]{1,0:T(8,128)(2,1)}, u32[]{:S(2)}, u32[]{:S(2)}) collective-permute-start(bf16[1024,128]{1,0:T(8,128)(2,1)S(1)} %copy-done.1), channel_id=1, source_target_pairs={{0,16},{16,0},{1,17},{17,1},{2,18},{18,2},{3,19},{19,3},{4,20},{20... | collective-permute-start | bytes 786440 | tf_op jit(solution)/shard_map/ppermute | solution.py:362
  59.4 14.3 %collective-permute-start = (bf16[16,72,290]{2,1,0:T(8,128)(2,1)S(1)}, bf16[16,72,290]{2,1,0:T(8,128)(2,1)}, u32[]{:S(2)}, u32[]{:S(2)}) collective-permute-start(bf16[16,72,290]{2,1,0:T(8,128)(2,1)S(1)} %bitcast.22), channel_id=1, source_target_pairs={{0,16},{16,0},{1,17},{17,1},{2,18},{18,2},{3,19},{19,3},{4,20},{20... | collective-permute-start | bytes 2004488 | tf_op jit(solution)/shard_map/ppermute | solution.py:332
  62.6 11.1 %collective-permute-start.6 = (bf16[2,288,256]{2,1,0:T(8,128)(2,1)}, bf16[2,288,256]{2,1,0:T(8,128)(2,1)}, u32[]{:S(2)}, u32[]{:S(2)}) collective-permute-start(bf16[2,288,256]{2,1,0:T(8,128)(2,1)} %slice.46), channel_id=1, source_target_pairs={{96,0},{0,32},{32,64},{64,96},{97,1},{1,33},{33,65},{65,97},{98,2}... | collective-permute-start | bytes 884744 | tf_op jit(solution)/shard_map/ppermute | solution.py:329
  65.3 9.0 %collective-permute-start.4 = (bf16[2,288,256]{2,1,0:T(8,128)(2,1)}, bf16[2,288,256]{2,1,0:T(8,128)(2,1)}, u32[]{:S(2)}, u32[]{:S(2)}) collective-permute-start(bf16[2,288,256]{2,1,0:T(8,128)(2,1)} %slice.45), channel_id=1, source_target_pairs={{32,0},{64,32},{96,64},{0,96},{33,1},{65,33},{97,65},{1,97},{34,2}... | collective-permute-start | bytes 884744 | tf_op jit(solution)/shard_map/ppermute | solution.py:328
  77.4 20.4 %all-to-all-start.1 = ((bf16[16,144,128]{2,1,0:T(8,128)(2,1)}), bf16[16,144,128]{2,1,0:T(8,128)(2,1)S(1)}, u32[]{:S(2)}, u32[]{:S(2)}) async-start(bf16[16,144,128]{2,1,0:T(8,128)(2,1)} %broadcast_in_dim.54), calls=%async_computation.1 | async-start | bytes 1179648 | tf_op jit(solution)/shard_map/all_to_all | solution.py:27
  85.4 17.5 %collective-permute-start.8 = (bf16[4,144,256]{2,1,0:T(8,128)(2,1)S(1)}, bf16[4,144,256]{2,1,0:T(8,128)(2,1)S(1)}, u32[]{:S(2)}, u32[]{:S(2)}) collective-permute-start(bf16[4,144,256]{2,1,0:T(8,128)(2,1)S(1)} %slice.47.own), channel_id=1, source_target_pairs={{96,0},{0,32},{32,64},{64,96},{97,1},{1,33},{33,65},{65,97},{98,2}... | collective-permute-start | bytes 884744 | tf_op jit(solution)/shard_map/ppermute | solution.py:368
  88.7 14.2 %collective-permute-start.7 = (bf16[4,144,256]{2,1,0:T(8,128)(2,1)S(1)}, bf16[4,144,256]{2,1,0:T(8,128)(2,1)S(1)}, u32[]{:S(2)}, u32[]{:S(2)}) collective-permute-start(bf16[4,144,256]{2,1,0:T(8,128)(2,1)S(1)} %slice.47.own), channel_id=1, source_target_pairs={{32,0},{64,32},{96,64},{0,96},{33,1},{65,33},{97,65},{1,97},{34,2}... | collective-permute-start | bytes 884744 | tf_op jit(solution)/shard_map/ppermute | solution.py:367
  102.9 26.6 %all-to-all-start.2 = ((bf16[16,160,128]{2,1,0:T(8,128)(2,1)}), bf16[16,160,128]{2,1,0:T(8,128)(2,1)S(1)}, u32[]{:S(2)}, u32[]{:S(2)}) async-start(bf16[16,160,128]{2,1,0:T(8,128)(2,1)} %bitcast.13), calls=%async_computation.2 | async-start | bytes 1310720 | tf_op jit(solution)/shard_map/all_to_all | solution.py:385
  110.0 29.4 %collective-permute-start.13 = (bf16[2,144,256]{2,1,0:T(8,128)(2,1)S(1)}, bf16[2,144,256]{2,1,0:T(8,128)(2,1)S(1)}, u32[]{:S(2)}, u32[]{:S(2)}) collective-permute-start(bf16[2,144,256]{2,1,0:T(8,128)(2,1)S(1)} %slice.40), channel_id=1, source_target_pairs={{96,0},{0,32},{32,64},{64,96},{97,1},{1,33},{33,65},{65,97},{98,2}... | collective-permute-start | bytes 442376 | tf_op jit(solution)/shard_map/ppermute | solution.py:381
  113.3 26.1 %collective-permute-start.12 = (bf16[2,144,256]{2,1,0:T(8,128)(2,1)S(1)}, bf16[2,144,256]{2,1,0:T(8,128)(2,1)S(1)}, u32[]{:S(2)}, u32[]{:S(2)}) collective-permute-start(bf16[2,144,256]{2,1,0:T(8,128)(2,1)S(1)} %slice.39), channel_id=1, source_target_pairs={{32,0},{64,32},{96,64},{0,96},{33,1},{65,33},{97,65},{1,97},{34,2}... | collective-permute-start | bytes 442376 | tf_op jit(solution)/shard_map/ppermute | solution.py:380
  116.6 9.5 %collective-permute-start.11 = (bf16[2,144,128]{2,1,0:T(8,128)(2,1)S(1)}, bf16[2,144,128]{2,1,0:T(8,128)(2,1)S(1)}, u32[]{:S(2)}, u32[]{:S(2)}) collective-permute-start(bf16[2,144,128]{2,1,0:T(8,128)(2,1)S(1)} %bitcast.26), channel_id=1, source_target_pairs={{96,0},{0,32},{32,64},{64,96},{97,1},{1,33},{33,65},{65,97},{98,2}... | collective-permute-start | bytes 221192 | tf_op jit(solution)/shard_map/ppermute | solution.py:375
  118.6 7.4 %collective-permute-start.10 = (bf16[2,144,128]{2,1,0:T(8,128)(2,1)S(1)}, bf16[2,144,128]{2,1,0:T(8,128)(2,1)S(1)}, u32[]{:S(2)}, u32[]{:S(2)}) collective-permute-start(bf16[2,144,128]{2,1,0:T(8,128)(2,1)S(1)} %bitcast.27), channel_id=1, source_target_pairs={{64,0},{96,32},{0,64},{32,96},{65,1},{97,33},{1,65},{33,97},{66,2}... | collective-permute-start | bytes 221192 | tf_op jit(solution)/shard_map/ppermute | solution.py:375
  122.9 5.5 %collective-permute-start.9 = (bf16[2,144,128]{2,1,0:T(8,128)(2,1)S(1)}, bf16[2,144,128]{2,1,0:T(8,128)(2,1)S(1)}, u32[]{:S(2)}, u32[]{:S(2)}) collective-permute-start(bf16[2,144,128]{2,1,0:T(8,128)(2,1)S(1)} %bitcast.28), channel_id=1, source_target_pairs={{32,0},{64,32},{96,64},{0,96},{33,1},{65,33},{97,65},{1,97},{34,2}... | collective-permute-start | bytes 221192 | tf_op jit(solution)/shard_map/ppermute | solution.py:375
  141.6 31.5 %all-to-all-start.3 = ((bf16[16,176,128]{2,1,0:T(8,128)(2,1)}), bf16[16,176,128]{2,1,0:T(8,128)(2,1)S(1)}, u32[]{:S(2)}, u32[]{:S(2)}) async-start(bf16[16,176,128]{2,1,0:T(8,128)(2,1)} %spread.1), calls=%async_computation.3 | async-start | bytes 1441792 | tf_op jit(solution)/shard_map/all_to_all | solution.py:392
  173.1 21.0 %copy-start.3 = (bf16[72,288]{1,0:T(8,128)(2,1)S(1)}, bf16[72,288]{1,0:T(8,128)(2,1)}, u32[]{:S(2)}) copy-start(bf16[72,288]{1,0:T(8,128)(2,1)} %param.12) | copy-start | bytes 124420
  174.2 19.8 %all-to-all-start.4 = ((f32[32,1,72]{2,1,0:T(1,128)}), f32[32,1,72]{2,1,0:T(1,128)S(1)}, u32[]{:S(2)}, u32[]{:S(2)}) async-start(f32[32,1,72]{2,1,0:T(1,128)} %bitcast.16), calls=%async_computation.4 | async-start | bytes 32768 | tf_op jit(solution)/shard_map/all_to_all | solution.py:399
  186.3 7.8 %collective-permute-start.14 = (f32[72,144]{1,0:T(8,128)S(1)}, f32[72,144]{1,0:T(8,128)S(1)}, u32[]{:S(2)}, u32[]{:S(2)}) collective-permute-start(f32[72,144]{1,0:T(8,128)S(1)} %fusion.11), channel_id=1, source_target_pairs={{0,16},{16,0},{1,17},{17,1},{2,18},{18,2},{3,19},{19,3},{4,20},{20... | collective-permute-start | bytes 124424 | tf_op jit(solution)/shard_map/ppermute | solution.py:404
  188.5 6.4 %collective-permute-start.15 = (bf16[2304,128]{1,0:T(8,128)(2,1)S(1)}, bf16[2304,128]{1,0:T(8,128)(2,1)S(1)}, u32[]{:S(2)}, u32[]{:S(2)}) collective-permute-start(bf16[2304,128]{1,0:T(8,128)(2,1)S(1)} %all_gather.35.mine), channel_id=1, source_target_pairs={{0,16},{16,0},{1,17},{17,1},{2,18},{18,2},{3,19},{19,3},{4,20},{20... | collective-permute-start | bytes 1769480 | tf_op jit(solution)/shard_map/ppermute | solution.py:400
  (4 other events, 41.5 us)

commit v11 on v10

--- a/solution.py
+++ b/solution.py
@@ -135,7 +135,7 @@
     )(meta, queries, k_cache, v_cache, k_other, v_other)
 
 
-def attend_new_kernel(meta, queries, own, right, far, left, num, den, kind):
+def attend_new_kernel(meta, queries, near, far, num, den, kind):
     here = meta[3 * REQS + 3]
     on_core_0 = meta[3 * REQS + 2] == 0
     rows, count = queries.shape[0], 4
@@ -148,8 +148,9 @@
         start = jnp.where(inside, at, start)
         limit = jnp.where(inside, jnp.minimum(row, at + meta[REQS + request + part] - 1), limit)
     total, weights = jnp.zeros((rows, HD), F32), jnp.zeros((rows, 1), F32)
-    for step, block in enumerate((own, right, far, left)):
-        at = lax.rem(here + step, count) * rows
+    for step in range(count):
+        block = (near if step < 2 else far)[step % 2]
+        at = lax.bitwise_xor(here, step) * rows
         logits = lax.dot_general(queries[...], block[0], (((1,), (1,)), ((), ())), preferred_element_type=F32)
         column = lax.broadcasted_iota(jnp.int32, logits.shape, 1) + at
         weight = jnp.exp(soft_cap * jnp.tanh(logits * (1.0 / soft_cap)))
@@ -161,7 +162,7 @@
     den[...] = weights
 
 
-def attend_new(meta, queries, fresh_rows):
+def attend_new(meta, queries, near, far):
     vmem = pl.BlockSpec(memory_space=pltpu.VMEM)
     rows = queries.shape[0]
     return pl.pallas_call(
@@ -169,13 +170,13 @@
         out_shape=(
             jax.ShapeDtypeStruct((rows, HD), F32),
             jax.ShapeDtypeStruct((rows, 1), F32),
-            jax.ShapeDtypeStruct((len(fresh_rows) * rows, HD), BF16),
+            jax.ShapeDtypeStruct((4 * rows, HD), BF16),
         ),
-        in_specs=[pl.BlockSpec(memory_space=pltpu.SMEM)] + [vmem] * (1 + len(fresh_rows)),
+        in_specs=[pl.BlockSpec(memory_space=pltpu.SMEM)] + [vmem] * 3,
         out_specs=(vmem, vmem, vmem),
         compiler_params=pltpu.CompilerParams(vmem_limit_bytes=16 << 20),
         name="attend_new",
-    )(meta, queries, *fresh_rows)
+    )(meta, queries, near, far)
 
 
 def write_kernel(meta, mine, others, k_old, v_old, k_pool, v_pool):
@@ -367,13 +368,12 @@
     out_right = lax.ppermute(w_out, "x", from_right)
     out_left = lax.ppermute(w_out, "x", from_left)
     near_rows = lax.all_gather(fresh_rows, "c", axis=0)
+    near_rows = jnp.stack([near_rows, lax.ppermute(near_rows, "x", [(i, i ^ 1) for i in range(4)])])
     all_queries = everywhere(queries, CHIPS, n_chips).reshape(-1, HD)
     all_queries, near_rows = lax.optimization_barrier((all_queries, near_rows))
     sums = attend(meta, all_queries, k_cache, v_cache, k_other, v_other)
     sums, near_rows, out_right, out_left = lax.optimization_barrier((sums, near_rows, out_right, out_left))
-    near_rows = [near_rows] + [
-        lax.ppermute(near_rows, "x", [((i + step) % 4, i) for i in range(4)]) for step in (1, 2, 3)
-    ]
+    far_rows = lax.ppermute(near_rows, "x", [(i, i ^ 2) for i in range(4)])
     out_columns = [
         w_out,
         out_right,
@@ -383,7 +383,7 @@
     ]
 
     parts = lax.all_to_all(sums.reshape(n_chips, -1, HD), CHIPS, 0, 0)
-    new_num, new_den, kind = attend_new(meta, queries, near_rows)
+    new_num, new_den, kind = attend_new(meta, queries, near_rows, far_rows)
     attended = divide(meta, parts, new_num, new_den)
     attended = lax.all_gather(attended, "c", axis=0)
     partial_out = spread(meta, attended, out_columns, n_gy)

time: 198 us -> 195 us (0.985)
  blocking collectives: 69.4 us -> 64.3 us
  waiting for transfers between devices: 7.69 us -> 10.6 us
    all_gather x1, blocking collectives: 9.11 us -> 5.1 us  [on_device(): attended = lax.all_gather(attended, 'c', axis=0)]
    all_to_all x1, starting transfers between devices: 8.46 us -> 11.8 us  [on_device(): total = jnp.sum(lax.all_to_all(partial_out, GY, 0, 0).astype(F32), axis=0)]
    ppermute x3 -> x2, waiting for transfers between devices: 2.44 us -> 4.8 us  [the longest x1 4.29 us: on_device(): lax.ppermute(near_rows, 'x', [(i, i ^ 1) for i in range(4)])]
    ppermute x3 -> x2, starting transfers between devices: 9.45 us -> 7.09 us  [the longest x1 4.77 us: on_device(): far_rows = lax.ppermute(near_rows, 'x', [(i, i ^ 2) for i in range(4)])]
    all_to_all x1, starting transfers between devices: 12.1 us -> 9.95 us  [on_device(): squares = lax.all_to_all(squares, ('c',) + GY, 0, 0)]
  transfers between devices with their start and end apart: 21 -> 20, of which waited for: 4 -> 5; matrix products, arithmetic and copies ran while one was open for 3% -> 3% of each run, Pallas kernels for 3% -> 3%
where the time goes in v11:
time: 195 us; the launch traced here: 193 us
  starting transfers between devices  92.1 us (47%)
  blocking collectives  64.3 us (33%)
  Pallas kernels  12.5 us (6%)
  waiting for transfers between devices  10.6 us (5%)
  local copies, waits for them, and re-layouts  7.12 us (4%)
  other arithmetic  5.78 us (3%)
    all_gather x1, blocking collectives, on_device(): weights = lax.all_gather(weights, 'zh', axis=0)  22.5 us
    all_gather x1, blocking collectives, on_device(): kind = lax.all_gather(kind, 'zh', axis=0, tiled=True)  22 us
    all_to_all x2, starting transfers between devices, everywhere(): lax.all_to_all(jnp.broadcast_to(value[None], (count,) + value.shape), axe...  14.9 us
    all_to_all x1, starting transfers between devices, on_device(): total = jnp.sum(lax.all_to_all(partial_out, GY, 0, 0).astype(F32), axis=0)  11.8 us
    all_to_all x1, starting transfers between devices, on_device(): squares = lax.all_to_all(squares, ('c',) + GY, 0, 0)  9.95 us
    all_to_all x1, starting transfers between devices, on_device(): parts = lax.all_to_all(sums.reshape(n_chips, -1, HD), CHIPS, 0, 0)  7.74 us
    ppermute x1, starting transfers between devices, on_device(): k_other = lax.ppermute(k_cache, 'c', swap)  5.88 us
    all_gather x1, blocking collectives, on_device(): gained = lax.all_gather(gained, 'zl', axis=0, tiled=True)  5.12 us
  transfers between devices with their start and end apart: 20, of which 5 were waited for; matrix products, arithmetic and copies ran while one was open for 3% of the time, Pallas kernels for 3%

profile of v11, /device:TPU:1, one launch (start us, length us, event | category | flops | bytes accessed | tf_op | source)
XLA Modules:
  0.0 193.5 jit_solution(18276683036891290224)
XLA Ops:
  4.2 5.1 %all_gather.27 = bf16[144,290]{1,0:T(8,128)(2,1)S(1)} all-gather(bf16[72,290]{1,0:T(8,128)(2,1)S(1)} %pad_maximum_fusion.7), channel_id=1, replica_groups=mesh['zh'=4,'x'=4,'c'=2,'y'=8,'zl'=2] {'zl'}, dimensions={0}, use_global_device_ids=true | all-gather | bytes 125280 | tf_op jit(solution)/shard_map/all_gather | solution.py:315
  10.3 7.0 %all-to-all-start = ((bf16[8,144,290]{2,1,0:T(8,128)(2,1)}), bf16[8,144,290]{2,1,0:T(8,128)(2,1)S(1)}, u32[]{:S(2)}, u32[]{:S(2)}) async-start(bf16[8,144,290]{2,1,0:T(8,128)(2,1)} %broadcast_in_dim.29), calls=%async_computation | async-start | bytes 1769472 | tf_op jit(solution)/shard_map/all_to_all | solution.py:27
  17.3 5.0 %all_gather.28 = bf16[288,512]{1,0:T(8,128)(2,1)S(1)} all-gather(bf16[144,512]{1,0:T(8,128)(2,1)S(1)} %pad_maximum_fusion.3), channel_id=1, replica_groups=mesh['zh'=4,'x'=4,'c'=2,'y'=8,'zl'=2] {'c'}, dimensions={0}, use_global_device_ids=true | all-gather | bytes 442368 | tf_op jit(solution)/shard_map/all_gather | solution.py:318
  22.3 22.5 %all-gather = bf16[1728,256]{1,0:T(8,128)(2,1)S(1)} all-gather(bf16[432,256]{1,0:T(8,128)(2,1)S(1)} %pad_maximum_fusion.1), channel_id=2, replica_groups=mesh['zh'=4,'x'=4,'c'=2,'y'=8,'zl'=2] {'zh'}, dimensions={0}, use_global_device_ids=true | all-gather | bytes 1105920 | tf_op jit(solution)/shard_map/all_gather | solution.py:322
  44.9 3.1 %collective-permute-start.5 = (bf16[4,288,256]{2,1,0:T(8,128)(2,1)S(1)}, bf16[4,288,256]{2,1,0:T(8,128)(2,1)S(1)}, u32[]{:S(2)}, u32[]{:S(2)}) collective-permute-start(bf16[4,288,256]{2,1,0:T(8,128)(2,1)S(1)} %slice.44.own), channel_id=1, source_target_pairs={{96,0},{0,32},{32,64},{64,96},{97,1},{1,33},{33,65},{65,97},{98,2}... | collective-permute-start | bytes 1769480 | tf_op jit(solution)/shard_map/ppermute | solution.py:328
  48.0 3.4 %collective-permute-start.3 = (bf16[4,288,256]{2,1,0:T(8,128)(2,1)S(1)}, bf16[4,288,256]{2,1,0:T(8,128)(2,1)S(1)}, u32[]{:S(2)}, u32[]{:S(2)}) collective-permute-start(bf16[4,288,256]{2,1,0:T(8,128)(2,1)S(1)} %slice.44.own), channel_id=1, source_target_pairs={{32,0},{64,32},{96,64},{0,96},{33,1},{65,33},{97,65},{1,97},{34,2}... | collective-permute-start | bytes 1769480 | tf_op jit(solution)/shard_map/ppermute | solution.py:327
  51.4 5.9 %collective-permute-start.1 = (bf16[1024,128]{1,0:T(8,128)(2,1)S(1)}, bf16[1024,128]{1,0:T(8,128)(2,1)}, u32[]{:S(2)}, u32[]{:S(2)}) collective-permute-start(bf16[1024,128]{1,0:T(8,128)(2,1)S(1)} %copy-done), channel_id=1, source_target_pairs={{0,16},{16,0},{1,17},{17,1},{2,18},{18,2},{3,19},{19,3},{4,20},{20... | collective-permute-start | bytes 786440 | tf_op jit(solution)/shard_map/ppermute | solution.py:362
  59.4 2.4 %collective-permute-start = (bf16[16,72,290]{2,1,0:T(8,128)(2,1)S(1)}, bf16[16,72,290]{2,1,0:T(8,128)(2,1)}, u32[]{:S(2)}, u32[]{:S(2)}) collective-permute-start(bf16[16,72,290]{2,1,0:T(8,128)(2,1)S(1)} %bitcast.24), channel_id=1, source_target_pairs={{0,16},{16,0},{1,17},{17,1},{2,18},{18,2},{3,19},{19,3},{4,20},{20... | collective-permute-start | bytes 2004488 | tf_op jit(solution)/shard_map/ppermute | solution.py:333
  65.3 4.6 %collective-permute-start.4 = (bf16[2,288,256]{2,1,0:T(8,128)(2,1)}, bf16[2,288,256]{2,1,0:T(8,128)(2,1)}, u32[]{:S(2)}, u32[]{:S(2)}) collective-permute-start(bf16[2,288,256]{2,1,0:T(8,128)(2,1)} %slice.45), channel_id=1, source_target_pairs={{32,0},{64,32},{96,64},{0,96},{33,1},{65,33},{97,65},{1,97},{34,2}... | collective-permute-start | bytes 884744 | tf_op jit(solution)/shard_map/ppermute | solution.py:329
  77.4 8.0 %all-to-all-start.1 = ((bf16[16,144,128]{2,1,0:T(8,128)(2,1)}), bf16[16,144,128]{2,1,0:T(8,128)(2,1)S(1)}, u32[]{:S(2)}, u32[]{:S(2)}) async-start(bf16[16,144,128]{2,1,0:T(8,128)(2,1)} %broadcast_in_dim.54), calls=%async_computation.1 | async-start | bytes 1179648 | tf_op jit(solution)/shard_map/all_to_all | solution.py:27
  85.4 3.3 %collective-permute-start.9 = (bf16[4,144,256]{2,1,0:T(8,128)(2,1)S(1)}, bf16[4,144,256]{2,1,0:T(8,128)(2,1)S(1)}, u32[]{:S(2)}, u32[]{:S(2)}) collective-permute-start(bf16[4,144,256]{2,1,0:T(8,128)(2,1)S(1)} %slice.47.own), channel_id=1, source_target_pairs={{96,0},{0,32},{32,64},{64,96},{97,1},{1,33},{33,65},{65,97},{98,2}... | collective-permute-start | bytes 884744 | tf_op jit(solution)/shard_map/ppermute | solution.py:369
  88.7 3.2 %collective-permute-start.8 = (bf16[4,144,256]{2,1,0:T(8,128)(2,1)S(1)}, bf16[4,144,256]{2,1,0:T(8,128)(2,1)S(1)}, u32[]{:S(2)}, u32[]{:S(2)}) collective-permute-start(bf16[4,144,256]{2,1,0:T(8,128)(2,1)S(1)} %slice.47.own), channel_id=1, source_target_pairs={{32,0},{64,32},{96,64},{0,96},{33,1},{65,33},{97,65},{1,97},{34,2}... | collective-permute-start | bytes 884744 | tf_op jit(solution)/shard_map/ppermute | solution.py:368
  91.9 4.6 %all-gather.1 = bf16[288,128]{1,0:T(8,128)(2,1)S(1)} all-gather(bf16[144,128]{1,0:T(8,128)(2,1)S(1)} %get-tuple-element.34), channel_id=3, replica_groups=mesh['zh'=4,'x'=4,'c'=2,'y'=8,'zl'=2] {'c'}, dimensions={0}, use_global_device_ids=true | all-gather | bytes 110592 | tf_op jit(solution)/shard_map/all_gather | solution.py:370
  96.6 2.3 %collective-permute-start.7 = (bf16[2,144,128]{2,1,0:T(8,128)(2,1)S(1)}, bf16[2,144,128]{2,1,0:T(8,128)(2,1)S(1)}, u32[]{:S(2)}, u32[]{:S(2)}) collective-permute-start(bf16[2,144,128]{2,1,0:T(8,128)(2,1)S(1)} %bitcast.33), channel_id=1, source_target_pairs={{0,32},{32,0},{64,96},{96,64},{1,33},{33,1},{65,97},{97,65},{2,34}... | collective-permute-start | bytes 221192 | tf_op jit(solution)/shard_map/ppermute | solution.py:371
  98.9 4.3 %collective-permute-done.7 = bf16[2,144,128]{2,1,0:T(8,128)(2,1)S(1)} collective-permute-done((bf16[2,144,128]{2,1,0:T(8,128)(2,1)S(1)}, bf16[2,144,128]{2,1,0:T(8,128)(2,1)S(1)}, u32[]{:S(2)}, u32[]{:S(2)}) %collective-permute-start.7) | collective-permute-done | bytes 73760 | tf_op jit(solution)/shard_map/ppermute | solution.py:371
  103.2 4.7 %attend.1 = bf16[2560,128]{1,0:T(8,128)(2,1)} custom-call(s32[40]{0:T(128)S(1)} %concatenate.62.meta, bf16[2304,128]{1,0:T(8,128)(2,1)S(1)} %bitcast.26, bf16[1024,128]{1,0:T(8,128)(2,1)S(1)} %copy-done, bf16[1024,128]{1,0:T(8,128)(2,1)S(1)} %copy-done.1, bf16[1024,128]{1,0:T(8,128)(2,1)} %collective-permute-done.1.k_other, ...), custom_call_target="tpu_custom_call" | custom-call | tf_op jit(solution)/shard_map/attend/pallas_call | solution.py:123
  107.9 7.7 %all-to-all-start.2 = ((bf16[16,160,128]{2,1,0:T(8,128)(2,1)}), bf16[16,160,128]{2,1,0:T(8,128)(2,1)S(1)}, u32[]{:S(2)}, u32[]{:S(2)}) async-start(bf16[16,160,128]{2,1,0:T(8,128)(2,1)} %bitcast.15), calls=%async_computation.2 | async-start | bytes 1310720 | tf_op jit(solution)/shard_map/all_to_all | solution.py:385
  115.7 4.8 %collective-permute-start.10 = (bf16[2,2,144,128]{3,2,1,0:T(8,128)(2,1)S(1)}, bf16[2,2,144,128]{3,2,1,0:T(8,128)(2,1)S(1)}, u32[]{:S(2)}, u32[]{:S(2)}) collective-permute-start(bf16[2,2,144,128]{3,2,1,0:T(8,128)(2,1)S(1)} %pad_maximum_fusion.4.near), channel_id=1, source_target_pairs={{0,64},{32,96},{64,0},{96,32},{1,65},{33,97},{65,1},{97,33},{2,66}... | collective-permute-start | bytes 442376 | tf_op jit(solution)/shard_map/ppermute | solution.py:376
  122.7 4.3 %collective-permute-start.11 = (bf16[2,144,256]{2,1,0:T(8,128)(2,1)S(1)}, bf16[2,144,256]{2,1,0:T(8,128)(2,1)S(1)}, u32[]{:S(2)}, u32[]{:S(2)}) collective-permute-start(bf16[2,144,256]{2,1,0:T(8,128)(2,1)S(1)} %slice.39), channel_id=1, source_target_pairs={{32,0},{64,32},{96,64},{0,96},{33,1},{65,33},{97,65},{1,97},{34,2}... | collective-permute-start | bytes 442376 | tf_op jit(solution)/shard_map/ppermute | solution.py:380
  131.1 5.1 %all-gather.2 = bf16[288,128]{1,0:T(8,128)(2,1)S(1)} all-gather(bf16[144,128]{1,0:T(8,128)(2,1)S(1)} %divide.1), channel_id=4, replica_groups=mesh['zh'=4,'x'=4,'c'=2,'y'=8,'zl'=2] {'c'}, dimensions={0}, use_global_device_ids=true | all-gather | bytes 110592 | tf_op jit(solution)/shard_map/all_gather | solution.py:388
  138.4 11.8 %all-to-all-start.3 = ((bf16[16,176,128]{2,1,0:T(8,128)(2,1)}), bf16[16,176,128]{2,1,0:T(8,128)(2,1)S(1)}, u32[]{:S(2)}, u32[]{:S(2)}) async-start(bf16[16,176,128]{2,1,0:T(8,128)(2,1)} %spread.1), calls=%async_computation.3 | async-start | bytes 1441792 | tf_op jit(solution)/shard_map/all_to_all | solution.py:392
  150.2 22.0 %all_gather.35.mine = bf16[2304,128]{1,0:T(8,128)(2,1)S(1)} all-gather(bf16[576,128]{1,0:T(8,128)(2,1)S(1)} %get-tuple-element.48), channel_id=1, replica_groups=mesh['zh'=4,'x'=4,'c'=2,'y'=8,'zl'=2] {'zh'}, dimensions={0}, use_global_device_ids=true | all-gather | bytes 737280 | tf_op jit(solution)/shard_map/all_gather | solution.py:391
  173.3 10.0 %all-to-all-start.4 = ((f32[32,1,72]{2,1,0:T(1,128)}), f32[32,1,72]{2,1,0:T(1,128)S(1)}, u32[]{:S(2)}, u32[]{:S(2)}) async-start(f32[32,1,72]{2,1,0:T(1,128)} %bitcast.18), calls=%async_computation.4 | async-start | bytes 32768 | tf_op jit(solution)/shard_map/all_to_all | solution.py:399
  187.6 3.4 %all-to-all-done.4 = f32[32,1,72]{2,1,0:T(1,128)S(1)} async-done(((f32[32,1,72]{2,1,0:T(1,128)}), f32[32,1,72]{2,1,0:T(1,128)S(1)}, u32[]{:S(2)}, u32[]{:S(2)}) %all-to-all-start.4) | async-done | bytes 9248 | tf_op jit(solution)/shard_map/all_to_all | solution.py:399
  (84 shorter events, 34.0 us)
Async XLA Ops:
  10.3 49.1 %all-to-all-start = ((bf16[8,144,290]{2,1,0:T(8,128)(2,1)}), bf16[8,144,290]{2,1,0:T(8,128)(2,1)S(1)}, u32[]{:S(2)}, u32[]{:S(2)}) async-start(bf16[8,144,290]{2,1,0:T(8,128)(2,1)} %broadcast_in_dim.29), calls=%async_computation | async-start | bytes 1769472 | tf_op jit(solution)/shard_map/all_to_all | solution.py:27
  22.3 29.1 %copy-start = (bf16[1024,128]{1,0:T(8,128)(2,1)S(1)}, bf16[1024,128]{1,0:T(8,128)(2,1)}, u32[]{:S(2)}) copy-start(bf16[1024,128]{1,0:T(8,128)(2,1)} %k_old.1) | copy-start | bytes 786436
  22.3 35.0 %copy-start.1 = (bf16[1024,128]{1,0:T(8,128)(2,1)S(1)}, bf16[1024,128]{1,0:T(8,128)(2,1)}, u32[]{:S(2)}) copy-start(bf16[1024,128]{1,0:T(8,128)(2,1)} %v_old.1) | copy-start | bytes 786436
  44.8 14.5 %copy-start.5 = (s32[12]{0:T(128)S(1)}, s32[12]{0:T(128)}, u32[]{:S(2)}) copy-start(s32[12]{0:T(128)} %param.21) | copy-start | bytes 148
  44.9 17.0 %collective-permute-start.5 = (bf16[4,288,256]{2,1,0:T(8,128)(2,1)S(1)}, bf16[4,288,256]{2,1,0:T(8,128)(2,1)S(1)}, u32[]{:S(2)}, u32[]{:S(2)}) collective-permute-start(bf16[4,288,256]{2,1,0:T(8,128)(2,1)S(1)} %slice.44.own), channel_id=1, source_target_pairs={{96,0},{0,32},{32,64},{64,96},{97,1},{1,33},{33,65},{65,97},{98,2}... | collective-permute-start | bytes 1769480 | tf_op jit(solution)/shard_map/ppermute | solution.py:328
  48.0 16.5 %collective-permute-start.3 = (bf16[4,288,256]{2,1,0:T(8,128)(2,1)S(1)}, bf16[4,288,256]{2,1,0:T(8,128)(2,1)S(1)}, u32[]{:S(2)}, u32[]{:S(2)}) collective-permute-start(bf16[4,288,256]{2,1,0:T(8,128)(2,1)S(1)} %slice.44.own), channel_id=1, source_target_pairs={{32,0},{64,32},{96,64},{0,96},{33,1},{65,33},{97,65},{1,97},{34,2}... | collective-permute-start | bytes 1769480 | tf_op jit(solution)/shard_map/ppermute | solution.py:327
  51.4 22.3 %collective-permute-start.1 = (bf16[1024,128]{1,0:T(8,128)(2,1)S(1)}, bf16[1024,128]{1,0:T(8,128)(2,1)}, u32[]{:S(2)}, u32[]{:S(2)}) collective-permute-start(bf16[1024,128]{1,0:T(8,128)(2,1)S(1)} %copy-done), channel_id=1, source_target_pairs={{0,16},{16,0},{1,17},{17,1},{2,18},{18,2},{3,19},{19,3},{4,20},{20... | collective-permute-start | bytes 786440 | tf_op jit(solution)/shard_map/ppermute | solution.py:362
  57.3 16.4 %collective-permute-start.2 = (bf16[1024,128]{1,0:T(8,128)(2,1)S(1)}, bf16[1024,128]{1,0:T(8,128)(2,1)}, u32[]{:S(2)}, u32[]{:S(2)}) collective-permute-start(bf16[1024,128]{1,0:T(8,128)(2,1)S(1)} %copy-done.1), channel_id=1, source_target_pairs={{0,16},{16,0},{1,17},{17,1},{2,18},{18,2},{3,19},{19,3},{4,20},{20... | collective-permute-start | bytes 786440 | tf_op jit(solution)/shard_map/ppermute | solution.py:363
  59.4 14.3 %collective-permute-start = (bf16[16,72,290]{2,1,0:T(8,128)(2,1)S(1)}, bf16[16,72,290]{2,1,0:T(8,128)(2,1)}, u32[]{:S(2)}, u32[]{:S(2)}) collective-permute-start(bf16[16,72,290]{2,1,0:T(8,128)(2,1)S(1)} %bitcast.24), channel_id=1, source_target_pairs={{0,16},{16,0},{1,17},{17,1},{2,18},{18,2},{3,19},{19,3},{4,20},{20... | collective-permute-start | bytes 2004488 | tf_op jit(solution)/shard_map/ppermute | solution.py:333
  62.6 11.1 %collective-permute-start.6 = (bf16[2,288,256]{2,1,0:T(8,128)(2,1)}, bf16[2,288,256]{2,1,0:T(8,128)(2,1)}, u32[]{:S(2)}, u32[]{:S(2)}) collective-permute-start(bf16[2,288,256]{2,1,0:T(8,128)(2,1)} %slice.46), channel_id=1, source_target_pairs={{96,0},{0,32},{32,64},{64,96},{97,1},{1,33},{33,65},{65,97},{98,2}... | collective-permute-start | bytes 884744 | tf_op jit(solution)/shard_map/ppermute | solution.py:330
  65.3 9.0 %collective-permute-start.4 = (bf16[2,288,256]{2,1,0:T(8,128)(2,1)}, bf16[2,288,256]{2,1,0:T(8,128)(2,1)}, u32[]{:S(2)}, u32[]{:S(2)}) collective-permute-start(bf16[2,288,256]{2,1,0:T(8,128)(2,1)} %slice.45), channel_id=1, source_target_pairs={{32,0},{64,32},{96,64},{0,96},{33,1},{65,33},{97,65},{1,97},{34,2}... | collective-permute-start | bytes 884744 | tf_op jit(solution)/shard_map/ppermute | solution.py:329
  77.4 25.8 %all-to-all-start.1 = ((bf16[16,144,128]{2,1,0:T(8,128)(2,1)}), bf16[16,144,128]{2,1,0:T(8,128)(2,1)S(1)}, u32[]{:S(2)}, u32[]{:S(2)}) async-start(bf16[16,144,128]{2,1,0:T(8,128)(2,1)} %broadcast_in_dim.54), calls=%async_computation.1 | async-start | bytes 1179648 | tf_op jit(solution)/shard_map/all_to_all | solution.py:27
  85.4 22.5 %collective-permute-start.9 = (bf16[4,144,256]{2,1,0:T(8,128)(2,1)S(1)}, bf16[4,144,256]{2,1,0:T(8,128)(2,1)S(1)}, u32[]{:S(2)}, u32[]{:S(2)}) collective-permute-start(bf16[4,144,256]{2,1,0:T(8,128)(2,1)S(1)} %slice.47.own), channel_id=1, source_target_pairs={{96,0},{0,32},{32,64},{64,96},{97,1},{1,33},{33,65},{65,97},{98,2}... | collective-permute-start | bytes 884744 | tf_op jit(solution)/shard_map/ppermute | solution.py:369
  88.7 19.2 %collective-permute-start.8 = (bf16[4,144,256]{2,1,0:T(8,128)(2,1)S(1)}, bf16[4,144,256]{2,1,0:T(8,128)(2,1)S(1)}, u32[]{:S(2)}, u32[]{:S(2)}) collective-permute-start(bf16[4,144,256]{2,1,0:T(8,128)(2,1)S(1)} %slice.47.own), channel_id=1, source_target_pairs={{32,0},{64,32},{96,64},{0,96},{33,1},{65,33},{97,65},{1,97},{34,2}... | collective-permute-start | bytes 884744 | tf_op jit(solution)/shard_map/ppermute | solution.py:368
  96.6 6.6 %collective-permute-start.7 = (bf16[2,144,128]{2,1,0:T(8,128)(2,1)S(1)}, bf16[2,144,128]{2,1,0:T(8,128)(2,1)S(1)}, u32[]{:S(2)}, u32[]{:S(2)}) collective-permute-start(bf16[2,144,128]{2,1,0:T(8,128)(2,1)S(1)} %bitcast.33), channel_id=1, source_target_pairs={{0,32},{32,0},{64,96},{96,64},{1,33},{33,1},{65,97},{97,65},{2,34}... | collective-permute-start | bytes 221192 | tf_op jit(solution)/shard_map/ppermute | solution.py:371
  107.9 22.4 %all-to-all-start.2 = ((bf16[16,160,128]{2,1,0:T(8,128)(2,1)}), bf16[16,160,128]{2,1,0:T(8,128)(2,1)S(1)}, u32[]{:S(2)}, u32[]{:S(2)}) async-start(bf16[16,160,128]{2,1,0:T(8,128)(2,1)} %bitcast.15), calls=%async_computation.2 | async-start | bytes 1310720 | tf_op jit(solution)/shard_map/all_to_all | solution.py:385
  115.7 11.8 %collective-permute-start.10 = (bf16[2,2,144,128]{3,2,1,0:T(8,128)(2,1)S(1)}, bf16[2,2,144,128]{3,2,1,0:T(8,128)(2,1)S(1)}, u32[]{:S(2)}, u32[]{:S(2)}) collective-permute-start(bf16[2,2,144,128]{3,2,1,0:T(8,128)(2,1)S(1)} %pad_maximum_fusion.4.near), channel_id=1, source_target_pairs={{0,64},{32,96},{64,0},{96,32},{1,65},{33,97},{65,1},{97,33},{2,66}... | collective-permute-start | bytes 442376 | tf_op jit(solution)/shard_map/ppermute | solution.py:376
  120.5 15.7 %collective-permute-start.12 = (bf16[2,144,256]{2,1,0:T(8,128)(2,1)S(1)}, bf16[2,144,256]{2,1,0:T(8,128)(2,1)S(1)}, u32[]{:S(2)}, u32[]{:S(2)}) collective-permute-start(bf16[2,144,256]{2,1,0:T(8,128)(2,1)S(1)} %slice.40), channel_id=1, source_target_pairs={{96,0},{0,32},{32,64},{64,96},{97,1},{1,33},{33,65},{65,97},{98,2}... | collective-permute-start | bytes 442376 | tf_op jit(solution)/shard_map/ppermute | solution.py:381
  122.7 13.5 %collective-permute-start.11 = (bf16[2,144,256]{2,1,0:T(8,128)(2,1)S(1)}, bf16[2,144,256]{2,1,0:T(8,128)(2,1)S(1)}, u32[]{:S(2)}, u32[]{:S(2)}) collective-permute-start(bf16[2,144,256]{2,1,0:T(8,128)(2,1)S(1)} %slice.39), channel_id=1, source_target_pairs={{32,0},{64,32},{96,64},{0,96},{33,1},{65,33},{97,65},{1,97},{34,2}... | collective-permute-start | bytes 442376 | tf_op jit(solution)/shard_map/ppermute | solution.py:380
  138.4 33.9 %all-to-all-start.3 = ((bf16[16,176,128]{2,1,0:T(8,128)(2,1)}), bf16[16,176,128]{2,1,0:T(8,128)(2,1)S(1)}, u32[]{:S(2)}, u32[]{:S(2)}) async-start(bf16[16,176,128]{2,1,0:T(8,128)(2,1)} %spread.1), calls=%async_computation.3 | async-start | bytes 1441792 | tf_op jit(solution)/shard_map/all_to_all | solution.py:392
  172.2 18.9 %copy-start.3 = (bf16[72,288]{1,0:T(8,128)(2,1)S(1)}, bf16[72,288]{1,0:T(8,128)(2,1)}, u32[]{:S(2)}) copy-start(bf16[72,288]{1,0:T(8,128)(2,1)} %param.12) | copy-start | bytes 124420
  173.3 17.7 %all-to-all-start.4 = ((f32[32,1,72]{2,1,0:T(1,128)}), f32[32,1,72]{2,1,0:T(1,128)S(1)}, u32[]{:S(2)}, u32[]{:S(2)}) async-start(f32[32,1,72]{2,1,0:T(1,128)} %bitcast.18), calls=%async_computation.4 | async-start | bytes 32768 | tf_op jit(solution)/shard_map/all_to_all | solution.py:399
  183.3 7.8 %collective-permute-start.13 = (f32[72,144]{1,0:T(8,128)S(1)}, f32[72,144]{1,0:T(8,128)S(1)}, u32[]{:S(2)}, u32[]{:S(2)}) collective-permute-start(f32[72,144]{1,0:T(8,128)S(1)} %fusion.11), channel_id=1, source_target_pairs={{0,16},{16,0},{1,17},{17,1},{2,18},{18,2},{3,19},{19,3},{4,20},{20... | collective-permute-start | bytes 124424 | tf_op jit(solution)/shard_map/ppermute | solution.py:404
  185.4 6.4 %collective-permute-start.14 = (bf16[2304,128]{1,0:T(8,128)(2,1)S(1)}, bf16[2304,128]{1,0:T(8,128)(2,1)S(1)}, u32[]{:S(2)}, u32[]{:S(2)}) collective-permute-start(bf16[2304,128]{1,0:T(8,128)(2,1)S(1)} %all_gather.35.mine), channel_id=1, source_target_pairs={{0,16},{16,0},{1,17},{17,1},{2,18},{18,2},{3,19},{19,3},{4,20},{20... | collective-permute-start | bytes 1769480 | tf_op jit(solution)/shard_map/ppermute | solution.py:400
  (3 other events, 30.4 us)

commit v12 on v11

--- a/solution.py
+++ b/solution.py
@@ -310,13 +310,15 @@
     high = lax.reduce_precision(squares, 8, 7)
     gained = float_in * (1.0 + pre_gain.astype(F32))
     gained = jnp.concatenate([gained, high, squares - high], axis=1).astype(BF16)
-    weights = jnp.concatenate([w_q[:, :HD], w_k, w_q[:, HD:], w_v], axis=1)
+    swap = [(0, 1), (1, 0)]
+    first, second = jnp.concatenate([w_q[:, :HD], w_k], axis=1), jnp.concatenate([w_q[:, HD:], w_v], axis=1)
+    weights = jnp.where(core == 0, first, second)
+    came = lax.ppermute(jnp.where(core == 0, second, first), "c", swap)
     gained, weights = lax.optimization_barrier((gained, weights))
     gained = lax.all_gather(gained, "zl", axis=0, tiled=True)
+    gained, came = lax.optimization_barrier((gained, came))
     gained = everywhere(gained, "y", n_gy // 2).reshape(n_gy, tok_rows, -1)
-
-    weights = lax.all_gather(weights, "c", axis=0, tiled=True)
-    weights = lax.dynamic_slice_in_dim(weights, core * cols, cols, 1)
+    weights = jnp.concatenate([jnp.where(core == 0, weights, came), jnp.where(core == 0, came, weights)], axis=0)
     inner = weights.shape[0]
     weights = jnp.concatenate([weights, w_o.T], axis=0)
     weights = lax.all_gather(weights, "zh", axis=0)
@@ -329,7 +331,6 @@
     ahead = lax.ppermute(right[:2], "x", from_right)
     behind = lax.ppermute(left[2:], "x", from_left)
     columns = [weights, right, ahead, behind, left]
-    swap = [(0, 1), (1, 0)]
     other = lax.ppermute(gained, "c", swap)
 
     chip_rows = me // 2 * (2 * tok_rows)
@@ -368,11 +369,14 @@
     out_right = lax.ppermute(w_out, "x", from_right)
     out_left = lax.ppermute(w_out, "x", from_left)
     near_rows = lax.all_gather(fresh_rows, "c", axis=0)
-    near_rows = jnp.stack([near_rows, lax.ppermute(near_rows, "x", [(i, i ^ 1) for i in range(4)])])
+    partner_rows = lax.ppermute(near_rows, "x", [(i, i ^ 1) for i in range(4)])
     all_queries = everywhere(queries, CHIPS, n_chips).reshape(-1, HD)
     all_queries, near_rows = lax.optimization_barrier((all_queries, near_rows))
     sums = attend(meta, all_queries, k_cache, v_cache, k_other, v_other)
-    sums, near_rows, out_right, out_left = lax.optimization_barrier((sums, near_rows, out_right, out_left))
+    sums, near_rows, partner_rows, out_right, out_left = lax.optimization_barrier(
+        (sums, near_rows, partner_rows, out_right, out_left)
+    )
+    near_rows = jnp.stack([near_rows, partner_rows])
     far_rows = lax.ppermute(near_rows, "x", [(i, i ^ 2) for i in range(4)])
     out_columns = [
         w_out,

time: 195 us -> 192 us (0.985)
  blocking collectives: 64.3 us -> 54 us
  waiting for transfers between devices: 10.6 us -> 19 us
    ppermute x1 -> x2, starting transfers between devices: 2.32 us -> 11.1 us  [the longest x1 8.79 us: on_device(): came = lax.ppermute(jnp.where(core == 0, second, first), 'c', swap)]
    all_to_all x1, starting transfers between devices: 11.8 us -> 6.73 us  [on_device(): total = jnp.sum(lax.all_to_all(partial_out, GY, 0, 0).astype(F32), axis=0)]
    all_to_all x1, waiting for transfers between devices: 1.77 us -> 6.86 us  [on_device(): parts = lax.all_to_all(sums.reshape(n_chips, -1, HD), CHIPS, 0, 0)]
    all_gather x1 -> x0, blocking collectives: 4.99 us -> none  [on_device(): weights = lax.all_gather(weights, 'c', axis=0, tiled=True)]
    all_to_all x2, starting transfers between devices: 14.9 us -> 10.5 us  [everywhere(): lax.all_to_all(jnp.broadcast_to(value[None], (count,) + value.shape), axe...]
    ppermute x1 -> x2, waiting for transfers between devices: 4.29 us -> 0.01 us  [the longest x1 0.01 us: on_device(): came = lax.ppermute(jnp.where(core == 0, second, first), 'c', swap)]
    all_to_all x2, waiting for transfers between devices: 0.01 us -> 3.97 us  [everywhere(): lax.all_to_all(jnp.broadcast_to(value[None], (count,) + value.shape), axe...]
    ppermute x1, waiting for transfers between devices: 0.01 us -> 3.18 us  [on_device(): behind = lax.ppermute(left[2:], 'x', from_left)]
  transfers between devices with their start and end apart: 20 -> 21, of which waited for: 5 -> 5; matrix products, arithmetic and copies ran while one was open for 3% -> 3% of each run, Pallas kernels for 3% -> 4%
where the time goes in v12:
time: 192 us; the launch traced here: 191 us
  starting transfers between devices  91.2 us (48%)
  blocking collectives  54 us (28%)
  waiting for transfers between devices  19 us (10%)
  Pallas kernels  13.8 us (7%)
  local copies, waits for them, and re-layouts  7.32 us (4%)
  other arithmetic  4.23 us (2%)
    all_gather x1, blocking collectives, on_device(): kind = lax.all_gather(kind, 'zh', axis=0, tiled=True)  21.8 us
    all_gather x1, blocking collectives, on_device(): weights = lax.all_gather(weights, 'zh', axis=0)  20.6 us
    all_to_all x2, starting transfers between devices, everywhere(): lax.all_to_all(jnp.broadcast_to(value[None], (count,) + value.shape), axe...  10.5 us
    all_to_all x1, starting transfers between devices, on_device(): squares = lax.all_to_all(squares, ('c',) + GY, 0, 0)  10.2 us
    ppermute x1, starting transfers between devices, on_device(): came = lax.ppermute(jnp.where(core == 0, second, first), 'c', swap)  8.79 us
    ppermute x1, starting transfers between devices, on_device(): k_other = lax.ppermute(k_cache, 'c', swap)  7.9 us
    all_to_all x1, waiting for transfers between devices, on_device(): parts = lax.all_to_all(sums.reshape(n_chips, -1, HD), CHIPS, 0, 0)  6.86 us
    all_to_all x1, starting transfers between devices, on_device(): total = jnp.sum(lax.all_to_all(partial_out, GY, 0, 0).astype(F32), axis=0)  6.73 us
  transfers between devices with their start and end apart: 21, of which 5 were waited for; matrix products, arithmetic and copies ran while one was open for 3% of the time, Pallas kernels for 4%

profile of v12, /device:TPU:1, one launch (start us, length us, event | category | flops | bytes accessed | tf_op | source)
XLA Modules:
  0.0 190.8 jit_solution(17589026347989899907)
XLA Ops:
  2.3 8.8 %collective-permute-start = (bf16[144,256]{1,0:T(8,128)(2,1)S(1)}, bf16[144,256]{1,0:T(8,128)(2,1)S(1)}, u32[]{:S(2)}, u32[]{:S(2)}) collective-permute-start(bf16[144,256]{1,0:T(8,128)(2,1)S(1)} %get-tuple-element.65), channel_id=1, source_target_pairs={{0,16},{16,0},{1,17},{17,1},{2,18},{18,2},{3,19},{19,3},{4,20},{20... | collective-permute-start | bytes 221192 | tf_op jit(solution)/shard_map/ppermute | solution.py:316
  13.0 4.2 %all_gather.24 = bf16[144,290]{1,0:T(8,128)(2,1)S(1)} all-gather(bf16[72,290]{1,0:T(8,128)(2,1)S(1)} %pad_maximum_fusion.8), channel_id=1, replica_groups=mesh['zh'=4,'x'=4,'c'=2,'y'=8,'zl'=2] {'zl'}, dimensions={0}, use_global_device_ids=true | all-gather | bytes 125280 | tf_op jit(solution)/shard_map/all_gather | solution.py:318
  18.2 3.7 %all-to-all-start = ((bf16[8,144,290]{2,1,0:T(8,128)(2,1)}), bf16[8,144,290]{2,1,0:T(8,128)(2,1)S(1)}, u32[]{:S(2)}, u32[]{:S(2)}) async-start(bf16[8,144,290]{2,1,0:T(8,128)(2,1)} %broadcast_in_dim.29), calls=%async_computation | async-start | bytes 1769472 | tf_op jit(solution)/shard_map/all_to_all | solution.py:27
  22.0 20.6 %all-gather = bf16[1728,256]{1,0:T(8,128)(2,1)S(1)} all-gather(bf16[432,256]{1,0:T(8,128)(2,1)S(1)} %pad_maximum_fusion.1), channel_id=2, replica_groups=mesh['zh'=4,'x'=4,'c'=2,'y'=8,'zl'=2] {'zh'}, dimensions={0}, use_global_device_ids=true | all-gather | bytes 1105920 | tf_op jit(solution)/shard_map/all_gather | solution.py:324
  43.6 3.1 %collective-permute-start.6 = (bf16[4,288,256]{2,1,0:T(8,128)(2,1)S(1)}, bf16[4,288,256]{2,1,0:T(8,128)(2,1)S(1)}, u32[]{:S(2)}, u32[]{:S(2)}) collective-permute-start(bf16[4,288,256]{2,1,0:T(8,128)(2,1)S(1)} %slice.44.own), channel_id=1, source_target_pairs={{96,0},{0,32},{32,64},{64,96},{97,1},{1,33},{33,65},{65,97},{98,2}... | collective-permute-start | bytes 1769480 | tf_op jit(solution)/shard_map/ppermute | solution.py:330
  46.7 3.4 %collective-permute-start.4 = (bf16[4,288,256]{2,1,0:T(8,128)(2,1)S(1)}, bf16[4,288,256]{2,1,0:T(8,128)(2,1)S(1)}, u32[]{:S(2)}, u32[]{:S(2)}) collective-permute-start(bf16[4,288,256]{2,1,0:T(8,128)(2,1)S(1)} %slice.44.own), channel_id=1, source_target_pairs={{32,0},{64,32},{96,64},{0,96},{33,1},{65,33},{97,65},{1,97},{34,2}... | collective-permute-start | bytes 1769480 | tf_op jit(solution)/shard_map/ppermute | solution.py:329
  50.1 7.9 %collective-permute-start.2 = (bf16[1024,128]{1,0:T(8,128)(2,1)S(1)}, bf16[1024,128]{1,0:T(8,128)(2,1)}, u32[]{:S(2)}, u32[]{:S(2)}) collective-permute-start(bf16[1024,128]{1,0:T(8,128)(2,1)S(1)} %copy-done), channel_id=1, source_target_pairs={{0,16},{16,0},{1,17},{17,1},{2,18},{18,2},{3,19},{19,3},{4,20},{20... | collective-permute-start | bytes 786440 | tf_op jit(solution)/shard_map/ppermute | solution.py:363
  66.0 4.6 %collective-permute-start.5 = (bf16[2,288,256]{2,1,0:T(8,128)(2,1)}, bf16[2,288,256]{2,1,0:T(8,128)(2,1)}, u32[]{:S(2)}, u32[]{:S(2)}) collective-permute-start(bf16[2,288,256]{2,1,0:T(8,128)(2,1)} %slice.45), channel_id=1, source_target_pairs={{32,0},{64,32},{96,64},{0,96},{33,1},{65,33},{97,65},{1,97},{34,2}... | collective-permute-start | bytes 884744 | tf_op jit(solution)/shard_map/ppermute | solution.py:331
  72.2 3.2 %collective-permute-done.7.behind = bf16[2,288,256]{2,1,0:T(8,128)(2,1)} collective-permute-done((bf16[2,288,256]{2,1,0:T(8,128)(2,1)}, bf16[2,288,256]{2,1,0:T(8,128)(2,1)}, u32[]{:S(2)}, u32[]{:S(2)}) %collective-permute-start.7) | collective-permute-done | bytes 294944 | tf_op jit(solution)/shard_map/ppermute | solution.py:332
  80.1 6.8 %all-to-all-start.1 = ((bf16[16,144,128]{2,1,0:T(8,128)(2,1)}), bf16[16,144,128]{2,1,0:T(8,128)(2,1)S(1)}, u32[]{:S(2)}, u32[]{:S(2)}) async-start(bf16[16,144,128]{2,1,0:T(8,128)(2,1)} %broadcast_in_dim.54), calls=%async_computation.1 | async-start | bytes 1179648 | tf_op jit(solution)/shard_map/all_to_all | solution.py:27
  86.9 3.3 %collective-permute-start.10 = (bf16[4,144,256]{2,1,0:T(8,128)(2,1)S(1)}, bf16[4,144,256]{2,1,0:T(8,128)(2,1)S(1)}, u32[]{:S(2)}, u32[]{:S(2)}) collective-permute-start(bf16[4,144,256]{2,1,0:T(8,128)(2,1)S(1)} %slice.47.own), channel_id=1, source_target_pairs={{96,0},{0,32},{32,64},{64,96},{97,1},{1,33},{33,65},{65,97},{98,2}... | collective-permute-start | bytes 884744 | tf_op jit(solution)/shard_map/ppermute | solution.py:370
  90.1 3.2 %collective-permute-start.9 = (bf16[4,144,256]{2,1,0:T(8,128)(2,1)S(1)}, bf16[4,144,256]{2,1,0:T(8,128)(2,1)S(1)}, u32[]{:S(2)}, u32[]{:S(2)}) collective-permute-start(bf16[4,144,256]{2,1,0:T(8,128)(2,1)S(1)} %slice.47.own), channel_id=1, source_target_pairs={{32,0},{64,32},{96,64},{0,96},{33,1},{65,33},{97,65},{1,97},{34,2}... | collective-permute-start | bytes 884744 | tf_op jit(solution)/shard_map/ppermute | solution.py:369
  93.4 3.7 %all-gather.1 = bf16[288,128]{1,0:T(8,128)(2,1)S(1)} all-gather(bf16[144,128]{1,0:T(8,128)(2,1)S(1)} %get-tuple-element.39), channel_id=3, replica_groups=mesh['zh'=4,'x'=4,'c'=2,'y'=8,'zl'=2] {'c'}, dimensions={0}, use_global_device_ids=true | all-gather | bytes 110592 | tf_op jit(solution)/shard_map/all_gather | solution.py:371
  99.4 4.0 %all-to-all-done.1 = bf16[16,144,128]{2,1,0:T(8,128)(2,1)S(1)} async-done(((bf16[16,144,128]{2,1,0:T(8,128)(2,1)}), bf16[16,144,128]{2,1,0:T(8,128)(2,1)S(1)}, u32[]{:S(2)}, u32[]{:S(2)}) %all-to-all-start.1) | async-done | bytes 589856 | tf_op jit(solution)/shard_map/all_to_all | solution.py:27
  103.4 5.5 %attend.1 = bf16[2560,128]{1,0:T(8,128)(2,1)} custom-call(s32[40]{0:T(128)S(1)} %concatenate.65.meta, bf16[2304,128]{1,0:T(8,128)(2,1)S(1)} %bitcast.26, bf16[1024,128]{1,0:T(8,128)(2,1)S(1)} %copy-done, bf16[1024,128]{1,0:T(8,128)(2,1)S(1)} %copy-done.1, bf16[1024,128]{1,0:T(8,128)(2,1)} %collective-permute-done.2.k_other, ...), custom_call_target="tpu_custom_call" | custom-call | tf_op jit(solution)/shard_map/attend/pallas_call | solution.py:123
  108.8 5.4 %all-to-all-start.2 = ((bf16[16,160,128]{2,1,0:T(8,128)(2,1)}), bf16[16,160,128]{2,1,0:T(8,128)(2,1)S(1)}, u32[]{:S(2)}, u32[]{:S(2)}) async-start(bf16[16,160,128]{2,1,0:T(8,128)(2,1)} %bitcast.13), calls=%async_computation.2 | async-start | bytes 1310720 | tf_op jit(solution)/shard_map/all_to_all | solution.py:389
  114.3 4.8 %collective-permute-start.11 = (bf16[2,2,144,128]{3,2,1,0:T(8,128)(2,1)S(1)}, bf16[2,2,144,128]{3,2,1,0:T(8,128)(2,1)S(1)}, u32[]{:S(2)}, u32[]{:S(2)}) collective-permute-start(bf16[2,2,144,128]{3,2,1,0:T(8,128)(2,1)S(1)} %pad_maximum_fusion.3.near), channel_id=1, source_target_pairs={{0,64},{32,96},{64,0},{96,32},{1,65},{33,97},{65,1},{97,33},{2,66}... | collective-permute-start | bytes 442376 | tf_op jit(solution)/shard_map/ppermute | solution.py:380
  121.3 4.3 %collective-permute-start.12 = (bf16[2,144,256]{2,1,0:T(8,128)(2,1)S(1)}, bf16[2,144,256]{2,1,0:T(8,128)(2,1)S(1)}, u32[]{:S(2)}, u32[]{:S(2)}) collective-permute-start(bf16[2,144,256]{2,1,0:T(8,128)(2,1)S(1)} %slice.39), channel_id=1, source_target_pairs={{32,0},{64,32},{96,64},{0,96},{33,1},{65,33},{97,65},{1,97},{34,2}... | collective-permute-start | bytes 442376 | tf_op jit(solution)/shard_map/ppermute | solution.py:384
  126.7 6.9 %all-to-all-done.2.parts = bf16[16,160,128]{2,1,0:T(8,128)(2,1)S(1)} async-done(((bf16[16,160,128]{2,1,0:T(8,128)(2,1)}), bf16[16,160,128]{2,1,0:T(8,128)(2,1)S(1)}, u32[]{:S(2)}, u32[]{:S(2)}) %all-to-all-start.2) | async-done | bytes 655392 | tf_op jit(solution)/shard_map/all_to_all | solution.py:389
  134.3 3.7 %all-gather.2 = bf16[288,128]{1,0:T(8,128)(2,1)S(1)} all-gather(bf16[144,128]{1,0:T(8,128)(2,1)S(1)} %divide.1), channel_id=4, replica_groups=mesh['zh'=4,'x'=4,'c'=2,'y'=8,'zl'=2] {'c'}, dimensions={0}, use_global_device_ids=true | all-gather | bytes 110592 | tf_op jit(solution)/shard_map/all_gather | solution.py:392
  140.2 6.7 %all-to-all-start.3 = ((bf16[16,176,128]{2,1,0:T(8,128)(2,1)}), bf16[16,176,128]{2,1,0:T(8,128)(2,1)S(1)}, u32[]{:S(2)}, u32[]{:S(2)}) async-start(bf16[16,176,128]{2,1,0:T(8,128)(2,1)} %spread.1), calls=%async_computation.3 | async-start | bytes 1441792 | tf_op jit(solution)/shard_map/all_to_all | solution.py:396
  147.0 21.8 %all_gather.31.mine = bf16[2304,128]{1,0:T(8,128)(2,1)S(1)} all-gather(bf16[576,128]{1,0:T(8,128)(2,1)S(1)} %get-tuple-element.54), channel_id=1, replica_groups=mesh['zh'=4,'x'=4,'c'=2,'y'=8,'zl'=2] {'zh'}, dimensions={0}, use_global_device_ids=true | all-gather | bytes 737280 | tf_op jit(solution)/shard_map/all_gather | solution.py:395
  169.8 10.2 %all-to-all-start.4 = ((f32[32,1,72]{2,1,0:T(1,128)}), f32[32,1,72]{2,1,0:T(1,128)S(1)}, u32[]{:S(2)}, u32[]{:S(2)}) async-start(f32[32,1,72]{2,1,0:T(1,128)} %bitcast.18), calls=%async_computation.4 | async-start | bytes 32768 | tf_op jit(solution)/shard_map/all_to_all | solution.py:403
  184.4 3.4 %all-to-all-done.4 = f32[32,1,72]{2,1,0:T(1,128)S(1)} async-done(((f32[32,1,72]{2,1,0:T(1,128)}), f32[32,1,72]{2,1,0:T(1,128)S(1)}, u32[]{:S(2)}, u32[]{:S(2)}) %all-to-all-start.4) | async-done | bytes 9248 | tf_op jit(solution)/shard_map/all_to_all | solution.py:403
  (89 shorter events, 36.6 us)
Async XLA Ops:
  2.3 14.9 %collective-permute-start = (bf16[144,256]{1,0:T(8,128)(2,1)S(1)}, bf16[144,256]{1,0:T(8,128)(2,1)S(1)}, u32[]{:S(2)}, u32[]{:S(2)}) collective-permute-start(bf16[144,256]{1,0:T(8,128)(2,1)S(1)} %get-tuple-element.65), channel_id=1, source_target_pairs={{0,16},{16,0},{1,17},{17,1},{2,18},{18,2},{3,19},{19,3},{4,20},{20... | collective-permute-start | bytes 221192 | tf_op jit(solution)/shard_map/ppermute | solution.py:316
  18.2 41.9 %all-to-all-start = ((bf16[8,144,290]{2,1,0:T(8,128)(2,1)}), bf16[8,144,290]{2,1,0:T(8,128)(2,1)S(1)}, u32[]{:S(2)}, u32[]{:S(2)}) async-start(bf16[8,144,290]{2,1,0:T(8,128)(2,1)} %broadcast_in_dim.29), calls=%async_computation | async-start | bytes 1769472 | tf_op jit(solution)/shard_map/all_to_all | solution.py:27
  21.9 28.2 %copy-start = (bf16[1024,128]{1,0:T(8,128)(2,1)S(1)}, bf16[1024,128]{1,0:T(8,128)(2,1)}, u32[]{:S(2)}) copy-start(bf16[1024,128]{1,0:T(8,128)(2,1)} %k_old.1) | copy-start | bytes 786436
  22.0 36.1 %copy-start.1 = (bf16[1024,128]{1,0:T(8,128)(2,1)S(1)}, bf16[1024,128]{1,0:T(8,128)(2,1)}, u32[]{:S(2)}) copy-start(bf16[1024,128]{1,0:T(8,128)(2,1)} %v_old.1) | copy-start | bytes 786436
  43.6 27.3 %copy-start.7 = (s32[12]{0:T(128)S(1)}, s32[12]{0:T(128)}, u32[]{:S(2)}) copy-start(s32[12]{0:T(128)} %param.22) | copy-start | bytes 148
  43.6 19.0 %collective-permute-start.6 = (bf16[4,288,256]{2,1,0:T(8,128)(2,1)S(1)}, bf16[4,288,256]{2,1,0:T(8,128)(2,1)S(1)}, u32[]{:S(2)}, u32[]{:S(2)}) collective-permute-start(bf16[4,288,256]{2,1,0:T(8,128)(2,1)S(1)} %slice.44.own), channel_id=1, source_target_pairs={{96,0},{0,32},{32,64},{64,96},{97,1},{1,33},{33,65},{65,97},{98,2}... | collective-permute-start | bytes 1769480 | tf_op jit(solution)/shard_map/ppermute | solution.py:330
  46.7 18.5 %collective-permute-start.4 = (bf16[4,288,256]{2,1,0:T(8,128)(2,1)S(1)}, bf16[4,288,256]{2,1,0:T(8,128)(2,1)S(1)}, u32[]{:S(2)}, u32[]{:S(2)}) collective-permute-start(bf16[4,288,256]{2,1,0:T(8,128)(2,1)S(1)} %slice.44.own), channel_id=1, source_target_pairs={{32,0},{64,32},{96,64},{0,96},{33,1},{65,33},{97,65},{1,97},{34,2}... | collective-permute-start | bytes 1769480 | tf_op jit(solution)/shard_map/ppermute | solution.py:329
  50.1 22.0 %collective-permute-start.2 = (bf16[1024,128]{1,0:T(8,128)(2,1)S(1)}, bf16[1024,128]{1,0:T(8,128)(2,1)}, u32[]{:S(2)}, u32[]{:S(2)}) collective-permute-start(bf16[1024,128]{1,0:T(8,128)(2,1)S(1)} %copy-done), channel_id=1, source_target_pairs={{0,16},{16,0},{1,17},{17,1},{2,18},{18,2},{3,19},{19,3},{4,20},{20... | collective-permute-start | bytes 786440 | tf_op jit(solution)/shard_map/ppermute | solution.py:363
  58.0 14.1 %collective-permute-start.3 = (bf16[1024,128]{1,0:T(8,128)(2,1)S(1)}, bf16[1024,128]{1,0:T(8,128)(2,1)}, u32[]{:S(2)}, u32[]{:S(2)}) collective-permute-start(bf16[1024,128]{1,0:T(8,128)(2,1)S(1)} %copy-done.1), channel_id=1, source_target_pairs={{0,16},{16,0},{1,17},{17,1},{2,18},{18,2},{3,19},{19,3},{4,20},{20... | collective-permute-start | bytes 786440 | tf_op jit(solution)/shard_map/ppermute | solution.py:364
  60.1 12.0 %collective-permute-start.1 = (bf16[16,72,290]{2,1,0:T(8,128)(2,1)S(1)}, bf16[16,72,290]{2,1,0:T(8,128)(2,1)}, u32[]{:S(2)}, u32[]{:S(2)}) collective-permute-start(bf16[16,72,290]{2,1,0:T(8,128)(2,1)S(1)} %bitcast.24), channel_id=1, source_target_pairs={{0,16},{16,0},{1,17},{17,1},{2,18},{18,2},{3,19},{19,3},{4,20},{20... | collective-permute-start | bytes 2004488 | tf_op jit(solution)/shard_map/ppermute | solution.py:334
  63.3 12.0 %collective-permute-start.7 = (bf16[2,288,256]{2,1,0:T(8,128)(2,1)}, bf16[2,288,256]{2,1,0:T(8,128)(2,1)}, u32[]{:S(2)}, u32[]{:S(2)}) collective-permute-start(bf16[2,288,256]{2,1,0:T(8,128)(2,1)} %slice.46), channel_id=1, source_target_pairs={{96,0},{0,32},{32,64},{64,96},{97,1},{1,33},{33,65},{65,97},{98,2}... | collective-permute-start | bytes 884744 | tf_op jit(solution)/shard_map/ppermute | solution.py:332
  66.0 11.0 %collective-permute-start.5 = (bf16[2,288,256]{2,1,0:T(8,128)(2,1)}, bf16[2,288,256]{2,1,0:T(8,128)(2,1)}, u32[]{:S(2)}, u32[]{:S(2)}) collective-permute-start(bf16[2,288,256]{2,1,0:T(8,128)(2,1)} %slice.45), channel_id=1, source_target_pairs={{32,0},{64,32},{96,64},{0,96},{33,1},{65,33},{97,65},{1,97},{34,2}... | collective-permute-start | bytes 884744 | tf_op jit(solution)/shard_map/ppermute | solution.py:331
  80.1 23.3 %all-to-all-start.1 = ((bf16[16,144,128]{2,1,0:T(8,128)(2,1)}), bf16[16,144,128]{2,1,0:T(8,128)(2,1)S(1)}, u32[]{:S(2)}, u32[]{:S(2)}) async-start(bf16[16,144,128]{2,1,0:T(8,128)(2,1)} %broadcast_in_dim.54), calls=%async_computation.1 | async-start | bytes 1179648 | tf_op jit(solution)/shard_map/all_to_all | solution.py:27
  86.9 22.0 %collective-permute-start.10 = (bf16[4,144,256]{2,1,0:T(8,128)(2,1)S(1)}, bf16[4,144,256]{2,1,0:T(8,128)(2,1)S(1)}, u32[]{:S(2)}, u32[]{:S(2)}) collective-permute-start(bf16[4,144,256]{2,1,0:T(8,128)(2,1)S(1)} %slice.47.own), channel_id=1, source_target_pairs={{96,0},{0,32},{32,64},{64,96},{97,1},{1,33},{33,65},{65,97},{98,2}... | collective-permute-start | bytes 884744 | tf_op jit(solution)/shard_map/ppermute | solution.py:370
  90.1 18.7 %collective-permute-start.9 = (bf16[4,144,256]{2,1,0:T(8,128)(2,1)S(1)}, bf16[4,144,256]{2,1,0:T(8,128)(2,1)S(1)}, u32[]{:S(2)}, u32[]{:S(2)}) collective-permute-start(bf16[4,144,256]{2,1,0:T(8,128)(2,1)S(1)} %slice.47.own), channel_id=1, source_target_pairs={{32,0},{64,32},{96,64},{0,96},{33,1},{65,33},{97,65},{1,97},{34,2}... | collective-permute-start | bytes 884744 | tf_op jit(solution)/shard_map/ppermute | solution.py:369
  97.1 11.8 %collective-permute-start.8 = (bf16[2,144,128]{2,1,0:T(8,128)(2,1)S(1)}, bf16[2,144,128]{2,1,0:T(8,128)(2,1)S(1)}, u32[]{:S(2)}, u32[]{:S(2)}) collective-permute-start(bf16[2,144,128]{2,1,0:T(8,128)(2,1)S(1)} %bitcast.33), channel_id=1, source_target_pairs={{0,32},{32,0},{64,96},{96,64},{1,33},{33,1},{65,97},{97,65},{2,34}... | collective-permute-start | bytes 221192 | tf_op jit(solution)/shard_map/ppermute | solution.py:372
  108.8 24.7 %all-to-all-start.2 = ((bf16[16,160,128]{2,1,0:T(8,128)(2,1)}), bf16[16,160,128]{2,1,0:T(8,128)(2,1)S(1)}, u32[]{:S(2)}, u32[]{:S(2)}) async-start(bf16[16,160,128]{2,1,0:T(8,128)(2,1)} %bitcast.13), calls=%async_computation.2 | async-start | bytes 1310720 | tf_op jit(solution)/shard_map/all_to_all | solution.py:389
  114.3 11.3 %collective-permute-start.11 = (bf16[2,2,144,128]{3,2,1,0:T(8,128)(2,1)S(1)}, bf16[2,2,144,128]{3,2,1,0:T(8,128)(2,1)S(1)}, u32[]{:S(2)}, u32[]{:S(2)}) collective-permute-start(bf16[2,2,144,128]{3,2,1,0:T(8,128)(2,1)S(1)} %pad_maximum_fusion.3.near), channel_id=1, source_target_pairs={{0,64},{32,96},{64,0},{96,32},{1,65},{33,97},{65,1},{97,33},{2,66}... | collective-permute-start | bytes 442376 | tf_op jit(solution)/shard_map/ppermute | solution.py:380
  119.1 18.9 %collective-permute-start.13 = (bf16[2,144,256]{2,1,0:T(8,128)(2,1)S(1)}, bf16[2,144,256]{2,1,0:T(8,128)(2,1)S(1)}, u32[]{:S(2)}, u32[]{:S(2)}) collective-permute-start(bf16[2,144,256]{2,1,0:T(8,128)(2,1)S(1)} %slice.40), channel_id=1, source_target_pairs={{96,0},{0,32},{32,64},{64,96},{97,1},{1,33},{33,65},{65,97},{98,2}... | collective-permute-start | bytes 442376 | tf_op jit(solution)/shard_map/ppermute | solution.py:385
  121.3 16.7 %collective-permute-start.12 = (bf16[2,144,256]{2,1,0:T(8,128)(2,1)S(1)}, bf16[2,144,256]{2,1,0:T(8,128)(2,1)S(1)}, u32[]{:S(2)}, u32[]{:S(2)}) collective-permute-start(bf16[2,144,256]{2,1,0:T(8,128)(2,1)S(1)} %slice.39), channel_id=1, source_target_pairs={{32,0},{64,32},{96,64},{0,96},{33,1},{65,33},{97,65},{1,97},{34,2}... | collective-permute-start | bytes 442376 | tf_op jit(solution)/shard_map/ppermute | solution.py:384
  140.2 28.5 %all-to-all-start.3 = ((bf16[16,176,128]{2,1,0:T(8,128)(2,1)}), bf16[16,176,128]{2,1,0:T(8,128)(2,1)S(1)}, u32[]{:S(2)}, u32[]{:S(2)}) async-start(bf16[16,176,128]{2,1,0:T(8,128)(2,1)} %spread.1), calls=%async_computation.3 | async-start | bytes 1441792 | tf_op jit(solution)/shard_map/all_to_all | solution.py:396
  169.8 18.0 %all-to-all-start.4 = ((f32[32,1,72]{2,1,0:T(1,128)}), f32[32,1,72]{2,1,0:T(1,128)S(1)}, u32[]{:S(2)}, u32[]{:S(2)}) async-start(f32[32,1,72]{2,1,0:T(1,128)} %bitcast.18), calls=%async_computation.4 | async-start | bytes 32768 | tf_op jit(solution)/shard_map/all_to_all | solution.py:403
  180.1 7.8 %collective-permute-start.14 = (f32[72,144]{1,0:T(8,128)S(1)}, f32[72,144]{1,0:T(8,128)S(1)}, u32[]{:S(2)}, u32[]{:S(2)}) collective-permute-start(f32[72,144]{1,0:T(8,128)S(1)} %fusion.11), channel_id=1, source_target_pairs={{0,16},{16,0},{1,17},{17,1},{2,18},{18,2},{3,19},{19,3},{4,20},{20... | collective-permute-start | bytes 124424 | tf_op jit(solution)/shard_map/ppermute | solution.py:408
  182.2 6.4 %collective-permute-start.15 = (bf16[2304,128]{1,0:T(8,128)(2,1)S(1)}, bf16[2304,128]{1,0:T(8,128)(2,1)S(1)}, u32[]{:S(2)}, u32[]{:S(2)}) collective-permute-start(bf16[2304,128]{1,0:T(8,128)(2,1)S(1)} %all_gather.31.mine), channel_id=1, source_target_pairs={{0,16},{16,0},{1,17},{17,1},{2,18},{18,2},{3,19},{19,3},{4,20},{20... | collective-permute-start | bytes 1769480 | tf_op jit(solution)/shard_map/ppermute | solution.py:404
  (6 other events, 75.3 us)

commit v13 on v12

--- a/solution.py
+++ b/solution.py
@@ -66,7 +66,7 @@
     )(meta, mine, others, turns, *columns)
 
 
-def attend_kernel(meta, queries, k_own, v_own, k_other, v_other, sums, num, den, totals):
+def attend_kernel(meta, queries, k_own, v_own, others, sums, num, den, totals):
     own = k_own.shape[0]
     first = meta[3 * REQS]
     core = meta[3 * REQS + 2]
@@ -78,7 +78,7 @@
         cached, offset = meta[r], meta[2 * REQS + r]
         num[...] = jnp.zeros_like(num)
         den[...] = jnp.zeros_like(den)
-        for keys, values, at in ((k_own, v_own, core), (k_other, v_other, 1 - core)):
+        for keys, values, at in ((k_own, v_own, core), (others.at[:own, :], others.at[own:, :], 1 - core)):
             begin = offset - first - at * own
             low, high = jnp.maximum(begin, 0), jnp.minimum(begin + cached, own)
 
@@ -116,14 +116,14 @@
         sums[block * chunk + 3 * PIECE : (block + 1) * chunk, :] = rows.astype(BF16)
 
 
-def attend(meta, queries, k_cache, v_cache, k_other, v_other):
+def attend(meta, queries, k_cache, v_cache, others):
     blocks = REQS * NEWTOK // (3 * PIECE)
     chunk = 3 * PIECE + 16
     vmem = pl.BlockSpec(memory_space=pltpu.VMEM)
     return pl.pallas_call(
         attend_kernel,
         out_shape=jax.ShapeDtypeStruct((blocks * chunk, HD), BF16),
-        in_specs=[pl.BlockSpec(memory_space=pltpu.SMEM)] + [vmem] * 5,
+        in_specs=[pl.BlockSpec(memory_space=pltpu.SMEM)] + [vmem] * 4,
         out_specs=vmem,
         scratch_shapes=[
             pltpu.VMEM((NEWTOK, HD), F32),
@@ -132,7 +132,7 @@
         ],
         compiler_params=pltpu.CompilerParams(vmem_limit_bytes=32 << 20),
         name="attend",
-    )(meta, queries, k_cache, v_cache, k_other, v_other)
+    )(meta, queries, k_cache, v_cache, others)
 
 
 def attend_new_kernel(meta, queries, near, far, num, den, kind):
@@ -360,19 +360,18 @@
             jnp.stack([me // 2 * (2 * k_cache.shape[0]), chip_rows, core, lax.axis_index("x")]).astype(jnp.int32),
         ]
     )
-    k_other = lax.ppermute(k_cache, "c", swap)
-    v_other = lax.ppermute(v_cache, "c", swap)
-    other, k_other, v_other = lax.optimization_barrier((other, k_other, v_other))
+    caches = jnp.concatenate([k_cache, v_cache], axis=0)
     queries, fresh_rows = project(meta, gained, other, turns, columns)
 
-    queries, fresh_rows, w_out = lax.optimization_barrier((queries, fresh_rows, w_out))
+    queries, fresh_rows, w_out, caches = lax.optimization_barrier((queries, fresh_rows, w_out, caches))
+    caches = lax.ppermute(caches, "c", swap)
     out_right = lax.ppermute(w_out, "x", from_right)
     out_left = lax.ppermute(w_out, "x", from_left)
     near_rows = lax.all_gather(fresh_rows, "c", axis=0)
     partner_rows = lax.ppermute(near_rows, "x", [(i, i ^ 1) for i in range(4)])
     all_queries = everywhere(queries, CHIPS, n_chips).reshape(-1, HD)
     all_queries, near_rows = lax.optimization_barrier((all_queries, near_rows))
-    sums = attend(meta, all_queries, k_cache, v_cache, k_other, v_other)
+    sums = attend(meta, all_queries, k_cache, v_cache, caches)
     sums, near_rows, partner_rows, out_right, out_left = lax.optimization_barrier(
         (sums, near_rows, partner_rows, out_right, out_left)
     )

time: 192 us -> 191 us (level)
  starting transfers between devices: 91.2 us -> 103 us
  waiting for transfers between devices: 19 us -> 7.74 us
    ppermute x1, starting transfers between devices: 2.41 us -> 7.9 us  [on_device(): other = lax.ppermute(gained, 'c', swap)]
    all_to_all x1, starting transfers between devices: 6.73 us -> 11.9 us  [on_device(): total = jnp.sum(lax.all_to_all(partial_out, GY, 0, 0).astype(F32), axis=0)]
    all_to_all x1, waiting for transfers between devices: 6.86 us -> 1.76 us  [on_device(): parts = lax.all_to_all(sums.reshape(n_chips, -1, HD), CHIPS, 0, 0)]
    all_to_all x2, waiting for transfers between devices: 3.97 us -> 0.01 us  [everywhere(): lax.all_to_all(jnp.broadcast_to(value[None], (count,) + value.shape), axe...]
    ppermute x1, waiting for transfers between devices: 3.18 us -> 0.01 us  [on_device(): behind = lax.ppermute(left[2:], 'x', from_left)]
    all_to_all x1, starting transfers between devices: 5.44 us -> 7.72 us  [on_device(): parts = lax.all_to_all(sums.reshape(n_chips, -1, HD), CHIPS, 0, 0)]
    ppermute x2 -> x1, starting transfers between devices: 9.82 us -> 8.26 us  [on_device(): caches = lax.ppermute(caches, 'c', swap)]
  transfers between devices with their start and end apart: 21 -> 20, of which waited for: 5 -> 5; matrix products, arithmetic and copies ran while one was open for 3% -> 4% of each run, Pallas kernels for 4% -> 4%
where the time goes in v13:
time: 191 us; the launch traced here: 190 us
  starting transfers between devices  103 us (54%)
  blocking collectives  52.9 us (28%)
  Pallas kernels  13.1 us (7%)
  waiting for transfers between devices  7.74 us (4%)
  local copies, waits for them, and re-layouts  7.11 us (4%)
  other arithmetic  5.07 us (3%)
    all_gather x1, blocking collectives, on_device(): kind = lax.all_gather(kind, 'zh', axis=0, tiled=True)  21.2 us
    all_gather x1, blocking collectives, on_device(): weights = lax.all_gather(weights, 'zh', axis=0)  20.5 us
    all_to_all x1, starting transfers between devices, on_device(): total = jnp.sum(lax.all_to_all(partial_out, GY, 0, 0).astype(F32), axis=0)  11.9 us
    all_to_all x2, starting transfers between devices, everywhere(): lax.all_to_all(jnp.broadcast_to(value[None], (count,) + value.shape), axe...  10.4 us
    all_to_all x1, starting transfers between devices, on_device(): squares = lax.all_to_all(squares, ('c',) + GY, 0, 0)  10.1 us
    ppermute x1, starting transfers between devices, on_device(): came = lax.ppermute(jnp.where(core == 0, second, first), 'c', swap)  8.79 us
    ppermute x1, starting transfers between devices, on_device(): caches = lax.ppermute(caches, 'c', swap)  8.26 us
    ppermute x1, starting transfers between devices, on_device(): other = lax.ppermute(gained, 'c', swap)  7.9 us
  transfers between devices with their start and end apart: 20, of which 5 were waited for; matrix products, arithmetic and copies ran while one was open for 4% of the time, Pallas kernels for 4%

profile of v13, /device:TPU:1, one launch (start us, length us, event | category | flops | bytes accessed | tf_op | source)
XLA Modules:
  0.0 189.7 jit_solution(15005549735951494482)
XLA Ops:
  2.3 8.8 %collective-permute-start = (bf16[144,256]{1,0:T(8,128)(2,1)S(1)}, bf16[144,256]{1,0:T(8,128)(2,1)S(1)}, u32[]{:S(2)}, u32[]{:S(2)}) collective-permute-start(bf16[144,256]{1,0:T(8,128)(2,1)S(1)} %get-tuple-element.61), channel_id=1, source_target_pairs={{0,16},{16,0},{1,17},{17,1},{2,18},{18,2},{3,19},{19,3},{4,20},{20... | collective-permute-start | bytes 221192 | tf_op jit(solution)/shard_map/ppermute | solution.py:316
  13.0 4.2 %all_gather.24 = bf16[144,290]{1,0:T(8,128)(2,1)S(1)} all-gather(bf16[72,290]{1,0:T(8,128)(2,1)S(1)} %pad_maximum_fusion.9), channel_id=1, replica_groups=mesh['zh'=4,'x'=4,'c'=2,'y'=8,'zl'=2] {'zl'}, dimensions={0}, use_global_device_ids=true | all-gather | bytes 125280 | tf_op jit(solution)/shard_map/all_gather | solution.py:318
  18.2 3.7 %all-to-all-start = ((bf16[8,144,290]{2,1,0:T(8,128)(2,1)}), bf16[8,144,290]{2,1,0:T(8,128)(2,1)S(1)}, u32[]{:S(2)}, u32[]{:S(2)}) async-start(bf16[8,144,290]{2,1,0:T(8,128)(2,1)} %broadcast_in_dim.29), calls=%async_computation | async-start | bytes 1769472 | tf_op jit(solution)/shard_map/all_to_all | solution.py:27
  22.1 20.5 %all-gather = bf16[1728,256]{1,0:T(8,128)(2,1)S(1)} all-gather(bf16[432,256]{1,0:T(8,128)(2,1)S(1)} %pad_maximum_fusion.2), channel_id=2, replica_groups=mesh['zh'=4,'x'=4,'c'=2,'y'=8,'zl'=2] {'zh'}, dimensions={0}, use_global_device_ids=true | all-gather | bytes 1105920 | tf_op jit(solution)/shard_map/all_gather | solution.py:324
  42.6 3.1 %collective-permute-start.4 = (bf16[4,288,256]{2,1,0:T(8,128)(2,1)S(1)}, bf16[4,288,256]{2,1,0:T(8,128)(2,1)S(1)}, u32[]{:S(2)}, u32[]{:S(2)}) collective-permute-start(bf16[4,288,256]{2,1,0:T(8,128)(2,1)S(1)} %slice.44.own), channel_id=1, source_target_pairs={{96,0},{0,32},{32,64},{64,96},{97,1},{1,33},{33,65},{65,97},{98,2}... | collective-permute-start | bytes 1769480 | tf_op jit(solution)/shard_map/ppermute | solution.py:330
  45.8 3.4 %collective-permute-start.2 = (bf16[4,288,256]{2,1,0:T(8,128)(2,1)S(1)}, bf16[4,288,256]{2,1,0:T(8,128)(2,1)S(1)}, u32[]{:S(2)}, u32[]{:S(2)}) collective-permute-start(bf16[4,288,256]{2,1,0:T(8,128)(2,1)S(1)} %slice.44.own), channel_id=1, source_target_pairs={{32,0},{64,32},{96,64},{0,96},{33,1},{65,33},{97,65},{1,97},{34,2}... | collective-permute-start | bytes 1769480 | tf_op jit(solution)/shard_map/ppermute | solution.py:329
  49.2 7.9 %collective-permute-start.1 = (bf16[16,72,290]{2,1,0:T(8,128)(2,1)S(1)}, bf16[16,72,290]{2,1,0:T(8,128)(2,1)}, u32[]{:S(2)}, u32[]{:S(2)}) collective-permute-start(bf16[16,72,290]{2,1,0:T(8,128)(2,1)S(1)} %bitcast.24), channel_id=1, source_target_pairs={{0,16},{16,0},{1,17},{17,1},{2,18},{18,2},{3,19},{19,3},{4,20},{20... | collective-permute-start | bytes 2004488 | tf_op jit(solution)/shard_map/ppermute | solution.py:334
  61.0 4.6 %collective-permute-start.3 = (bf16[2,288,256]{2,1,0:T(8,128)(2,1)}, bf16[2,288,256]{2,1,0:T(8,128)(2,1)}, u32[]{:S(2)}, u32[]{:S(2)}) collective-permute-start(bf16[2,288,256]{2,1,0:T(8,128)(2,1)} %slice.45), channel_id=1, source_target_pairs={{32,0},{64,32},{96,64},{0,96},{33,1},{65,33},{97,65},{1,97},{34,2}... | collective-permute-start | bytes 884744 | tf_op jit(solution)/shard_map/ppermute | solution.py:331
  69.6 2.2 %project.1 = (bf16[144,128]{1,0:T(8,128)(2,1)S(1)}, bf16[144,128]{1,0:T(8,128)(2,1)S(1)}) custom-call(s32[40]{0:T(128)S(1)} %concatenate.68.meta, bf16[16,72,290]{2,1,0:T(8,128)(2,1)S(1)} %bitcast.25, bf16[16,72,290]{2,1,0:T(8,128)(2,1)} %collective-permute-done.1.others, f32[4,144,128]{2,1,0:T(8,128)S(1)} %pad_maximum_fusion.1.turns, ...), custom_call_target="tpu_custom_call" | custom-call | tf_op jit(solution)/shard_map/project/pallas_call | solution.py:59
  72.7 6.7 %all-to-all-start.1 = ((bf16[16,144,128]{2,1,0:T(8,128)(2,1)}), bf16[16,144,128]{2,1,0:T(8,128)(2,1)S(1)}, u32[]{:S(2)}, u32[]{:S(2)}) async-start(bf16[16,144,128]{2,1,0:T(8,128)(2,1)} %broadcast_in_dim.54), calls=%async_computation.1 | async-start | bytes 1179648 | tf_op jit(solution)/shard_map/all_to_all | solution.py:27
  79.4 8.3 %collective-permute-start.6 = (bf16[2048,128]{1,0:T(8,128)(2,1)S(1)}, bf16[2048,128]{1,0:T(8,128)(2,1)S(1)}, u32[]{:S(2)}, u32[]{:S(2)}) collective-permute-start(bf16[2048,128]{1,0:T(8,128)(2,1)S(1)} %copy-done.4), channel_id=1, source_target_pairs={{0,16},{16,0},{1,17},{17,1},{2,18},{18,2},{3,19},{19,3},{4,20},{20... | collective-permute-start | bytes 1572872 | tf_op jit(solution)/shard_map/ppermute | solution.py:367
  87.7 3.5 %collective-permute-start.9 = (bf16[4,144,256]{2,1,0:T(8,128)(2,1)S(1)}, bf16[4,144,256]{2,1,0:T(8,128)(2,1)S(1)}, u32[]{:S(2)}, u32[]{:S(2)}) collective-permute-start(bf16[4,144,256]{2,1,0:T(8,128)(2,1)S(1)} %copy-done.2), channel_id=1, source_target_pairs={{96,0},{0,32},{32,64},{64,96},{97,1},{1,33},{33,65},{65,97},{98,2}... | collective-permute-start | bytes 884744 | tf_op jit(solution)/shard_map/ppermute | solution.py:369
  91.2 3.2 %collective-permute-start.8 = (bf16[4,144,256]{2,1,0:T(8,128)(2,1)S(1)}, bf16[4,144,256]{2,1,0:T(8,128)(2,1)S(1)}, u32[]{:S(2)}, u32[]{:S(2)}) collective-permute-start(bf16[4,144,256]{2,1,0:T(8,128)(2,1)S(1)} %copy-done.2), channel_id=1, source_target_pairs={{32,0},{64,32},{96,64},{0,96},{33,1},{65,33},{97,65},{1,97},{34,2}... | collective-permute-start | bytes 884744 | tf_op jit(solution)/shard_map/ppermute | solution.py:368
  96.3 2.3 %collective-permute-start.7 = (bf16[2,144,128]{2,1,0:T(8,128)(2,1)S(1)}, bf16[2,144,128]{2,1,0:T(8,128)(2,1)S(1)}, u32[]{:S(2)}, u32[]{:S(2)}) collective-permute-start(bf16[2,144,128]{2,1,0:T(8,128)(2,1)S(1)} %bitcast.33), channel_id=1, source_target_pairs={{0,32},{32,0},{64,96},{96,64},{1,33},{33,1},{65,97},{97,65},{2,34}... | collective-permute-start | bytes 221192 | tf_op jit(solution)/shard_map/ppermute | solution.py:371
  98.6 5.0 %attend.1 = bf16[2560,128]{1,0:T(8,128)(2,1)} custom-call(s32[40]{0:T(128)S(1)} %concatenate.68.meta, bf16[2304,128]{1,0:T(8,128)(2,1)S(1)} %bitcast.26, bf16[1024,128]{1,0:T(8,128)(2,1)S(1)} %copy-done, bf16[1024,128]{1,0:T(8,128)(2,1)S(1)} %copy-done.1, bf16[2048,128]{1,0:T(8,128)(2,1)S(1)} %collective-permute-done.6.others), custom_call_target="tpu_custom_call" | custom-call | tf_op jit(solution)/shard_map/attend/pallas_call | solution.py:123
  104.3 7.7 %all-to-all-start.2 = ((bf16[16,160,128]{2,1,0:T(8,128)(2,1)}), bf16[16,160,128]{2,1,0:T(8,128)(2,1)S(1)}, u32[]{:S(2)}, u32[]{:S(2)}) async-start(bf16[16,160,128]{2,1,0:T(8,128)(2,1)} %bitcast.13), calls=%async_computation.2 | async-start | bytes 1310720 | tf_op jit(solution)/shard_map/all_to_all | solution.py:388
  112.1 4.8 %collective-permute-start.10 = (bf16[2,2,144,128]{3,2,1,0:T(8,128)(2,1)S(1)}, bf16[2,2,144,128]{3,2,1,0:T(8,128)(2,1)S(1)}, u32[]{:S(2)}, u32[]{:S(2)}) collective-permute-start(bf16[2,2,144,128]{3,2,1,0:T(8,128)(2,1)S(1)} %pad_maximum_fusion.4.near), channel_id=1, source_target_pairs={{0,64},{32,96},{64,0},{96,32},{1,65},{33,97},{65,1},{97,33},{2,66}... | collective-permute-start | bytes 442376 | tf_op jit(solution)/shard_map/ppermute | solution.py:379
  116.9 2.2 %collective-permute-start.12 = (bf16[2,144,256]{2,1,0:T(8,128)(2,1)S(1)}, bf16[2,144,256]{2,1,0:T(8,128)(2,1)S(1)}, u32[]{:S(2)}, u32[]{:S(2)}) collective-permute-start(bf16[2,144,256]{2,1,0:T(8,128)(2,1)S(1)} %slice.40), channel_id=1, source_target_pairs={{96,0},{0,32},{32,64},{64,96},{97,1},{1,33},{33,65},{65,97},{98,2}... | collective-permute-start | bytes 442376 | tf_op jit(solution)/shard_map/ppermute | solution.py:384
  119.1 4.3 %collective-permute-start.11 = (bf16[2,144,256]{2,1,0:T(8,128)(2,1)S(1)}, bf16[2,144,256]{2,1,0:T(8,128)(2,1)S(1)}, u32[]{:S(2)}, u32[]{:S(2)}) collective-permute-start(bf16[2,144,256]{2,1,0:T(8,128)(2,1)S(1)} %slice.39), channel_id=1, source_target_pairs={{32,0},{64,32},{96,64},{0,96},{33,1},{65,33},{97,65},{1,97},{34,2}... | collective-permute-start | bytes 442376 | tf_op jit(solution)/shard_map/ppermute | solution.py:383
  127.6 5.1 %all-gather.2 = bf16[288,128]{1,0:T(8,128)(2,1)S(1)} all-gather(bf16[144,128]{1,0:T(8,128)(2,1)S(1)} %divide.1), channel_id=4, replica_groups=mesh['zh'=4,'x'=4,'c'=2,'y'=8,'zl'=2] {'c'}, dimensions={0}, use_global_device_ids=true | all-gather | bytes 110592 | tf_op jit(solution)/shard_map/all_gather | solution.py:391
  134.8 11.9 %all-to-all-start.3 = ((bf16[16,176,128]{2,1,0:T(8,128)(2,1)}), bf16[16,176,128]{2,1,0:T(8,128)(2,1)S(1)}, u32[]{:S(2)}, u32[]{:S(2)}) async-start(bf16[16,176,128]{2,1,0:T(8,128)(2,1)} %spread.1), calls=%async_computation.3 | async-start | bytes 1441792 | tf_op jit(solution)/shard_map/all_to_all | solution.py:395
  146.8 21.2 %all_gather.31.mine = bf16[2304,128]{1,0:T(8,128)(2,1)S(1)} all-gather(bf16[576,128]{1,0:T(8,128)(2,1)S(1)} %get-tuple-element.50), channel_id=1, replica_groups=mesh['zh'=4,'x'=4,'c'=2,'y'=8,'zl'=2] {'zh'}, dimensions={0}, use_global_device_ids=true | all-gather | bytes 737280 | tf_op jit(solution)/shard_map/all_gather | solution.py:394
  169.1 10.1 %all-to-all-start.4 = ((f32[32,1,72]{2,1,0:T(1,128)}), f32[32,1,72]{2,1,0:T(1,128)S(1)}, u32[]{:S(2)}, u32[]{:S(2)}) async-start(f32[32,1,72]{2,1,0:T(1,128)} %bitcast.18), calls=%async_computation.4 | async-start | bytes 32768 | tf_op jit(solution)/shard_map/all_to_all | solution.py:402
  183.5 3.4 %all-to-all-done.4 = f32[32,1,72]{2,1,0:T(1,128)S(1)} async-done(((f32[32,1,72]{2,1,0:T(1,128)}), f32[32,1,72]{2,1,0:T(1,128)S(1)}, u32[]{:S(2)}, u32[]{:S(2)}) %all-to-all-start.4) | async-done | bytes 9248 | tf_op jit(solution)/shard_map/all_to_all | solution.py:402
  (92 shorter events, 30.6 us)
Async XLA Ops:
  2.3 15.0 %collective-permute-start = (bf16[144,256]{1,0:T(8,128)(2,1)S(1)}, bf16[144,256]{1,0:T(8,128)(2,1)S(1)}, u32[]{:S(2)}, u32[]{:S(2)}) collective-permute-start(bf16[144,256]{1,0:T(8,128)(2,1)S(1)} %get-tuple-element.61), channel_id=1, source_target_pairs={{0,16},{16,0},{1,17},{17,1},{2,18},{18,2},{3,19},{19,3},{4,20},{20... | collective-permute-start | bytes 221192 | tf_op jit(solution)/shard_map/ppermute | solution.py:316
  18.2 31.0 %all-to-all-start = ((bf16[8,144,290]{2,1,0:T(8,128)(2,1)}), bf16[8,144,290]{2,1,0:T(8,128)(2,1)S(1)}, u32[]{:S(2)}, u32[]{:S(2)}) async-start(bf16[8,144,290]{2,1,0:T(8,128)(2,1)} %broadcast_in_dim.29), calls=%async_computation | async-start | bytes 1769472 | tf_op jit(solution)/shard_map/all_to_all | solution.py:27
  42.6 15.0 %collective-permute-start.4 = (bf16[4,288,256]{2,1,0:T(8,128)(2,1)S(1)}, bf16[4,288,256]{2,1,0:T(8,128)(2,1)S(1)}, u32[]{:S(2)}, u32[]{:S(2)}) collective-permute-start(bf16[4,288,256]{2,1,0:T(8,128)(2,1)S(1)} %slice.44.own), channel_id=1, source_target_pairs={{96,0},{0,32},{32,64},{64,96},{97,1},{1,33},{33,65},{65,97},{98,2}... | collective-permute-start | bytes 1769480 | tf_op jit(solution)/shard_map/ppermute | solution.py:330
  45.8 14.5 %collective-permute-start.2 = (bf16[4,288,256]{2,1,0:T(8,128)(2,1)S(1)}, bf16[4,288,256]{2,1,0:T(8,128)(2,1)S(1)}, u32[]{:S(2)}, u32[]{:S(2)}) collective-permute-start(bf16[4,288,256]{2,1,0:T(8,128)(2,1)S(1)} %slice.44.own), channel_id=1, source_target_pairs={{32,0},{64,32},{96,64},{0,96},{33,1},{65,33},{97,65},{1,97},{34,2}... | collective-permute-start | bytes 1769480 | tf_op jit(solution)/shard_map/ppermute | solution.py:329
  49.2 20.3 %collective-permute-start.1 = (bf16[16,72,290]{2,1,0:T(8,128)(2,1)S(1)}, bf16[16,72,290]{2,1,0:T(8,128)(2,1)}, u32[]{:S(2)}, u32[]{:S(2)}) collective-permute-start(bf16[16,72,290]{2,1,0:T(8,128)(2,1)S(1)} %bitcast.24), channel_id=1, source_target_pairs={{0,16},{16,0},{1,17},{17,1},{2,18},{18,2},{3,19},{19,3},{4,20},{20... | collective-permute-start | bytes 2004488 | tf_op jit(solution)/shard_map/ppermute | solution.py:334
  57.6 8.1 %copy-start = (bf16[1024,128]{1,0:T(8,128)(2,1)S(1)}, bf16[1024,128]{1,0:T(8,128)(2,1)}, u32[]{:S(2)}) copy-start(bf16[1024,128]{1,0:T(8,128)(2,1)} %k_old.1) | copy-start | bytes 786436
  58.4 9.9 %collective-permute-start.5 = (bf16[2,288,256]{2,1,0:T(8,128)(2,1)}, bf16[2,288,256]{2,1,0:T(8,128)(2,1)}, u32[]{:S(2)}, u32[]{:S(2)}) collective-permute-start(bf16[2,288,256]{2,1,0:T(8,128)(2,1)} %slice.46), channel_id=1, source_target_pairs={{96,0},{0,32},{32,64},{64,96},{97,1},{1,33},{33,65},{65,97},{98,2}... | collective-permute-start | bytes 884744 | tf_op jit(solution)/shard_map/ppermute | solution.py:332
  61.0 8.5 %collective-permute-start.3 = (bf16[2,288,256]{2,1,0:T(8,128)(2,1)}, bf16[2,288,256]{2,1,0:T(8,128)(2,1)}, u32[]{:S(2)}, u32[]{:S(2)}) collective-permute-start(bf16[2,288,256]{2,1,0:T(8,128)(2,1)} %slice.45), channel_id=1, source_target_pairs={{32,0},{64,32},{96,64},{0,96},{33,1},{65,33},{97,65},{1,97},{34,2}... | collective-permute-start | bytes 884744 | tf_op jit(solution)/shard_map/ppermute | solution.py:331
  71.8 15.9 %copy-start.2 = (bf16[4,144,256]{2,1,0:T(8,128)(2,1)S(1)}, bf16[4,144,256]{2,1,0:T(8,128)(2,1)}, u32[]{:S(2)}) copy-start(bf16[4,144,256]{2,1,0:T(8,128)(2,1)} %slice.47.own) | copy-start | bytes 884740
  72.7 25.9 %all-to-all-start.1 = ((bf16[16,144,128]{2,1,0:T(8,128)(2,1)}), bf16[16,144,128]{2,1,0:T(8,128)(2,1)S(1)}, u32[]{:S(2)}, u32[]{:S(2)}) async-start(bf16[16,144,128]{2,1,0:T(8,128)(2,1)} %broadcast_in_dim.54), calls=%async_computation.1 | async-start | bytes 1179648 | tf_op jit(solution)/shard_map/all_to_all | solution.py:27
  79.4 19.2 %collective-permute-start.6 = (bf16[2048,128]{1,0:T(8,128)(2,1)S(1)}, bf16[2048,128]{1,0:T(8,128)(2,1)S(1)}, u32[]{:S(2)}, u32[]{:S(2)}) collective-permute-start(bf16[2048,128]{1,0:T(8,128)(2,1)S(1)} %copy-done.4), channel_id=1, source_target_pairs={{0,16},{16,0},{1,17},{17,1},{2,18},{18,2},{3,19},{19,3},{4,20},{20... | collective-permute-start | bytes 1572872 | tf_op jit(solution)/shard_map/ppermute | solution.py:367
  87.7 16.6 %collective-permute-start.9 = (bf16[4,144,256]{2,1,0:T(8,128)(2,1)S(1)}, bf16[4,144,256]{2,1,0:T(8,128)(2,1)S(1)}, u32[]{:S(2)}, u32[]{:S(2)}) collective-permute-start(bf16[4,144,256]{2,1,0:T(8,128)(2,1)S(1)} %copy-done.2), channel_id=1, source_target_pairs={{96,0},{0,32},{32,64},{64,96},{97,1},{1,33},{33,65},{65,97},{98,2}... | collective-permute-start | bytes 884744 | tf_op jit(solution)/shard_map/ppermute | solution.py:369
  91.2 13.1 %collective-permute-start.8 = (bf16[4,144,256]{2,1,0:T(8,128)(2,1)S(1)}, bf16[4,144,256]{2,1,0:T(8,128)(2,1)S(1)}, u32[]{:S(2)}, u32[]{:S(2)}) collective-permute-start(bf16[4,144,256]{2,1,0:T(8,128)(2,1)S(1)} %copy-done.2), channel_id=1, source_target_pairs={{32,0},{64,32},{96,64},{0,96},{33,1},{65,33},{97,65},{1,97},{34,2}... | collective-permute-start | bytes 884744 | tf_op jit(solution)/shard_map/ppermute | solution.py:368
  96.3 8.0 %collective-permute-start.7 = (bf16[2,144,128]{2,1,0:T(8,128)(2,1)S(1)}, bf16[2,144,128]{2,1,0:T(8,128)(2,1)S(1)}, u32[]{:S(2)}, u32[]{:S(2)}) collective-permute-start(bf16[2,144,128]{2,1,0:T(8,128)(2,1)S(1)} %bitcast.33), channel_id=1, source_target_pairs={{0,32},{32,0},{64,96},{96,64},{1,33},{33,1},{65,97},{97,65},{2,34}... | collective-permute-start | bytes 221192 | tf_op jit(solution)/shard_map/ppermute | solution.py:371
  104.3 22.5 %all-to-all-start.2 = ((bf16[16,160,128]{2,1,0:T(8,128)(2,1)}), bf16[16,160,128]{2,1,0:T(8,128)(2,1)S(1)}, u32[]{:S(2)}, u32[]{:S(2)}) async-start(bf16[16,160,128]{2,1,0:T(8,128)(2,1)} %bitcast.13), calls=%async_computation.2 | async-start | bytes 1310720 | tf_op jit(solution)/shard_map/all_to_all | solution.py:388
  112.1 11.9 %collective-permute-start.10 = (bf16[2,2,144,128]{3,2,1,0:T(8,128)(2,1)S(1)}, bf16[2,2,144,128]{3,2,1,0:T(8,128)(2,1)S(1)}, u32[]{:S(2)}, u32[]{:S(2)}) collective-permute-start(bf16[2,2,144,128]{3,2,1,0:T(8,128)(2,1)S(1)} %pad_maximum_fusion.4.near), channel_id=1, source_target_pairs={{0,64},{32,96},{64,0},{96,32},{1,65},{33,97},{65,1},{97,33},{2,66}... | collective-permute-start | bytes 442376 | tf_op jit(solution)/shard_map/ppermute | solution.py:379
  116.9 15.8 %collective-permute-start.12 = (bf16[2,144,256]{2,1,0:T(8,128)(2,1)S(1)}, bf16[2,144,256]{2,1,0:T(8,128)(2,1)S(1)}, u32[]{:S(2)}, u32[]{:S(2)}) collective-permute-start(bf16[2,144,256]{2,1,0:T(8,128)(2,1)S(1)} %slice.40), channel_id=1, source_target_pairs={{96,0},{0,32},{32,64},{64,96},{97,1},{1,33},{33,65},{65,97},{98,2}... | collective-permute-start | bytes 442376 | tf_op jit(solution)/shard_map/ppermute | solution.py:384
  119.1 13.6 %collective-permute-start.11 = (bf16[2,144,256]{2,1,0:T(8,128)(2,1)S(1)}, bf16[2,144,256]{2,1,0:T(8,128)(2,1)S(1)}, u32[]{:S(2)}, u32[]{:S(2)}) collective-permute-start(bf16[2,144,256]{2,1,0:T(8,128)(2,1)S(1)} %slice.39), channel_id=1, source_target_pairs={{32,0},{64,32},{96,64},{0,96},{33,1},{65,33},{97,65},{1,97},{34,2}... | collective-permute-start | bytes 442376 | tf_op jit(solution)/shard_map/ppermute | solution.py:383
  134.8 11.9 %copy-start.8 = (bf16[288]{0:T(512)(128)(2,1)S(1)}, bf16[288]{0:T(512)(128)(2,1)}, u32[]{:S(2)}) copy-start(bf16[288]{0:T(512)(128)(2,1)} %param.18) | copy-start | bytes 1732
  134.8 33.2 %all-to-all-start.3 = ((bf16[16,176,128]{2,1,0:T(8,128)(2,1)}), bf16[16,176,128]{2,1,0:T(8,128)(2,1)S(1)}, u32[]{:S(2)}, u32[]{:S(2)}) async-start(bf16[16,176,128]{2,1,0:T(8,128)(2,1)} %spread.1), calls=%async_computation.3 | async-start | bytes 1441792 | tf_op jit(solution)/shard_map/all_to_all | solution.py:395
  168.0 19.0 %copy-start.5 = (bf16[72,288]{1,0:T(8,128)(2,1)S(1)}, bf16[72,288]{1,0:T(8,128)(2,1)}, u32[]{:S(2)}) copy-start(bf16[72,288]{1,0:T(8,128)(2,1)} %param.12) | copy-start | bytes 124420
  169.1 17.9 %all-to-all-start.4 = ((f32[32,1,72]{2,1,0:T(1,128)}), f32[32,1,72]{2,1,0:T(1,128)S(1)}, u32[]{:S(2)}, u32[]{:S(2)}) async-start(f32[32,1,72]{2,1,0:T(1,128)} %bitcast.18), calls=%async_computation.4 | async-start | bytes 32768 | tf_op jit(solution)/shard_map/all_to_all | solution.py:402
  179.2 7.8 %collective-permute-start.13 = (f32[72,144]{1,0:T(8,128)S(1)}, f32[72,144]{1,0:T(8,128)S(1)}, u32[]{:S(2)}, u32[]{:S(2)}) collective-permute-start(f32[72,144]{1,0:T(8,128)S(1)} %fusion.11), channel_id=1, source_target_pairs={{0,16},{16,0},{1,17},{17,1},{2,18},{18,2},{3,19},{19,3},{4,20},{20... | collective-permute-start | bytes 124424 | tf_op jit(solution)/shard_map/ppermute | solution.py:407
  181.3 6.4 %collective-permute-start.14 = (bf16[2304,128]{1,0:T(8,128)(2,1)S(1)}, bf16[2304,128]{1,0:T(8,128)(2,1)S(1)}, u32[]{:S(2)}, u32[]{:S(2)}) collective-permute-start(bf16[2304,128]{1,0:T(8,128)(2,1)S(1)} %all_gather.31.mine), channel_id=1, source_target_pairs={{0,16},{16,0},{1,17},{17,1},{2,18},{18,2},{3,19},{19,3},{4,20},{20... | collective-permute-start | bytes 1769480 | tf_op jit(solution)/shard_map/ppermute | solution.py:403
  (7 other events, 46.0 us)

commit v14 on v13

--- a/solution.py
+++ b/solution.py
@@ -265,7 +265,9 @@
     count = 4
     rows = attended.shape[1]
     heads = jnp.concatenate([attended[h] for h in range(attended.shape[0])], axis=1)
-    padded = jnp.concatenate([heads, jnp.zeros((2 * HD - rows, heads.shape[1]), BF16)], axis=0)
+    tail, empty = heads[HD:], jnp.zeros((HD, heads.shape[1]), BF16)
+    low = jnp.concatenate([tail, empty[16:]], axis=0)
+    high = jnp.concatenate([empty[:16], tail, empty[32:]], axis=0)
     last = (((1,), (1,)), ((), ()))
     for step in range(count):
         along = lax.rem(here + step, count)
@@ -276,17 +278,19 @@
             else:
                 weights = (own, right, None, left)[step][block]
             wide = lax.dot_general(heads, weights[:HD], last, preferred_element_type=F32)
-            rest = lax.dot_general(weights[HD:], padded, last, preferred_element_type=F32)
+            rest = lax.dot_general(weights[HD:], heads[:HD], last, preferred_element_type=F32)
             out[at, :rows, :] = wide.astype(BF16)
-            out[at, rows : rows + 16, :] = rest[:, :HD].astype(BF16)
-            out[at, rows + 16 :, :] = rest[:, HD:].astype(BF16)
+            out[at, rows : rows + 16, :] = rest.astype(BF16)
+            corner = lax.dot_general(weights[HD : HD + 8], low, last, preferred_element_type=F32)
+            corner += lax.dot_general(weights[HD + 8 :], high, last, preferred_element_type=F32)
+            out[at, rows + 16 :, :] = corner.astype(BF16)
 
 
 def spread(meta, attended, columns, chunks):
     vmem = pl.BlockSpec(memory_space=pltpu.VMEM)
     return pl.pallas_call(
         spread_kernel,
-        out_shape=jax.ShapeDtypeStruct((chunks, attended.shape[1] + 32, HD), BF16),
+        out_shape=jax.ShapeDtypeStruct((chunks, attended.shape[1] + 24, HD), BF16),
         in_specs=[pl.BlockSpec(memory_space=pltpu.SMEM)] + [vmem] * (1 + len(columns)),
         out_specs=vmem,
         compiler_params=pltpu.CompilerParams(vmem_limit_bytes=32 << 20),
@@ -394,7 +398,8 @@
     kind = lax.all_gather(kind, "zh", axis=0, tiled=True)
     total = jnp.sum(lax.all_to_all(partial_out, GY, 0, 0).astype(F32), axis=0)
     rows = 2 * tok_rows
-    rest = jnp.concatenate([total[rows : rows + 16], total[rows + 16 :, : rows - HD]], axis=1)
+    corner = jnp.concatenate([total[rows + 16 :, :16], total[rows + 16 :, 16:32]], axis=0)
+    rest = jnp.concatenate([total[rows : rows + 16], corner], axis=1)
     branch = jnp.concatenate([total[:rows], rest.T], axis=1)
     squares = jnp.sum(branch * branch, axis=1).reshape(2, 1, 1, tok_rows)
     squares = jnp.broadcast_to(squares, (2, n_gy, 1, tok_rows)).reshape(2 * n_gy, 1, tok_rows)

time: 191 us -> 191 us (level)
  transfers between devices with their start and end apart: 20 -> 20, of which waited for: 5 -> 5; matrix products, arithmetic and copies ran while one was open for 4% -> 4% of each run, Pallas kernels for 4% -> 3%
where the time goes in v14:
time: 191 us; the launch traced here: 189 us
  starting transfers between devices  103 us (54%)
  blocking collectives  52.2 us (27%)
  Pallas kernels  12.5 us (7%)
  waiting for transfers between devices  8.16 us (4%)
  local copies, waits for them, and re-layouts  7.14 us (4%)
  other arithmetic  5.06 us (3%)
    all_gather x1, blocking collectives, on_device(): kind = lax.all_gather(kind, 'zh', axis=0, tiled=True)  20.5 us
    all_gather x1, blocking collectives, on_device(): weights = lax.all_gather(weights, 'zh', axis=0)  20.5 us
    all_to_all x1, starting transfers between devices, on_device(): total = jnp.sum(lax.all_to_all(partial_out, GY, 0, 0).astype(F32), axis=0)  11.9 us
    all_to_all x1, starting transfers between devices, on_device(): squares = lax.all_to_all(squares, ('c',) + GY, 0, 0)  10.5 us
    all_to_all x2, starting transfers between devices, everywhere(): lax.all_to_all(jnp.broadcast_to(value[None], (count,) + value.shape), axe...  10.4 us
    ppermute x1, starting transfers between devices, on_device(): came = lax.ppermute(jnp.where(core == 0, second, first), 'c', swap)  8.79 us
    ppermute x1, starting transfers between devices, on_device(): caches = lax.ppermute(caches, 'c', swap)  8.25 us
    ppermute x1, starting transfers between devices, on_device(): other = lax.ppermute(gained, 'c', swap)  7.9 us
  transfers between devices with their start and end apart: 20, of which 5 were waited for; matrix products, arithmetic and copies ran while one was open for 4% of the time, Pallas kernels for 3%

profile of v14, /device:TPU:1, one launch (start us, length us, event | category | flops | bytes accessed | tf_op | source)
XLA Modules:
  0.0 189.2 jit_solution(3993255731042461328)
XLA Ops:
  2.3 8.8 %collective-permute-start = (bf16[144,256]{1,0:T(8,128)(2,1)S(1)}, bf16[144,256]{1,0:T(8,128)(2,1)S(1)}, u32[]{:S(2)}, u32[]{:S(2)}) collective-permute-start(bf16[144,256]{1,0:T(8,128)(2,1)S(1)} %get-tuple-element.61), channel_id=1, source_target_pairs={{0,16},{16,0},{1,17},{17,1},{2,18},{18,2},{3,19},{19,3},{4,20},{20... | collective-permute-start | bytes 221192 | tf_op jit(solution)/shard_map/ppermute | solution.py:320
  13.0 4.2 %all_gather.24 = bf16[144,290]{1,0:T(8,128)(2,1)S(1)} all-gather(bf16[72,290]{1,0:T(8,128)(2,1)S(1)} %pad_maximum_fusion.9), channel_id=1, replica_groups=mesh['zh'=4,'x'=4,'c'=2,'y'=8,'zl'=2] {'zl'}, dimensions={0}, use_global_device_ids=true | all-gather | bytes 125280 | tf_op jit(solution)/shard_map/all_gather | solution.py:322
  18.2 3.7 %all-to-all-start = ((bf16[8,144,290]{2,1,0:T(8,128)(2,1)}), bf16[8,144,290]{2,1,0:T(8,128)(2,1)S(1)}, u32[]{:S(2)}, u32[]{:S(2)}) async-start(bf16[8,144,290]{2,1,0:T(8,128)(2,1)} %broadcast_in_dim.29), calls=%async_computation | async-start | bytes 1769472 | tf_op jit(solution)/shard_map/all_to_all | solution.py:27
  22.1 20.5 %all-gather = bf16[1728,256]{1,0:T(8,128)(2,1)S(1)} all-gather(bf16[432,256]{1,0:T(8,128)(2,1)S(1)} %pad_maximum_fusion.2), channel_id=2, replica_groups=mesh['zh'=4,'x'=4,'c'=2,'y'=8,'zl'=2] {'zh'}, dimensions={0}, use_global_device_ids=true | all-gather | bytes 1105920 | tf_op jit(solution)/shard_map/all_gather | solution.py:328
  42.6 3.1 %collective-permute-start.4 = (bf16[4,288,256]{2,1,0:T(8,128)(2,1)S(1)}, bf16[4,288,256]{2,1,0:T(8,128)(2,1)S(1)}, u32[]{:S(2)}, u32[]{:S(2)}) collective-permute-start(bf16[4,288,256]{2,1,0:T(8,128)(2,1)S(1)} %slice.48.own), channel_id=1, source_target_pairs={{96,0},{0,32},{32,64},{64,96},{97,1},{1,33},{33,65},{65,97},{98,2}... | collective-permute-start | bytes 1769480 | tf_op jit(solution)/shard_map/ppermute | solution.py:334
  45.8 3.4 %collective-permute-start.2 = (bf16[4,288,256]{2,1,0:T(8,128)(2,1)S(1)}, bf16[4,288,256]{2,1,0:T(8,128)(2,1)S(1)}, u32[]{:S(2)}, u32[]{:S(2)}) collective-permute-start(bf16[4,288,256]{2,1,0:T(8,128)(2,1)S(1)} %slice.48.own), channel_id=1, source_target_pairs={{32,0},{64,32},{96,64},{0,96},{33,1},{65,33},{97,65},{1,97},{34,2}... | collective-permute-start | bytes 1769480 | tf_op jit(solution)/shard_map/ppermute | solution.py:333
  49.2 7.9 %collective-permute-start.1 = (bf16[16,72,290]{2,1,0:T(8,128)(2,1)S(1)}, bf16[16,72,290]{2,1,0:T(8,128)(2,1)}, u32[]{:S(2)}, u32[]{:S(2)}) collective-permute-start(bf16[16,72,290]{2,1,0:T(8,128)(2,1)S(1)} %bitcast.24), channel_id=1, source_target_pairs={{0,16},{16,0},{1,17},{17,1},{2,18},{18,2},{3,19},{19,3},{4,20},{20... | collective-permute-start | bytes 2004488 | tf_op jit(solution)/shard_map/ppermute | solution.py:338
  61.0 4.6 %collective-permute-start.3 = (bf16[2,288,256]{2,1,0:T(8,128)(2,1)}, bf16[2,288,256]{2,1,0:T(8,128)(2,1)}, u32[]{:S(2)}, u32[]{:S(2)}) collective-permute-start(bf16[2,288,256]{2,1,0:T(8,128)(2,1)} %slice.49), channel_id=1, source_target_pairs={{32,0},{64,32},{96,64},{0,96},{33,1},{65,33},{97,65},{1,97},{34,2}... | collective-permute-start | bytes 884744 | tf_op jit(solution)/shard_map/ppermute | solution.py:335
  69.5 2.2 %project.1 = (bf16[144,128]{1,0:T(8,128)(2,1)S(1)}, bf16[144,128]{1,0:T(8,128)(2,1)S(1)}) custom-call(s32[40]{0:T(128)S(1)} %concatenate.71.meta, bf16[16,72,290]{2,1,0:T(8,128)(2,1)S(1)} %bitcast.25, bf16[16,72,290]{2,1,0:T(8,128)(2,1)} %collective-permute-done.1.others, f32[4,144,128]{2,1,0:T(8,128)S(1)} %pad_maximum_fusion.1.turns, ...), custom_call_target="tpu_custom_call" | custom-call | tf_op jit(solution)/shard_map/project/pallas_call | solution.py:59
  72.6 6.7 %all-to-all-start.1 = ((bf16[16,144,128]{2,1,0:T(8,128)(2,1)}), bf16[16,144,128]{2,1,0:T(8,128)(2,1)S(1)}, u32[]{:S(2)}, u32[]{:S(2)}) async-start(bf16[16,144,128]{2,1,0:T(8,128)(2,1)} %broadcast_in_dim.54), calls=%async_computation.1 | async-start | bytes 1179648 | tf_op jit(solution)/shard_map/all_to_all | solution.py:27
  79.4 8.3 %collective-permute-start.6 = (bf16[2048,128]{1,0:T(8,128)(2,1)S(1)}, bf16[2048,128]{1,0:T(8,128)(2,1)S(1)}, u32[]{:S(2)}, u32[]{:S(2)}) collective-permute-start(bf16[2048,128]{1,0:T(8,128)(2,1)S(1)} %copy-done.4), channel_id=1, source_target_pairs={{0,16},{16,0},{1,17},{17,1},{2,18},{18,2},{3,19},{19,3},{4,20},{20... | collective-permute-start | bytes 1572872 | tf_op jit(solution)/shard_map/ppermute | solution.py:371
  87.6 3.5 %collective-permute-start.9 = (bf16[4,144,256]{2,1,0:T(8,128)(2,1)S(1)}, bf16[4,144,256]{2,1,0:T(8,128)(2,1)S(1)}, u32[]{:S(2)}, u32[]{:S(2)}) collective-permute-start(bf16[4,144,256]{2,1,0:T(8,128)(2,1)S(1)} %copy-done.2), channel_id=1, source_target_pairs={{96,0},{0,32},{32,64},{64,96},{97,1},{1,33},{33,65},{65,97},{98,2}... | collective-permute-start | bytes 884744 | tf_op jit(solution)/shard_map/ppermute | solution.py:373
  91.2 3.2 %collective-permute-start.8 = (bf16[4,144,256]{2,1,0:T(8,128)(2,1)S(1)}, bf16[4,144,256]{2,1,0:T(8,128)(2,1)S(1)}, u32[]{:S(2)}, u32[]{:S(2)}) collective-permute-start(bf16[4,144,256]{2,1,0:T(8,128)(2,1)S(1)} %copy-done.2), channel_id=1, source_target_pairs={{32,0},{64,32},{96,64},{0,96},{33,1},{65,33},{97,65},{1,97},{34,2}... | collective-permute-start | bytes 884744 | tf_op jit(solution)/shard_map/ppermute | solution.py:372
  96.2 2.3 %collective-permute-start.7 = (bf16[2,144,128]{2,1,0:T(8,128)(2,1)S(1)}, bf16[2,144,128]{2,1,0:T(8,128)(2,1)S(1)}, u32[]{:S(2)}, u32[]{:S(2)}) collective-permute-start(bf16[2,144,128]{2,1,0:T(8,128)(2,1)S(1)} %bitcast.33), channel_id=1, source_target_pairs={{0,32},{32,0},{64,96},{96,64},{1,33},{33,1},{65,97},{97,65},{2,34}... | collective-permute-start | bytes 221192 | tf_op jit(solution)/shard_map/ppermute | solution.py:375
  98.6 4.6 %attend.1 = bf16[2560,128]{1,0:T(8,128)(2,1)} custom-call(s32[40]{0:T(128)S(1)} %concatenate.71.meta, bf16[2304,128]{1,0:T(8,128)(2,1)S(1)} %bitcast.26, bf16[1024,128]{1,0:T(8,128)(2,1)S(1)} %copy-done, bf16[1024,128]{1,0:T(8,128)(2,1)S(1)} %copy-done.1, bf16[2048,128]{1,0:T(8,128)(2,1)S(1)} %collective-permute-done.6.others), custom_call_target="tpu_custom_call" | custom-call | tf_op jit(solution)/shard_map/attend/pallas_call | solution.py:123
  104.3 7.7 %all-to-all-start.2 = ((bf16[16,160,128]{2,1,0:T(8,128)(2,1)}), bf16[16,160,128]{2,1,0:T(8,128)(2,1)S(1)}, u32[]{:S(2)}, u32[]{:S(2)}) async-start(bf16[16,160,128]{2,1,0:T(8,128)(2,1)} %bitcast.13), calls=%async_computation.2 | async-start | bytes 1310720 | tf_op jit(solution)/shard_map/all_to_all | solution.py:392
  112.0 4.8 %collective-permute-start.10 = (bf16[2,2,144,128]{3,2,1,0:T(8,128)(2,1)S(1)}, bf16[2,2,144,128]{3,2,1,0:T(8,128)(2,1)S(1)}, u32[]{:S(2)}, u32[]{:S(2)}) collective-permute-start(bf16[2,2,144,128]{3,2,1,0:T(8,128)(2,1)S(1)} %pad_maximum_fusion.4.near), channel_id=1, source_target_pairs={{0,64},{32,96},{64,0},{96,32},{1,65},{33,97},{65,1},{97,33},{2,66}... | collective-permute-start | bytes 442376 | tf_op jit(solution)/shard_map/ppermute | solution.py:383
  119.0 4.3 %collective-permute-start.11 = (bf16[2,144,256]{2,1,0:T(8,128)(2,1)S(1)}, bf16[2,144,256]{2,1,0:T(8,128)(2,1)S(1)}, u32[]{:S(2)}, u32[]{:S(2)}) collective-permute-start(bf16[2,144,256]{2,1,0:T(8,128)(2,1)S(1)} %slice.42), channel_id=1, source_target_pairs={{32,0},{64,32},{96,64},{0,96},{33,1},{65,33},{97,65},{1,97},{34,2}... | collective-permute-start | bytes 442376 | tf_op jit(solution)/shard_map/ppermute | solution.py:387
  127.5 5.1 %all-gather.2 = bf16[288,128]{1,0:T(8,128)(2,1)S(1)} all-gather(bf16[144,128]{1,0:T(8,128)(2,1)S(1)} %divide.1), channel_id=4, replica_groups=mesh['zh'=4,'x'=4,'c'=2,'y'=8,'zl'=2] {'c'}, dimensions={0}, use_global_device_ids=true | all-gather | bytes 110592 | tf_op jit(solution)/shard_map/all_gather | solution.py:395
  132.6 2.3 %spread.1 = bf16[16,168,128]{2,1,0:T(8,128)(2,1)} custom-call(s32[40]{0:T(128)S(1)} %concatenate.71.meta, bf16[2,144,128]{2,1,0:T(8,128)(2,1)S(1)} %bitcast.27, bf16[4,144,256]{2,1,0:T(8,128)(2,1)S(1)} %copy-done.2, bf16[4,144,256]{2,1,0:T(8,128)(2,1)S(1)} %collective-permute-done.8.right, bf16[2,144,256]{2,1,0:T(8,128)(2,1)S(1)} %collective-permute-done.11.ahead, ...), custom_call_target="tpu_custom_call" | custom-call | tf_op jit(solution)/shard_map/spread/pallas_call | solution.py:291
  134.9 11.9 %all-to-all-start.3 = ((bf16[16,168,128]{2,1,0:T(8,128)(2,1)}), bf16[16,168,128]{2,1,0:T(8,128)(2,1)S(1)}, u32[]{:S(2)}, u32[]{:S(2)}) async-start(bf16[16,168,128]{2,1,0:T(8,128)(2,1)} %spread.1), calls=%async_computation.3 | async-start | bytes 1376256 | tf_op jit(solution)/shard_map/all_to_all | solution.py:399
  146.8 20.5 %all_gather.31.mine = bf16[2304,128]{1,0:T(8,128)(2,1)S(1)} all-gather(bf16[576,128]{1,0:T(8,128)(2,1)S(1)} %get-tuple-element.50), channel_id=1, replica_groups=mesh['zh'=4,'x'=4,'c'=2,'y'=8,'zl'=2] {'zh'}, dimensions={0}, use_global_device_ids=true | all-gather | bytes 737280 | tf_op jit(solution)/shard_map/all_gather | solution.py:398
  168.5 10.5 %all-to-all-start.4 = ((f32[32,1,72]{2,1,0:T(1,128)}), f32[32,1,72]{2,1,0:T(1,128)S(1)}, u32[]{:S(2)}, u32[]{:S(2)}) async-start(f32[32,1,72]{2,1,0:T(1,128)} %bitcast.18), calls=%async_computation.4 | async-start | bytes 32768 | tf_op jit(solution)/shard_map/all_to_all | solution.py:407
  183.3 3.4 %all-to-all-done.4 = f32[32,1,72]{2,1,0:T(1,128)S(1)} async-done(((f32[32,1,72]{2,1,0:T(1,128)}), f32[32,1,72]{2,1,0:T(1,128)S(1)}, u32[]{:S(2)}, u32[]{:S(2)}) %all-to-all-start.4) | async-done | bytes 9248 | tf_op jit(solution)/shard_map/all_to_all | solution.py:407
  (92 shorter events, 30.7 us)
Async XLA Ops:
  2.3 15.0 %collective-permute-start = (bf16[144,256]{1,0:T(8,128)(2,1)S(1)}, bf16[144,256]{1,0:T(8,128)(2,1)S(1)}, u32[]{:S(2)}, u32[]{:S(2)}) collective-permute-start(bf16[144,256]{1,0:T(8,128)(2,1)S(1)} %get-tuple-element.61), channel_id=1, source_target_pairs={{0,16},{16,0},{1,17},{17,1},{2,18},{18,2},{3,19},{19,3},{4,20},{20... | collective-permute-start | bytes 221192 | tf_op jit(solution)/shard_map/ppermute | solution.py:320
  18.2 31.0 %all-to-all-start = ((bf16[8,144,290]{2,1,0:T(8,128)(2,1)}), bf16[8,144,290]{2,1,0:T(8,128)(2,1)S(1)}, u32[]{:S(2)}, u32[]{:S(2)}) async-start(bf16[8,144,290]{2,1,0:T(8,128)(2,1)} %broadcast_in_dim.29), calls=%async_computation | async-start | bytes 1769472 | tf_op jit(solution)/shard_map/all_to_all | solution.py:27
  42.6 15.0 %collective-permute-start.4 = (bf16[4,288,256]{2,1,0:T(8,128)(2,1)S(1)}, bf16[4,288,256]{2,1,0:T(8,128)(2,1)S(1)}, u32[]{:S(2)}, u32[]{:S(2)}) collective-permute-start(bf16[4,288,256]{2,1,0:T(8,128)(2,1)S(1)} %slice.48.own), channel_id=1, source_target_pairs={{96,0},{0,32},{32,64},{64,96},{97,1},{1,33},{33,65},{65,97},{98,2}... | collective-permute-start | bytes 1769480 | tf_op jit(solution)/shard_map/ppermute | solution.py:334
  45.8 14.5 %collective-permute-start.2 = (bf16[4,288,256]{2,1,0:T(8,128)(2,1)S(1)}, bf16[4,288,256]{2,1,0:T(8,128)(2,1)S(1)}, u32[]{:S(2)}, u32[]{:S(2)}) collective-permute-start(bf16[4,288,256]{2,1,0:T(8,128)(2,1)S(1)} %slice.48.own), channel_id=1, source_target_pairs={{32,0},{64,32},{96,64},{0,96},{33,1},{65,33},{97,65},{1,97},{34,2}... | collective-permute-start | bytes 1769480 | tf_op jit(solution)/shard_map/ppermute | solution.py:333
  49.2 20.3 %collective-permute-start.1 = (bf16[16,72,290]{2,1,0:T(8,128)(2,1)S(1)}, bf16[16,72,290]{2,1,0:T(8,128)(2,1)}, u32[]{:S(2)}, u32[]{:S(2)}) collective-permute-start(bf16[16,72,290]{2,1,0:T(8,128)(2,1)S(1)} %bitcast.24), channel_id=1, source_target_pairs={{0,16},{16,0},{1,17},{17,1},{2,18},{18,2},{3,19},{19,3},{4,20},{20... | collective-permute-start | bytes 2004488 | tf_op jit(solution)/shard_map/ppermute | solution.py:338
  57.6 8.1 %copy-start = (bf16[1024,128]{1,0:T(8,128)(2,1)S(1)}, bf16[1024,128]{1,0:T(8,128)(2,1)}, u32[]{:S(2)}) copy-start(bf16[1024,128]{1,0:T(8,128)(2,1)} %k_old.1) | copy-start | bytes 786436
  58.3 9.9 %collective-permute-start.5 = (bf16[2,288,256]{2,1,0:T(8,128)(2,1)}, bf16[2,288,256]{2,1,0:T(8,128)(2,1)}, u32[]{:S(2)}, u32[]{:S(2)}) collective-permute-start(bf16[2,288,256]{2,1,0:T(8,128)(2,1)} %slice.50), channel_id=1, source_target_pairs={{96,0},{0,32},{32,64},{64,96},{97,1},{1,33},{33,65},{65,97},{98,2}... | collective-permute-start | bytes 884744 | tf_op jit(solution)/shard_map/ppermute | solution.py:336
  61.0 8.5 %collective-permute-start.3 = (bf16[2,288,256]{2,1,0:T(8,128)(2,1)}, bf16[2,288,256]{2,1,0:T(8,128)(2,1)}, u32[]{:S(2)}, u32[]{:S(2)}) collective-permute-start(bf16[2,288,256]{2,1,0:T(8,128)(2,1)} %slice.49), channel_id=1, source_target_pairs={{32,0},{64,32},{96,64},{0,96},{33,1},{65,33},{97,65},{1,97},{34,2}... | collective-permute-start | bytes 884744 | tf_op jit(solution)/shard_map/ppermute | solution.py:335
  71.7 15.9 %copy-start.2 = (bf16[4,144,256]{2,1,0:T(8,128)(2,1)S(1)}, bf16[4,144,256]{2,1,0:T(8,128)(2,1)}, u32[]{:S(2)}) copy-start(bf16[4,144,256]{2,1,0:T(8,128)(2,1)} %slice.51.own) | copy-start | bytes 884740
  72.6 25.9 %all-to-all-start.1 = ((bf16[16,144,128]{2,1,0:T(8,128)(2,1)}), bf16[16,144,128]{2,1,0:T(8,128)(2,1)S(1)}, u32[]{:S(2)}, u32[]{:S(2)}) async-start(bf16[16,144,128]{2,1,0:T(8,128)(2,1)} %broadcast_in_dim.54), calls=%async_computation.1 | async-start | bytes 1179648 | tf_op jit(solution)/shard_map/all_to_all | solution.py:27
  79.4 19.2 %collective-permute-start.6 = (bf16[2048,128]{1,0:T(8,128)(2,1)S(1)}, bf16[2048,128]{1,0:T(8,128)(2,1)S(1)}, u32[]{:S(2)}, u32[]{:S(2)}) collective-permute-start(bf16[2048,128]{1,0:T(8,128)(2,1)S(1)} %copy-done.4), channel_id=1, source_target_pairs={{0,16},{16,0},{1,17},{17,1},{2,18},{18,2},{3,19},{19,3},{4,20},{20... | collective-permute-start | bytes 1572872 | tf_op jit(solution)/shard_map/ppermute | solution.py:371
  87.6 16.6 %collective-permute-start.9 = (bf16[4,144,256]{2,1,0:T(8,128)(2,1)S(1)}, bf16[4,144,256]{2,1,0:T(8,128)(2,1)S(1)}, u32[]{:S(2)}, u32[]{:S(2)}) collective-permute-start(bf16[4,144,256]{2,1,0:T(8,128)(2,1)S(1)} %copy-done.2), channel_id=1, source_target_pairs={{96,0},{0,32},{32,64},{64,96},{97,1},{1,33},{33,65},{65,97},{98,2}... | collective-permute-start | bytes 884744 | tf_op jit(solution)/shard_map/ppermute | solution.py:373
  91.2 13.1 %collective-permute-start.8 = (bf16[4,144,256]{2,1,0:T(8,128)(2,1)S(1)}, bf16[4,144,256]{2,1,0:T(8,128)(2,1)S(1)}, u32[]{:S(2)}, u32[]{:S(2)}) collective-permute-start(bf16[4,144,256]{2,1,0:T(8,128)(2,1)S(1)} %copy-done.2), channel_id=1, source_target_pairs={{32,0},{64,32},{96,64},{0,96},{33,1},{65,33},{97,65},{1,97},{34,2}... | collective-permute-start | bytes 884744 | tf_op jit(solution)/shard_map/ppermute | solution.py:372
  96.2 8.0 %collective-permute-start.7 = (bf16[2,144,128]{2,1,0:T(8,128)(2,1)S(1)}, bf16[2,144,128]{2,1,0:T(8,128)(2,1)S(1)}, u32[]{:S(2)}, u32[]{:S(2)}) collective-permute-start(bf16[2,144,128]{2,1,0:T(8,128)(2,1)S(1)} %bitcast.33), channel_id=1, source_target_pairs={{0,32},{32,0},{64,96},{96,64},{1,33},{33,1},{65,97},{97,65},{2,34}... | collective-permute-start | bytes 221192 | tf_op jit(solution)/shard_map/ppermute | solution.py:375
  104.3 22.5 %all-to-all-start.2 = ((bf16[16,160,128]{2,1,0:T(8,128)(2,1)}), bf16[16,160,128]{2,1,0:T(8,128)(2,1)S(1)}, u32[]{:S(2)}, u32[]{:S(2)}) async-start(bf16[16,160,128]{2,1,0:T(8,128)(2,1)} %bitcast.13), calls=%async_computation.2 | async-start | bytes 1310720 | tf_op jit(solution)/shard_map/all_to_all | solution.py:392
  112.0 11.9 %collective-permute-start.10 = (bf16[2,2,144,128]{3,2,1,0:T(8,128)(2,1)S(1)}, bf16[2,2,144,128]{3,2,1,0:T(8,128)(2,1)S(1)}, u32[]{:S(2)}, u32[]{:S(2)}) collective-permute-start(bf16[2,2,144,128]{3,2,1,0:T(8,128)(2,1)S(1)} %pad_maximum_fusion.4.near), channel_id=1, source_target_pairs={{0,64},{32,96},{64,0},{96,32},{1,65},{33,97},{65,1},{97,33},{2,66}... | collective-permute-start | bytes 442376 | tf_op jit(solution)/shard_map/ppermute | solution.py:383
  116.8 15.8 %collective-permute-start.12 = (bf16[2,144,256]{2,1,0:T(8,128)(2,1)S(1)}, bf16[2,144,256]{2,1,0:T(8,128)(2,1)S(1)}, u32[]{:S(2)}, u32[]{:S(2)}) collective-permute-start(bf16[2,144,256]{2,1,0:T(8,128)(2,1)S(1)} %slice.43), channel_id=1, source_target_pairs={{96,0},{0,32},{32,64},{64,96},{97,1},{1,33},{33,65},{65,97},{98,2}... | collective-permute-start | bytes 442376 | tf_op jit(solution)/shard_map/ppermute | solution.py:388
  119.0 13.6 %collective-permute-start.11 = (bf16[2,144,256]{2,1,0:T(8,128)(2,1)S(1)}, bf16[2,144,256]{2,1,0:T(8,128)(2,1)S(1)}, u32[]{:S(2)}, u32[]{:S(2)}) collective-permute-start(bf16[2,144,256]{2,1,0:T(8,128)(2,1)S(1)} %slice.42), channel_id=1, source_target_pairs={{32,0},{64,32},{96,64},{0,96},{33,1},{65,33},{97,65},{1,97},{34,2}... | collective-permute-start | bytes 442376 | tf_op jit(solution)/shard_map/ppermute | solution.py:387
  134.9 11.9 %copy-start.8 = (bf16[288]{0:T(512)(128)(2,1)S(1)}, bf16[288]{0:T(512)(128)(2,1)}, u32[]{:S(2)}) copy-start(bf16[288]{0:T(512)(128)(2,1)} %param.18) | copy-start | bytes 1732
  134.9 32.5 %all-to-all-start.3 = ((bf16[16,168,128]{2,1,0:T(8,128)(2,1)}), bf16[16,168,128]{2,1,0:T(8,128)(2,1)S(1)}, u32[]{:S(2)}, u32[]{:S(2)}) async-start(bf16[16,168,128]{2,1,0:T(8,128)(2,1)} %spread.1), calls=%async_computation.3 | async-start | bytes 1376256 | tf_op jit(solution)/shard_map/all_to_all | solution.py:399
  167.4 19.4 %copy-start.5 = (bf16[72,288]{1,0:T(8,128)(2,1)S(1)}, bf16[72,288]{1,0:T(8,128)(2,1)}, u32[]{:S(2)}) copy-start(bf16[72,288]{1,0:T(8,128)(2,1)} %param.12) | copy-start | bytes 124420
  168.5 18.2 %all-to-all-start.4 = ((f32[32,1,72]{2,1,0:T(1,128)}), f32[32,1,72]{2,1,0:T(1,128)S(1)}, u32[]{:S(2)}, u32[]{:S(2)}) async-start(f32[32,1,72]{2,1,0:T(1,128)} %bitcast.18), calls=%async_computation.4 | async-start | bytes 32768 | tf_op jit(solution)/shard_map/all_to_all | solution.py:407
  179.0 7.8 %collective-permute-start.13 = (f32[72,144]{1,0:T(8,128)S(1)}, f32[72,144]{1,0:T(8,128)S(1)}, u32[]{:S(2)}, u32[]{:S(2)}) collective-permute-start(f32[72,144]{1,0:T(8,128)S(1)} %fusion.11), channel_id=1, source_target_pairs={{0,16},{16,0},{1,17},{17,1},{2,18},{18,2},{3,19},{19,3},{4,20},{20... | collective-permute-start | bytes 124424 | tf_op jit(solution)/shard_map/ppermute | solution.py:412
  181.1 6.4 %collective-permute-start.14 = (bf16[2304,128]{1,0:T(8,128)(2,1)S(1)}, bf16[2304,128]{1,0:T(8,128)(2,1)S(1)}, u32[]{:S(2)}, u32[]{:S(2)}) collective-permute-start(bf16[2304,128]{1,0:T(8,128)(2,1)S(1)} %all_gather.31.mine), channel_id=1, source_target_pairs={{0,16},{16,0},{1,17},{17,1},{2,18},{18,2},{3,19},{19,3},{4,20},{20... | collective-permute-start | bytes 1769480 | tf_op jit(solution)/shard_map/ppermute | solution.py:408
  (7 other events, 45.9 us)
